TPU v7x, 256 devices: a whole 4x4x8 slice. The times are simulated.
256 devices in a mesh: slab: 2 (over z_lo), freq: 8 (over y, core), energy: 16 (over x, z_hi).
Axes of the slice: x: 4, y: 4, z: 8 (z_hi: 4, z_lo: 2; z = z_hi * 2 + z_lo), core: 2. Of those that a mesh axis runs over, the one named last changes fastest.
Arguments:
- lesser: bfloat16 [32, 4, 2, 512, 512], P('energy', 'slab'), may hold values from -6 to 6
- retarded: bfloat16 [32, 4, 2, 512, 512], P('energy', 'slab'), may hold values from -0.25 to 0.25
- coupling: bfloat16 [16, 512, 512], P('freq'), may hold values from -0.125 to 0.125
- occupations: float32 [16], P('freq'), may hold values from 0.1 to 3
- offsets: int32 [16], P('freq'), may hold values from 1 to 2
- intersection: float32 [4], P('slab'), may hold values from 0.2 to 0.6
Outputs:
- updated: float32 [32, 4, 2, 512, 512], P('energy', 'slab', None, 'freq')
All inputs are finite; a program needn't handle non-finite values.
Results may differ from a plain program's by a relative error of at most 0.017.
Values may be sent and summed in bfloat16 or wider, within the bound.
No kernel may reach another device: no remote copies, remote signals or barrier semaphores. Data moves between devices by JAX's collectives and lax.ppermute only.
A program may use at most 128 MiB of HBM per device.

v0:
```python
import jax
import jax.numpy as jnp
from jax import lax
from jax.sharding import PartitionSpec as P

NO = 512
OFFMAX = 2


def with_halo(block, sides, width):
    for axis, dim in sides:
        count = lax.axis_size(axis)
        forward = [(i, i + 1) for i in range(count - 1)]
        backward = [(target, source) for source, target in forward]
        low = lax.ppermute(
            lax.slice_in_dim(block, block.shape[dim] - width, None, axis=dim), axis, forward
        )
        high = lax.ppermute(lax.slice_in_dim(block, 0, width, axis=dim), axis, backward)
        block = jnp.concatenate([low, block, high], axis=dim)
    return block


def side_by_side(arrays, axis, dim, along):
    ends, at = ([], 0)
    for a in arrays[:-1]:
        at += a.shape[along]
        ends.append(at)
    both = jnp.concatenate(arrays, axis=along)
    return tuple(jnp.split(lax.all_gather(both, axis, axis=dim, tiled=True), ends, axis=along))


def shards(lesser, retarded, coupling, occupations, offsets, intersection):
    freq_count = lax.axis_size("freq")
    row_count = NO // freq_count
    row_first = lax.axis_index("freq") * row_count
    own_rows = lax.dynamic_slice_in_dim(lesser, row_first, row_count, 3)
    extended = with_halo(own_rows, (("energy", 0),), OFFMAX)
    lower_rim, upper_rim = side_by_side(
        (extended[:OFFMAX], extended[extended.shape[0] - OFFMAX :]), "freq", 3, 0
    )
    padded = jnp.concatenate([lower_rim, lesser, upper_rim], axis=0)
    energy_count = lesser.shape[0]
    positions = jnp.arange(energy_count, dtype=jnp.int32)[None, :] + OFFMAX
    lower_green = jnp.take(padded, positions - offsets[:, None], axis=0)
    upper_green = jnp.take(padded, positions + offsets[:, None], axis=0)
    scale = occupations[:, None, None, None, None, None]
    mixture = (
        scale * lower_green.astype(jnp.float32) + (scale + 1.0) * upper_green.astype(jnp.float32)
    ).astype(jnp.bfloat16)
    real_green = retarded[:, :, 0]
    imag_green = retarded[:, :, 1]
    real_rows = lax.dynamic_slice_in_dim(real_green, row_first, row_count, 2)
    imag_rows = lax.dynamic_slice_in_dim(imag_green, row_first, row_count, 2)
    left_product = jnp.einsum(
        "fri,fescij->fescrj", coupling, mixture, preferred_element_type=jnp.float32
    ).astype(jnp.bfloat16)
    self_energy = lax.psum_scatter(
        jnp.einsum(
            "fescrj,fkj->resck", left_product, coupling, preferred_element_type=jnp.float32
        ).astype(jnp.bfloat16),
        "freq",
        scatter_dimension=0,
        tiled=True,
    )
    beside_all = with_halo(self_energy, (("slab", 2),), 1)
    beside = beside_all[:, :, :-2].astype(jnp.float32) + beside_all[:, :, 2:].astype(jnp.float32)
    total = self_energy.astype(jnp.float32) + intersection[None, None, :, None, None] * beside
    combined = total.astype(jnp.bfloat16)
    real_self = combined[:, :, :, 0]
    imag_self = combined[:, :, :, 1]

    def by_transpose(left_side, right_side):
        return jnp.einsum(
            "resj,eskj->resk", left_side, right_side, preferred_element_type=jnp.float32
        )

    real_part = by_transpose(real_self, real_green) + by_transpose(imag_self, imag_green)
    imag_part = by_transpose(imag_self, real_green) - by_transpose(real_self, imag_green)
    product = jnp.stack([real_part, imag_part], axis=3).astype(jnp.bfloat16)
    y_piece = lax.all_gather(product, "freq", axis=0, tiled=True)
    real_piece = y_piece[:, :, :, 0]
    imag_piece = y_piece[:, :, :, 1]

    def plain_product(left_side, right_side):
        return jnp.einsum(
            "esrm,mesk->esrk", left_side, right_side, preferred_element_type=jnp.float32
        )

    out_real = plain_product(real_rows, real_piece) - plain_product(imag_rows, imag_piece)
    out_imag = plain_product(real_rows, imag_piece) + plain_product(imag_rows, real_piece)
    return jnp.stack([out_real, out_imag], axis=2)


def solution(mesh):
    return jax.shard_map(
        shards,
        mesh=mesh,
        in_specs=(
            P("energy", "slab", None, None, None),
            P("energy", "slab", None, None, None),
            P("freq", None, None),
            P("freq"),
            P("freq"),
            P("slab"),
        ),
        out_specs=P("energy", "slab", None, "freq", None),
        check_vma=False,
    )
```

profile of v0, /device:TPU:38, one launch (start us, length us, event | category | flops | bytes accessed | tf_op | source)
XLA Modules:
  0.0 256.2 jit_solution(18127753419018629902)
XLA Ops:
  6.6 1.2 constant_dynamic-slice_fusion
  7.7 5.2 %collective-permute-start = (bf16[2,2,2,64,512]{4,3,2,1,0:T(8,128)(2,1)S(1)}, bf16[2,2,2,64,512]{4,3,2,1,0:T(8,128)(2,1)S(1)}, u32[]{:S(2)}, u32[]{:S(2)}) collective-permute-start(bf16[2,2,2,64,512]{4,3,2,1,0:T(8,128)(2,1)S(1)} %constant_dynamic-slice_fusion), channel_id=1, source_target_pairs={{0,1},{1,2},{2,3},{3,4},{4,5},{5,6},{6,7},{7,8},{8,9},{9,10},{10,1... | collective-permute-start | bytes 1572872 | tf_op jit(solution)/shard_map/ppermute | solution.py:15
  12.9 4.3 %collective-permute-start.1 = (bf16[2,2,2,64,512]{4,3,2,1,0:T(8,128)(2,1)S(1)}, bf16[2,2,2,64,512]{4,3,2,1,0:T(8,128)(2,1)S(1)}, u32[]{:S(2)}, u32[]{:S(2)}) collective-permute-start(bf16[2,2,2,64,512]{4,3,2,1,0:T(8,128)(2,1)S(1)} %constant_dynamic-slice_fusion), channel_id=1, source_target_pairs={{1,0},{2,1},{3,2},{4,3},{5,4},{6,5},{7,6},{8,7},{9,8},{10,9},{11,1... | collective-permute-start | bytes 1572872 | tf_op jit(solution)/shard_map/ppermute | solution.py:18
  17.2 21.2 %collective-permute-done = bf16[2,2,2,64,512]{4,3,2,1,0:T(8,128)(2,1)S(1)} collective-permute-done((bf16[2,2,2,64,512]{4,3,2,1,0:T(8,128)(2,1)S(1)}, bf16[2,2,2,64,512]{4,3,2,1,0:T(8,128)(2,1)S(1)}, u32[]{:S(2)}, u32[]{:S(2)}) %collective-permute-start) | collective-permute-done | bytes 524320 | tf_op jit(solution)/shard_map/ppermute | solution.py:15
  38.5 1.1 pad_maximum_fusion.1
  40.0 54.9 %all-gather.3.cloned.1.call-done = bf16[4,2,2,512,512]{4,3,2,1,0:T(8,128)(2,1)} async-done(((bf16[4,2,2,64,512]{4,3,2,1,0:T(8,128)(2,1)}), bf16[4,2,2,512,512]{4,3,2,1,0:T(8,128)(2,1)}) %all-gather.3.cloned.1.call-update) | async-done | bytes 8388624 | tf_op jit(solution)/shard_map/all_gather | solution.py:29
  94.9 4.0 %fusion.67 = (bf16[2,2,2,512,512]{4,3,2,1,0:T(8,128)(2,1)S(1)}, bf16[2,2,2,512,512]{4,3,2,1,0:T(8,128)(2,1)S(1)}) fusion(bf16[4,2,2,512,512]{4,3,2,1,0:T(8,128)(2,1)} %all-gather.3.cloned.1.call-done), kind=kLoop, calls=%fused_computation.76 | loop fusion | bytes 16777216 | tf_op jit(solution)/shard_map/split | solution.py:29
  99.6 7.0 %pad_maximum_fusion = bf16[6,2,2,512,512]{4,3,2,1,0:T(8,128)(2,1)S(1)} fusion(bf16[2,2,2,512,512]{4,3,2,1,0:T(8,128)(2,1)S(1)} %get-tuple-element.9, bf16[2,2,2,512,512]{4,3,2,1,0:T(8,128)(2,1)S(1)} %copy-done.4, bf16[2,2,2,512,512]{4,3,2,1,0:T(8,128)(2,1)S(1)} %get-tuple-element.8), kind=kLoop, calls=%fused_computation.5 | loop fusion | flops 12582912 | bytes 25165824 | tf_op jit(solution)/shard_map/concatenate | solution.py:41
  106.6 4.9 %fusion.66 = (bf16[6,2,2,256,512]{4,3,2,1,0:T(8,128)(2,1)}, bf16[6,2,2,256,512]{4,3,2,1,0:T(8,128)(2,1)}) fusion(bf16[6,2,2,512,512]{4,3,2,1,0:T(8,128)(2,1)S(1)} %pad_maximum_fusion), kind=kLoop, calls=%fused_computation.75 | loop fusion | bytes 25165824 | tf_op jit(solution)/shard_map/jit(_take)/gather | solution.py:44
  111.5 5.5 %gather_fusion = bf16[4,2,2,256,512]{4,3,2,1,0:T(8,128)(2,1)} fusion(bf16[6,2,2,256,512]{4,3,2,1,0:T(8,128)(2,1)} %get-tuple-element.6, s32[1024]{0:T(1024)S(1)} %pad_clamp_fusion.1), kind=kCustom, calls=%fused_computation.clone | custom fusion | bytes 8388624 | tf_op jit(solution)/shard_map/jit(_take)/gather | solution.py:44
  117.0 5.5 %gather_fusion.1 = bf16[4,2,2,256,512]{4,3,2,1,0:T(8,128)(2,1)} fusion(bf16[6,2,2,256,512]{4,3,2,1,0:T(8,128)(2,1)} %get-tuple-element.7, s32[1024]{0:T(1024)S(1)} %pad_clamp_fusion.1), kind=kCustom, calls=%fused_computation.1.clone | custom fusion | bytes 8388624 | tf_op jit(solution)/shard_map/jit(_take)/gather | solution.py:44
  122.6 5.6 %gather_fusion.2 = bf16[4,2,2,256,512]{4,3,2,1,0:T(8,128)(2,1)} fusion(bf16[6,2,2,256,512]{4,3,2,1,0:T(8,128)(2,1)} %get-tuple-element.6, s32[1024]{0:T(1024)S(1)} %pad_clamp_fusion), kind=kCustom, calls=%fused_computation.2.clone | custom fusion | bytes 8388624 | tf_op jit(solution)/shard_map/jit(_take)/gather | solution.py:45
  128.2 5.7 %gather_fusion.3 = bf16[4,2,2,256,512]{4,3,2,1,0:T(8,128)(2,1)} fusion(bf16[6,2,2,256,512]{4,3,2,1,0:T(8,128)(2,1)} %get-tuple-element.7, s32[1024]{0:T(1024)S(1)} %pad_clamp_fusion), kind=kCustom, calls=%fused_computation.3.clone | custom fusion | bytes 8388624 | tf_op jit(solution)/shard_map/jit(_take)/gather | solution.py:45
  133.8 13.8 %fusion.9 = bf16[512,2,2,2,512]{4,0,3,2,1:T(8,128)(2,1)} fusion(bf16[2,512,512]{2,1,0:T(8,128)(2,1)S(1)} %copy-done, bf16[2,2,2,2,256,512]{5,4,3,2,1,0:T(8,128)(2,1)} %bitcast.97, bf16[2,2,2,2,256,512]{5,4,3,2,1,0:T(8,128)(2,1)} %bitcast.96, bf16[2,2,2,2,256,512]{5,4,3,2,1,0:T(8,128)(2,1)} %bitcast.99, bf16[2,2,2,2,256,512]{5,4,3,2,1,0:T(8,128)(2,1)} %bitcast.98, ...), kind=kOutput, calls=%fused_computation.14 | convolution fusion | flops 8663334912 | bytes 22020120 | tf_op jit(solution)/shard_map/fescrj,fkj->resck/dot_general | solution.py:58
  147.7 40.7 %reduce-scatter.2.cloned.1.call-done = bf16[64,2,2,2,512]{4,0,3,2,1:T(8,128)(2,1)} async-done(((bf16[512,2,2,2,512]{4,0,3,2,1:T(8,128)(2,1)}), bf16[64,2,2,2,512]{4,0,3,2,1:T(8,128)(2,1)}) %reduce-scatter.2.cloned.1.call-update) | async-done | bytes 524304 | tf_op jit(solution)/shard_map/reduce_scatter | solution.py:57
  188.4 1.2 fusion.68
  189.6 1.4 collective-permute-start.2
  191.1 4.6 %collective-permute-start.3 = (bf16[64,2,1,2,512]{4,0,3,2,1:T(8,128)(2,1)S(1)}, bf16[64,2,1,2,512]{4,0,3,2,1:T(8,128)(2,1)S(1)}, u32[]{:S(2)}, u32[]{:S(2)}) collective-permute-start(bf16[64,2,1,2,512]{4,0,3,2,1:T(8,128)(2,1)S(1)} %get-tuple-element.13), channel_id=1, source_target_pairs={{128,0},{129,1},{130,2},{131,3},{132,4},{133,5},{134,6},{135,7},{1... | collective-permute-start | bytes 786440 | tf_op jit(solution)/shard_map/ppermute | solution.py:18
  195.6 2.4 collective-permute-done.2
  198.0 1.5 collective-permute-done.3
  199.5 1.5 add_convert_fusion.1
  201.0 2.3 fusion.16
  203.3 0.8 fusion.14
  204.1 0.8 fusion.46
  204.8 0.8 fusion.49
  205.6 0.8 pad_maximum_fusion.5
  206.5 4.0 %slice_bitcast_fusion.7 = (bf16[2,2,1,512,512]{4,3,1,0,2:T(8,128)(2,1)S(1)}, bf16[2,2,1,512,512]{4,3,1,0,2:T(8,128)(2,1)}) fusion(bf16[2,2,2,512,512]{4,3,2,1,0:T(8,128)(2,1)} %param.9), kind=kLoop, calls=%fused_computation.34 | loop fusion | bytes 8388608
  210.4 31.7 %all-gather.5.cloned.1.call-done = bf16[512,2,2,2,512]{4,0,2,1,3:T(8,128)(2,1)} async-done(((bf16[64,2,2,2,512]{4,0,2,1,3:T(8,128)(2,1)}), bf16[512,2,2,2,512]{4,0,2,1,3:T(8,128)(2,1)}) %all-gather.5.cloned.1.call-update) | async-done | bytes 4194320 | tf_op jit(solution)/shard_map/all_gather | solution.py:80
  242.1 2.2 fusion.23
  244.3 2.2 fusion.22
  246.5 1.5 fusion.31
  248.6 1.0 copy.9
  (33 shorter events, 1.7 us)
Async XLA Ops:
  6.5 127.3 %copy-start = (bf16[2,512,512]{2,1,0:T(8,128)(2,1)S(1)}, bf16[2,512,512]{2,1,0:T(8,128)(2,1)}, u32[]{:S(2)}) copy-start(bf16[2,512,512]{2,1,0:T(8,128)(2,1)} %param.10) | copy-start | bytes 3145732
  6.5 33.1 %copy-start.5 = (s32[2]{0:T(128)S(1)}, s32[2]{0:T(128)}, u32[]{:S(2)}) copy-start(s32[2]{0:T(128)} %param.12) | copy-start | bytes 28
  6.5 33.3 %copy-start.7 = (f32[2]{0:T(128)S(1)}, f32[2]{0:T(128)}, u32[]{:S(2)}) copy-start(f32[2]{0:T(128)} %param.11) | copy-start | bytes 28
  6.5 88.4 %all-gather.3.cloned.1.call-start = ((), (), s32[]{:S(2)}) async-start(), calls=%async_computation.1 | async-start | bytes 9437184 | tf_op jit(solution)/shard_map/all_gather | solution.py:29
  7.7 30.7 %collective-permute-start = (bf16[2,2,2,64,512]{4,3,2,1,0:T(8,128)(2,1)S(1)}, bf16[2,2,2,64,512]{4,3,2,1,0:T(8,128)(2,1)S(1)}, u32[]{:S(2)}, u32[]{:S(2)}) collective-permute-start(bf16[2,2,2,64,512]{4,3,2,1,0:T(8,128)(2,1)S(1)} %constant_dynamic-slice_fusion), channel_id=1, source_target_pairs={{0,1},{1,2},{2,3},{3,4},{4,5},{5,6},{6,7},{7,8},{8,9},{9,10},{10,1... | collective-permute-start | bytes 1572872 | tf_op jit(solution)/shard_map/ppermute | solution.py:15
  12.9 25.5 %collective-permute-start.1 = (bf16[2,2,2,64,512]{4,3,2,1,0:T(8,128)(2,1)S(1)}, bf16[2,2,2,64,512]{4,3,2,1,0:T(8,128)(2,1)S(1)}, u32[]{:S(2)}, u32[]{:S(2)}) collective-permute-start(bf16[2,2,2,64,512]{4,3,2,1,0:T(8,128)(2,1)S(1)} %constant_dynamic-slice_fusion), channel_id=1, source_target_pairs={{1,0},{2,1},{3,2},{4,3},{5,4},{6,5},{7,6},{8,7},{9,8},{10,9},{11,1... | collective-permute-start | bytes 1572872 | tf_op jit(solution)/shard_map/ppermute | solution.py:18
  39.5 148.9 %reduce-scatter.2.cloned.1.call-start = ((), (), s32[]{:S(2)}) async-start(), calls=%async_computation.2 | async-start | bytes 4718592 | tf_op jit(solution)/shard_map/reduce_scatter | solution.py:57
  94.9 4.7 %copy-start.4 = (bf16[2,2,2,512,512]{4,3,2,1,0:T(8,128)(2,1)S(1)}, bf16[2,2,2,512,512]{4,3,2,1,0:T(8,128)(2,1)}, u32[]{:S(2)}) copy-start(bf16[2,2,2,512,512]{4,3,2,1,0:T(8,128)(2,1)} %param.8) | copy-start | bytes 12582916
  147.6 51.9 %copy-start.6 = (f32[2]{0:T(128)S(1)}, f32[2]{0:T(128)}, u32[]{:S(2)}) copy-start(f32[2]{0:T(128)} %param.13) | copy-start | bytes 28
  147.7 94.5 %all-gather.5.cloned.1.call-start = ((), (), s32[]{:S(2)}) async-start(), calls=%async_computation.3 | async-start | bytes 4718592 | tf_op jit(solution)/shard_map/all_gather | solution.py:80
  188.4 14.9 %copy-start.2 = (bf16[2,2,2,512,512]{4,3,2,1,0:T(8,128)(2,1)S(1)}, bf16[2,2,2,512,512]{4,3,2,1,0:T(8,128)(2,1)}, u32[]{:S(2)}) copy-start(bf16[2,2,2,512,512]{4,3,2,1,0:T(8,128)(2,1)} %param.9) | copy-start | bytes 12582916
  189.6 8.4 %collective-permute-start.2 = (bf16[64,2,1,2,512]{4,0,3,2,1:T(8,128)(2,1)S(1)}, bf16[64,2,1,2,512]{4,0,3,2,1:T(8,128)(2,1)S(1)}, u32[]{:S(2)}, u32[]{:S(2)}) collective-permute-start(bf16[64,2,1,2,512]{4,0,3,2,1:T(8,128)(2,1)S(1)} %get-tuple-element.12), channel_id=1, source_target_pairs={{0,128},{1,129},{2,130},{3,131},{4,132},{5,133},{6,134},{7,135},{8... | collective-permute-start | bytes 786440 | tf_op jit(solution)/shard_map/ppermute | solution.py:15
  191.1 8.4 %collective-permute-start.3 = (bf16[64,2,1,2,512]{4,0,3,2,1:T(8,128)(2,1)S(1)}, bf16[64,2,1,2,512]{4,0,3,2,1:T(8,128)(2,1)S(1)}, u32[]{:S(2)}, u32[]{:S(2)}) collective-permute-start(bf16[64,2,1,2,512]{4,0,3,2,1:T(8,128)(2,1)S(1)} %get-tuple-element.13), channel_id=1, source_target_pairs={{128,0},{129,1},{130,2},{131,3},{132,4},{133,5},{134,6},{135,7},{1... | collective-permute-start | bytes 786440 | tf_op jit(solution)/shard_map/ppermute | solution.py:18
  242.1 4.4 %copy-start.3 = (bf16[512,2,2,2,512]{4,0,2,1,3:T(8,128)(2,1)S(1)}, bf16[512,2,2,2,512]{4,0,2,1,3:T(8,128)(2,1)}, u32[]{:S(2)}) copy-start(bf16[512,2,2,2,512]{4,0,2,1,3:T(8,128)(2,1)} %all-gather.5.cloned.1.call-done) | copy-start | bytes 12582916
  246.5 3.2 %copy-start.1 = (bf16[2,512,512]{2,1,0:T(8,128)(2,1)S(1)}, bf16[2,512,512]{2,1,0:T(8,128)(2,1)}, u32[]{:S(2)}) copy-start(bf16[2,512,512]{2,1,0:T(8,128)(2,1)} %param.10) | copy-start | bytes 3145732
Sparse Core Ops, SparseCore 0:
  39.7 55.1 all-gather.2
  147.8 40.5 reduce-scatter.1
  206.6 35.4 all-gather.4
where the time goes:
time: 258 us; the launch traced here: 256 us
  waiting for transfers between devices  152 us (59%)
  local copies, waits for them, and re-layouts  39.5 us (15%)
  matrix products  24.8 us (10%)
  starting transfers between devices  15.6 us (6%)
  between operations  13.3 us (5%)
  other arithmetic  10.7 us (4%)
    all_gather x1, waiting for transfers between devices, side_by_side(): lax.all_gather(both, axis, axis=dim, tiled=True)  54.9 us
    reduce_scatter x1, waiting for transfers between devices, shards(): lax.psum_scatter(jnp.einsum('fescrj,fkj->resck', left_product, coupling,...  40.7 us
    all_gather x1, waiting for transfers between devices, shards(): y_piece = lax.all_gather(product, 'freq', axis=0, tiled=True)  31.7 us
    ppermute x2, waiting for transfers between devices, with_halo(): lax.ppermute(lax.slice_in_dim(block, block.shape[dim] - width, None, axis...  23.6 us
    gather x3, local copies, waits for them, and re-layouts, shards(): lower_green = jnp.take(padded, positions - offsets[:, None], axis=0)  16 us
    dot_general x1, matrix products, shards(): jnp.einsum('fescrj,fkj->resck', left_product, coupling, preferred_element...  13.8 us
    gather x2, local copies, waits for them, and re-layouts, shards(): upper_green = jnp.take(padded, positions + offsets[:, None], axis=0)  11.3 us
    ppermute x2, starting transfers between devices, with_halo(): lax.ppermute(lax.slice_in_dim(block, 0, width, axis=dim), axis, backward)  8.89 us
  transfers between devices with their start and end apart: 7, of which 6 were waited for; matrix products, arithmetic and copies ran while one was open for 2% of the time, Pallas kernels for 0%

commit v1 on v0

v1 whole, which is shorter than its diff:
```python
import functools
import jax
import jax.numpy as jnp
from jax import lax
from jax.experimental import pallas as pl
from jax.experimental.pallas import tpu as pltpu
from jax.sharding import PartitionSpec as P

NO = 512
ROWS = 64
F32 = jnp.float32
BF16 = jnp.bfloat16
MIB = 1 << 20


def any_spec():
    return pl.BlockSpec(memory_space=pl.ANY)


def smem_spec():
    return pl.BlockSpec(memory_space=pltpu.SMEM)


def vmem_spec():
    return pl.BlockSpec(memory_space=pltpu.VMEM)


def mul(a, b):
    return jnp.dot(a, b, preferred_element_type=F32)


def mul_t(a, b):
    return lax.dot_general(a, b, (((1,), (1,)), ((), ())), preferred_element_type=F32)


def sandwich_kernel(owners, first, last, place, table, lesser, g1, g2, g3, *rest):
    arrays = rest[: len(owners)]
    rest = rest[len(owners):]
    if not first:
        start, rest = rest[0], rest[1:]
    out, green, coup, acc, gsem, csem, asem = rest
    y, k, i, sl = place[0], place[1], place[2], place[3]
    copies = []
    for n, src in enumerate((lesser.at[1 - i, sl, k], g1, g2, g3)):
        copies.append(pltpu.make_async_copy(src, green.at[n], gsem.at[n]))
    for c in copies:
        c.start()
    moves, where = [], []
    for ref, (dy, dk, f0, count) in zip(arrays, owners):
        for t in range(count):
            n = len(moves)
            moves.append(pltpu.make_async_copy(ref.at[t], coup.at[n], csem.at[n]))
            moves[-1].start()
            where.append(2 * (2 * (y ^ dy) + (k ^ dk)) + f0 + t)
    if not first:
        begin = pltpu.make_async_copy(start, acc, asem.at[0])
        begin.start()
    for c in copies:
        c.wait()
    if not first:
        begin.wait()
    for n, f in enumerate(where):
        scale = table[0, f]
        far = table[1, f] > 1.5
        low = jnp.where(i == 0, jnp.where(far, 3, 1), jnp.where(far, 1, 0))
        high = jnp.where(i == 0, jnp.where(far, 2, 0), jnp.where(far, 3, 2))
        mixture = (
            scale * green[low].astype(F32) + (scale + 1.0) * green[high].astype(F32)
        ).astype(BF16)
        moves[n].wait()
        left = mul(coup[n], mixture).astype(BF16)
        term = mul_t(left, coup[n])
        if n == 0 and first:
            acc[...] = term
        elif n == len(where) - 1:
            out[...] = (acc[...] + term).astype(out.dtype)
        else:
            acc[...] += term


def sandwich(owners, place, table, lesser, greens, arrays, start, last):
    count = sum(o[3] for o in owners)
    first = start is None
    operands = [place, table, lesser, *greens, *arrays] + ([] if first else [start])
    flops = count * 4 * NO**3
    return pl.pallas_call(
        functools.partial(sandwich_kernel, owners, first, last),
        out_shape=jax.ShapeDtypeStruct((NO, NO), BF16 if last else F32),
        in_specs=[smem_spec(), smem_spec()] + [any_spec()] * (len(operands) - 2),
        out_specs=vmem_spec(),
        scratch_shapes=[
            pltpu.VMEM((4, NO, NO), BF16),
            pltpu.VMEM((count, NO, NO), BF16),
            pltpu.VMEM((NO, NO), F32),
            pltpu.SemaphoreType.DMA((4,)),
            pltpu.SemaphoreType.DMA((count,)),
            pltpu.SemaphoreType.DMA((1,)),
        ],
        compiler_params=pltpu.CompilerParams(vmem_limit_bytes=40 * MIB),
        cost_estimate=pl.CostEstimate(
            flops=flops, bytes_accessed=(count + 8) * NO * NO * 2, transcendentals=0
        ),
        name="sandwich_last" if last else "sandwich_first",
    )(*operands)


def update_kernel(place, own_c, other_c, retarded, own_out, out1, out2, out3, green, sem):
    y, k, i, sl = place[0], place[1], place[2], place[3]
    copy = pltpu.make_async_copy(retarded.at[i, sl], green, sem.at[0])
    copy.start()
    copy.wait()
    a, b = green[0], green[1]
    mine, other = own_c[...], other_c[...]
    real = jnp.where(k == 0, mine, other)
    imag = jnp.where(k == 0, other, mine)
    yr = (mul_t(real, a) + mul_t(imag, b)).astype(BF16)
    yi = (mul_t(imag, a) - mul_t(real, b)).astype(BF16)
    for dy, ref in ((0, own_out), (1, out1), (2, out2), (3, out3)):
        first = pl.multiple_of((2 * (y ^ dy) + k) * ROWS, ROWS)
        ar = green[0, pl.ds(first, ROWS), :]
        br = green[1, pl.ds(first, ROWS), :]
        ref[0] = (mul(ar, yr) - mul(br, yi)).astype(ref.dtype)
        ref[1] = (mul(ar, yi) + mul(br, yr)).astype(ref.dtype)


def update(place, own_c, other_c, retarded):
    piece = (2, ROWS, NO)
    return pl.pallas_call(
        update_kernel,
        out_shape=[jax.ShapeDtypeStruct(piece, F32)] + [jax.ShapeDtypeStruct(piece, BF16)] * 3,
        in_specs=[smem_spec(), vmem_spec(), vmem_spec(), any_spec()],
        out_specs=[vmem_spec()] * 4,
        scratch_shapes=[pltpu.VMEM((2, NO, NO), BF16), pltpu.SemaphoreType.DMA((1,))],
        compiler_params=pltpu.CompilerParams(vmem_limit_bytes=40 * MIB),
        cost_estimate=pl.CostEstimate(
            flops=12 * NO**3, bytes_accessed=5 * NO * NO * 2, transcendentals=0
        ),
        name="update",
    )(place, own_c, other_c, retarded)


def collect_kernel(place, own, p1, p2, p3, out):
    y, b = place[0], place[4]
    for dy, ref in ((0, own), (1, p1), (2, p2), (3, p3)):
        source = y ^ dy
        out[source // 2, (source % 2) ^ b] = ref[...].astype(F32)


def collect(place, pieces):
    return pl.pallas_call(
        collect_kernel,
        out_shape=jax.ShapeDtypeStruct((2, 2, 2, ROWS, NO), F32),
        in_specs=[smem_spec()] + [vmem_spec()] * 4,
        out_specs=vmem_spec(),
        compiler_params=pltpu.CompilerParams(vmem_limit_bytes=40 * MIB),
        name="collect",
    )(place, *pieces)


def shards(lesser, retarded, coupling, occupations, offsets, intersection):
    fr = lax.axis_index("freq")
    b = lax.axis_index("slab")
    y, k = fr // 2, fr % 2
    i, sl = y // 2, (y % 2) ^ b
    place = jnp.stack([y, k, i, sl, b]).astype(jnp.int32)

    def chip(x, dy):
        return lax.ppermute(x, "freq", [(d, d ^ (2 * dy)) for d in range(8)])

    def core(x):
        return lax.ppermute(x, "freq", [(d, d ^ 1) for d in range(8)])

    count = lax.axis_size("energy")
    up = [(e, e + 1) for e in range(count - 1)]
    down = [(t, s) for s, t in up]
    third = [
        (d * count + s, d * count + t) for d in range(8) for s, t in (up if d < 4 else down)
    ]
    g1 = lax.ppermute(lesser[1, sl, k], "energy", up)
    g2 = lax.ppermute(lesser[0, sl, k], "energy", down)
    g3 = lax.ppermute(lesser[i, sl, k], ("freq", "energy"), third)
    greens = (g1, g2, g3)
    table = jnp.stack([occupations, offsets.astype(F32)], axis=1)
    table = lax.all_gather(table, "freq", axis=0, tiled=True).T

    c1, c3 = chip(coupling, 1), chip(coupling, 3)
    q0 = chip(c3[0:1], 1)
    q1 = chip(c1[1:2], 3)
    s0, s1, s3 = core(coupling), core(c1), core(c3)
    r0, r1 = core(q0), core(q1)

    part = sandwich(
        [(0, 0, 0, 2), (0, 1, 0, 2), (1, 0, 0, 2), (3, 0, 0, 2), (1, 1, 0, 2), (3, 1, 0, 2)],
        place, table, lesser, greens, [coupling, s0, c1, c3, s1, s3], None, False,
    )
    own = sandwich(
        [(2, 0, 0, 1), (2, 0, 1, 1), (2, 1, 0, 1), (2, 1, 1, 1)],
        place, table, lesser, greens, [q0, q1, r0, r1], part, True,
    )
    inner = chip(own, 1)
    edge = [(s * 8 + d, (1 - s) * 8 + d) for s in range(2) for d in range(8) if (d // 2) % 2]
    outer = lax.ppermute(own, ("slab", "freq"), edge)
    combined = (
        own.astype(F32) + intersection[sl] * (inner.astype(F32) + outer.astype(F32))
    ).astype(BF16)
    mine, o1, o2, o3 = update(place, combined, core(combined), retarded)
    return collect(place, (mine, chip(o1, 1), chip(o2, 2), chip(o3, 3)))


def solution(mesh):
    return jax.shard_map(
        shards,
        mesh=mesh,
        in_specs=(
            P("energy", "slab", None, None, None),
            P("energy", "slab", None, None, None),
            P("freq", None, None),
            P("freq"),
            P("freq"),
            P("slab"),
        ),
        out_specs=P("energy", "slab", None, "freq", None),
        check_vma=False,
    )
```

time: 258 us -> 135 us (0.52)
  the two profiles are of different devices: /device:TPU:38 before, /device:TPU:1 now
where the time goes in v1:
time: 135 us
  starting transfers between devices  52.8 us (39%)
  waiting for transfers between devices  34 us (25%)
  Pallas kernels  20.4 us (15%)
  blocking collectives  18 us (13%)
  local copies, waits for them, and re-layouts  8.76 us (6%)
    ppermute x8, starting transfers between devices, chip(): return lax.ppermute(x, 'freq', [(d, d ^ 2 * dy) for d in range(8)])  31 us
    ppermute x8, waiting for transfers between devices, chip(): return lax.ppermute(x, 'freq', [(d, d ^ 2 * dy) for d in range(8)])  18.4 us
    all_gather x1, blocking collectives, shards(): table = lax.all_gather(table, 'freq', axis=0, tiled=True).T  18 us
    pallas_call x2, Pallas kernels, sandwich(): pl.pallas_call(functools.partial(sandwich_kernel, owners, first, last), o...  15.4 us
    ppermute x6, starting transfers between devices, core(): return lax.ppermute(x, 'freq', [(d, d ^ 1) for d in range(8)])  7.99 us
    ppermute x1, starting transfers between devices, shards(): g3 = lax.ppermute(lesser[i, sl, k], ('freq', 'energy'), third)  6.74 us
    ppermute x1, waiting for transfers between devices, shards(): g2 = lax.ppermute(lesser[0, sl, k], 'energy', down)  6.12 us
    ppermute x1, waiting for transfers between devices, shards(): g1 = lax.ppermute(lesser[1, sl, k], 'energy', up)  5.85 us
  transfers between devices with their start and end apart: 18, of which 8 were waited for; matrix products, arithmetic and copies ran while one was open for 4% of the time, Pallas kernels for 8%

profile of v1, /device:TPU:1, one launch (start us, length us, event | category | flops | bytes accessed | tf_op | source)
XLA Modules:
  0.0 135.0 jit_solution(766315801781688809)
XLA Ops:
  0.0 2.1 %collective-permute-start.5 = (bf16[2,512,512]{2,1,0:T(8,128)(2,1)}, bf16[2,512,512]{2,1,0:T(8,128)(2,1)}, u32[]{:S(2)}, u32[]{:S(2)}) collective-permute-start(bf16[2,512,512]{2,1,0:T(8,128)(2,1)} %rest_0_.1), channel_id=1, source_target_pairs={{0,32},{16,48},{32,0},{48,16},{64,96},{80,112},{96,64},{112,80},{1... | collective-permute-start | bytes 3145736 | tf_op jit(solution)/shard_map/ppermute | solution.py:168
  2.1 1.9 %collective-permute-start.3 = (bf16[2,512,512]{2,1,0:T(8,128)(2,1)}, bf16[2,512,512]{2,1,0:T(8,128)(2,1)}, u32[]{:S(2)}, u32[]{:S(2)}) collective-permute-start(bf16[2,512,512]{2,1,0:T(8,128)(2,1)} %rest_0_.1), channel_id=1, source_target_pairs={{0,96},{16,112},{32,64},{48,80},{64,32},{80,48},{96,0},{112,16},{1... | collective-permute-start | bytes 3145736 | tf_op jit(solution)/shard_map/ppermute | solution.py:168
  4.0 1.5 %dynamic-slice_bitcast_fusion = (bf16[512,512]{1,0:T(8,128)(2,1)S(1)}, bf16[512,512]{1,0:T(8,128)(2,1)S(1)}, bf16[512,512]{1,0:T(8,128)(2,1)S(1)}) fusion(bf16[2,2,2,512,512]{4,3,2,1,0:T(8,128)(2,1)} %lesser.3, s32[]{:T(128)S(6)} %select_n.38, s32[]{:T(128)S(6)} %select_n.36, s32[]{:T(128)S(6)} %select_n.37), kind=kLoop, calls=%fused_computation.1 | loop fusion | bytes 3145740 | tf_op jit(solution)/shard_map/squeeze | solution.py:181
  5.6 4.9 %collective-permute-start = (bf16[512,512]{1,0:T(8,128)(2,1)S(1)}, bf16[512,512]{1,0:T(8,128)(2,1)S(1)}, u32[]{:S(2)}, u32[]{:S(2)}) collective-permute-start(bf16[512,512]{1,0:T(8,128)(2,1)S(1)} %get-tuple-element.15), channel_id=1, source_target_pairs={{0,1},{1,2},{2,3},{3,4},{4,5},{5,6},{6,7},{7,8},{8,9},{9,10},{10,1... | collective-permute-start | bytes 1572872 | tf_op jit(solution)/shard_map/ppermute | solution.py:179
  10.5 1.3 collective-permute-start.1
  11.8 6.7 %collective-permute-start.2 = (bf16[512,512]{1,0:T(8,128)(2,1)S(1)}, bf16[512,512]{1,0:T(8,128)(2,1)S(1)}, u32[]{:S(2)}, u32[]{:S(2)}) collective-permute-start(bf16[512,512]{1,0:T(8,128)(2,1)S(1)} %get-tuple-element.13), channel_id=1, source_target_pairs={{0,1},{1,2},{2,3},{3,4},{4,5},{5,6},{6,7},{7,8},{8,9},{9,10},{10,1... | collective-permute-start | bytes 1572872 | tf_op jit(solution)/shard_map/ppermute | solution.py:181
  18.6 5.8 %collective-permute-done.g1 = bf16[512,512]{1,0:T(8,128)(2,1)S(1)} collective-permute-done((bf16[512,512]{1,0:T(8,128)(2,1)S(1)}, bf16[512,512]{1,0:T(8,128)(2,1)S(1)}, u32[]{:S(2)}, u32[]{:S(2)}) %collective-permute-start) | collective-permute-done | bytes 524320 | tf_op jit(solution)/shard_map/ppermute | solution.py:179
  24.4 5.7 %collective-permute-start.9 = (bf16[2,512,512]{2,1,0:T(8,128)(2,1)}, bf16[2,512,512]{2,1,0:T(8,128)(2,1)}, u32[]{:S(2)}, u32[]{:S(2)}) collective-permute-start(bf16[2,512,512]{2,1,0:T(8,128)(2,1)} %rest_0_.1), channel_id=1, source_target_pairs={{0,16},{16,0},{32,48},{48,32},{64,80},{80,64},{96,112},{112,96},{1... | collective-permute-start | bytes 3145736 | tf_op jit(solution)/shard_map/ppermute | solution.py:171
  30.2 0.5 collective-permute-start.11
  30.7 1.9 %slice.8 = bf16[1,512,512]{2,1,0:T(8,128)(2,1)} slice(bf16[2,512,512]{2,1,0:T(8,128)(2,1)} %collective-permute-done.3.rest_3_), slice={[0:1], [0:512], [0:512]} | slice | bytes 1048576 | tf_op jit(solution)/shard_map/slice | solution.py:187
  32.5 1.1 slice.9
  33.6 6.1 %collective-permute-done.1.g2 = bf16[512,512]{1,0:T(8,128)(2,1)S(1)} collective-permute-done((bf16[512,512]{1,0:T(8,128)(2,1)S(1)}, bf16[512,512]{1,0:T(8,128)(2,1)S(1)}, u32[]{:S(2)}, u32[]{:S(2)}) %collective-permute-start.1) | collective-permute-done | bytes 524320 | tf_op jit(solution)/shard_map/ppermute | solution.py:180
  40.0 2.2 %collective-permute-done.2.g3 = bf16[512,512]{1,0:T(8,128)(2,1)S(1)} collective-permute-done((bf16[512,512]{1,0:T(8,128)(2,1)S(1)}, bf16[512,512]{1,0:T(8,128)(2,1)S(1)}, u32[]{:S(2)}, u32[]{:S(2)}) %collective-permute-start.2) | collective-permute-done | bytes 524320 | tf_op jit(solution)/shard_map/ppermute | solution.py:181
  42.1 20.7 %collective-permute-start.6 = (bf16[1,512,512]{2,1,0:T(8,128)(2,1)S(1)}, bf16[1,512,512]{2,1,0:T(8,128)(2,1)S(1)}, u32[]{:S(2)}, u32[]{:S(2)}) collective-permute-start(bf16[1,512,512]{2,1,0:T(8,128)(2,1)S(1)} %slice.9), channel_id=1, source_target_pairs={{0,96},{16,112},{32,64},{48,80},{64,32},{80,48},{96,0},{112,16},{1... | collective-permute-start | bytes 1572872 | tf_op jit(solution)/shard_map/ppermute | solution.py:168
  63.0 18.0 %all-gather = f32[8,2,2]{2,1,0:T(2,128)S(1)} all-gather(f32[1,2,2]{2,1,0:T(2,128)S(1)} %bitcast.21), channel_id=1, replica_groups=mesh['slab'=2,'freq'=8,'energy'=16] {'freq'}, dimensions={0}, use_global_device_ids=true | all-gather | bytes 144 | tf_op jit(solution)/shard_map/all_gather | solution.py:184
  81.6 2.2 %copy-done = bf16[2,2,2,512,512]{4,3,2,1,0:T(8,128)(2,1)S(1)} copy-done((bf16[2,2,2,512,512]{4,3,2,1,0:T(8,128)(2,1)S(1)}, bf16[2,2,2,512,512]{4,3,2,1,0:T(8,128)(2,1)}, u32[]{:S(2)}) %copy-start) | copy-done | bytes 4194328
  83.8 1.2 copy-done.2
  85.1 10.8 %sandwich_first.1.rest_4_ = f32[512,512]{1,0:T(8,128)S(1)} custom-call(s32[5]{0:T(128)S(1)} %stack.32.place, f32[2,16]{1,0:T(2,128)S(1)} %bitcast.18, bf16[2,2,2,512,512]{4,3,2,1,0:T(8,128)(2,1)S(1)} %copy-done, bf16[512,512]{1,0:T(8,128)(2,1)S(1)} %collective-permute-done.g1, bf16[512,512]{1,0:T(8,128)(2,1)S(1)} %collective-permute-done.1.g2, ...), custom_call_target="tpu_custom_call" | custom-call | flops 6442450944 | bytes 10485760 | tf_op jit(solution)/shard_map/sandwich_first/pallas_call | solution.py:86
  95.9 4.6 %sandwich_last.1 = bf16[512,512]{1,0:T(8,128)(2,1)S(1)} custom-call(s32[5]{0:T(128)S(1)} %stack.32.place, f32[2,16]{1,0:T(2,128)S(1)} %bitcast.19, bf16[2,2,2,512,512]{4,3,2,1,0:T(8,128)(2,1)S(1)} %copy-done, bf16[512,512]{1,0:T(8,128)(2,1)S(1)} %collective-permute-done.g1, bf16[512,512]{1,0:T(8,128)(2,1)S(1)} %collective-permute-done.1.g2, ...), custom_call_target="tpu_custom_call" | custom-call | flops 2147483648 | bytes 6291456 | tf_op jit(solution)/shard_map/sandwich_last/pallas_call | solution.py:86
  100.6 0.9 collective-permute-start.13
  101.6 0.6 dynamic_slice.15
  102.1 11.7 %collective-permute-done.12 = bf16[512,512]{1,0:T(8,128)(2,1)S(1)} collective-permute-done((bf16[512,512]{1,0:T(8,128)(2,1)S(1)}, bf16[512,512]{1,0:T(8,128)(2,1)S(1)}, u32[]{:S(2)}, u32[]{:S(2)}) %collective-permute-start.12) | collective-permute-done | bytes 524320 | tf_op jit(solution)/shard_map/ppermute | solution.py:168
  113.8 0.9 add_convert_fusion.own_c
  114.7 1.2 collective-permute-start.14
  115.9 1.5 %collective-permute-done.14.other_c = bf16[512,512]{1,0:T(8,128)(2,1)S(1)} collective-permute-done((bf16[512,512]{1,0:T(8,128)(2,1)S(1)}, bf16[512,512]{1,0:T(8,128)(2,1)S(1)}, u32[]{:S(2)}, u32[]{:S(2)}) %collective-permute-start.14) | collective-permute-done | bytes 524320 | tf_op jit(solution)/shard_map/ppermute | solution.py:171
  117.5 3.4 %update.1 = (f32[2,64,512]{2,1,0:T(8,128)S(1)}, bf16[2,64,512]{2,1,0:T(8,128)(2,1)S(1)}, bf16[2,64,512]{2,1,0:T(8,128)(2,1)S(1)}, bf16[2,64,512]{2,1,0:T(8,128)(2,1)S(1)}) custom-call(s32[5]{0:T(128)S(1)} %stack.32.place, bf16[512,512]{1,0:T(8,128)(2,1)S(1)} %add_convert_fusion.own_c, bf16[512,512]{1,0:T(8,128)(2,1)S(1)} %collective-permute-done.14.other_c, ...), custom_call_target="tpu_custom_call" | custom-call | flops 1610612736 | bytes 2621440 | tf_op jit(solution)/shard_map/update/pallas_call | solution.py:128
  120.8 3.4 %collective-permute-start.15 = (bf16[2,64,512]{2,1,0:T(8,128)(2,1)S(1)}, bf16[2,64,512]{2,1,0:T(8,128)(2,1)S(1)}, u32[]{:S(2)}, u32[]{:S(2)}) collective-permute-start(bf16[2,64,512]{2,1,0:T(8,128)(2,1)S(1)} %get-tuple-element.10), channel_id=1, source_target_pairs={{0,32},{16,48},{32,0},{48,16},{64,96},{80,112},{96,64},{112,80},{1... | collective-permute-start | bytes 393224 | tf_op jit(solution)/shard_map/ppermute | solution.py:168
  124.3 2.5 %collective-permute-start.17 = (bf16[2,64,512]{2,1,0:T(8,128)(2,1)S(1)}, bf16[2,64,512]{2,1,0:T(8,128)(2,1)S(1)}, u32[]{:S(2)}, u32[]{:S(2)}) collective-permute-start(bf16[2,64,512]{2,1,0:T(8,128)(2,1)S(1)} %get-tuple-element.12), channel_id=1, source_target_pairs={{0,96},{16,112},{32,64},{48,80},{64,32},{80,48},{96,0},{112,16},{1... | collective-permute-start | bytes 393224 | tf_op jit(solution)/shard_map/ppermute | solution.py:168
  126.7 1.1 collective-permute-done.15.p1
  127.8 2.4 %collective-permute-done.16.p2 = bf16[2,64,512]{2,1,0:T(8,128)(2,1)S(1)} collective-permute-done((bf16[2,64,512]{2,1,0:T(8,128)(2,1)S(1)}, bf16[2,64,512]{2,1,0:T(8,128)(2,1)S(1)}, u32[]{:S(2)}, u32[]{:S(2)}) %collective-permute-start.16) | collective-permute-done | bytes 131104 | tf_op jit(solution)/shard_map/ppermute | solution.py:168
  130.2 3.2 %collective-permute-done.17.p3 = bf16[2,64,512]{2,1,0:T(8,128)(2,1)S(1)} collective-permute-done((bf16[2,64,512]{2,1,0:T(8,128)(2,1)S(1)}, bf16[2,64,512]{2,1,0:T(8,128)(2,1)S(1)}, u32[]{:S(2)}, u32[]{:S(2)}) %collective-permute-start.17) | collective-permute-done | bytes 131104 | tf_op jit(solution)/shard_map/ppermute | solution.py:168
  133.4 1.6 %collect.1 = f32[2,2,2,64,512]{4,3,2,1,0:T(8,128)} custom-call(s32[5]{0:T(128)S(1)} %stack.32.place, f32[2,64,512]{2,1,0:T(8,128)S(1)} %get-tuple-element.9.own, bf16[2,64,512]{2,1,0:T(8,128)(2,1)S(1)} %collective-permute-done.15.p1, bf16[2,64,512]{2,1,0:T(8,128)(2,1)S(1)} %collective-permute-done.16.p2, bf16[2,64,512]{2,1,0:T(8,128)(2,1)S(1)} %collective-permute-done.17.p3), custom_call_target="tpu_custom_call" | custom-call | tf_op jit(solution)/shard_map/collect/pallas_call | solution.py:150
  (31 shorter events, 1.2 us)
Async XLA Ops:
  0.0 62.9 %copy-start.4 = (s32[2]{0:T(128)S(1)}, s32[2]{0:T(128)}, u32[]{:S(2)}) copy-start(s32[2]{0:T(128)} %param.10) | copy-start | bytes 28
  0.0 62.9 %copy-start.3 = (f32[2]{0:T(128)S(1)}, f32[2]{0:T(128)}, u32[]{:S(2)}) copy-start(f32[2]{0:T(128)} %param.9) | copy-start | bytes 28
  0.0 30.2 %collective-permute-start.5 = (bf16[2,512,512]{2,1,0:T(8,128)(2,1)}, bf16[2,512,512]{2,1,0:T(8,128)(2,1)}, u32[]{:S(2)}, u32[]{:S(2)}) collective-permute-start(bf16[2,512,512]{2,1,0:T(8,128)(2,1)} %rest_0_.1), channel_id=1, source_target_pairs={{0,32},{16,48},{32,0},{48,16},{64,96},{80,112},{96,64},{112,80},{1... | collective-permute-start | bytes 3145736 | tf_op jit(solution)/shard_map/ppermute | solution.py:168
  2.1 28.0 %collective-permute-start.3 = (bf16[2,512,512]{2,1,0:T(8,128)(2,1)}, bf16[2,512,512]{2,1,0:T(8,128)(2,1)}, u32[]{:S(2)}, u32[]{:S(2)}) collective-permute-start(bf16[2,512,512]{2,1,0:T(8,128)(2,1)} %rest_0_.1), channel_id=1, source_target_pairs={{0,96},{16,112},{32,64},{48,80},{64,32},{80,48},{96,0},{112,16},{1... | collective-permute-start | bytes 3145736 | tf_op jit(solution)/shard_map/ppermute | solution.py:168
  5.6 18.8 %collective-permute-start = (bf16[512,512]{1,0:T(8,128)(2,1)S(1)}, bf16[512,512]{1,0:T(8,128)(2,1)S(1)}, u32[]{:S(2)}, u32[]{:S(2)}) collective-permute-start(bf16[512,512]{1,0:T(8,128)(2,1)S(1)} %get-tuple-element.15), channel_id=1, source_target_pairs={{0,1},{1,2},{2,3},{3,4},{4,5},{5,6},{6,7},{7,8},{8,9},{9,10},{10,1... | collective-permute-start | bytes 1572872 | tf_op jit(solution)/shard_map/ppermute | solution.py:179
  10.5 29.2 %collective-permute-start.1 = (bf16[512,512]{1,0:T(8,128)(2,1)S(1)}, bf16[512,512]{1,0:T(8,128)(2,1)S(1)}, u32[]{:S(2)}, u32[]{:S(2)}) collective-permute-start(bf16[512,512]{1,0:T(8,128)(2,1)S(1)} %get-tuple-element.14), channel_id=1, source_target_pairs={{1,0},{2,1},{3,2},{4,3},{5,4},{6,5},{7,6},{8,7},{9,8},{10,9},{11,1... | collective-permute-start | bytes 1572872 | tf_op jit(solution)/shard_map/ppermute | solution.py:180
  11.8 30.3 %collective-permute-start.2 = (bf16[512,512]{1,0:T(8,128)(2,1)S(1)}, bf16[512,512]{1,0:T(8,128)(2,1)S(1)}, u32[]{:S(2)}, u32[]{:S(2)}) collective-permute-start(bf16[512,512]{1,0:T(8,128)(2,1)S(1)} %get-tuple-element.13), channel_id=1, source_target_pairs={{0,1},{1,2},{2,3},{3,4},{4,5},{5,6},{6,7},{7,8},{8,9},{9,10},{10,1... | collective-permute-start | bytes 1572872 | tf_op jit(solution)/shard_map/ppermute | solution.py:181
  24.4 57.2 %collective-permute-start.9 = (bf16[2,512,512]{2,1,0:T(8,128)(2,1)}, bf16[2,512,512]{2,1,0:T(8,128)(2,1)}, u32[]{:S(2)}, u32[]{:S(2)}) collective-permute-start(bf16[2,512,512]{2,1,0:T(8,128)(2,1)} %rest_0_.1), channel_id=1, source_target_pairs={{0,16},{16,0},{32,48},{48,32},{64,80},{80,64},{96,112},{112,96},{1... | collective-permute-start | bytes 3145736 | tf_op jit(solution)/shard_map/ppermute | solution.py:171
  30.2 51.5 %collective-permute-start.10 = (bf16[2,512,512]{2,1,0:T(8,128)(2,1)}, bf16[2,512,512]{2,1,0:T(8,128)(2,1)}, u32[]{:S(2)}, u32[]{:S(2)}) collective-permute-start(bf16[2,512,512]{2,1,0:T(8,128)(2,1)} %collective-permute-done.5.rest_2_), channel_id=1, source_target_pairs={{0,16},{16,0},{32,48},{48,32},{64,80},{80,64},{96,112},{112,96},{1... | collective-permute-start | bytes 3145736 | tf_op jit(solution)/shard_map/ppermute | solution.py:171
  30.2 51.5 %collective-permute-start.11 = (bf16[2,512,512]{2,1,0:T(8,128)(2,1)}, bf16[2,512,512]{2,1,0:T(8,128)(2,1)}, u32[]{:S(2)}, u32[]{:S(2)}) collective-permute-start(bf16[2,512,512]{2,1,0:T(8,128)(2,1)} %collective-permute-done.3.rest_3_), channel_id=1, source_target_pairs={{0,16},{16,0},{32,48},{48,32},{64,80},{80,64},{96,112},{112,96},{1... | collective-permute-start | bytes 3145736 | tf_op jit(solution)/shard_map/ppermute | solution.py:171
  39.7 41.3 %collective-permute-start.4 = (bf16[1,512,512]{2,1,0:T(8,128)(2,1)}, bf16[1,512,512]{2,1,0:T(8,128)(2,1)S(1)}, u32[]{:S(2)}, u32[]{:S(2)}) collective-permute-start(bf16[1,512,512]{2,1,0:T(8,128)(2,1)} %slice.8), channel_id=1, source_target_pairs={{0,32},{16,48},{32,0},{48,16},{64,96},{80,112},{96,64},{112,80},{1... | collective-permute-start | bytes 1572872 | tf_op jit(solution)/shard_map/ppermute | solution.py:168
  42.1 39.2 %collective-permute-start.6 = (bf16[1,512,512]{2,1,0:T(8,128)(2,1)S(1)}, bf16[1,512,512]{2,1,0:T(8,128)(2,1)S(1)}, u32[]{:S(2)}, u32[]{:S(2)}) collective-permute-start(bf16[1,512,512]{2,1,0:T(8,128)(2,1)S(1)} %slice.9), channel_id=1, source_target_pairs={{0,96},{16,112},{32,64},{48,80},{64,32},{80,48},{96,0},{112,16},{1... | collective-permute-start | bytes 1572872 | tf_op jit(solution)/shard_map/ppermute | solution.py:168
  81.1 14.8 %collective-permute-start.7 = (bf16[1,512,512]{2,1,0:T(8,128)(2,1)S(1)}, bf16[1,512,512]{2,1,0:T(8,128)(2,1)S(1)}, u32[]{:S(2)}, u32[]{:S(2)}) collective-permute-start(bf16[1,512,512]{2,1,0:T(8,128)(2,1)S(1)} %collective-permute-done.4.rest_0_), channel_id=1, source_target_pairs={{0,16},{16,0},{32,48},{48,32},{64,80},{80,64},{96,112},{112,96},{1... | collective-permute-start | bytes 1572872 | tf_op jit(solution)/shard_map/ppermute | solution.py:171
  81.3 14.6 %collective-permute-start.8 = (bf16[1,512,512]{2,1,0:T(8,128)(2,1)S(1)}, bf16[1,512,512]{2,1,0:T(8,128)(2,1)S(1)}, u32[]{:S(2)}, u32[]{:S(2)}) collective-permute-start(bf16[1,512,512]{2,1,0:T(8,128)(2,1)S(1)} %collective-permute-done.6.rest_1_), channel_id=1, source_target_pairs={{0,16},{16,0},{32,48},{48,32},{64,80},{80,64},{96,112},{112,96},{1... | collective-permute-start | bytes 1572872 | tf_op jit(solution)/shard_map/ppermute | solution.py:171
  81.6 2.2 %copy-start = (bf16[2,2,2,512,512]{4,3,2,1,0:T(8,128)(2,1)S(1)}, bf16[2,2,2,512,512]{4,3,2,1,0:T(8,128)(2,1)}, u32[]{:S(2)}) copy-start(bf16[2,2,2,512,512]{4,3,2,1,0:T(8,128)(2,1)} %lesser.3) | copy-start | bytes 12582916
  83.8 1.2 copy-start.2
  95.9 5.7 %copy-start.5 = (f32[2]{0:T(128)S(1)}, f32[2]{0:T(128)}, u32[]{:S(2)}) copy-start(f32[2]{0:T(128)} %param.11) | copy-start | bytes 28
  95.9 21.6 %copy-start.1 = (bf16[2,2,2,512,512]{4,3,2,1,0:T(8,128)(2,1)S(1)}, bf16[2,2,2,512,512]{4,3,2,1,0:T(8,128)(2,1)}, u32[]{:S(2)}) copy-start(bf16[2,2,2,512,512]{4,3,2,1,0:T(8,128)(2,1)} %retarded.1) | copy-start | bytes 12582916
  100.5 13.3 %collective-permute-start.12 = (bf16[512,512]{1,0:T(8,128)(2,1)S(1)}, bf16[512,512]{1,0:T(8,128)(2,1)S(1)}, u32[]{:S(2)}, u32[]{:S(2)}) collective-permute-start(bf16[512,512]{1,0:T(8,128)(2,1)S(1)} %sandwich_last.1), channel_id=1, source_target_pairs={{0,32},{16,48},{32,0},{48,16},{64,96},{80,112},{96,64},{112,80},{1... | collective-permute-start | bytes 1572872 | tf_op jit(solution)/shard_map/ppermute | solution.py:168
  100.6 13.2 %collective-permute-start.13 = (bf16[512,512]{1,0:T(8,128)(2,1)S(1)}, bf16[512,512]{1,0:T(8,128)(2,1)S(1)}, u32[]{:S(2)}, u32[]{:S(2)}) collective-permute-start(bf16[512,512]{1,0:T(8,128)(2,1)S(1)} %sandwich_last.1), channel_id=1, source_target_pairs={{32,160},{48,176},{96,224},{112,240},{160,32},{176,48},{224,96},{2... | collective-permute-start | bytes 1572872 | tf_op jit(solution)/shard_map/ppermute | solution.py:202
  114.7 2.7 %collective-permute-start.14 = (bf16[512,512]{1,0:T(8,128)(2,1)S(1)}, bf16[512,512]{1,0:T(8,128)(2,1)S(1)}, u32[]{:S(2)}, u32[]{:S(2)}) collective-permute-start(bf16[512,512]{1,0:T(8,128)(2,1)S(1)} %add_convert_fusion.own_c), channel_id=1, source_target_pairs={{0,16},{16,0},{32,48},{48,32},{64,80},{80,64},{96,112},{112,96},{1... | collective-permute-start | bytes 1572872 | tf_op jit(solution)/shard_map/ppermute | solution.py:171
  120.8 7.0 %collective-permute-start.15 = (bf16[2,64,512]{2,1,0:T(8,128)(2,1)S(1)}, bf16[2,64,512]{2,1,0:T(8,128)(2,1)S(1)}, u32[]{:S(2)}, u32[]{:S(2)}) collective-permute-start(bf16[2,64,512]{2,1,0:T(8,128)(2,1)S(1)} %get-tuple-element.10), channel_id=1, source_target_pairs={{0,32},{16,48},{32,0},{48,16},{64,96},{80,112},{96,64},{112,80},{1... | collective-permute-start | bytes 393224 | tf_op jit(solution)/shard_map/ppermute | solution.py:168
  124.3 6.0 %collective-permute-start.16 = (bf16[2,64,512]{2,1,0:T(8,128)(2,1)S(1)}, bf16[2,64,512]{2,1,0:T(8,128)(2,1)S(1)}, u32[]{:S(2)}, u32[]{:S(2)}) collective-permute-start(bf16[2,64,512]{2,1,0:T(8,128)(2,1)S(1)} %get-tuple-element.11), channel_id=1, source_target_pairs={{0,64},{16,80},{32,96},{48,112},{64,0},{80,16},{96,32},{112,48},{1... | collective-permute-start | bytes 393224 | tf_op jit(solution)/shard_map/ppermute | solution.py:168
  124.3 9.1 %collective-permute-start.17 = (bf16[2,64,512]{2,1,0:T(8,128)(2,1)S(1)}, bf16[2,64,512]{2,1,0:T(8,128)(2,1)S(1)}, u32[]{:S(2)}, u32[]{:S(2)}) collective-permute-start(bf16[2,64,512]{2,1,0:T(8,128)(2,1)S(1)} %get-tuple-element.12), channel_id=1, source_target_pairs={{0,96},{16,112},{32,64},{48,80},{64,32},{80,48},{96,0},{112,16},{1... | collective-permute-start | bytes 393224 | tf_op jit(solution)/shard_map/ppermute | solution.py:168

commit v2 on v1

v2 whole, which is shorter than its diff:
```python
import functools
import jax
import jax.numpy as jnp
from jax import lax
from jax.experimental import pallas as pl
from jax.experimental.pallas import tpu as pltpu
from jax.sharding import PartitionSpec as P

NO = 512
ROWS = 64
F32 = jnp.float32
BF16 = jnp.bfloat16
MIB = 1 << 20


def hbm_spec():
    return pl.BlockSpec(memory_space=pltpu.HBM)


def smem_spec():
    return pl.BlockSpec(memory_space=pltpu.SMEM)


def vmem_spec():
    return pl.BlockSpec(memory_space=pltpu.VMEM)


def mul(a, b):
    return jnp.dot(a, b, preferred_element_type=F32)


def mul_t(a, b):
    return lax.dot_general(a, b, (((1,), (1,)), ((), ())), preferred_element_type=F32)


def sandwich_kernel(owners, first, last, place, table, own, g1, g2, g3, *rest):
    arrays = rest[: len(owners)]
    rest = rest[len(owners):]
    if first:
        home, rest = rest[0], rest[1:]
    else:
        start, rest = rest[0], rest[1:]
    out, green, acc, gsem, *rest = rest
    y, k, i = place[0], place[1], place[2]
    copies = [
        pltpu.make_async_copy(src, green.at[n], gsem.at[n])
        for n, src in enumerate((own, g1, g2, g3))
    ]
    for c in copies:
        c.start()
    todo = []
    for ref, (dy, dk, f0, count) in zip(arrays, owners):
        for t in range(count):
            todo.append((ref, t, 2 * (2 * (y ^ dy) + (k ^ dk)) + f0 + t, None))
    if first:
        coup, csem = rest
        move = pltpu.make_async_copy(home, coup, csem.at[0])
        move.start()
        for t in range(2):
            todo.append((coup, t, 2 * (2 * y + k) + t, move if t == 0 else None))
    for c in copies:
        c.wait()
    for n, (ref, t, f, move) in enumerate(todo):
        scale = table[0, f]
        far = table[1, f] > 1.5
        low = jnp.where(i == 0, jnp.where(far, 3, 1), jnp.where(far, 1, 0))
        high = jnp.where(i == 0, jnp.where(far, 2, 0), jnp.where(far, 3, 2))
        mixture = (
            scale * green[low].astype(F32) + (scale + 1.0) * green[high].astype(F32)
        ).astype(BF16)
        if move is not None:
            move.wait()
        left = mul(ref[t], mixture).astype(BF16)
        term = mul_t(left, ref[t])
        so_far = (None if first else start[...]) if n == 0 else acc[...]
        total = term if so_far is None else so_far + term
        if n == len(todo) - 1:
            out[...] = total.astype(out.dtype)
        else:
            acc[...] = total


def sandwich(owners, place, table, greens, arrays, home, start, last):
    first = start is None
    count = sum(o[3] for o in owners) + (2 if first else 0)
    operands = [place, table, *greens, *arrays, home if first else start]
    scratch = [
        pltpu.VMEM((4, NO, NO), BF16),
        pltpu.VMEM((NO, NO), F32),
        pltpu.SemaphoreType.DMA((4,)),
    ]
    if first:
        scratch += [pltpu.VMEM((2, NO, NO), BF16), pltpu.SemaphoreType.DMA((1,))]
    return pl.pallas_call(
        functools.partial(sandwich_kernel, owners, first, last),
        out_shape=jax.ShapeDtypeStruct((NO, NO), BF16 if last else F32),
        in_specs=[smem_spec(), smem_spec()]
        + [vmem_spec()] * (len(operands) - 3)
        + [hbm_spec() if first else vmem_spec()],
        out_specs=vmem_spec(),
        scratch_shapes=scratch,
        compiler_params=pltpu.CompilerParams(vmem_limit_bytes=24 * MIB),
        cost_estimate=pl.CostEstimate(
            flops=count * 4 * NO**3, bytes_accessed=(count + 8) * NO * NO * 2, transcendentals=0
        ),
        name="sandwich_last" if last else "sandwich_first",
    )(*operands)


def update_kernel(place, own_c, other_c, green, own_out, out1, out2, out3):
    y, k = place[0], place[1]
    a, b = green[0], green[1]
    mine, other = own_c[...], other_c[...]
    real = jnp.where(k == 0, mine, other)
    imag = jnp.where(k == 0, other, mine)
    yr = (mul_t(real, a) + mul_t(imag, b)).astype(BF16)
    yi = (mul_t(imag, a) - mul_t(real, b)).astype(BF16)
    for dy, ref in ((0, own_out), (1, out1), (2, out2), (3, out3)):
        first = pl.multiple_of((2 * (y ^ dy) + k) * ROWS, ROWS)
        ar = green[0, pl.ds(first, ROWS), :]
        br = green[1, pl.ds(first, ROWS), :]
        ref[0] = (mul(ar, yr) - mul(br, yi)).astype(ref.dtype)
        ref[1] = (mul(ar, yi) + mul(br, yr)).astype(ref.dtype)


def update(place, own_c, other_c, retarded):
    piece = (2, ROWS, NO)
    return pl.pallas_call(
        update_kernel,
        out_shape=[jax.ShapeDtypeStruct(piece, F32)] + [jax.ShapeDtypeStruct(piece, BF16)] * 3,
        in_specs=[smem_spec(), vmem_spec(), vmem_spec(), vmem_spec()],
        out_specs=[vmem_spec()] * 4,
        compiler_params=pltpu.CompilerParams(vmem_limit_bytes=24 * MIB),
        cost_estimate=pl.CostEstimate(
            flops=12 * NO**3, bytes_accessed=5 * NO * NO * 2, transcendentals=0
        ),
        name="update",
    )(place, own_c, other_c, retarded)


def collect_kernel(place, own, p1, p2, p3, out):
    y, b = place[0], place[4]
    for dy, ref in ((0, own), (1, p1), (2, p2), (3, p3)):
        source = y ^ dy
        out[source // 2, (source % 2) ^ b] = ref[...].astype(F32)


def collect(place, pieces):
    return pl.pallas_call(
        collect_kernel,
        out_shape=jax.ShapeDtypeStruct((2, 2, 2, ROWS, NO), F32),
        in_specs=[smem_spec()] + [vmem_spec()] * 4,
        out_specs=vmem_spec(),
        compiler_params=pltpu.CompilerParams(vmem_limit_bytes=24 * MIB),
        name="collect",
    )(place, *pieces)


def shards(lesser, retarded, coupling, occupations, offsets, intersection):
    fr = lax.axis_index("freq")
    b = lax.axis_index("slab")
    y, k = fr // 2, fr % 2
    i, sl = y // 2, (y % 2) ^ b
    place = jnp.stack([y, k, i, sl, b]).astype(jnp.int32)

    def chip(x, dy):
        return lax.ppermute(x, "freq", [(d, d ^ (2 * dy)) for d in range(8)])

    def core(x):
        return lax.ppermute(x, "freq", [(d, d ^ 1) for d in range(8)])

    count = lax.axis_size("energy")
    up = [(e, e + 1) for e in range(count - 1)]
    down = [(t, s) for s, t in up]
    third = [
        (d * count + s, d * count + t) for d in range(8) for s, t in (up if d < 4 else down)
    ]
    g1 = lax.ppermute(lesser[1, sl, k], "energy", up)
    g2 = lax.ppermute(lesser[0, sl, k], "energy", down)
    g3 = lax.ppermute(lesser[i, sl, k], ("freq", "energy"), third)
    greens = (lesser[1 - i, sl, k], g1, g2, g3)
    table = jnp.stack([occupations, offsets.astype(F32)], axis=1)
    table = lax.all_gather(table, "freq", axis=0, tiled=True).T

    c1, c3, s0 = chip(coupling, 1), chip(coupling, 3), core(coupling)
    c1, c3, table, green = lax.optimization_barrier((c1, c3, table, retarded[i, sl]))
    q0 = chip(c3[0:1], 1)
    q1 = chip(c1[1:2], 3)
    c1, c3, q0, q1 = lax.optimization_barrier((c1, c3, q0, q1))
    s1, s3, r0, r1 = core(c1), core(c3), core(q0), core(q1)

    part = sandwich(
        [(1, 0, 0, 2), (3, 0, 0, 2), (2, 0, 0, 1), (2, 0, 1, 1)],
        place, table, greens, [c1, c3, q0, q1], coupling, None, False,
    )
    own = sandwich(
        [(0, 1, 0, 2), (1, 1, 0, 2), (3, 1, 0, 2), (2, 1, 0, 1), (2, 1, 1, 1)],
        place, table, greens, [s0, s1, s3, r0, r1], None, part, True,
    )
    inner = chip(own, 1)
    edge = [(s * 8 + d, (1 - s) * 8 + d) for s in range(2) for d in range(8) if (d // 2) % 2]
    outer = lax.ppermute(own, ("slab", "freq"), edge)
    combined = (
        own.astype(F32) + intersection[sl] * (inner.astype(F32) + outer.astype(F32))
    ).astype(BF16)
    mine, o1, o2, o3 = update(place, combined, core(combined), green)
    return collect(place, (mine, chip(o1, 1), chip(o2, 2), chip(o3, 3)))


def solution(mesh):
    return jax.shard_map(
        shards,
        mesh=mesh,
        in_specs=(
            P("energy", "slab", None, None, None),
            P("energy", "slab", None, None, None),
            P("freq", None, None),
            P("freq"),
            P("freq"),
            P("slab"),
        ),
        out_specs=P("energy", "slab", None, "freq", None),
        check_vma=False,
    )
```

time: 135 us -> 150 us (1.11)
  the two profiles are of different devices: /device:TPU:1 before, /device:TPU:38 now
where the time goes in v2:
time: 150 us; the launch traced here: 147 us
  waiting for transfers between devices  59 us (39%)
  starting transfers between devices  32.6 us (22%)
  blocking collectives  27.1 us (18%)
  Pallas kernels  18.6 us (12%)
  local copies, waits for them, and re-layouts  7.38 us (5%)
  other arithmetic  2.19 us (1%)
    all_gather x1, blocking collectives, shards(): table = lax.all_gather(table, 'freq', axis=0, tiled=True).T  27.1 us
    ppermute x8, waiting for transfers between devices, chip(): return lax.ppermute(x, 'freq', [(d, d ^ 2 * dy) for d in range(8)])  23.9 us
    ppermute x1, waiting for transfers between devices, shards(): g1 = lax.ppermute(lesser[1, sl, k], 'energy', up)  23.8 us
    ppermute x8, starting transfers between devices, chip(): return lax.ppermute(x, 'freq', [(d, d ^ 2 * dy) for d in range(8)])  16.5 us
    pallas_call x2, Pallas kernels, sandwich(): pl.pallas_call(functools.partial(sandwich_kernel, owners, first, last), o...  13.7 us
    ppermute x1, waiting for transfers between devices, shards(): g3 = lax.ppermute(lesser[i, sl, k], ('freq', 'energy'), third)  9.43 us
    ppermute x1, starting transfers between devices, shards(): g1 = lax.ppermute(lesser[1, sl, k], 'energy', up)  5.18 us
    ppermute x1, starting transfers between devices, shards(): g3 = lax.ppermute(lesser[i, sl, k], ('freq', 'energy'), third)  5.17 us
  transfers between devices with their start and end apart: 18, of which 7 were waited for; matrix products, arithmetic and copies ran while one was open for 3% of the time, Pallas kernels for 5%

profile of v2, /device:TPU:38, one launch (start us, length us, event | category | flops | bytes accessed | tf_op | source)
XLA Modules:
  0.0 147.2 jit_solution(16708705498090374506)
XLA Ops:
  0.0 1.6 %collective-permute-start = (bf16[2,512,512]{2,1,0:T(8,128)(2,1)}, bf16[2,512,512]{2,1,0:T(8,128)(2,1)S(1)}, u32[]{:S(2)}, u32[]{:S(2)}) collective-permute-start(bf16[2,512,512]{2,1,0:T(8,128)(2,1)} %rest_4_.1), channel_id=1, source_target_pairs={{0,32},{16,48},{32,0},{48,16},{64,96},{80,112},{96,64},{112,80},{1... | collective-permute-start | bytes 3145736 | tf_op jit(solution)/shard_map/ppermute | solution.py:167
  1.6 2.2 %collective-permute-start.1 = (bf16[2,512,512]{2,1,0:T(8,128)(2,1)}, bf16[2,512,512]{2,1,0:T(8,128)(2,1)}, u32[]{:S(2)}, u32[]{:S(2)}) collective-permute-start(bf16[2,512,512]{2,1,0:T(8,128)(2,1)} %rest_4_.1), channel_id=1, source_target_pairs={{0,96},{16,112},{32,64},{48,80},{64,32},{80,48},{96,0},{112,16},{1... | collective-permute-start | bytes 3145736 | tf_op jit(solution)/shard_map/ppermute | solution.py:167
  3.8 0.7 convert_bitcast_fusion
  4.4 0.7 pad_maximum_fusion
  5.2 27.1 %all-gather = f32[8,2,2]{2,1,0:T(2,128)S(1)} all-gather(f32[1,2,2]{2,1,0:T(2,128)S(1)} %bitcast.25), channel_id=1, replica_groups=mesh['slab'=2,'freq'=8,'energy'=16] {'freq'}, dimensions={0}, use_global_device_ids=true | all-gather | bytes 144 | tf_op jit(solution)/shard_map/all_gather | solution.py:183
  32.4 1.4 dynamic-slice_bitcast_fusion.green
  33.8 1.2 slice.6
  35.8 5.2 %collective-permute-start.2 = (bf16[512,512]{1,0:T(8,128)(2,1)S(1)}, bf16[512,512]{1,0:T(8,128)(2,1)S(1)}, u32[]{:S(2)}, u32[]{:S(2)}) collective-permute-start(bf16[512,512]{1,0:T(8,128)(2,1)S(1)} %get-tuple-element.30), channel_id=1, source_target_pairs={{0,1},{1,2},{2,3},{3,4},{4,5},{5,6},{6,7},{7,8},{8,9},{9,10},{10,1... | collective-permute-start | bytes 1572872 | tf_op jit(solution)/shard_map/ppermute | solution.py:178
  41.1 4.3 %collective-permute-start.3 = (bf16[512,512]{1,0:T(8,128)(2,1)S(1)}, bf16[512,512]{1,0:T(8,128)(2,1)S(1)}, u32[]{:S(2)}, u32[]{:S(2)}) collective-permute-start(bf16[512,512]{1,0:T(8,128)(2,1)S(1)} %get-tuple-element.32), channel_id=1, source_target_pairs={{1,0},{2,1},{3,2},{4,3},{5,4},{6,5},{7,6},{8,7},{9,8},{10,9},{11,1... | collective-permute-start | bytes 1572872 | tf_op jit(solution)/shard_map/ppermute | solution.py:179
  45.4 3.9 %collective-permute-done.6.rest_2_ = bf16[1,512,512]{2,1,0:T(8,128)(2,1)} collective-permute-done((bf16[1,512,512]{2,1,0:T(8,128)(2,1)S(1)}, bf16[1,512,512]{2,1,0:T(8,128)(2,1)}, u32[]{:S(2)}, u32[]{:S(2)}) %collective-permute-start.6) | collective-permute-done | bytes 524320 | tf_op jit(solution)/shard_map/ppermute | solution.py:167
  49.4 5.2 %collective-permute-start.4 = (bf16[512,512]{1,0:T(8,128)(2,1)S(1)}, bf16[512,512]{1,0:T(8,128)(2,1)S(1)}, u32[]{:S(2)}, u32[]{:S(2)}) collective-permute-start(bf16[512,512]{1,0:T(8,128)(2,1)S(1)} %get-tuple-element.29), channel_id=1, source_target_pairs={{0,1},{1,2},{2,3},{3,4},{4,5},{5,6},{6,7},{7,8},{8,9},{9,10},{10,1... | collective-permute-start | bytes 1572872 | tf_op jit(solution)/shard_map/ppermute | solution.py:180
  54.6 23.8 %collective-permute-done.2.g1 = bf16[512,512]{1,0:T(8,128)(2,1)S(1)} collective-permute-done((bf16[512,512]{1,0:T(8,128)(2,1)S(1)}, bf16[512,512]{1,0:T(8,128)(2,1)S(1)}, u32[]{:S(2)}, u32[]{:S(2)}) %collective-permute-start.2) | collective-permute-done | bytes 524320 | tf_op jit(solution)/shard_map/ppermute | solution.py:178
  78.4 0.8 copy-done
  79.2 0.5 collective-permute-start.10
  79.7 9.4 %collective-permute-done.4.g3 = bf16[512,512]{1,0:T(8,128)(2,1)S(1)} collective-permute-done((bf16[512,512]{1,0:T(8,128)(2,1)S(1)}, bf16[512,512]{1,0:T(8,128)(2,1)S(1)}, u32[]{:S(2)}, u32[]{:S(2)}) %collective-permute-start.4) | collective-permute-done | bytes 524320 | tf_op jit(solution)/shard_map/ppermute | solution.py:180
  89.2 0.8 copy-done.3
  90.0 1.0 copy-done.1
  91.1 1.0 copy-done.4
  92.1 6.8 %sandwich_first.1.rest_5_ = f32[512,512]{1,0:T(8,128)S(1)} custom-call(s32[5]{0:T(128)S(1)} %stack.32.place, f32[2,16]{1,0:T(2,128)S(1)} %bitcast.22, bf16[512,512]{1,0:T(8,128)(2,1)S(1)} %get-tuple-element.31.own, bf16[512,512]{1,0:T(8,128)(2,1)S(1)} %collective-permute-done.2.g1, bf16[512,512]{1,0:T(8,128)(2,1)S(1)} %copy-done.1, ...), custom_call_target="tpu_custom_call" | custom-call | flops 4294967296 | bytes 8388608 | tf_op jit(solution)/shard_map/sandwich_first/pallas_call | solution.py:94
  99.0 6.9 %sandwich_last.1 = bf16[512,512]{1,0:T(8,128)(2,1)S(1)} custom-call(s32[5]{0:T(128)S(1)} %stack.32.place, f32[2,16]{1,0:T(2,128)S(1)} %bitcast.23, bf16[512,512]{1,0:T(8,128)(2,1)S(1)} %get-tuple-element.31.own, bf16[512,512]{1,0:T(8,128)(2,1)S(1)} %collective-permute-done.2.g1, bf16[512,512]{1,0:T(8,128)(2,1)S(1)} %copy-done.2, ...), custom_call_target="tpu_custom_call" | custom-call | flops 4294967296 | bytes 8388608 | tf_op jit(solution)/shard_map/sandwich_last/pallas_call | solution.py:94
  106.0 1.8 %collective-permute-start.12 = (bf16[512,512]{1,0:T(8,128)(2,1)S(1)}, bf16[512,512]{1,0:T(8,128)(2,1)S(1)}, u32[]{:S(2)}, u32[]{:S(2)}) collective-permute-start(bf16[512,512]{1,0:T(8,128)(2,1)S(1)} %sandwich_last.1), channel_id=1, source_target_pairs={{0,32},{16,48},{32,0},{48,16},{64,96},{80,112},{96,64},{112,80},{1... | collective-permute-start | bytes 1572872 | tf_op jit(solution)/shard_map/ppermute | solution.py:167
  107.8 0.7 collective-permute-start.13
  108.5 0.6 dynamic_slice.23
  109.1 11.3 %collective-permute-done.12 = bf16[512,512]{1,0:T(8,128)(2,1)S(1)} collective-permute-done((bf16[512,512]{1,0:T(8,128)(2,1)S(1)}, bf16[512,512]{1,0:T(8,128)(2,1)S(1)}, u32[]{:S(2)}, u32[]{:S(2)}) %collective-permute-start.12) | collective-permute-done | bytes 524320 | tf_op jit(solution)/shard_map/ppermute | solution.py:167
  120.4 0.9 add_convert_fusion.own_c
  121.4 1.9 %collective-permute-done.14.other_c = bf16[512,512]{1,0:T(8,128)(2,1)S(1)} collective-permute-done((bf16[512,512]{1,0:T(8,128)(2,1)S(1)}, bf16[512,512]{1,0:T(8,128)(2,1)S(1)}, u32[]{:S(2)}, u32[]{:S(2)}) %collective-permute-start.14) | collective-permute-done | bytes 524320 | tf_op jit(solution)/shard_map/ppermute | solution.py:170
  123.3 3.2 %update.1 = (f32[2,64,512]{2,1,0:T(8,128)S(1)}, bf16[2,64,512]{2,1,0:T(8,128)(2,1)S(1)}, bf16[2,64,512]{2,1,0:T(8,128)(2,1)S(1)}, bf16[2,64,512]{2,1,0:T(8,128)(2,1)S(1)}) custom-call(s32[5]{0:T(128)S(1)} %stack.32.place, bf16[512,512]{1,0:T(8,128)(2,1)S(1)} %add_convert_fusion.own_c, bf16[512,512]{1,0:T(8,128)(2,1)S(1)} %collective-permute-done.14.other_c, ...), custom_call_target="tpu_custom_call" | custom-call | flops 1610612736 | bytes 2621440 | tf_op jit(solution)/shard_map/update/pallas_call | solution.py:128
  126.5 3.7 %collective-permute-start.15 = (bf16[2,64,512]{2,1,0:T(8,128)(2,1)S(1)}, bf16[2,64,512]{2,1,0:T(8,128)(2,1)S(1)}, u32[]{:S(2)}, u32[]{:S(2)}) collective-permute-start(bf16[2,64,512]{2,1,0:T(8,128)(2,1)S(1)} %get-tuple-element.26), channel_id=1, source_target_pairs={{0,32},{16,48},{32,0},{48,16},{64,96},{80,112},{96,64},{112,80},{1... | collective-permute-start | bytes 393224 | tf_op jit(solution)/shard_map/ppermute | solution.py:167
  130.2 6.7 %collective-permute-start.16 = (bf16[2,64,512]{2,1,0:T(8,128)(2,1)S(1)}, bf16[2,64,512]{2,1,0:T(8,128)(2,1)S(1)}, u32[]{:S(2)}, u32[]{:S(2)}) collective-permute-start(bf16[2,64,512]{2,1,0:T(8,128)(2,1)S(1)} %get-tuple-element.27), channel_id=1, source_target_pairs={{0,64},{16,80},{32,96},{48,112},{64,0},{80,16},{96,32},{112,48},{1... | collective-permute-start | bytes 393224 | tf_op jit(solution)/shard_map/ppermute | solution.py:167
  136.9 6.4 %collective-permute-done.16.p2 = bf16[2,64,512]{2,1,0:T(8,128)(2,1)S(1)} collective-permute-done((bf16[2,64,512]{2,1,0:T(8,128)(2,1)S(1)}, bf16[2,64,512]{2,1,0:T(8,128)(2,1)S(1)}, u32[]{:S(2)}, u32[]{:S(2)}) %collective-permute-start.16) | collective-permute-done | bytes 131104 | tf_op jit(solution)/shard_map/ppermute | solution.py:167
  143.3 2.2 %collective-permute-done.17.p3 = bf16[2,64,512]{2,1,0:T(8,128)(2,1)S(1)} collective-permute-done((bf16[2,64,512]{2,1,0:T(8,128)(2,1)S(1)}, bf16[2,64,512]{2,1,0:T(8,128)(2,1)S(1)}, u32[]{:S(2)}, u32[]{:S(2)}) %collective-permute-start.17) | collective-permute-done | bytes 131104 | tf_op jit(solution)/shard_map/ppermute | solution.py:167
  145.6 1.6 %collect.1 = f32[2,2,2,64,512]{4,3,2,1,0:T(8,128)} custom-call(s32[5]{0:T(128)S(1)} %stack.32.place, f32[2,64,512]{2,1,0:T(8,128)S(1)} %get-tuple-element.25.own, bf16[2,64,512]{2,1,0:T(8,128)(2,1)S(1)} %collective-permute-done.15.p1, bf16[2,64,512]{2,1,0:T(8,128)(2,1)S(1)} %collective-permute-done.16.p2, bf16[2,64,512]{2,1,0:T(8,128)(2,1)S(1)} %collective-permute-done.17.p3), custom_call_target="tpu_custom_call" | custom-call | tf_op jit(solution)/shard_map/collect/pallas_call | solution.py:149
  (36 shorter events, 1.4 us)
Async XLA Ops:
  0.0 33.8 %collective-permute-start = (bf16[2,512,512]{2,1,0:T(8,128)(2,1)}, bf16[2,512,512]{2,1,0:T(8,128)(2,1)S(1)}, u32[]{:S(2)}, u32[]{:S(2)}) collective-permute-start(bf16[2,512,512]{2,1,0:T(8,128)(2,1)} %rest_4_.1), channel_id=1, source_target_pairs={{0,32},{16,48},{32,0},{48,16},{64,96},{80,112},{96,64},{112,80},{1... | collective-permute-start | bytes 3145736 | tf_op jit(solution)/shard_map/ppermute | solution.py:167
  1.6 32.2 %collective-permute-start.1 = (bf16[2,512,512]{2,1,0:T(8,128)(2,1)}, bf16[2,512,512]{2,1,0:T(8,128)(2,1)}, u32[]{:S(2)}, u32[]{:S(2)}) collective-permute-start(bf16[2,512,512]{2,1,0:T(8,128)(2,1)} %rest_4_.1), channel_id=1, source_target_pairs={{0,96},{16,112},{32,64},{48,80},{64,32},{80,48},{96,0},{112,16},{1... | collective-permute-start | bytes 3145736 | tf_op jit(solution)/shard_map/ppermute | solution.py:167
  32.4 3.3 %copy-start.6 = (bf16[2,2,2,512,512]{4,3,2,1,0:T(8,128)(2,1)S(1)}, bf16[2,2,2,512,512]{4,3,2,1,0:T(8,128)(2,1)}, u32[]{:S(2)}) copy-start(bf16[2,2,2,512,512]{4,3,2,1,0:T(8,128)(2,1)} %param.6) | copy-start | bytes 12582916
  35.0 14.3 %collective-permute-start.6 = (bf16[1,512,512]{2,1,0:T(8,128)(2,1)S(1)}, bf16[1,512,512]{2,1,0:T(8,128)(2,1)}, u32[]{:S(2)}, u32[]{:S(2)}) collective-permute-start(bf16[1,512,512]{2,1,0:T(8,128)(2,1)S(1)} %slice.6), channel_id=1, source_target_pairs={{0,32},{16,48},{32,0},{48,16},{64,96},{80,112},{96,64},{112,80},{1... | collective-permute-start | bytes 1572872 | tf_op jit(solution)/shard_map/ppermute | solution.py:167
  35.2 19.4 %collective-permute-start.7 = (bf16[1,512,512]{2,1,0:T(8,128)(2,1)S(1)}, bf16[1,512,512]{2,1,0:T(8,128)(2,1)}, u32[]{:S(2)}, u32[]{:S(2)}) collective-permute-start(bf16[1,512,512]{2,1,0:T(8,128)(2,1)S(1)} %slice.7), channel_id=1, source_target_pairs={{0,96},{16,112},{32,64},{48,80},{64,32},{80,48},{96,0},{112,16},{1... | collective-permute-start | bytes 1572872 | tf_op jit(solution)/shard_map/ppermute | solution.py:167
  35.8 42.6 %collective-permute-start.2 = (bf16[512,512]{1,0:T(8,128)(2,1)S(1)}, bf16[512,512]{1,0:T(8,128)(2,1)S(1)}, u32[]{:S(2)}, u32[]{:S(2)}) collective-permute-start(bf16[512,512]{1,0:T(8,128)(2,1)S(1)} %get-tuple-element.30), channel_id=1, source_target_pairs={{0,1},{1,2},{2,3},{3,4},{4,5},{5,6},{6,7},{7,8},{8,9},{9,10},{10,1... | collective-permute-start | bytes 1572872 | tf_op jit(solution)/shard_map/ppermute | solution.py:178
  41.0 58.0 %collective-permute-start.5 = (bf16[2,512,512]{2,1,0:T(8,128)(2,1)}, bf16[2,512,512]{2,1,0:T(8,128)(2,1)}, u32[]{:S(2)}, u32[]{:S(2)}) collective-permute-start(bf16[2,512,512]{2,1,0:T(8,128)(2,1)} %rest_4_.1), channel_id=1, source_target_pairs={{0,16},{16,0},{32,48},{48,32},{64,80},{80,64},{96,112},{112,96},{1... | collective-permute-start | bytes 3145736 | tf_op jit(solution)/shard_map/ppermute | solution.py:170
  41.1 37.3 %collective-permute-start.3 = (bf16[512,512]{1,0:T(8,128)(2,1)S(1)}, bf16[512,512]{1,0:T(8,128)(2,1)S(1)}, u32[]{:S(2)}, u32[]{:S(2)}) collective-permute-start(bf16[512,512]{1,0:T(8,128)(2,1)S(1)} %get-tuple-element.32), channel_id=1, source_target_pairs={{1,0},{2,1},{3,2},{4,3},{5,4},{6,5},{7,6},{8,7},{9,8},{10,9},{11,1... | collective-permute-start | bytes 1572872 | tf_op jit(solution)/shard_map/ppermute | solution.py:179
  49.4 39.8 %collective-permute-start.4 = (bf16[512,512]{1,0:T(8,128)(2,1)S(1)}, bf16[512,512]{1,0:T(8,128)(2,1)S(1)}, u32[]{:S(2)}, u32[]{:S(2)}) collective-permute-start(bf16[512,512]{1,0:T(8,128)(2,1)S(1)} %get-tuple-element.29), channel_id=1, source_target_pairs={{0,1},{1,2},{2,3},{3,4},{4,5},{5,6},{6,7},{7,8},{8,9},{9,10},{10,1... | collective-permute-start | bytes 1572872 | tf_op jit(solution)/shard_map/ppermute | solution.py:180
  54.5 44.4 %collective-permute-start.8 = (bf16[2,512,512]{2,1,0:T(8,128)(2,1)S(1)}, bf16[2,512,512]{2,1,0:T(8,128)(2,1)}, u32[]{:S(2)}, u32[]{:S(2)}) collective-permute-start(bf16[2,512,512]{2,1,0:T(8,128)(2,1)S(1)} %collective-permute-done.rest_0_), channel_id=1, source_target_pairs={{0,16},{16,0},{32,48},{48,32},{64,80},{80,64},{96,112},{112,96},{1... | collective-permute-start | bytes 3145736 | tf_op jit(solution)/shard_map/ppermute | solution.py:170
  78.4 20.6 %collective-permute-start.9 = (bf16[2,512,512]{2,1,0:T(8,128)(2,1)}, bf16[2,512,512]{2,1,0:T(8,128)(2,1)}, u32[]{:S(2)}, u32[]{:S(2)}) collective-permute-start(bf16[2,512,512]{2,1,0:T(8,128)(2,1)} %collective-permute-done.1.rest_1_), channel_id=1, source_target_pairs={{0,16},{16,0},{32,48},{48,32},{64,80},{80,64},{96,112},{112,96},{1... | collective-permute-start | bytes 3145736 | tf_op jit(solution)/shard_map/ppermute | solution.py:170
  78.4 0.8 copy-start
  79.2 19.7 %collective-permute-start.10 = (bf16[1,512,512]{2,1,0:T(8,128)(2,1)}, bf16[1,512,512]{2,1,0:T(8,128)(2,1)}, u32[]{:S(2)}, u32[]{:S(2)}) collective-permute-start(bf16[1,512,512]{2,1,0:T(8,128)(2,1)} %collective-permute-done.6.rest_2_), channel_id=1, source_target_pairs={{0,16},{16,0},{32,48},{48,32},{64,80},{80,64},{96,112},{112,96},{1... | collective-permute-start | bytes 1572872 | tf_op jit(solution)/shard_map/ppermute | solution.py:170
  89.2 0.8 copy-start.3
  90.0 9.0 %collective-permute-start.11 = (bf16[1,512,512]{2,1,0:T(8,128)(2,1)}, bf16[1,512,512]{2,1,0:T(8,128)(2,1)}, u32[]{:S(2)}, u32[]{:S(2)}) collective-permute-start(bf16[1,512,512]{2,1,0:T(8,128)(2,1)} %collective-permute-done.7.rest_3_), channel_id=1, source_target_pairs={{0,16},{16,0},{32,48},{48,32},{64,80},{80,64},{96,112},{112,96},{1... | collective-permute-start | bytes 1572872 | tf_op jit(solution)/shard_map/ppermute | solution.py:170
  90.0 1.0 copy-start.1
  91.1 1.0 copy-start.4
  92.1 6.9 %copy-start.2 = (bf16[512,512]{1,0:T(8,128)(2,1)S(1)}, bf16[512,512]{1,0:T(8,128)(2,1)}, u32[]{:S(2)}) copy-start(bf16[512,512]{1,0:T(8,128)(2,1)} %copy-done) | copy-start | bytes 1572868
  92.1 6.9 %copy-start.5 = (bf16[512,512]{1,0:T(8,128)(2,1)S(1)}, bf16[512,512]{1,0:T(8,128)(2,1)}, u32[]{:S(2)}) copy-start(bf16[512,512]{1,0:T(8,128)(2,1)} %copy-done.3) | copy-start | bytes 1572868
  98.9 9.5 %copy-start.7 = (f32[2]{0:T(128)S(1)}, f32[2]{0:T(128)}, u32[]{:S(2)}) copy-start(f32[2]{0:T(128)} %param.11) | copy-start | bytes 28
  106.0 14.4 %collective-permute-start.12 = (bf16[512,512]{1,0:T(8,128)(2,1)S(1)}, bf16[512,512]{1,0:T(8,128)(2,1)S(1)}, u32[]{:S(2)}, u32[]{:S(2)}) collective-permute-start(bf16[512,512]{1,0:T(8,128)(2,1)S(1)} %sandwich_last.1), channel_id=1, source_target_pairs={{0,32},{16,48},{32,0},{48,16},{64,96},{80,112},{96,64},{112,80},{1... | collective-permute-start | bytes 1572872 | tf_op jit(solution)/shard_map/ppermute | solution.py:167
  107.8 12.6 %collective-permute-start.13 = (bf16[512,512]{1,0:T(8,128)(2,1)S(1)}, bf16[512,512]{1,0:T(8,128)(2,1)S(1)}, u32[]{:S(2)}, u32[]{:S(2)}) collective-permute-start(bf16[512,512]{1,0:T(8,128)(2,1)S(1)} %sandwich_last.1), channel_id=1, source_target_pairs={{32,160},{48,176},{96,224},{112,240},{160,32},{176,48},{224,96},{2... | collective-permute-start | bytes 1572872 | tf_op jit(solution)/shard_map/ppermute | solution.py:202
  121.3 2.0 %collective-permute-start.14 = (bf16[512,512]{1,0:T(8,128)(2,1)S(1)}, bf16[512,512]{1,0:T(8,128)(2,1)S(1)}, u32[]{:S(2)}, u32[]{:S(2)}) collective-permute-start(bf16[512,512]{1,0:T(8,128)(2,1)S(1)} %add_convert_fusion.own_c), channel_id=1, source_target_pairs={{0,16},{16,0},{32,48},{48,32},{64,80},{80,64},{96,112},{112,96},{1... | collective-permute-start | bytes 1572872 | tf_op jit(solution)/shard_map/ppermute | solution.py:170
  126.5 10.4 %collective-permute-start.15 = (bf16[2,64,512]{2,1,0:T(8,128)(2,1)S(1)}, bf16[2,64,512]{2,1,0:T(8,128)(2,1)S(1)}, u32[]{:S(2)}, u32[]{:S(2)}) collective-permute-start(bf16[2,64,512]{2,1,0:T(8,128)(2,1)S(1)} %get-tuple-element.26), channel_id=1, source_target_pairs={{0,32},{16,48},{32,0},{48,16},{64,96},{80,112},{96,64},{112,80},{1... | collective-permute-start | bytes 393224 | tf_op jit(solution)/shard_map/ppermute | solution.py:167
  130.2 13.1 %collective-permute-start.16 = (bf16[2,64,512]{2,1,0:T(8,128)(2,1)S(1)}, bf16[2,64,512]{2,1,0:T(8,128)(2,1)S(1)}, u32[]{:S(2)}, u32[]{:S(2)}) collective-permute-start(bf16[2,64,512]{2,1,0:T(8,128)(2,1)S(1)} %get-tuple-element.27), channel_id=1, source_target_pairs={{0,64},{16,80},{32,96},{48,112},{64,0},{80,16},{96,32},{112,48},{1... | collective-permute-start | bytes 393224 | tf_op jit(solution)/shard_map/ppermute | solution.py:167
  136.9 8.7 %collective-permute-start.17 = (bf16[2,64,512]{2,1,0:T(8,128)(2,1)S(1)}, bf16[2,64,512]{2,1,0:T(8,128)(2,1)S(1)}, u32[]{:S(2)}, u32[]{:S(2)}) collective-permute-start(bf16[2,64,512]{2,1,0:T(8,128)(2,1)S(1)} %get-tuple-element.28), channel_id=1, source_target_pairs={{0,96},{16,112},{32,64},{48,80},{64,32},{80,48},{96,0},{112,16},{1... | collective-permute-start | bytes 393224 | tf_op jit(solution)/shard_map/ppermute | solution.py:167

commit v3 on v0

v3 whole, which is shorter than its diff:
```python
import functools
import jax
import jax.numpy as jnp
from jax import lax
from jax.experimental import pallas as pl
from jax.experimental.pallas import tpu as pltpu
from jax.sharding import PartitionSpec as P

NO = 512
ROWS = 64
TAIL = 16
F32 = jnp.float32
BF16 = jnp.bfloat16
MIB = 1 << 20
HBM = pl.BlockSpec(memory_space=pltpu.HBM)
SMEM = pl.BlockSpec(memory_space=pltpu.SMEM)
VMEM = pl.BlockSpec(memory_space=pltpu.VMEM)
PARAMS = pltpu.CompilerParams(vmem_limit_bytes=24 * MIB)


def shape(dims, kind):
    return jax.ShapeDtypeStruct(dims, kind)


def mul(a, b):
    return jnp.dot(a, b, preferred_element_type=F32)


def mul_t(a, b):
    return lax.dot_general(a, b, (((1,), (1,)), ((), ())), preferred_element_type=F32)


def prepare_kernel(place, occupations, offsets, coupling, lesser, packed, near, far, tail, sem):
    k, sl, c = place[1], place[2], place[4]
    copies = [
        pltpu.make_async_copy(lesser.at[1 - k, sl, c], near, sem.at[0]),
        pltpu.make_async_copy(lesser.at[k, sl, c], far, sem.at[1]),
    ]
    for t in range(2):
        copies.append(
            pltpu.make_async_copy(coupling.at[t], packed.at[t, pl.ds(0, NO)], sem.at[2 + t])
        )
    for copy in copies:
        copy.start()
    row = lax.broadcasted_iota(jnp.int32, (TAIL, NO), 0)
    for t in range(2):
        whole = jnp.full((TAIL, NO), occupations[t], F32)
        high = whole.astype(BF16).astype(F32)
        middle = (whole - high).astype(BF16).astype(F32)
        low = whole - high - middle
        steps = jnp.full((TAIL, NO), offsets[t], jnp.int32).astype(F32)
        rows = jnp.where(row == 0, high, jnp.where(row == 1, middle, jnp.where(row == 2, low, steps)))
        tail[t] = rows.astype(BF16)
        copies.append(
            pltpu.make_async_copy(tail.at[t], packed.at[t, pl.ds(NO, TAIL)], sem.at[4 + t])
        )
        copies[-1].start()
    for copy in copies:
        copy.wait()


def prepare(place, occupations, offsets, coupling, lesser):
    return pl.pallas_call(
        prepare_kernel,
        out_shape=[shape((2, NO + TAIL, NO), BF16)] + [shape((NO, NO), BF16)] * 2,
        in_specs=[SMEM] * 3 + [HBM] * 2,
        out_specs=[HBM] * 3,
        scratch_shapes=[pltpu.VMEM((2, TAIL, NO), BF16), pltpu.SemaphoreType.DMA((6,))],
        compiler_params=pltpu.CompilerParams(vmem_limit_bytes=60 * MIB),
        name="prepare",
    )(place, occupations, offsets, coupling, lesser)


def add_terms(k, green, todo, coup, csem, begin):
    def copy_of(n):
        return pltpu.make_async_copy(todo[n], coup.at[n], csem.at[n])

    def arrive(n):
        copy_of(n).wait()
        tail = coup[n, NO:, :].astype(F32)
        scale = tail[0:1] + tail[1:2] + tail[2:3]
        return scale, (jnp.max(tail[3:4, 0:128]) > 1.5).astype(jnp.int32)

    for n in range(min(3, len(todo))):
        copy_of(n).start()
    begin()
    numbers = arrive(0)
    for n in range(len(todo)):
        scale, far = numbers
        if n + 3 < len(todo):
            copy_of(n + 3).start()
        if n + 1 < len(todo):
            numbers = arrive(n + 1)
        low = (1 - k) + 2 * far
        high = k + 2 * far
        mixture = (
            scale * green[low].astype(F32) + (scale + 1.0) * green[high].astype(F32)
        ).astype(BF16)
        weights = coup[n, :NO, :]
        left = mul(weights, mixture).astype(BF16)
        yield mul_t(left, weights)


def first_kernel(place, own, near, shared, far, home, s0, c1, c3, out, green, coup, gsem, csem):
    k = place[1]
    copies = [
        pltpu.make_async_copy(src, green.at[n], gsem.at[n])
        for n, src in enumerate((own, near, shared, far))
    ]
    for copy in copies:
        copy.start()

    def begin():
        for copy in copies:
            copy.wait()

    todo = [ref.at[t] for ref in (home, s0, c1, c3) for t in range(2)]
    for n, term in enumerate(add_terms(k, green, todo, coup, csem, begin)):
        out[...] = term if n == 0 else out[...] + term


def last_kernel(
    place, green, start, s1, s3, c2, s2, retarded,
    out, whole, blocks, coup, acc, csem, rsem,
):
    y, k, sl = place[0], place[1], place[2]
    copies = [pltpu.make_async_copy(retarded.at[k, sl], whole, rsem.at[0])]
    for dest in range(8):
        target = 2 * y + k ^ dest
        first = pl.multiple_of(target * ROWS, ROWS)
        copies.append(
            pltpu.make_async_copy(
                retarded.at[k, sl, :, pl.ds(first, ROWS)],
                blocks.at[:, pl.ds(dest * ROWS, ROWS)],
                rsem.at[1 + dest],
            )
        )
    todo = [ref.at[t] for ref in (s1, s3, c2, s2) for t in range(2)]

    def begin():
        for copy in copies:
            copy.start()

    for n, term in enumerate(add_terms(k, green, todo, coup, csem, begin)):
        total = (start if n == 0 else acc)[...] + term
        if n == len(todo) - 1:
            out[...] = total.astype(BF16)
        else:
            acc[...] = total
    for copy in copies:
        copy.wait()


def sandwich_first(place, own, near, shared, far, arrays):
    return pl.pallas_call(
        first_kernel,
        out_shape=[shape((NO, NO), F32), shape((4, NO, NO), BF16)],
        in_specs=[SMEM] + [HBM] * 8,
        out_specs=[VMEM] * 2,
        scratch_shapes=[
            pltpu.VMEM((8, NO + TAIL, NO), BF16),
            pltpu.SemaphoreType.DMA((4,)),
            pltpu.SemaphoreType.DMA((8,)),
        ],
        compiler_params=PARAMS,
        cost_estimate=pl.CostEstimate(
            flops=8 * 4 * NO**3, bytes_accessed=18 * NO * NO * 2, transcendentals=0
        ),
        name="sandwich_first",
    )(place, own, near, shared, far, *arrays)


def sandwich_last(place, green, start, arrays, retarded):
    return pl.pallas_call(
        last_kernel,
        out_shape=[shape((NO, NO), BF16), shape((2, NO, NO), BF16), shape((2, NO, NO), BF16)],
        in_specs=[SMEM] + [VMEM] * 2 + [HBM] * 5,
        out_specs=[VMEM] * 3,
        scratch_shapes=[
            pltpu.VMEM((8, NO + TAIL, NO), BF16),
            pltpu.VMEM((NO, NO), F32),
            pltpu.SemaphoreType.DMA((8,)),
            pltpu.SemaphoreType.DMA((9,)),
        ],
        compiler_params=PARAMS,
        cost_estimate=pl.CostEstimate(
            flops=8 * 4 * NO**3, bytes_accessed=18 * NO * NO * 2, transcendentals=0
        ),
        name="sandwich_last",
    )(place, green, start, *arrays, retarded)


def update_kernel(place, weight, own, inner, outer, whole, blocks, *outs):
    sl, c = place[2], place[4]
    beside = inner[...].astype(F32) + outer[...].astype(F32)
    combined = (own[...].astype(F32) + weight[sl] * beside).astype(BF16)
    a_side = mul_t(combined, whole[0]).astype(BF16)
    b_side = mul_t(combined, whole[1]).astype(BF16)
    a, b = blocks[0], blocks[1]
    real = mul(a, a_side) + mul(b, b_side)
    imag = mul(b, a_side) - mul(a, b_side)
    first = jnp.where(c == 0, real, -imag)
    second = jnp.where(c == 0, imag, real)
    for dest, ref in enumerate(outs):
        rows = slice(dest * ROWS, (dest + 1) * ROWS)
        ref[0] = first[rows].astype(ref.dtype)
        ref[1] = second[rows].astype(ref.dtype)


def update(place, weight, own, inner, outer, whole, blocks):
    piece = (2, ROWS, NO)
    return pl.pallas_call(
        update_kernel,
        out_shape=[shape(piece, F32)] + [shape(piece, BF16)] * 7,
        in_specs=[SMEM] * 2 + [VMEM] * 5,
        out_specs=[VMEM] * 8,
        compiler_params=PARAMS,
        cost_estimate=pl.CostEstimate(
            flops=12 * NO**3, bytes_accessed=10 * NO * NO * 2, transcendentals=0
        ),
        name="update",
    )(place, weight, own, inner, outer, whole, blocks)


def collect_kernel(place, *refs):
    *pieces, out = refs
    y, k, b = place[0], place[1], place[3]
    for dk in range(2):
        for dp in range(2):
            total = pieces[2 * dp + dk][...].astype(F32) + pieces[2 * (dp + 2) + dk][...].astype(F32)
            out[k ^ dk, ((y ^ dp) & 1) ^ b] = total


def collect(place, pieces):
    return pl.pallas_call(
        collect_kernel,
        out_shape=shape((2, 2, 2, ROWS, NO), F32),
        in_specs=[SMEM] + [VMEM] * 8,
        out_specs=VMEM,
        compiler_params=PARAMS,
        name="collect",
    )(place, *pieces)


def shards(lesser, retarded, coupling, occupations, offsets, intersection):
    fr = lax.axis_index("freq")
    b = lax.axis_index("slab")
    y, k = fr >> 1, fr & 1
    place = jnp.stack([y, k, (y & 1) ^ b, b, y >> 1]).astype(jnp.int32)

    def flip(x, bits):
        return lax.ppermute(x, "freq", [(d, d ^ bits) for d in range(8)])

    count = lax.axis_size("energy")
    across = []
    for d in range(8):
        for e in range(count):
            target = e + 1 if d % 2 == 0 else e - 1
            if 0 <= target < count:
                across.append((d * count + e, d * count + target))

    packed, own, mine = prepare(place, occupations, offsets, coupling, lesser)
    c2, c1, c3 = flip(packed, 4), flip(packed, 2), flip(packed, 6)
    near = lax.ppermute(own, ("freq", "energy"), across)
    far = lax.ppermute(mine, ("freq", "energy"), across)
    s0 = flip(packed, 1)
    shared, s1, s3, s2 = flip(near, 1), flip(c1, 1), flip(c3, 1), flip(c2, 1)

    part, green = sandwich_first(place, own, near, shared, far, [packed, s0, c1, c3])
    total, whole, blocks = sandwich_last(place, green, part, [s1, s3, c2, s2], retarded)
    inner = flip(total, 2)
    edge = [(s * 8 + d, (1 - s) * 8 + d) for s in range(2) for d in range(8) if (d // 2) % 2]
    outer = lax.ppermute(total, ("slab", "freq"), edge)
    pieces = update(place, intersection, total, inner, outer, whole, blocks)
    return collect(place, [pieces[0]] + [flip(pieces[n], n) for n in range(1, 8)])


def solution(mesh):
    return jax.shard_map(
        shards,
        mesh=mesh,
        in_specs=(
            P("energy", "slab", None, None, None),
            P("energy", "slab", None, None, None),
            P("freq", None, None),
            P("freq"),
            P("freq"),
            P("slab"),
        ),
        out_specs=P("energy", "slab", None, "freq", None),
        check_vma=False,
    )
```

time: 258 us -> 181 us (0.70)
  waiting for transfers between devices: 152 us -> 64.4 us
  Pallas kernels: 0 us -> 84 us
  local copies, waits for them, and re-layouts: 39.5 us -> 2.97 us
  matrix products: 24.8 us -> 0 us
  between operations: 13.3 us -> 0.14 us
  starting transfers between devices: 15.6 us -> 28 us
  other arithmetic: 10.7 us -> 0 us
    all_gather x2 -> x0, waiting for transfers between devices: 86.6 us -> none  [the longest x1 54.9 us: side_by_side(): lax.all_gather(both, axis, axis=dim, tiled=True)]
    pallas_call x0 -> x5, Pallas kernels: none -> 84 us  [the longest x1 65.5 us: prepare(): pl.pallas_call(prepare_kernel, out_shape=[shape((2, NO + TAIL, NO), BF16)...]
    reduce_scatter x1 -> x0, waiting for transfers between devices: 40.7 us -> none  [shards(): lax.psum_scatter(jnp.einsum('fescrj,fkj->resck', left_product, coupling,...]
    ppermute x4 -> x19, waiting for transfers between devices: 25.1 us -> 64.4 us  [the longest x16 50.5 us: flip(): return lax.ppermute(x, 'freq', [(d, d ^ bits) for d in range(8)])]
    gather x5 -> x0, local copies, waits for them, and re-layouts: 27.2 us -> none  [the longest x3 16 us: shards(): lower_green = jnp.take(padded, positions - offsets[:, None], axis=0)]
    dot_general x9 -> x0, matrix products: 24.8 us -> none  [the longest x1 13.8 us: shards(): jnp.einsum('fescrj,fkj->resck', left_product, coupling, preferred_element...]
    ppermute x4 -> x19, starting transfers between devices: 15.5 us -> 28 us  [the longest x16 19.8 us: flip(): return lax.ppermute(x, 'freq', [(d, d ^ bits) for d in range(8)])]
    concatenate x2 -> x0, other arithmetic: 8.07 us -> none  [the longest x1 7.01 us: shards(): padded = jnp.concatenate([lower_rim, lesser, upper_rim], axis=0)]
  transfers between devices with their start and end apart: 7 -> 19, of which waited for: 6 -> 9; matrix products, arithmetic and copies ran while one was open for 2% -> 0% of each run, Pallas kernels for 0% -> 4%
where the time goes in v3:
time: 181 us; the launch traced here: 179 us
  Pallas kernels  84 us (46%)
  waiting for transfers between devices  64.4 us (36%)
  starting transfers between devices  28 us (15%)
  local copies, waits for them, and re-layouts  2.97 us (2%)
    pallas_call x1, Pallas kernels, prepare(): pl.pallas_call(prepare_kernel, out_shape=[shape((2, NO + TAIL, NO), BF16)...  65.5 us
    ppermute x16, waiting for transfers between devices, flip(): return lax.ppermute(x, 'freq', [(d, d ^ bits) for d in range(8)])  50.5 us
    ppermute x16, starting transfers between devices, flip(): return lax.ppermute(x, 'freq', [(d, d ^ bits) for d in range(8)])  19.8 us
    ppermute x1, waiting for transfers between devices, shards(): near = lax.ppermute(own, ('freq', 'energy'), across)  13.9 us
    pallas_call x1, Pallas kernels, sandwich_last(): pl.pallas_call(last_kernel, out_shape=[shape((NO, NO), BF16), shape((2, N...  7.56 us
    pallas_call x1, Pallas kernels, sandwich_first(): pl.pallas_call(first_kernel, out_shape=[shape((NO, NO), F32), shape((4, N...  6.79 us
    ppermute x1, starting transfers between devices, shards(): near = lax.ppermute(own, ('freq', 'energy'), across)  5.17 us
  transfers between devices with their start and end apart: 19, of which 9 were waited for; matrix products, arithmetic and copies ran while one was open for 0% of the time, Pallas kernels for 4%

profile of v3, /device:TPU:38, one launch (start us, length us, event | category | flops | bytes accessed | tf_op | source)
XLA Modules:
  0.0 179.4 jit_solution(11223393754345986921)
XLA Ops:
  0.0 0.7 stack.23.place
  0.7 65.5 %prepare.1 = (bf16[2,528,512]{2,1,0:T(8,128)(2,1)}, bf16[512,512]{1,0:T(8,128)(2,1)}, bf16[512,512]{1,0:T(8,128)(2,1)}) custom-call(s32[5]{0:T(128)} %stack.23.place, f32[2]{0:T(128)} %occupations.1, s32[2]{0:T(128)} %offsets.1, bf16[2,512,512]{2,1,0:T(8,128)(2,1)} %coupling.1, bf16[2,2,2,512,512]{4,3,2,1,0:T(8,128)(2,1)} %lesser.1), custom_call_target="tpu_custom_call" | custom-call | tf_op jit(solution)/shard_map/prepare/pallas_call | solution.py:63
  66.2 1.7 collective-permute-start.4
  67.8 2.2 %collective-permute-start.5 = (bf16[2,528,512]{2,1,0:T(8,128)(2,1)}, bf16[2,528,512]{2,1,0:T(8,128)(2,1)S(1)}, u32[]{:S(2)}, u32[]{:S(2)}) collective-permute-start(bf16[2,528,512]{2,1,0:T(8,128)(2,1)} %get-tuple-element.23.home), channel_id=1, source_target_pairs={{0,96},{16,112},{32,64},{48,80},{64,32},{80,48},{96,0},{112,16},{1... | collective-permute-start | bytes 3244040 | tf_op jit(solution)/shard_map/ppermute | solution.py:252
  70.0 0.7 collective-permute-start.8
  70.7 5.2 %collective-permute-start = (bf16[512,512]{1,0:T(8,128)(2,1)}, bf16[512,512]{1,0:T(8,128)(2,1)S(1)}, u32[]{:S(2)}, u32[]{:S(2)}) collective-permute-start(bf16[512,512]{1,0:T(8,128)(2,1)} %get-tuple-element.21.own), channel_id=1, source_target_pairs={{0,1},{1,2},{2,3},{3,4},{4,5},{5,6},{6,7},{7,8},{8,9},{9,10},{10,1... | collective-permute-start | bytes 1572872 | tf_op jit(solution)/shard_map/ppermute | solution.py:264
  75.9 1.5 collective-permute-start.3
  77.4 13.9 %collective-permute-done.near = bf16[512,512]{1,0:T(8,128)(2,1)S(1)} collective-permute-done((bf16[512,512]{1,0:T(8,128)(2,1)}, bf16[512,512]{1,0:T(8,128)(2,1)S(1)}, u32[]{:S(2)}, u32[]{:S(2)}) %collective-permute-start) | collective-permute-done | bytes 524320 | tf_op jit(solution)/shard_map/ppermute | solution.py:264
  91.3 2.3 %collective-permute-start.2 = (bf16[512,512]{1,0:T(8,128)(2,1)}, bf16[512,512]{1,0:T(8,128)(2,1)S(1)}, u32[]{:S(2)}, u32[]{:S(2)}) collective-permute-start(bf16[512,512]{1,0:T(8,128)(2,1)} %get-tuple-element.22), channel_id=1, source_target_pairs={{0,1},{1,2},{2,3},{3,4},{4,5},{5,6},{6,7},{7,8},{8,9},{9,10},{10,1... | collective-permute-start | bytes 1572872 | tf_op jit(solution)/shard_map/ppermute | solution.py:265
  93.6 1.4 collective-permute-start.6
  95.1 21.3 %collective-permute-done.5.c3 = bf16[2,528,512]{2,1,0:T(8,128)(2,1)S(1)} collective-permute-done((bf16[2,528,512]{2,1,0:T(8,128)(2,1)}, bf16[2,528,512]{2,1,0:T(8,128)(2,1)S(1)}, u32[]{:S(2)}, u32[]{:S(2)}) %collective-permute-start.5) | collective-permute-done | bytes 1081376 | tf_op jit(solution)/shard_map/ppermute | solution.py:252
  116.4 1.4 collective-permute-done.8.c2
  117.8 0.5 collective-permute-start.1
  118.3 3.1 %collective-permute-done.1.shared = bf16[512,512]{1,0:T(8,128)(2,1)S(1)} collective-permute-done((bf16[512,512]{1,0:T(8,128)(2,1)S(1)}, bf16[512,512]{1,0:T(8,128)(2,1)S(1)}, u32[]{:S(2)}, u32[]{:S(2)}) %collective-permute-start.1) | collective-permute-done | bytes 524320 | tf_op jit(solution)/shard_map/ppermute | solution.py:252
  121.4 1.2 copy-done.2
  122.6 1.0 copy-done.3
  123.6 6.8 %sandwich_first.1 = (f32[512,512]{1,0:T(8,128)S(1)}, bf16[4,512,512]{2,1,0:T(8,128)(2,1)S(1)}) custom-call(s32[5]{0:T(128)S(1)} %copy-done, bf16[512,512]{1,0:T(8,128)(2,1)S(1)} %copy-done.3, bf16[512,512]{1,0:T(8,128)(2,1)S(1)} %collective-permute-done.near, bf16[512,512]{1,0:T(8,128)(2,1)S(1)} %collective-permute-done.1.shared, ...), custom_call_target="tpu_custom_call" | custom-call | flops 4294967296 | bytes 9437184 | tf_op jit(solution)/shard_map/sandwich_first/pallas_call | solution.py:155
  130.5 7.6 %sandwich_last.1 = (bf16[512,512]{1,0:T(8,128)(2,1)S(1)}, bf16[2,512,512]{2,1,0:T(8,128)(2,1)S(1)}, bf16[2,512,512]{2,1,0:T(8,128)(2,1)S(1)}) custom-call(s32[5]{0:T(128)S(1)} %copy-done, bf16[4,512,512]{2,1,0:T(8,128)(2,1)S(1)} %get-tuple-element.24.green, f32[512,512]{1,0:T(8,128)S(1)} %get-tuple-element.25.start, ...), custom_call_target="tpu_custom_call" | custom-call | flops 4294967296 | bytes 9437184 | tf_op jit(solution)/shard_map/sandwich_last/pallas_call | solution.py:174
  138.1 0.8 collective-permute-start.10
  138.8 0.7 collective-permute-start.11
  139.5 12.6 %collective-permute-done.10.inner = bf16[512,512]{1,0:T(8,128)(2,1)S(1)} collective-permute-done((bf16[512,512]{1,0:T(8,128)(2,1)S(1)}, bf16[512,512]{1,0:T(8,128)(2,1)S(1)}, u32[]{:S(2)}, u32[]{:S(2)}) %collective-permute-start.10) | collective-permute-done | bytes 524320 | tf_op jit(solution)/shard_map/ppermute | solution.py:252
  152.1 2.5 %update.1 = (f32[2,64,512]{2,1,0:T(8,128)S(1)}, bf16[2,64,512]{2,1,0:T(8,128)(2,1)S(1)}, bf16[2,64,512]{2,1,0:T(8,128)(2,1)S(1)}, bf16[2,64,512]{2,1,0:T(8,128)(...) custom-call(s32[5]{0:T(128)S(1)} %copy-done, ...), custom_call_target="tpu_custom_call" | custom-call | flops 1610612736 | bytes 5242880 | tf_op jit(solution)/shard_map/update/pallas_call | solution.py:212
  154.6 0.3 collective-permute-start.12
  154.9 3.7 %collective-permute-start.13 = (bf16[2,64,512]{2,1,0:T(8,128)(2,1)S(1)}, bf16[2,64,512]{2,1,0:T(8,128)(2,1)S(1)}, u32[]{:S(2)}, u32[]{:S(2)}) collective-permute-start(bf16[2,64,512]{2,1,0:T(8,128)(2,1)S(1)} %get-tuple-element.31), channel_id=1, source_target_pairs={{0,32},{16,48},{32,0},{48,16},{64,96},{80,112},{96,64},{112,80},{1... | collective-permute-start | bytes 393224 | tf_op jit(solution)/shard_map/ppermute | solution.py:252
  158.7 3.3 %collective-permute-start.15 = (bf16[2,64,512]{2,1,0:T(8,128)(2,1)S(1)}, bf16[2,64,512]{2,1,0:T(8,128)(2,1)S(1)}, u32[]{:S(2)}, u32[]{:S(2)}) collective-permute-start(bf16[2,64,512]{2,1,0:T(8,128)(2,1)S(1)} %get-tuple-element.33), channel_id=1, source_target_pairs={{0,64},{16,80},{32,96},{48,112},{64,0},{80,16},{96,32},{112,48},{1... | collective-permute-start | bytes 393224 | tf_op jit(solution)/shard_map/ppermute | solution.py:252
  162.1 3.5 %collective-permute-start.17 = (bf16[2,64,512]{2,1,0:T(8,128)(2,1)S(1)}, bf16[2,64,512]{2,1,0:T(8,128)(2,1)S(1)}, u32[]{:S(2)}, u32[]{:S(2)}) collective-permute-start(bf16[2,64,512]{2,1,0:T(8,128)(2,1)S(1)} %get-tuple-element.35), channel_id=1, source_target_pairs={{0,96},{16,112},{32,64},{48,80},{64,32},{80,48},{96,0},{112,16},{1... | collective-permute-start | bytes 393224 | tf_op jit(solution)/shard_map/ppermute | solution.py:252
  165.5 0.1 collective-permute-start.18
  165.7 6.3 %collective-permute-done.15.refs_4_ = bf16[2,64,512]{2,1,0:T(8,128)(2,1)S(1)} collective-permute-done((bf16[2,64,512]{2,1,0:T(8,128)(2,1)S(1)}, bf16[2,64,512]{2,1,0:T(8,128)(2,1)S(1)}, u32[]{:S(2)}, u32[]{:S(2)}) %collective-permute-start.15) | collective-permute-done | bytes 131104 | tf_op jit(solution)/shard_map/ppermute | solution.py:252
  172.0 1.9 %collective-permute-done.16.refs_5_ = bf16[2,64,512]{2,1,0:T(8,128)(2,1)S(1)} collective-permute-done((bf16[2,64,512]{2,1,0:T(8,128)(2,1)S(1)}, bf16[2,64,512]{2,1,0:T(8,128)(2,1)S(1)}, u32[]{:S(2)}, u32[]{:S(2)}) %collective-permute-start.16) | collective-permute-done | bytes 131104 | tf_op jit(solution)/shard_map/ppermute | solution.py:252
  173.8 1.6 collective-permute-done.17.refs_6_
  175.5 2.3 %collective-permute-done.18.refs_7_ = bf16[2,64,512]{2,1,0:T(8,128)(2,1)S(1)} collective-permute-done((bf16[2,64,512]{2,1,0:T(8,128)(2,1)S(1)}, bf16[2,64,512]{2,1,0:T(8,128)(2,1)S(1)}, u32[]{:S(2)}, u32[]{:S(2)}) %collective-permute-start.18) | collective-permute-done | bytes 131104 | tf_op jit(solution)/shard_map/ppermute | solution.py:252
  177.8 1.6 collect.1
  (22 shorter events, 0.1 us)
Async XLA Ops:
  0.7 120.7 %copy-start = (s32[5]{0:T(128)S(1)}, s32[5]{0:T(128)}, u32[]{:S(2)}) copy-start(s32[5]{0:T(128)} %stack.23.place) | copy-start | bytes 64
  66.2 27.4 %collective-permute-start.4 = (bf16[2,528,512]{2,1,0:T(8,128)(2,1)}, bf16[2,528,512]{2,1,0:T(8,128)(2,1)S(1)}, u32[]{:S(2)}, u32[]{:S(2)}) collective-permute-start(bf16[2,528,512]{2,1,0:T(8,128)(2,1)} %get-tuple-element.23.home), channel_id=1, source_target_pairs={{0,32},{16,48},{32,0},{48,16},{64,96},{80,112},{96,64},{112,80},{1... | collective-permute-start | bytes 3244040 | tf_op jit(solution)/shard_map/ppermute | solution.py:252
  67.8 48.5 %collective-permute-start.5 = (bf16[2,528,512]{2,1,0:T(8,128)(2,1)}, bf16[2,528,512]{2,1,0:T(8,128)(2,1)S(1)}, u32[]{:S(2)}, u32[]{:S(2)}) collective-permute-start(bf16[2,528,512]{2,1,0:T(8,128)(2,1)} %get-tuple-element.23.home), channel_id=1, source_target_pairs={{0,96},{16,112},{32,64},{48,80},{64,32},{80,48},{96,0},{112,16},{1... | collective-permute-start | bytes 3244040 | tf_op jit(solution)/shard_map/ppermute | solution.py:252
  70.0 47.7 %collective-permute-start.8 = (bf16[2,528,512]{2,1,0:T(8,128)(2,1)}, bf16[2,528,512]{2,1,0:T(8,128)(2,1)S(1)}, u32[]{:S(2)}, u32[]{:S(2)}) collective-permute-start(bf16[2,528,512]{2,1,0:T(8,128)(2,1)} %get-tuple-element.23.home), channel_id=1, source_target_pairs={{0,64},{16,80},{32,96},{48,112},{64,0},{80,16},{96,32},{112,48},{1... | collective-permute-start | bytes 3244040 | tf_op jit(solution)/shard_map/ppermute | solution.py:252
  70.7 20.5 %collective-permute-start = (bf16[512,512]{1,0:T(8,128)(2,1)}, bf16[512,512]{1,0:T(8,128)(2,1)S(1)}, u32[]{:S(2)}, u32[]{:S(2)}) collective-permute-start(bf16[512,512]{1,0:T(8,128)(2,1)} %get-tuple-element.21.own), channel_id=1, source_target_pairs={{0,1},{1,2},{2,3},{3,4},{4,5},{5,6},{6,7},{7,8},{8,9},{9,10},{10,1... | collective-permute-start | bytes 1572872 | tf_op jit(solution)/shard_map/ppermute | solution.py:264
  75.9 45.4 %collective-permute-start.3 = (bf16[2,528,512]{2,1,0:T(8,128)(2,1)}, bf16[2,528,512]{2,1,0:T(8,128)(2,1)S(1)}, u32[]{:S(2)}, u32[]{:S(2)}) collective-permute-start(bf16[2,528,512]{2,1,0:T(8,128)(2,1)} %get-tuple-element.23.home), channel_id=1, source_target_pairs={{0,16},{16,0},{32,48},{48,32},{64,80},{80,64},{96,112},{112,96},{1... | collective-permute-start | bytes 3244040 | tf_op jit(solution)/shard_map/ppermute | solution.py:252
  91.3 39.2 %copy-start.1 = (bf16[2,2,2,512,512]{4,3,2,1,0:T(8,128)(2,1)S(1)}, bf16[2,2,2,512,512]{4,3,2,1,0:T(8,128)(2,1)}, u32[]{:S(2)}) copy-start(bf16[2,2,2,512,512]{4,3,2,1,0:T(8,128)(2,1)} %retarded.1) | copy-start | bytes 12582916
  91.3 26.5 %collective-permute-start.2 = (bf16[512,512]{1,0:T(8,128)(2,1)}, bf16[512,512]{1,0:T(8,128)(2,1)S(1)}, u32[]{:S(2)}, u32[]{:S(2)}) collective-permute-start(bf16[512,512]{1,0:T(8,128)(2,1)} %get-tuple-element.22), channel_id=1, source_target_pairs={{0,1},{1,2},{2,3},{3,4},{4,5},{5,6},{6,7},{7,8},{8,9},{9,10},{10,1... | collective-permute-start | bytes 1572872 | tf_op jit(solution)/shard_map/ppermute | solution.py:265
  93.6 36.8 %collective-permute-start.6 = (bf16[2,528,512]{2,1,0:T(8,128)(2,1)S(1)}, bf16[2,528,512]{2,1,0:T(8,128)(2,1)S(1)}, u32[]{:S(2)}, u32[]{:S(2)}) collective-permute-start(bf16[2,528,512]{2,1,0:T(8,128)(2,1)S(1)} %collective-permute-done.4.c1), channel_id=1, source_target_pairs={{0,16},{16,0},{32,48},{48,32},{64,80},{80,64},{96,112},{112,96},{1... | collective-permute-start | bytes 3244040 | tf_op jit(solution)/shard_map/ppermute | solution.py:252
  116.4 14.1 %collective-permute-start.7 = (bf16[2,528,512]{2,1,0:T(8,128)(2,1)S(1)}, bf16[2,528,512]{2,1,0:T(8,128)(2,1)S(1)}, u32[]{:S(2)}, u32[]{:S(2)}) collective-permute-start(bf16[2,528,512]{2,1,0:T(8,128)(2,1)S(1)} %collective-permute-done.5.c3), channel_id=1, source_target_pairs={{0,16},{16,0},{32,48},{48,32},{64,80},{80,64},{96,112},{112,96},{1... | collective-permute-start | bytes 3244040 | tf_op jit(solution)/shard_map/ppermute | solution.py:252
  117.8 12.7 %collective-permute-start.9 = (bf16[2,528,512]{2,1,0:T(8,128)(2,1)S(1)}, bf16[2,528,512]{2,1,0:T(8,128)(2,1)S(1)}, u32[]{:S(2)}, u32[]{:S(2)}) collective-permute-start(bf16[2,528,512]{2,1,0:T(8,128)(2,1)S(1)} %collective-permute-done.8.c2), channel_id=1, source_target_pairs={{0,16},{16,0},{32,48},{48,32},{64,80},{80,64},{96,112},{112,96},{1... | collective-permute-start | bytes 3244040 | tf_op jit(solution)/shard_map/ppermute | solution.py:252
  117.8 3.6 %collective-permute-start.1 = (bf16[512,512]{1,0:T(8,128)(2,1)S(1)}, bf16[512,512]{1,0:T(8,128)(2,1)S(1)}, u32[]{:S(2)}, u32[]{:S(2)}) collective-permute-start(bf16[512,512]{1,0:T(8,128)(2,1)S(1)} %collective-permute-done.near), channel_id=1, source_target_pairs={{0,16},{16,0},{32,48},{48,32},{64,80},{80,64},{96,112},{112,96},{1... | collective-permute-start | bytes 1572872 | tf_op jit(solution)/shard_map/ppermute | solution.py:252
  121.4 1.2 copy-start.2
  122.6 1.0 copy-start.3
  130.5 21.6 %copy-start.4 = (f32[2]{0:T(128)S(1)}, f32[2]{0:T(128)}, u32[]{:S(2)}) copy-start(f32[2]{0:T(128)} %weight.1) | copy-start | bytes 28
  138.1 14.1 %collective-permute-start.10 = (bf16[512,512]{1,0:T(8,128)(2,1)S(1)}, bf16[512,512]{1,0:T(8,128)(2,1)S(1)}, u32[]{:S(2)}, u32[]{:S(2)}) collective-permute-start(bf16[512,512]{1,0:T(8,128)(2,1)S(1)} %get-tuple-element.26.own), channel_id=1, source_target_pairs={{0,32},{16,48},{32,0},{48,16},{64,96},{80,112},{96,64},{112,80},{1... | collective-permute-start | bytes 1572872 | tf_op jit(solution)/shard_map/ppermute | solution.py:252
  138.8 13.3 %collective-permute-start.11 = (bf16[512,512]{1,0:T(8,128)(2,1)S(1)}, bf16[512,512]{1,0:T(8,128)(2,1)S(1)}, u32[]{:S(2)}, u32[]{:S(2)}) collective-permute-start(bf16[512,512]{1,0:T(8,128)(2,1)S(1)} %get-tuple-element.26.own), channel_id=1, source_target_pairs={{32,160},{48,176},{96,224},{112,240},{160,32},{176,48},{224,96},{2... | collective-permute-start | bytes 1572872 | tf_op jit(solution)/shard_map/ppermute | solution.py:273
  154.6 7.4 %collective-permute-start.12 = (bf16[2,64,512]{2,1,0:T(8,128)(2,1)S(1)}, bf16[2,64,512]{2,1,0:T(8,128)(2,1)S(1)}, u32[]{:S(2)}, u32[]{:S(2)}) collective-permute-start(bf16[2,64,512]{2,1,0:T(8,128)(2,1)S(1)} %get-tuple-element.30), channel_id=1, source_target_pairs={{0,16},{16,0},{32,48},{48,32},{64,80},{80,64},{96,112},{112,96},{1... | collective-permute-start | bytes 393224 | tf_op jit(solution)/shard_map/ppermute | solution.py:252
  154.9 10.6 %collective-permute-start.13 = (bf16[2,64,512]{2,1,0:T(8,128)(2,1)S(1)}, bf16[2,64,512]{2,1,0:T(8,128)(2,1)S(1)}, u32[]{:S(2)}, u32[]{:S(2)}) collective-permute-start(bf16[2,64,512]{2,1,0:T(8,128)(2,1)S(1)} %get-tuple-element.31), channel_id=1, source_target_pairs={{0,32},{16,48},{32,0},{48,16},{64,96},{80,112},{96,64},{112,80},{1... | collective-permute-start | bytes 393224 | tf_op jit(solution)/shard_map/ppermute | solution.py:252
  158.7 7.0 %collective-permute-start.14 = (bf16[2,64,512]{2,1,0:T(8,128)(2,1)S(1)}, bf16[2,64,512]{2,1,0:T(8,128)(2,1)S(1)}, u32[]{:S(2)}, u32[]{:S(2)}) collective-permute-start(bf16[2,64,512]{2,1,0:T(8,128)(2,1)S(1)} %get-tuple-element.32), channel_id=1, source_target_pairs={{0,48},{16,32},{32,16},{48,0},{64,112},{80,96},{96,80},{112,64},{1... | collective-permute-start | bytes 393224 | tf_op jit(solution)/shard_map/ppermute | solution.py:252
  158.7 13.3 %collective-permute-start.15 = (bf16[2,64,512]{2,1,0:T(8,128)(2,1)S(1)}, bf16[2,64,512]{2,1,0:T(8,128)(2,1)S(1)}, u32[]{:S(2)}, u32[]{:S(2)}) collective-permute-start(bf16[2,64,512]{2,1,0:T(8,128)(2,1)S(1)} %get-tuple-element.33), channel_id=1, source_target_pairs={{0,64},{16,80},{32,96},{48,112},{64,0},{80,16},{96,32},{112,48},{1... | collective-permute-start | bytes 393224 | tf_op jit(solution)/shard_map/ppermute | solution.py:252
  162.0 11.8 %collective-permute-start.16 = (bf16[2,64,512]{2,1,0:T(8,128)(2,1)S(1)}, bf16[2,64,512]{2,1,0:T(8,128)(2,1)S(1)}, u32[]{:S(2)}, u32[]{:S(2)}) collective-permute-start(bf16[2,64,512]{2,1,0:T(8,128)(2,1)S(1)} %get-tuple-element.34), channel_id=1, source_target_pairs={{0,80},{16,64},{32,112},{48,96},{64,16},{80,0},{96,48},{112,32},{1... | collective-permute-start | bytes 393224 | tf_op jit(solution)/shard_map/ppermute | solution.py:252
  162.1 13.4 %collective-permute-start.17 = (bf16[2,64,512]{2,1,0:T(8,128)(2,1)S(1)}, bf16[2,64,512]{2,1,0:T(8,128)(2,1)S(1)}, u32[]{:S(2)}, u32[]{:S(2)}) collective-permute-start(bf16[2,64,512]{2,1,0:T(8,128)(2,1)S(1)} %get-tuple-element.35), channel_id=1, source_target_pairs={{0,96},{16,112},{32,64},{48,80},{64,32},{80,48},{96,0},{112,16},{1... | collective-permute-start | bytes 393224 | tf_op jit(solution)/shard_map/ppermute | solution.py:252
  165.5 12.3 %collective-permute-start.18 = (bf16[2,64,512]{2,1,0:T(8,128)(2,1)S(1)}, bf16[2,64,512]{2,1,0:T(8,128)(2,1)S(1)}, u32[]{:S(2)}, u32[]{:S(2)}) collective-permute-start(bf16[2,64,512]{2,1,0:T(8,128)(2,1)S(1)} %get-tuple-element.36), channel_id=1, source_target_pairs={{0,112},{16,96},{32,80},{48,64},{64,48},{80,32},{96,16},{112,0},{1... | collective-permute-start | bytes 393224 | tf_op jit(solution)/shard_map/ppermute | solution.py:252

commit v4 on v3

v4 whole, which is shorter than its diff:
```python
import functools
import jax
import jax.numpy as jnp
from jax import lax
from jax.experimental import pallas as pl
from jax.experimental.pallas import tpu as pltpu
from jax.sharding import PartitionSpec as P

NO = 512
ROWS = 64
TAIL = 16
F32 = jnp.float32
BF16 = jnp.bfloat16
MIB = 1 << 20
HBM = pl.BlockSpec(memory_space=pltpu.HBM)
SMEM = pl.BlockSpec(memory_space=pltpu.SMEM)
VMEM = pl.BlockSpec(memory_space=pltpu.VMEM)
PARAMS = pltpu.CompilerParams(vmem_limit_bytes=24 * MIB)


def shape(dims, kind):
    return jax.ShapeDtypeStruct(dims, kind)


def mul(a, b):
    return jnp.dot(a, b, preferred_element_type=F32)


def mul_t(a, b):
    return lax.dot_general(a, b, (((1,), (1,)), ((), ())), preferred_element_type=F32)


def prepare_kernel(
    place, occupations, offsets, coupling, lesser, packed, half, near, far, sem
):
    k, sl, c, x = place[1], place[2], place[4], place[5]
    copies = [
        pltpu.make_async_copy(lesser.at[1 - k, sl, c], near, sem.at[0]),
        pltpu.make_async_copy(lesser.at[k, sl, c], far, sem.at[1]),
        pltpu.make_async_copy(coupling.at[x], half.at[pl.ds(0, NO)], sem.at[2]),
    ]
    for t in range(2):
        copies.append(
            pltpu.make_async_copy(coupling.at[t], packed.at[t, pl.ds(0, NO)], sem.at[3 + t])
        )
    for copy in copies:
        copy.start()
    row = lax.broadcasted_iota(jnp.int32, (TAIL, NO), 0)

    def tail_of(t):
        whole = jnp.full((TAIL, NO), occupations[t], F32)
        high = whole.astype(BF16).astype(F32)
        middle = (whole - high).astype(BF16).astype(F32)
        low = whole - high - middle
        steps = jnp.full((TAIL, NO), offsets[t], jnp.int32).astype(F32)
        rows = jnp.where(row == 2, low, steps)
        return jnp.where(row == 0, high, jnp.where(row == 1, middle, rows)).astype(BF16)

    packed[0, NO:] = tail_of(0)
    packed[1, NO:] = tail_of(1)
    half[NO:] = tail_of(x)
    for copy in copies:
        copy.wait()


def prepare(place, occupations, offsets, coupling, lesser):
    block = (NO + TAIL, NO)
    return pl.pallas_call(
        prepare_kernel,
        out_shape=[shape((2, *block), BF16), shape(block, BF16)] + [shape((NO, NO), BF16)] * 2,
        in_specs=[SMEM] * 3 + [HBM] * 2,
        out_specs=[VMEM] * 4,
        scratch_shapes=[pltpu.SemaphoreType.DMA((5,))],
        compiler_params=pltpu.CompilerParams(vmem_limit_bytes=60 * MIB),
        name="prepare",
    )(place, occupations, offsets, coupling, lesser)


def add_terms(k, green, todo):
    def numbers_of(block):
        tail = block[NO:, :].astype(F32)
        scale = tail[0:1] + tail[1:2] + tail[2:3]
        return scale, (jnp.max(tail[3:4, 0:128]) > 1.5).astype(jnp.int32)

    back = k.astype(F32)
    numbers = numbers_of(todo[0])
    for n, block in enumerate(todo):
        scale, far = numbers
        if n + 1 < len(todo):
            numbers = numbers_of(todo[n + 1])
        mixture = (
            (scale + (1.0 - back)) * green[2 * far].astype(F32)
            + (scale + back) * green[2 * far + 1].astype(F32)
        ).astype(BF16)
        weights = block[:NO, :]
        left = mul(weights, mixture).astype(BF16)
        yield mul_t(left, weights)


def blocks_of(refs):
    todo = []
    for ref in refs:
        todo += [ref.at[t] for t in range(2)] if len(ref.shape) == 3 else [ref]
    return todo


def first_kernel(place, own, near, shared, far, home, c1, c3, half, other, out, green, gsem):
    copies = [
        pltpu.make_async_copy(src, green.at[n], gsem.at[n])
        for n, src in enumerate((own, near, shared, far))
    ]
    for copy in copies:
        copy.start()
    for copy in copies:
        copy.wait()
    todo = blocks_of((home, c1, c3, half, other))
    for n, term in enumerate(add_terms(place[1], green, todo)):
        out[...] = term if n == 0 else out[...] + term


def last_kernel(
    place, green, start, s0, s1, s3, half, other, retarded, out, whole, acc, rsem
):
    k, sl = place[1], place[2]
    copies = [pltpu.make_async_copy(retarded.at[k, sl], whole, rsem.at[0])]
    todo = blocks_of((s0, s1, s3, half, other))
    for copy in copies:
        copy.start()
    for n, term in enumerate(add_terms(k, green, todo)):
        total = (start if n == 0 else acc)[...] + term
        if n == len(todo) - 1:
            out[...] = total.astype(BF16)
        else:
            acc[...] = total
    for copy in copies:
        copy.wait()


COST = pl.CostEstimate(flops=8 * 4 * NO**3, bytes_accessed=18 * NO * NO * 2, transcendentals=0)


def sandwich_first(place, greens, arrays):
    return pl.pallas_call(
        first_kernel,
        out_shape=[shape((NO, NO), F32), shape((4, NO, NO), BF16)],
        in_specs=[SMEM] + [VMEM] * 9,
        out_specs=[VMEM] * 2,
        scratch_shapes=[pltpu.SemaphoreType.DMA((4,))],
        compiler_params=PARAMS,
        cost_estimate=COST,
        name="sandwich_first",
    )(place, *greens, *arrays)


def sandwich_last(place, green, start, arrays, retarded):
    return pl.pallas_call(
        last_kernel,
        out_shape=[shape((NO, NO), BF16), shape((2, NO, NO), BF16)],
        in_specs=[SMEM] + [VMEM] * 7 + [HBM],
        out_specs=[VMEM] * 2,
        scratch_shapes=[pltpu.VMEM((NO, NO), F32), pltpu.SemaphoreType.DMA((1,))],
        compiler_params=PARAMS,
        cost_estimate=COST,
        name="sandwich_last",
    )(place, green, start, *arrays, retarded)


def update_kernel(place, weight, own, inner, outer, green, out):
    sl, c = place[2], place[4]
    beside = inner[...].astype(F32) + outer[...].astype(F32)
    combined = (own[...].astype(F32) + weight[sl] * beside).astype(BF16)
    a, b = green[0], green[1]
    a_side = mul_t(combined, a).astype(BF16)
    b_side = mul_t(combined, b).astype(BF16)
    real = mul(a, a_side) + mul(b, b_side)
    imag = mul(b, a_side) - mul(a, b_side)
    first = jnp.where(c == 0, real, -imag).astype(BF16)
    second = jnp.where(c == 0, imag, real).astype(BF16)
    for dest in range(8):
        rows = slice(dest * ROWS, (dest + 1) * ROWS)
        out[dest, 0] = first[rows]
        out[dest, 1] = second[rows]


def update(place, weight, own, inner, outer, green):
    return pl.pallas_call(
        update_kernel,
        out_shape=shape((8, 2, ROWS, NO), BF16),
        in_specs=[SMEM] * 2 + [VMEM] * 4,
        out_specs=VMEM,
        compiler_params=PARAMS,
        cost_estimate=pl.CostEstimate(
            flops=12 * NO**3, bytes_accessed=10 * NO * NO * 2, transcendentals=0
        ),
        name="update",
    )(place, weight, own, inner, outer, green)


def collect_kernel(place, pieces, out):
    b = place[3]
    for k in range(2):
        for parity in range(2):
            source = 2 * parity + k
            total = pieces[source].astype(F32) + pieces[source + 4].astype(F32)
            out[k, parity ^ b] = total


def collect(place, pieces):
    return pl.pallas_call(
        collect_kernel,
        out_shape=shape((2, 2, 2, ROWS, NO), F32),
        in_specs=[SMEM, VMEM],
        out_specs=VMEM,
        compiler_params=PARAMS,
        name="collect",
    )(place, pieces)


def shards(lesser, retarded, coupling, occupations, offsets, intersection):
    fr = lax.axis_index("freq")
    b = lax.axis_index("slab")
    y, k = fr >> 1, fr & 1
    x = (lax.axis_index("energy") >> 2) & 1
    place = jnp.stack([y, k, (y & 1) ^ b, b, y >> 1, x]).astype(jnp.int32)

    def flip(x, bits):
        return lax.ppermute(x, "freq", [(d, d ^ bits) for d in range(8)])

    count = lax.axis_size("energy")
    across = []
    for d in range(8):
        for e in range(count):
            target = e + 1 if d % 2 == 0 else e - 1
            if 0 <= target < count:
                across.append((d * count + e, d * count + target))

    packed, part, own, mine = prepare(place, occupations, offsets, coupling, lesser)
    half = flip(part, 4)
    other = lax.ppermute(half, "energy", [(e, e ^ 4) for e in range(count)])
    c1, c3 = flip(packed, 2), flip(packed, 6)
    near = lax.ppermute(own, ("freq", "energy"), across)
    far = lax.ppermute(mine, ("freq", "energy"), across)
    shared = flip(near, 1)
    swapped = [flip(x, 1) for x in (packed, c1, c3, half, other)]

    first, green = sandwich_first(
        place, [own, near, shared, far], [packed, c1, c3, half, other]
    )
    total, whole = sandwich_last(place, green, first, swapped, retarded)
    inner = flip(total, 2)
    edge = [(s * 8 + d, (1 - s) * 8 + d) for s in range(2) for d in range(8) if (d // 2) % 2]
    outer = lax.ppermute(total, ("slab", "freq"), edge)
    pieces = update(place, intersection, total, inner, outer, whole)
    return collect(place, lax.all_to_all(pieces, "freq", 0, 0))


def solution(mesh):
    return jax.shard_map(
        shards,
        mesh=mesh,
        in_specs=(
            P("energy", "slab", None, None, None),
            P("energy", "slab", None, None, None),
            P("freq", None, None),
            P("freq"),
            P("freq"),
            P("slab"),
        ),
        out_specs=P("energy", "slab", None, "freq", None),
        check_vma=False,
    )
```

time: 181 us -> 112 us (0.62)
  Pallas kernels: 84 us -> 19.3 us
  blocking collectives: 0 us -> 20.8 us
  waiting for transfers between devices: 64.4 us -> 49.5 us
  starting transfers between devices: 28 us -> 18 us
    pallas_call x2, Pallas kernels: 68 us -> 6.48 us  [the longest x1 3.97 us: prepare(): pl.pallas_call(prepare_kernel, out_shape=[shape((2, *block), BF16), shape...]
    ppermute x16 -> x10, waiting for transfers between devices: 50.5 us -> 27.2 us  [flip(): return lax.ppermute(x, 'freq', [(d, d ^ bits) for d in range(8)])]
    all_to_all x0 -> x1, blocking collectives: none -> 20.8 us  [shards(): return collect(place, lax.all_to_all(pieces, 'freq', 0, 0))]
    ppermute x16 -> x10, starting transfers between devices: 19.8 us -> 5.53 us  [flip(): return lax.ppermute(x, 'freq', [(d, d ^ bits) for d in range(8)])]
    ppermute x0 -> x1, waiting for transfers between devices: none -> 7.11 us  [shards(): other = lax.ppermute(half, 'energy', [(e, e ^ 4) for e in range(count)])]
    ppermute x1, starting transfers between devices: 2.32 us -> 5.75 us  [shards(): far = lax.ppermute(mine, ('freq', 'energy'), across)]
    pallas_call x1, Pallas kernels: 7.56 us -> 5.55 us  [sandwich_last(): pl.pallas_call(last_kernel, out_shape=[shape((NO, NO), BF16), shape((2, N...]
  transfers between devices with their start and end apart: 19 -> 14, of which waited for: 9 -> 5; matrix products, arithmetic and copies ran while one was open for 0% -> 0% of each run, Pallas kernels for 4% -> 5%
where the time goes in v4:
time: 112 us; the launch traced here: 111 us
  waiting for transfers between devices  49.5 us (44%)
  blocking collectives  20.8 us (19%)
  Pallas kernels  19.3 us (17%)
  starting transfers between devices  18 us (16%)
  local copies, waits for them, and re-layouts  2.94 us (3%)
    ppermute x10, waiting for transfers between devices, flip(): return lax.ppermute(x, 'freq', [(d, d ^ bits) for d in range(8)])  27.2 us
    all_to_all x1, blocking collectives, shards(): return collect(place, lax.all_to_all(pieces, 'freq', 0, 0))  20.8 us
    ppermute x1, waiting for transfers between devices, shards(): near = lax.ppermute(own, ('freq', 'energy'), across)  15.2 us
    ppermute x1, waiting for transfers between devices, shards(): other = lax.ppermute(half, 'energy', [(e, e ^ 4) for e in range(count)])  7.11 us
    ppermute x1, starting transfers between devices, shards(): far = lax.ppermute(mine, ('freq', 'energy'), across)  5.75 us
    pallas_call x1, Pallas kernels, sandwich_first(): pl.pallas_call(first_kernel, out_shape=[shape((NO, NO), F32), shape((4, N...  5.63 us
    pallas_call x1, Pallas kernels, sandwich_last(): pl.pallas_call(last_kernel, out_shape=[shape((NO, NO), BF16), shape((2, N...  5.55 us
    ppermute x10, starting transfers between devices, flip(): return lax.ppermute(x, 'freq', [(d, d ^ bits) for d in range(8)])  5.53 us
  transfers between devices with their start and end apart: 14, of which 5 were waited for; matrix products, arithmetic and copies ran while one was open for 0% of the time, Pallas kernels for 5%

profile of v4, /device:TPU:38, one launch (start us, length us, event | category | flops | bytes accessed | tf_op | source)
XLA Modules:
  0.0 110.6 jit_solution(17213711685276874132)
XLA Ops:
  0.0 0.7 stack.27.place
  0.7 4.0 %prepare.1 = (bf16[2,528,512]{2,1,0:T(8,128)(2,1)}, bf16[528,512]{1,0:T(8,128)(2,1)}, bf16[512,512]{1,0:T(8,128)(2,1)}, bf16[512,512]{1,0:T(8,128)(2,1)}) custom-call(s32[6]{0:T(128)} %stack.27.place, f32[2]{0:T(128)} %occupations.1, s32[2]{0:T(128)} %offsets.1, bf16[2,512,512]{2,1,0:T(8,128)(2,1)} %coupling.1, bf16[2,2,2,512,512]{4,3,2,1,0:T(8,128)(2,1)} %lesser.1), custom_call_target="tpu_custom_call" | custom-call | tf_op jit(solution)/shard_map/prepare/pallas_call | solution.py:68
  4.6 1.7 %collective-permute-start.3 = (bf16[2,528,512]{2,1,0:T(8,128)(2,1)}, bf16[2,528,512]{2,1,0:T(8,128)(2,1)S(1)}, u32[]{:S(2)}, u32[]{:S(2)}) collective-permute-start(bf16[2,528,512]{2,1,0:T(8,128)(2,1)} %get-tuple-element.15.home), channel_id=1, source_target_pairs={{0,32},{16,48},{32,0},{48,16},{64,96},{80,112},{96,64},{112,80},{1... | collective-permute-start | bytes 3244040 | tf_op jit(solution)/shard_map/ppermute | solution.py:227
  6.3 2.2 %collective-permute-start.4 = (bf16[2,528,512]{2,1,0:T(8,128)(2,1)}, bf16[2,528,512]{2,1,0:T(8,128)(2,1)S(1)}, u32[]{:S(2)}, u32[]{:S(2)}) collective-permute-start(bf16[2,528,512]{2,1,0:T(8,128)(2,1)} %get-tuple-element.15.home), channel_id=1, source_target_pairs={{0,96},{16,112},{32,64},{48,80},{64,32},{80,48},{96,0},{112,16},{1... | collective-permute-start | bytes 3244040 | tf_op jit(solution)/shard_map/ppermute | solution.py:227
  8.5 0.7 collective-permute-start.5
  9.2 5.2 %collective-permute-start = (bf16[512,512]{1,0:T(8,128)(2,1)}, bf16[512,512]{1,0:T(8,128)(2,1)S(1)}, u32[]{:S(2)}, u32[]{:S(2)}) collective-permute-start(bf16[512,512]{1,0:T(8,128)(2,1)} %get-tuple-element.13.own), channel_id=1, source_target_pairs={{0,1},{1,2},{2,3},{3,4},{4,5},{5,6},{6,7},{7,8},{8,9},{9,10},{10,1... | collective-permute-start | bytes 1572872 | tf_op jit(solution)/shard_map/ppermute | solution.py:241
  14.4 0.0 copy-start.1
  14.4 5.8 %collective-permute-start.2 = (bf16[512,512]{1,0:T(8,128)(2,1)}, bf16[512,512]{1,0:T(8,128)(2,1)S(1)}, u32[]{:S(2)}, u32[]{:S(2)}) collective-permute-start(bf16[512,512]{1,0:T(8,128)(2,1)} %get-tuple-element.14), channel_id=1, source_target_pairs={{0,1},{1,2},{2,3},{3,4},{4,5},{5,6},{6,7},{7,8},{8,9},{9,10},{10,1... | collective-permute-start | bytes 1572872 | tf_op jit(solution)/shard_map/ppermute | solution.py:242
  20.1 15.2 %collective-permute-done.near = bf16[512,512]{1,0:T(8,128)(2,1)S(1)} collective-permute-done((bf16[512,512]{1,0:T(8,128)(2,1)}, bf16[512,512]{1,0:T(8,128)(2,1)S(1)}, u32[]{:S(2)}, u32[]{:S(2)}) %collective-permute-start) | collective-permute-done | bytes 524320 | tf_op jit(solution)/shard_map/ppermute | solution.py:241
  35.4 0.0 collective-permute-start.7
  35.4 9.3 %collective-permute-done.5.half = bf16[528,512]{1,0:T(8,128)(2,1)S(1)} collective-permute-done((bf16[528,512]{1,0:T(8,128)(2,1)}, bf16[528,512]{1,0:T(8,128)(2,1)S(1)}, u32[]{:S(2)}, u32[]{:S(2)}) %collective-permute-start.5) | collective-permute-done | bytes 540704 | tf_op jit(solution)/shard_map/ppermute | solution.py:227
  44.6 0.8 collective-permute-start.6
  45.5 0.0 collective-permute-done.3.c1
  45.5 0.0 collective-permute-start.8
  45.5 0.0 collective-permute-done.4.c3
  45.5 0.5 collective-permute-start.9
  46.0 0.1 collective-permute-start.1
  46.1 4.4 %collective-permute-done.1.shared = bf16[512,512]{1,0:T(8,128)(2,1)S(1)} collective-permute-done((bf16[512,512]{1,0:T(8,128)(2,1)S(1)}, bf16[512,512]{1,0:T(8,128)(2,1)S(1)}, u32[]{:S(2)}, u32[]{:S(2)}) %collective-permute-start.1) | collective-permute-done | bytes 524320 | tf_op jit(solution)/shard_map/ppermute | solution.py:227
  50.5 0.1 collective-permute-start.10
  50.6 7.1 %collective-permute-done.6.other = bf16[528,512]{1,0:T(8,128)(2,1)S(1)} collective-permute-done((bf16[528,512]{1,0:T(8,128)(2,1)S(1)}, bf16[528,512]{1,0:T(8,128)(2,1)S(1)}, u32[]{:S(2)}, u32[]{:S(2)}) %collective-permute-start.6) | collective-permute-done | bytes 540704 | tf_op jit(solution)/shard_map/ppermute | solution.py:239
  57.7 0.0 collective-permute-start.11
  57.7 1.2 %copy-done.2 = bf16[2,528,512]{2,1,0:T(8,128)(2,1)S(1)} copy-done((bf16[2,528,512]{2,1,0:T(8,128)(2,1)S(1)}, bf16[2,528,512]{2,1,0:T(8,128)(2,1)}, u32[]{:S(2)}) %copy-start.2) | copy-done | bytes 1081368
  59.0 1.0 copy-done.3
  60.0 5.6 %sandwich_first.1 = (f32[512,512]{1,0:T(8,128)S(1)}, bf16[4,512,512]{2,1,0:T(8,128)(2,1)S(1)}) custom-call(s32[6]{0:T(128)S(1)} %copy-done, bf16[512,512]{1,0:T(8,128)(2,1)S(1)} %copy-done.3, bf16[512,512]{1,0:T(8,128)(2,1)S(1)} %collective-permute-done.near, bf16[512,512]{1,0:T(8,128)(2,1)S(1)} %collective-permute-done.1.shared, ...), custom_call_target="tpu_custom_call" | custom-call | flops 4294967296 | bytes 9437184 | tf_op jit(solution)/shard_map/sandwich_first/pallas_call | solution.py:143
  65.7 0.0 copy-start.4
  65.7 5.5 %sandwich_last.1 = (bf16[512,512]{1,0:T(8,128)(2,1)S(1)}, bf16[2,512,512]{2,1,0:T(8,128)(2,1)S(1)}) custom-call(s32[6]{0:T(128)S(1)} %copy-done, bf16[4,512,512]{2,1,0:T(8,128)(2,1)S(1)} %get-tuple-element.17.green, f32[512,512]{1,0:T(8,128)S(1)} %get-tuple-element.18.start, bf16[2,528,512]{2,1,0:T(8,128)(2,1)S(1)} %collective-permute-done.7.s0, ...), custom_call_target="tpu_custom_call" | custom-call | flops 4294967296 | bytes 9437184 | tf_op jit(solution)/shard_map/sandwich_last/pallas_call | solution.py:156
  71.3 0.2 collective-permute-start.12
  71.5 0.7 collective-permute-start.13
  72.2 13.5 %collective-permute-done.12.inner = bf16[512,512]{1,0:T(8,128)(2,1)S(1)} collective-permute-done((bf16[512,512]{1,0:T(8,128)(2,1)S(1)}, bf16[512,512]{1,0:T(8,128)(2,1)S(1)}, u32[]{:S(2)}, u32[]{:S(2)}) %collective-permute-start.12) | collective-permute-done | bytes 524320 | tf_op jit(solution)/shard_map/ppermute | solution.py:227
  85.7 2.5 %update.1 = bf16[8,2,64,512]{3,2,1,0:T(8,128)(2,1)S(1)} custom-call(s32[6]{0:T(128)S(1)} %copy-done, f32[2]{0:T(128)S(1)} %copy-done.4, bf16[512,512]{1,0:T(8,128)(2,1)S(1)} %get-tuple-element.19.own, bf16[512,512]{1,0:T(8,128)(2,1)S(1)} %collective-permute-done.12.inner, bf16[512,512]{1,0:T(8,128)(2,1)S(1)} %collective-permute-done.13.outer, ...), custom_call_target="tpu_custom_call" | custom-call | flops 1610612736 | bytes 5242880 | tf_op jit(solution)/shard_map/update/pallas_call | solution.py:186
  88.2 20.8 %all_to_all.5.pieces = bf16[8,2,64,512]{3,2,1,0:T(8,128)(2,1)S(1)} all-to-all(bf16[8,2,64,512]{3,2,1,0:T(8,128)(2,1)S(1)} %update.1), channel_id=1, replica_groups=mesh['slab'=2,'freq'=8,'energy'=16] {'freq'}, dimensions={0} | all-to-all | bytes 2097152 | tf_op jit(solution)/shard_map/all_to_all | solution.py:254
  109.0 1.6 %collect.1 = f32[2,2,2,64,512]{4,3,2,1,0:T(8,128)} custom-call(s32[6]{0:T(128)S(1)} %copy-done, bf16[8,2,64,512]{3,2,1,0:T(8,128)(2,1)S(1)} %all_to_all.5.pieces), custom_call_target="tpu_custom_call" | custom-call | tf_op jit(solution)/shard_map/collect/pallas_call | solution.py:209
  (13 shorter events, 0.0 us)
Async XLA Ops:
  0.7 57.1 %copy-start = (s32[6]{0:T(128)S(1)}, s32[6]{0:T(128)}, u32[]{:S(2)}) copy-start(s32[6]{0:T(128)} %stack.27.place) | copy-start | bytes 76
  4.6 40.8 %collective-permute-start.3 = (bf16[2,528,512]{2,1,0:T(8,128)(2,1)}, bf16[2,528,512]{2,1,0:T(8,128)(2,1)S(1)}, u32[]{:S(2)}, u32[]{:S(2)}) collective-permute-start(bf16[2,528,512]{2,1,0:T(8,128)(2,1)} %get-tuple-element.15.home), channel_id=1, source_target_pairs={{0,32},{16,48},{32,0},{48,16},{64,96},{80,112},{96,64},{112,80},{1... | collective-permute-start | bytes 3244040 | tf_op jit(solution)/shard_map/ppermute | solution.py:227
  6.3 39.2 %collective-permute-start.4 = (bf16[2,528,512]{2,1,0:T(8,128)(2,1)}, bf16[2,528,512]{2,1,0:T(8,128)(2,1)S(1)}, u32[]{:S(2)}, u32[]{:S(2)}) collective-permute-start(bf16[2,528,512]{2,1,0:T(8,128)(2,1)} %get-tuple-element.15.home), channel_id=1, source_target_pairs={{0,96},{16,112},{32,64},{48,80},{64,32},{80,48},{96,0},{112,16},{1... | collective-permute-start | bytes 3244040 | tf_op jit(solution)/shard_map/ppermute | solution.py:227
  8.5 36.1 %collective-permute-start.5 = (bf16[528,512]{1,0:T(8,128)(2,1)}, bf16[528,512]{1,0:T(8,128)(2,1)S(1)}, u32[]{:S(2)}, u32[]{:S(2)}) collective-permute-start(bf16[528,512]{1,0:T(8,128)(2,1)} %get-tuple-element.16), channel_id=1, source_target_pairs={{0,64},{16,80},{32,96},{48,112},{64,0},{80,16},{96,32},{112,48},{1... | collective-permute-start | bytes 1622024 | tf_op jit(solution)/shard_map/ppermute | solution.py:227
  9.2 26.2 %collective-permute-start = (bf16[512,512]{1,0:T(8,128)(2,1)}, bf16[512,512]{1,0:T(8,128)(2,1)S(1)}, u32[]{:S(2)}, u32[]{:S(2)}) collective-permute-start(bf16[512,512]{1,0:T(8,128)(2,1)} %get-tuple-element.13.own), channel_id=1, source_target_pairs={{0,1},{1,2},{2,3},{3,4},{4,5},{5,6},{6,7},{7,8},{8,9},{9,10},{10,1... | collective-permute-start | bytes 1572872 | tf_op jit(solution)/shard_map/ppermute | solution.py:241
  14.4 51.3 %copy-start.1 = (bf16[2,2,2,512,512]{4,3,2,1,0:T(8,128)(2,1)S(1)}, bf16[2,2,2,512,512]{4,3,2,1,0:T(8,128)(2,1)}, u32[]{:S(2)}) copy-start(bf16[2,2,2,512,512]{4,3,2,1,0:T(8,128)(2,1)} %retarded.1) | copy-start | bytes 12582916
  14.4 31.6 %collective-permute-start.2 = (bf16[512,512]{1,0:T(8,128)(2,1)}, bf16[512,512]{1,0:T(8,128)(2,1)S(1)}, u32[]{:S(2)}, u32[]{:S(2)}) collective-permute-start(bf16[512,512]{1,0:T(8,128)(2,1)} %get-tuple-element.14), channel_id=1, source_target_pairs={{0,1},{1,2},{2,3},{3,4},{4,5},{5,6},{6,7},{7,8},{8,9},{9,10},{10,1... | collective-permute-start | bytes 1572872 | tf_op jit(solution)/shard_map/ppermute | solution.py:242
  35.4 30.3 %collective-permute-start.7 = (bf16[2,528,512]{2,1,0:T(8,128)(2,1)}, bf16[2,528,512]{2,1,0:T(8,128)(2,1)S(1)}, u32[]{:S(2)}, u32[]{:S(2)}) collective-permute-start(bf16[2,528,512]{2,1,0:T(8,128)(2,1)} %get-tuple-element.15.home), channel_id=1, source_target_pairs={{0,16},{16,0},{32,48},{48,32},{64,80},{80,64},{96,112},{112,96},{1... | collective-permute-start | bytes 3244040 | tf_op jit(solution)/shard_map/ppermute | solution.py:227
  44.6 13.1 %collective-permute-start.6 = (bf16[528,512]{1,0:T(8,128)(2,1)S(1)}, bf16[528,512]{1,0:T(8,128)(2,1)S(1)}, u32[]{:S(2)}, u32[]{:S(2)}) collective-permute-start(bf16[528,512]{1,0:T(8,128)(2,1)S(1)} %collective-permute-done.5.half), channel_id=1, source_target_pairs={{0,4},{1,5},{2,6},{3,7},{4,0},{5,1},{6,2},{7,3},{8,12},{9,13},{10,... | collective-permute-start | bytes 1622024 | tf_op jit(solution)/shard_map/ppermute | solution.py:239
  45.5 20.2 %collective-permute-start.8 = (bf16[2,528,512]{2,1,0:T(8,128)(2,1)S(1)}, bf16[2,528,512]{2,1,0:T(8,128)(2,1)S(1)}, u32[]{:S(2)}, u32[]{:S(2)}) collective-permute-start(bf16[2,528,512]{2,1,0:T(8,128)(2,1)S(1)} %collective-permute-done.3.c1), channel_id=1, source_target_pairs={{0,16},{16,0},{32,48},{48,32},{64,80},{80,64},{96,112},{112,96},{1... | collective-permute-start | bytes 3244040 | tf_op jit(solution)/shard_map/ppermute | solution.py:227
  45.5 20.2 %collective-permute-start.9 = (bf16[2,528,512]{2,1,0:T(8,128)(2,1)S(1)}, bf16[2,528,512]{2,1,0:T(8,128)(2,1)S(1)}, u32[]{:S(2)}, u32[]{:S(2)}) collective-permute-start(bf16[2,528,512]{2,1,0:T(8,128)(2,1)S(1)} %collective-permute-done.4.c3), channel_id=1, source_target_pairs={{0,16},{16,0},{32,48},{48,32},{64,80},{80,64},{96,112},{112,96},{1... | collective-permute-start | bytes 3244040 | tf_op jit(solution)/shard_map/ppermute | solution.py:227
  46.0 4.5 %collective-permute-start.1 = (bf16[512,512]{1,0:T(8,128)(2,1)S(1)}, bf16[512,512]{1,0:T(8,128)(2,1)S(1)}, u32[]{:S(2)}, u32[]{:S(2)}) collective-permute-start(bf16[512,512]{1,0:T(8,128)(2,1)S(1)} %collective-permute-done.near), channel_id=1, source_target_pairs={{0,16},{16,0},{32,48},{48,32},{64,80},{80,64},{96,112},{112,96},{1... | collective-permute-start | bytes 1572872 | tf_op jit(solution)/shard_map/ppermute | solution.py:227
  50.5 15.2 %collective-permute-start.10 = (bf16[528,512]{1,0:T(8,128)(2,1)S(1)}, bf16[528,512]{1,0:T(8,128)(2,1)S(1)}, u32[]{:S(2)}, u32[]{:S(2)}) collective-permute-start(bf16[528,512]{1,0:T(8,128)(2,1)S(1)} %collective-permute-done.5.half), channel_id=1, source_target_pairs={{0,16},{16,0},{32,48},{48,32},{64,80},{80,64},{96,112},{112,96},{1... | collective-permute-start | bytes 1622024 | tf_op jit(solution)/shard_map/ppermute | solution.py:227
  57.7 8.0 %collective-permute-start.11 = (bf16[528,512]{1,0:T(8,128)(2,1)S(1)}, bf16[528,512]{1,0:T(8,128)(2,1)S(1)}, u32[]{:S(2)}, u32[]{:S(2)}) collective-permute-start(bf16[528,512]{1,0:T(8,128)(2,1)S(1)} %collective-permute-done.6.other), channel_id=1, source_target_pairs={{0,16},{16,0},{32,48},{48,32},{64,80},{80,64},{96,112},{112,96},{1... | collective-permute-start | bytes 1622024 | tf_op jit(solution)/shard_map/ppermute | solution.py:227
  57.7 1.2 %copy-start.2 = (bf16[2,528,512]{2,1,0:T(8,128)(2,1)S(1)}, bf16[2,528,512]{2,1,0:T(8,128)(2,1)}, u32[]{:S(2)}) copy-start(bf16[2,528,512]{2,1,0:T(8,128)(2,1)} %get-tuple-element.15.home) | copy-start | bytes 3244036
  59.0 1.0 copy-start.3
  65.7 20.0 %copy-start.4 = (f32[2]{0:T(128)S(1)}, f32[2]{0:T(128)}, u32[]{:S(2)}) copy-start(f32[2]{0:T(128)} %weight.1) | copy-start | bytes 28
  71.3 14.4 %collective-permute-start.12 = (bf16[512,512]{1,0:T(8,128)(2,1)S(1)}, bf16[512,512]{1,0:T(8,128)(2,1)S(1)}, u32[]{:S(2)}, u32[]{:S(2)}) collective-permute-start(bf16[512,512]{1,0:T(8,128)(2,1)S(1)} %get-tuple-element.19.own), channel_id=1, source_target_pairs={{0,32},{16,48},{32,0},{48,16},{64,96},{80,112},{96,64},{112,80},{1... | collective-permute-start | bytes 1572872 | tf_op jit(solution)/shard_map/ppermute | solution.py:227
  71.5 14.2 %collective-permute-start.13 = (bf16[512,512]{1,0:T(8,128)(2,1)S(1)}, bf16[512,512]{1,0:T(8,128)(2,1)S(1)}, u32[]{:S(2)}, u32[]{:S(2)}) collective-permute-start(bf16[512,512]{1,0:T(8,128)(2,1)S(1)} %get-tuple-element.19.own), channel_id=1, source_target_pairs={{32,160},{48,176},{96,224},{112,240},{160,32},{176,48},{224,96},{2... | collective-permute-start | bytes 1572872 | tf_op jit(solution)/shard_map/ppermute | solution.py:252

commit v5 on v4

--- a/solution.py
+++ b/solution.py
@@ -104,7 +104,7 @@
     return todo
 
 
-def first_kernel(place, own, near, shared, far, home, c1, c3, half, other, out, green, gsem):
+def first_kernel(place, own, near, shared, far, c1, c3, half, other, out, green, gsem):
     copies = [
         pltpu.make_async_copy(src, green.at[n], gsem.at[n])
         for n, src in enumerate((own, near, shared, far))
@@ -113,17 +113,17 @@
         copy.start()
     for copy in copies:
         copy.wait()
-    todo = blocks_of((home, c1, c3, half, other))
+    todo = blocks_of((c1, c3, half, other))
     for n, term in enumerate(add_terms(place[1], green, todo)):
         out[...] = term if n == 0 else out[...] + term
 
 
 def last_kernel(
-    place, green, start, s0, s1, s3, half, other, retarded, out, whole, acc, rsem
+    place, green, start, home, s0, s1, s3, half, other, retarded, out, whole, acc, rsem
 ):
     k, sl = place[1], place[2]
     copies = [pltpu.make_async_copy(retarded.at[k, sl], whole, rsem.at[0])]
-    todo = blocks_of((s0, s1, s3, half, other))
+    todo = blocks_of((home, s0, s1, s3, half, other))
     for copy in copies:
         copy.start()
     for n, term in enumerate(add_terms(k, green, todo)):
@@ -136,18 +136,21 @@
         copy.wait()
 
 
-COST = pl.CostEstimate(flops=8 * 4 * NO**3, bytes_accessed=18 * NO * NO * 2, transcendentals=0)
+def cost(count):
+    return pl.CostEstimate(
+        flops=count * 4 * NO**3, bytes_accessed=(count + 10) * NO * NO * 2, transcendentals=0
+    )
 
 
 def sandwich_first(place, greens, arrays):
     return pl.pallas_call(
         first_kernel,
         out_shape=[shape((NO, NO), F32), shape((4, NO, NO), BF16)],
-        in_specs=[SMEM] + [VMEM] * 9,
+        in_specs=[SMEM] + [VMEM] * 8,
         out_specs=[VMEM] * 2,
         scratch_shapes=[pltpu.SemaphoreType.DMA((4,))],
         compiler_params=PARAMS,
-        cost_estimate=COST,
+        cost_estimate=cost(6),
         name="sandwich_first",
     )(place, *greens, *arrays)
 
@@ -156,11 +159,11 @@
     return pl.pallas_call(
         last_kernel,
         out_shape=[shape((NO, NO), BF16), shape((2, NO, NO), BF16)],
-        in_specs=[SMEM] + [VMEM] * 7 + [HBM],
+        in_specs=[SMEM] + [VMEM] * 8 + [HBM],
         out_specs=[VMEM] * 2,
         scratch_shapes=[pltpu.VMEM((NO, NO), F32), pltpu.SemaphoreType.DMA((1,))],
         compiler_params=PARAMS,
-        cost_estimate=COST,
+        cost_estimate=cost(10),
         name="sandwich_last",
     )(place, green, start, *arrays, retarded)
 
@@ -236,17 +239,16 @@
 
     packed, part, own, mine = prepare(place, occupations, offsets, coupling, lesser)
     half = flip(part, 4)
+    near = lax.ppermute(own, ("freq", "energy"), across)
+    half, near, packed = lax.optimization_barrier((half, near, packed))
+    c1, c3 = flip(packed, 2), flip(packed, 6)
+    far = lax.ppermute(mine, ("freq", "energy"), across)
     other = lax.ppermute(half, "energy", [(e, e ^ 4) for e in range(count)])
-    c1, c3 = flip(packed, 2), flip(packed, 6)
-    near = lax.ppermute(own, ("freq", "energy"), across)
-    far = lax.ppermute(mine, ("freq", "energy"), across)
-    shared = flip(near, 1)
+    own, shared = flip(mine, 1), flip(near, 1)
     swapped = [flip(x, 1) for x in (packed, c1, c3, half, other)]
 
-    first, green = sandwich_first(
-        place, [own, near, shared, far], [packed, c1, c3, half, other]
-    )
-    total, whole = sandwich_last(place, green, first, swapped, retarded)
+    first, green = sandwich_first(place, [own, near, shared, far], [c1, c3, half, other])
+    total, whole = sandwich_last(place, green, first, [packed, *swapped], retarded)
     inner = flip(total, 2)
     edge = [(s * 8 + d, (1 - s) * 8 + d) for s in range(2) for d in range(8) if (d // 2) % 2]
     outer = lax.ppermute(total, ("slab", "freq"), edge)

time: 112 us -> 110 us (0.982)
  local copies, waits for them, and re-layouts: 2.94 us -> 0.67 us
  waiting for transfers between devices: 49.5 us -> 50.7 us
  starting transfers between devices: 18 us -> 16.8 us
    ppermute x10 -> x11, waiting for transfers between devices: 27.2 us -> 35.3 us  [flip(): return lax.ppermute(x, 'freq', [(d, d ^ bits) for d in range(8)])]
    ppermute x1, waiting for transfers between devices: 7.11 us -> 0.01 us  [shards(): other = lax.ppermute(half, 'energy', [(e, e ^ 4) for e in range(count)])]
    ppermute x1, starting transfers between devices: 5.75 us -> 2.33 us  [shards(): far = lax.ppermute(mine, ('freq', 'energy'), across)]
    ppermute x10 -> x11, starting transfers between devices: 5.53 us -> 8.08 us  [flip(): return lax.ppermute(x, 'freq', [(d, d ^ bits) for d in range(8)])]
    unnamed x10 -> x8, local copies, waits for them, and re-layouts: 2.29 us -> 0.02 us
    pallas_call x1, Pallas kernels: 5.55 us -> 6.69 us  [sandwich_last(): pl.pallas_call(last_kernel, out_shape=[shape((NO, NO), BF16), shape((2, N...]
    pallas_call x1, Pallas kernels: 5.63 us -> 4.49 us  [sandwich_first(): pl.pallas_call(first_kernel, out_shape=[shape((NO, NO), F32), shape((4, N...]
  transfers between devices with their start and end apart: 14 -> 15, of which waited for: 5 -> 4; matrix products, arithmetic and copies ran while one was open for 0% -> 0% of each run, Pallas kernels for 5% -> 4%
where the time goes in v5:
time: 110 us; the launch traced here: 108 us
  waiting for transfers between devices  50.7 us (46%)
  blocking collectives  20.8 us (19%)
  Pallas kernels  19.3 us (18%)
  starting transfers between devices  16.8 us (15%)
    ppermute x11, waiting for transfers between devices, flip(): return lax.ppermute(x, 'freq', [(d, d ^ bits) for d in range(8)])  35.3 us
    all_to_all x1, blocking collectives, shards(): return collect(place, lax.all_to_all(pieces, 'freq', 0, 0))  20.8 us
    ppermute x1, waiting for transfers between devices, shards(): near = lax.ppermute(own, ('freq', 'energy'), across)  15.4 us
    ppermute x11, starting transfers between devices, flip(): return lax.ppermute(x, 'freq', [(d, d ^ bits) for d in range(8)])  8.08 us
    pallas_call x1, Pallas kernels, sandwich_last(): pl.pallas_call(last_kernel, out_shape=[shape((NO, NO), BF16), shape((2, N...  6.69 us
    ppermute x1, starting transfers between devices, shards(): near = lax.ppermute(own, ('freq', 'energy'), across)  5.17 us
    pallas_call x1, Pallas kernels, sandwich_first(): pl.pallas_call(first_kernel, out_shape=[shape((NO, NO), F32), shape((4, N...  4.49 us
    pallas_call x1, Pallas kernels, prepare(): pl.pallas_call(prepare_kernel, out_shape=[shape((2, *block), BF16), shape...  3.97 us
  transfers between devices with their start and end apart: 15, of which 4 were waited for; matrix products, arithmetic and copies ran while one was open for 0% of the time, Pallas kernels for 4%

profile of v5, /device:TPU:38, one launch (start us, length us, event | category | flops | bytes accessed | tf_op | source)
XLA Modules:
  0.0 108.4 jit_solution(10071871819722661594)
XLA Ops:
  0.0 0.7 stack.27.place
  0.7 4.0 %prepare.1 = (bf16[2,528,512]{2,1,0:T(8,128)(2,1)}, bf16[528,512]{1,0:T(8,128)(2,1)}, bf16[512,512]{1,0:T(8,128)(2,1)}, bf16[512,512]{1,0:T(8,128)(2,1)}) custom-call(s32[6]{0:T(128)} %stack.27.place, f32[2]{0:T(128)} %occupations.1, s32[2]{0:T(128)} %offsets.1, bf16[2,512,512]{2,1,0:T(8,128)(2,1)} %coupling.1, bf16[2,2,2,512,512]{4,3,2,1,0:T(8,128)(2,1)} %lesser.1), custom_call_target="tpu_custom_call" | custom-call | tf_op jit(solution)/shard_map/prepare/pallas_call | solution.py:68
  4.6 3.3 %collective-permute-start.1 = (bf16[528,512]{1,0:T(8,128)(2,1)}, bf16[528,512]{1,0:T(8,128)(2,1)S(1)}, u32[]{:S(2)}, u32[]{:S(2)}) collective-permute-start(bf16[528,512]{1,0:T(8,128)(2,1)} %get-tuple-element.17), channel_id=1, source_target_pairs={{0,64},{16,80},{32,96},{48,112},{64,0},{80,16},{96,32},{112,48},{1... | collective-permute-start | bytes 1622024 | tf_op jit(solution)/shard_map/ppermute | solution.py:230
  7.9 5.2 %collective-permute-start.2 = (bf16[512,512]{1,0:T(8,128)(2,1)}, bf16[512,512]{1,0:T(8,128)(2,1)S(1)}, u32[]{:S(2)}, u32[]{:S(2)}) collective-permute-start(bf16[512,512]{1,0:T(8,128)(2,1)} %get-tuple-element.18), channel_id=1, source_target_pairs={{0,1},{1,2},{2,3},{3,4},{4,5},{5,6},{6,7},{7,8},{8,9},{9,10},{10,1... | collective-permute-start | bytes 1572872 | tf_op jit(solution)/shard_map/ppermute | solution.py:242
  13.1 15.4 %collective-permute-done.2.near = bf16[512,512]{1,0:T(8,128)(2,1)S(1)} collective-permute-done((bf16[512,512]{1,0:T(8,128)(2,1)}, bf16[512,512]{1,0:T(8,128)(2,1)S(1)}, u32[]{:S(2)}, u32[]{:S(2)}) %collective-permute-start.2) | collective-permute-done | bytes 524320 | tf_op jit(solution)/shard_map/ppermute | solution.py:242
  28.5 1.1 collective-permute-start.6
  29.5 0.0 collective-permute-start.5
  29.5 2.3 %collective-permute-start.4 = (bf16[512,512]{1,0:T(8,128)(2,1)}, bf16[512,512]{1,0:T(8,128)(2,1)S(1)}, u32[]{:S(2)}, u32[]{:S(2)}) collective-permute-start(bf16[512,512]{1,0:T(8,128)(2,1)} %get-tuple-element.16), channel_id=1, source_target_pairs={{0,1},{1,2},{2,3},{3,4},{4,5},{5,6},{6,7},{7,8},{8,9},{9,10},{10,1... | collective-permute-start | bytes 1572872 | tf_op jit(solution)/shard_map/ppermute | solution.py:245
  31.9 2.5 %collective-permute-start.8 = (bf16[2,528,512]{2,1,0:T(8,128)(2,1)}, bf16[2,528,512]{2,1,0:T(8,128)(2,1)S(1)}, u32[]{:S(2)}, u32[]{:S(2)}) collective-permute-start(bf16[2,528,512]{2,1,0:T(8,128)(2,1)} %get-tuple-element.21.home), channel_id=1, source_target_pairs={{0,16},{16,0},{32,48},{48,32},{64,80},{80,64},{96,112},{112,96},{1... | collective-permute-start | bytes 3244040 | tf_op jit(solution)/shard_map/ppermute | solution.py:230
  34.4 0.5 collective-permute-start.7
  34.9 17.6 %collective-permute-done.6.c3 = bf16[2,528,512]{2,1,0:T(8,128)(2,1)S(1)} collective-permute-done((bf16[2,528,512]{2,1,0:T(8,128)(2,1)}, bf16[2,528,512]{2,1,0:T(8,128)(2,1)S(1)}, u32[]{:S(2)}, u32[]{:S(2)}) %collective-permute-start.6) | collective-permute-done | bytes 1081376 | tf_op jit(solution)/shard_map/ppermute | solution.py:230
  52.6 0.0 collective-permute-start.10
  52.6 0.0 collective-permute-done.5.c1
  52.6 0.5 collective-permute-start.9
  53.1 0.0 collective-permute-done.4.far
  53.1 0.1 collective-permute-start.3
  53.2 4.4 %collective-permute-done.3.shared = bf16[512,512]{1,0:T(8,128)(2,1)S(1)} collective-permute-done((bf16[512,512]{1,0:T(8,128)(2,1)S(1)}, bf16[512,512]{1,0:T(8,128)(2,1)S(1)}, u32[]{:S(2)}, u32[]{:S(2)}) %collective-permute-start.3) | collective-permute-done | bytes 524320 | tf_op jit(solution)/shard_map/ppermute | solution.py:230
  57.6 0.1 collective-permute-start.11
  57.7 0.0 collective-permute-done.7.other
  57.7 0.4 collective-permute-start.12
  58.1 4.5 %sandwich_first.1 = (f32[512,512]{1,0:T(8,128)S(1)}, bf16[4,512,512]{2,1,0:T(8,128)(2,1)S(1)}) custom-call(s32[6]{0:T(128)S(1)} %copy-done, bf16[512,512]{1,0:T(8,128)(2,1)S(1)} %collective-permute-done.own, bf16[512,512]{1,0:T(8,128)(2,1)S(1)} %collective-permute-done.2.near, bf16[512,512]{1,0:T(8,128)(2,1)S(1)} %collective-permute-done.3.shared, ...), custom_call_target="tpu_custom_call" | custom-call | flops 3221225472 | bytes 8388608 | tf_op jit(solution)/shard_map/sandwich_first/pallas_call | solution.py:146
  62.6 0.0 collective-permute-done.12.other
  62.6 0.0 collective-permute-done.8.s0
  62.6 0.0 collective-permute-done.9.s1
  62.7 0.0 copy-start.3
  62.7 6.7 %sandwich_last.1 = (bf16[512,512]{1,0:T(8,128)(2,1)S(1)}, bf16[2,512,512]{2,1,0:T(8,128)(2,1)S(1)}) custom-call(s32[6]{0:T(128)S(1)} %copy-done, bf16[4,512,512]{2,1,0:T(8,128)(2,1)S(1)} %get-tuple-element.23.green, f32[512,512]{1,0:T(8,128)S(1)} %get-tuple-element.24.start, bf16[2,528,512]{2,1,0:T(8,128)(2,1)S(1)} %copy-done.2, ...), custom_call_target="tpu_custom_call" | custom-call | flops 5368709120 | bytes 10485760 | tf_op jit(solution)/shard_map/sandwich_last/pallas_call | solution.py:159
  69.4 0.1 collective-permute-start.13
  69.5 0.7 collective-permute-start.14
  70.2 13.3 %collective-permute-done.13.inner = bf16[512,512]{1,0:T(8,128)(2,1)S(1)} collective-permute-done((bf16[512,512]{1,0:T(8,128)(2,1)S(1)}, bf16[512,512]{1,0:T(8,128)(2,1)S(1)}, u32[]{:S(2)}, u32[]{:S(2)}) %collective-permute-start.13) | collective-permute-done | bytes 524320 | tf_op jit(solution)/shard_map/ppermute | solution.py:230
  83.4 2.5 %update.1 = bf16[8,2,64,512]{3,2,1,0:T(8,128)(2,1)S(1)} custom-call(s32[6]{0:T(128)S(1)} %copy-done, f32[2]{0:T(128)S(1)} %copy-done.3, bf16[512,512]{1,0:T(8,128)(2,1)S(1)} %get-tuple-element.25.own, bf16[512,512]{1,0:T(8,128)(2,1)S(1)} %collective-permute-done.13.inner, bf16[512,512]{1,0:T(8,128)(2,1)S(1)} %collective-permute-done.14.outer, ...), custom_call_target="tpu_custom_call" | custom-call | flops 1610612736 | bytes 5242880 | tf_op jit(solution)/shard_map/update/pallas_call | solution.py:189
  86.0 20.8 %all_to_all.5.pieces = bf16[8,2,64,512]{3,2,1,0:T(8,128)(2,1)S(1)} all-to-all(bf16[8,2,64,512]{3,2,1,0:T(8,128)(2,1)S(1)} %update.1), channel_id=1, replica_groups=mesh['slab'=2,'freq'=8,'energy'=16] {'freq'}, dimensions={0} | all-to-all | bytes 2097152 | tf_op jit(solution)/shard_map/all_to_all | solution.py:256
  106.8 1.6 %collect.1 = f32[2,2,2,64,512]{4,3,2,1,0:T(8,128)} custom-call(s32[6]{0:T(128)S(1)} %copy-done, bf16[8,2,64,512]{3,2,1,0:T(8,128)(2,1)S(1)} %all_to_all.5.pieces), custom_call_target="tpu_custom_call" | custom-call | tf_op jit(solution)/shard_map/collect/pallas_call | solution.py:212
  (13 shorter events, 0.0 us)
Async XLA Ops:
  0.7 57.4 %copy-start = (s32[6]{0:T(128)S(1)}, s32[6]{0:T(128)}, u32[]{:S(2)}) copy-start(s32[6]{0:T(128)} %stack.27.place) | copy-start | bytes 76
  4.6 23.8 %collective-permute-start.1 = (bf16[528,512]{1,0:T(8,128)(2,1)}, bf16[528,512]{1,0:T(8,128)(2,1)S(1)}, u32[]{:S(2)}, u32[]{:S(2)}) collective-permute-start(bf16[528,512]{1,0:T(8,128)(2,1)} %get-tuple-element.17), channel_id=1, source_target_pairs={{0,64},{16,80},{32,96},{48,112},{64,0},{80,16},{96,32},{112,48},{1... | collective-permute-start | bytes 1622024 | tf_op jit(solution)/shard_map/ppermute | solution.py:230
  7.9 20.5 %collective-permute-start.2 = (bf16[512,512]{1,0:T(8,128)(2,1)}, bf16[512,512]{1,0:T(8,128)(2,1)S(1)}, u32[]{:S(2)}, u32[]{:S(2)}) collective-permute-start(bf16[512,512]{1,0:T(8,128)(2,1)} %get-tuple-element.18), channel_id=1, source_target_pairs={{0,1},{1,2},{2,3},{3,4},{4,5},{5,6},{6,7},{7,8},{8,9},{9,10},{10,1... | collective-permute-start | bytes 1572872 | tf_op jit(solution)/shard_map/ppermute | solution.py:242
  28.5 24.1 %collective-permute-start.6 = (bf16[2,528,512]{2,1,0:T(8,128)(2,1)}, bf16[2,528,512]{2,1,0:T(8,128)(2,1)S(1)}, u32[]{:S(2)}, u32[]{:S(2)}) collective-permute-start(bf16[2,528,512]{2,1,0:T(8,128)(2,1)} %get-tuple-element.21.home), channel_id=1, source_target_pairs={{0,96},{16,112},{32,64},{48,80},{64,32},{80,48},{96,0},{112,16},{1... | collective-permute-start | bytes 3244040 | tf_op jit(solution)/shard_map/ppermute | solution.py:230
  29.5 23.1 %collective-permute-start.5 = (bf16[2,528,512]{2,1,0:T(8,128)(2,1)}, bf16[2,528,512]{2,1,0:T(8,128)(2,1)S(1)}, u32[]{:S(2)}, u32[]{:S(2)}) collective-permute-start(bf16[2,528,512]{2,1,0:T(8,128)(2,1)} %get-tuple-element.21.home), channel_id=1, source_target_pairs={{0,32},{16,48},{32,0},{48,16},{64,96},{80,112},{96,64},{112,80},{1... | collective-permute-start | bytes 3244040 | tf_op jit(solution)/shard_map/ppermute | solution.py:230
  29.5 33.1 %copy-start.1 = (bf16[2,2,2,512,512]{4,3,2,1,0:T(8,128)(2,1)S(1)}, bf16[2,2,2,512,512]{4,3,2,1,0:T(8,128)(2,1)}, u32[]{:S(2)}) copy-start(bf16[2,2,2,512,512]{4,3,2,1,0:T(8,128)(2,1)} %retarded.1) | copy-start | bytes 12582916
  29.5 33.1 %copy-start.2 = (bf16[2,528,512]{2,1,0:T(8,128)(2,1)S(1)}, bf16[2,528,512]{2,1,0:T(8,128)(2,1)}, u32[]{:S(2)}) copy-start(bf16[2,528,512]{2,1,0:T(8,128)(2,1)} %get-tuple-element.21.home) | copy-start | bytes 3244036
  29.5 4.9 %collective-permute-start = (bf16[512,512]{1,0:T(8,128)(2,1)}, bf16[512,512]{1,0:T(8,128)(2,1)S(1)}, u32[]{:S(2)}, u32[]{:S(2)}) collective-permute-start(bf16[512,512]{1,0:T(8,128)(2,1)} %get-tuple-element.16), channel_id=1, source_target_pairs={{0,16},{16,0},{32,48},{48,32},{64,80},{80,64},{96,112},{112,96},{1... | collective-permute-start | bytes 1572872 | tf_op jit(solution)/shard_map/ppermute | solution.py:230
  29.5 23.6 %collective-permute-start.4 = (bf16[512,512]{1,0:T(8,128)(2,1)}, bf16[512,512]{1,0:T(8,128)(2,1)S(1)}, u32[]{:S(2)}, u32[]{:S(2)}) collective-permute-start(bf16[512,512]{1,0:T(8,128)(2,1)} %get-tuple-element.16), channel_id=1, source_target_pairs={{0,1},{1,2},{2,3},{3,4},{4,5},{5,6},{6,7},{7,8},{8,9},{9,10},{10,1... | collective-permute-start | bytes 1572872 | tf_op jit(solution)/shard_map/ppermute | solution.py:245
  31.9 30.8 %collective-permute-start.8 = (bf16[2,528,512]{2,1,0:T(8,128)(2,1)}, bf16[2,528,512]{2,1,0:T(8,128)(2,1)S(1)}, u32[]{:S(2)}, u32[]{:S(2)}) collective-permute-start(bf16[2,528,512]{2,1,0:T(8,128)(2,1)} %get-tuple-element.21.home), channel_id=1, source_target_pairs={{0,16},{16,0},{32,48},{48,32},{64,80},{80,64},{96,112},{112,96},{1... | collective-permute-start | bytes 3244040 | tf_op jit(solution)/shard_map/ppermute | solution.py:230
  34.4 23.3 %collective-permute-start.7 = (bf16[528,512]{1,0:T(8,128)(2,1)S(1)}, bf16[528,512]{1,0:T(8,128)(2,1)S(1)}, u32[]{:S(2)}, u32[]{:S(2)}) collective-permute-start(bf16[528,512]{1,0:T(8,128)(2,1)S(1)} %collective-permute-done.1.half), channel_id=1, source_target_pairs={{0,4},{1,5},{2,6},{3,7},{4,0},{5,1},{6,2},{7,3},{8,12},{9,13},{10,... | collective-permute-start | bytes 1622024 | tf_op jit(solution)/shard_map/ppermute | solution.py:246
  52.6 10.1 %collective-permute-start.10 = (bf16[2,528,512]{2,1,0:T(8,128)(2,1)S(1)}, bf16[2,528,512]{2,1,0:T(8,128)(2,1)S(1)}, u32[]{:S(2)}, u32[]{:S(2)}) collective-permute-start(bf16[2,528,512]{2,1,0:T(8,128)(2,1)S(1)} %collective-permute-done.6.c3), channel_id=1, source_target_pairs={{0,16},{16,0},{32,48},{48,32},{64,80},{80,64},{96,112},{112,96},{1... | collective-permute-start | bytes 3244040 | tf_op jit(solution)/shard_map/ppermute | solution.py:230
  52.6 10.1 %collective-permute-start.9 = (bf16[2,528,512]{2,1,0:T(8,128)(2,1)S(1)}, bf16[2,528,512]{2,1,0:T(8,128)(2,1)S(1)}, u32[]{:S(2)}, u32[]{:S(2)}) collective-permute-start(bf16[2,528,512]{2,1,0:T(8,128)(2,1)S(1)} %collective-permute-done.5.c1), channel_id=1, source_target_pairs={{0,16},{16,0},{32,48},{48,32},{64,80},{80,64},{96,112},{112,96},{1... | collective-permute-start | bytes 3244040 | tf_op jit(solution)/shard_map/ppermute | solution.py:230
  53.1 4.5 %collective-permute-start.3 = (bf16[512,512]{1,0:T(8,128)(2,1)S(1)}, bf16[512,512]{1,0:T(8,128)(2,1)S(1)}, u32[]{:S(2)}, u32[]{:S(2)}) collective-permute-start(bf16[512,512]{1,0:T(8,128)(2,1)S(1)} %collective-permute-done.2.near), channel_id=1, source_target_pairs={{0,16},{16,0},{32,48},{48,32},{64,80},{80,64},{96,112},{112,96},{1... | collective-permute-start | bytes 1572872 | tf_op jit(solution)/shard_map/ppermute | solution.py:230
  57.6 5.0 %collective-permute-start.11 = (bf16[528,512]{1,0:T(8,128)(2,1)S(1)}, bf16[528,512]{1,0:T(8,128)(2,1)S(1)}, u32[]{:S(2)}, u32[]{:S(2)}) collective-permute-start(bf16[528,512]{1,0:T(8,128)(2,1)S(1)} %collective-permute-done.1.half), channel_id=1, source_target_pairs={{0,16},{16,0},{32,48},{48,32},{64,80},{80,64},{96,112},{112,96},{1... | collective-permute-start | bytes 1622024 | tf_op jit(solution)/shard_map/ppermute | solution.py:230
  57.7 4.9 %collective-permute-start.12 = (bf16[528,512]{1,0:T(8,128)(2,1)S(1)}, bf16[528,512]{1,0:T(8,128)(2,1)S(1)}, u32[]{:S(2)}, u32[]{:S(2)}) collective-permute-start(bf16[528,512]{1,0:T(8,128)(2,1)S(1)} %collective-permute-done.7.other), channel_id=1, source_target_pairs={{0,16},{16,0},{32,48},{48,32},{64,80},{80,64},{96,112},{112,96},{1... | collective-permute-start | bytes 1622024 | tf_op jit(solution)/shard_map/ppermute | solution.py:230
  62.7 20.8 %copy-start.3 = (f32[2]{0:T(128)S(1)}, f32[2]{0:T(128)}, u32[]{:S(2)}) copy-start(f32[2]{0:T(128)} %weight.1) | copy-start | bytes 28
  69.4 14.1 %collective-permute-start.13 = (bf16[512,512]{1,0:T(8,128)(2,1)S(1)}, bf16[512,512]{1,0:T(8,128)(2,1)S(1)}, u32[]{:S(2)}, u32[]{:S(2)}) collective-permute-start(bf16[512,512]{1,0:T(8,128)(2,1)S(1)} %get-tuple-element.25.own), channel_id=1, source_target_pairs={{0,32},{16,48},{32,0},{48,16},{64,96},{80,112},{96,64},{112,80},{1... | collective-permute-start | bytes 1572872 | tf_op jit(solution)/shard_map/ppermute | solution.py:230
  69.5 14.0 %collective-permute-start.14 = (bf16[512,512]{1,0:T(8,128)(2,1)S(1)}, bf16[512,512]{1,0:T(8,128)(2,1)S(1)}, u32[]{:S(2)}, u32[]{:S(2)}) collective-permute-start(bf16[512,512]{1,0:T(8,128)(2,1)S(1)} %get-tuple-element.25.own), channel_id=1, source_target_pairs={{32,160},{48,176},{96,224},{112,240},{160,32},{176,48},{224,96},{2... | collective-permute-start | bytes 1572872 | tf_op jit(solution)/shard_map/ppermute | solution.py:254

commit v6 on v5

--- a/solution.py
+++ b/solution.py
@@ -31,12 +31,12 @@
 
 
 def prepare_kernel(
-    place, occupations, offsets, coupling, lesser, packed, half, near, far, sem
+    place, occupations, offsets, coupling, lesser, packed, half, mine, pair, sem
 ):
     k, sl, c, x = place[1], place[2], place[4], place[5]
     copies = [
-        pltpu.make_async_copy(lesser.at[1 - k, sl, c], near, sem.at[0]),
-        pltpu.make_async_copy(lesser.at[k, sl, c], far, sem.at[1]),
+        pltpu.make_async_copy(lesser.at[k, sl, c], mine, sem.at[0]),
+        pltpu.make_async_copy(lesser.at[k, 1 - sl, c], pair, sem.at[1]),
         pltpu.make_async_copy(coupling.at[x], half.at[pl.ds(0, NO)], sem.at[2]),
     ]
     for t in range(2):
@@ -74,6 +74,22 @@
         compiler_params=pltpu.CompilerParams(vmem_limit_bytes=60 * MIB),
         name="prepare",
     )(place, occupations, offsets, coupling, lesser)
+
+
+def mix_kernel(place, weight, mine, pair, cross, out):
+    beside = pair[...].astype(F32) + cross[...].astype(F32)
+    out[...] = (mine[...].astype(F32) + weight[place[2]] * beside).astype(BF16)
+
+
+def mix(place, weight, mine, pair, cross):
+    return pl.pallas_call(
+        mix_kernel,
+        out_shape=shape((NO, NO), BF16),
+        in_specs=[SMEM] * 2 + [VMEM] * 3,
+        out_specs=VMEM,
+        compiler_params=PARAMS,
+        name="mix",
+    )(place, weight, mine, pair, cross)
 
 
 def add_terms(k, green, todo):
@@ -121,58 +137,15 @@
 def last_kernel(
     place, green, start, home, s0, s1, s3, half, other, retarded, out, whole, acc, rsem
 ):
-    k, sl = place[1], place[2]
-    copies = [pltpu.make_async_copy(retarded.at[k, sl], whole, rsem.at[0])]
+    k, sl, c = place[1], place[2], place[4]
+    copy = pltpu.make_async_copy(retarded.at[k, sl], whole, rsem.at[0])
+    copy.start()
     todo = blocks_of((home, s0, s1, s3, half, other))
-    for copy in copies:
-        copy.start()
     for n, term in enumerate(add_terms(k, green, todo)):
-        total = (start if n == 0 else acc)[...] + term
-        if n == len(todo) - 1:
-            out[...] = total.astype(BF16)
-        else:
-            acc[...] = total
-    for copy in copies:
-        copy.wait()
-
-
-def cost(count):
-    return pl.CostEstimate(
-        flops=count * 4 * NO**3, bytes_accessed=(count + 10) * NO * NO * 2, transcendentals=0
-    )
-
-
-def sandwich_first(place, greens, arrays):
-    return pl.pallas_call(
-        first_kernel,
-        out_shape=[shape((NO, NO), F32), shape((4, NO, NO), BF16)],
-        in_specs=[SMEM] + [VMEM] * 8,
-        out_specs=[VMEM] * 2,
-        scratch_shapes=[pltpu.SemaphoreType.DMA((4,))],
-        compiler_params=PARAMS,
-        cost_estimate=cost(6),
-        name="sandwich_first",
-    )(place, *greens, *arrays)
-
-
-def sandwich_last(place, green, start, arrays, retarded):
-    return pl.pallas_call(
-        last_kernel,
-        out_shape=[shape((NO, NO), BF16), shape((2, NO, NO), BF16)],
-        in_specs=[SMEM] + [VMEM] * 8 + [HBM],
-        out_specs=[VMEM] * 2,
-        scratch_shapes=[pltpu.VMEM((NO, NO), F32), pltpu.SemaphoreType.DMA((1,))],
-        compiler_params=PARAMS,
-        cost_estimate=cost(10),
-        name="sandwich_last",
-    )(place, green, start, *arrays, retarded)
-
-
-def update_kernel(place, weight, own, inner, outer, green, out):
-    sl, c = place[2], place[4]
-    beside = inner[...].astype(F32) + outer[...].astype(F32)
-    combined = (own[...].astype(F32) + weight[sl] * beside).astype(BF16)
-    a, b = green[0], green[1]
+        acc[...] = (start if n == 0 else acc)[...] + term
+    combined = acc[...].astype(BF16)
+    copy.wait()
+    a, b = whole[0], whole[1]
     a_side = mul_t(combined, a).astype(BF16)
     b_side = mul_t(combined, b).astype(BF16)
     real = mul(a, a_side) + mul(b, b_side)
@@ -185,18 +158,40 @@
         out[dest, 1] = second[rows]
 
 
-def update(place, weight, own, inner, outer, green):
-    return pl.pallas_call(
-        update_kernel,
+def cost(count):
+    return pl.CostEstimate(
+        flops=count * 4 * NO**3, bytes_accessed=(count + 10) * NO * NO * 2, transcendentals=0
+    )
+
+
+def sandwich_first(place, greens, arrays):
+    return pl.pallas_call(
+        first_kernel,
+        out_shape=[shape((NO, NO), F32), shape((4, NO, NO), BF16)],
+        in_specs=[SMEM] + [VMEM] * 8,
+        out_specs=[VMEM] * 2,
+        scratch_shapes=[pltpu.SemaphoreType.DMA((4,))],
+        compiler_params=PARAMS,
+        cost_estimate=cost(6),
+        name="sandwich_first",
+    )(place, *greens, *arrays)
+
+
+def sandwich_last(place, green, start, arrays, retarded):
+    return pl.pallas_call(
+        last_kernel,
         out_shape=shape((8, 2, ROWS, NO), BF16),
-        in_specs=[SMEM] * 2 + [VMEM] * 4,
+        in_specs=[SMEM] + [VMEM] * 8 + [HBM],
         out_specs=VMEM,
-        compiler_params=PARAMS,
-        cost_estimate=pl.CostEstimate(
-            flops=12 * NO**3, bytes_accessed=10 * NO * NO * 2, transcendentals=0
-        ),
-        name="update",
-    )(place, weight, own, inner, outer, green)
+        scratch_shapes=[
+            pltpu.VMEM((2, NO, NO), BF16),
+            pltpu.VMEM((NO, NO), F32),
+            pltpu.SemaphoreType.DMA((1,)),
+        ],
+        compiler_params=PARAMS,
+        cost_estimate=cost(13),
+        name="sandwich_last",
+    )(place, green, start, *arrays, retarded)
 
 
 def collect_kernel(place, pieces, out):
@@ -230,29 +225,32 @@
         return lax.ppermute(x, "freq", [(d, d ^ bits) for d in range(8)])
 
     count = lax.axis_size("energy")
-    across = []
+    near_pairs, far_pairs = [], []
     for d in range(8):
         for e in range(count):
-            target = e + 1 if d % 2 == 0 else e - 1
-            if 0 <= target < count:
-                across.append((d * count + e, d * count + target))
-
-    packed, part, own, mine = prepare(place, occupations, offsets, coupling, lesser)
+            for pairs, target, step in (
+                (near_pairs, d ^ 1, 1 if d % 2 else -1),
+                (far_pairs, d, -1 if d % 2 else 1),
+            ):
+                if 0 <= e + step < count:
+                    pairs.append((d * count + e, target * count + e + step))
+
+    packed, part, mine, pair = prepare(place, occupations, offsets, coupling, lesser)
     half = flip(part, 4)
-    near = lax.ppermute(own, ("freq", "energy"), across)
-    half, near, packed = lax.optimization_barrier((half, near, packed))
+    edge = [(s * 8 + d, (1 - s) * 8 + d) for s in range(2) for d in range(8) if (d // 2) % 2]
+    cross = lax.ppermute(mine, ("slab", "freq"), edge)
+    mixed = mix(place, intersection, mine, pair, cross)
+    half, mixed, packed = lax.optimization_barrier((half, mixed, packed))
     c1, c3 = flip(packed, 2), flip(packed, 6)
-    far = lax.ppermute(mine, ("freq", "energy"), across)
+    near = lax.ppermute(mixed, ("freq", "energy"), near_pairs)
+    far = lax.ppermute(mixed, ("freq", "energy"), far_pairs)
     other = lax.ppermute(half, "energy", [(e, e ^ 4) for e in range(count)])
-    own, shared = flip(mine, 1), flip(near, 1)
+    own, shared = flip(mixed, 1), flip(near, 1)
+    own, shared, far, packed = lax.optimization_barrier((own, shared, far, packed))
     swapped = [flip(x, 1) for x in (packed, c1, c3, half, other)]
 
     first, green = sandwich_first(place, [own, near, shared, far], [c1, c3, half, other])
-    total, whole = sandwich_last(place, green, first, [packed, *swapped], retarded)
-    inner = flip(total, 2)
-    edge = [(s * 8 + d, (1 - s) * 8 + d) for s in range(2) for d in range(8) if (d // 2) % 2]
-    outer = lax.ppermute(total, ("slab", "freq"), edge)
-    pieces = update(place, intersection, total, inner, outer, whole)
+    pieces = sandwich_last(place, green, first, [packed, *swapped], retarded)
     return collect(place, lax.all_to_all(pieces, "freq", 0, 0))
 
 

time: 110 us -> 107 us (0.973)
  waiting for transfers between devices: 50.7 us -> 39.8 us
  starting transfers between devices: 16.8 us -> 24 us
  local copies, waits for them, and re-layouts: 0.67 us -> 2.74 us
    ppermute x11 -> x10, waiting for transfers between devices: 35.3 us -> 9.62 us  [flip(): return lax.ppermute(x, 'freq', [(d, d ^ bits) for d in range(8)])]
    ppermute x1, waiting for transfers between devices: 0.01 us -> 11.8 us  [shards(): other = lax.ppermute(half, 'energy', [(e, e ^ 4) for e in range(count)])]
    ppermute x11 -> x10, starting transfers between devices: 8.08 us -> 11.7 us  [flip(): return lax.ppermute(x, 'freq', [(d, d ^ bits) for d in range(8)])]
    ppermute x3, starting transfers between devices: 8.19 us -> 11.4 us  [the longest x1 5.53 us: shards(): near = lax.ppermute(mixed, ('freq', 'energy'), near_pairs)]
    ppermute x3, waiting for transfers between devices: 15.4 us -> 18.4 us  [the longest x1 18 us: shards(): near = lax.ppermute(mixed, ('freq', 'energy'), near_pairs)]
    unnamed x8 -> x12, local copies, waits for them, and re-layouts: 0.02 us -> 2.09 us
  transfers between devices with their start and end apart: 15 -> 14, of which waited for: 4 -> 5; matrix products, arithmetic and copies ran while one was open for 0% -> 0% of each run, Pallas kernels for 4% -> 5%
where the time goes in v6:
time: 107 us; the launch traced here: 106 us
  waiting for transfers between devices  39.8 us (37%)
  starting transfers between devices  24 us (22%)
  blocking collectives  20.1 us (19%)
  Pallas kernels  19.6 us (18%)
  local copies, waits for them, and re-layouts  2.74 us (3%)
    all_to_all x1, blocking collectives, shards(): return collect(place, lax.all_to_all(pieces, 'freq', 0, 0))  20.1 us
    ppermute x1, waiting for transfers between devices, shards(): near = lax.ppermute(mixed, ('freq', 'energy'), near_pairs)  18 us
    ppermute x1, waiting for transfers between devices, shards(): other = lax.ppermute(half, 'energy', [(e, e ^ 4) for e in range(count)])  11.8 us
    ppermute x10, starting transfers between devices, flip(): return lax.ppermute(x, 'freq', [(d, d ^ bits) for d in range(8)])  11.7 us
    ppermute x10, waiting for transfers between devices, flip(): return lax.ppermute(x, 'freq', [(d, d ^ bits) for d in range(8)])  9.62 us
    pallas_call x1, Pallas kernels, sandwich_last(): pl.pallas_call(last_kernel, out_shape=shape((8, 2, ROWS, NO), BF16), in_s...  8.63 us
    ppermute x1, starting transfers between devices, shards(): near = lax.ppermute(mixed, ('freq', 'energy'), near_pairs)  5.53 us
    ppermute x1, starting transfers between devices, shards(): far = lax.ppermute(mixed, ('freq', 'energy'), far_pairs)  5.22 us
  transfers between devices with their start and end apart: 14, of which 5 were waited for; matrix products, arithmetic and copies ran while one was open for 0% of the time, Pallas kernels for 5%

profile of v6, /device:TPU:38, one launch (start us, length us, event | category | flops | bytes accessed | tf_op | source)
XLA Modules:
  0.0 106.3 jit_solution(889574429881270555)
XLA Ops:
  0.0 0.7 stack.27.place
  0.7 4.0 %prepare.1 = (bf16[2,528,512]{2,1,0:T(8,128)(2,1)}, bf16[528,512]{1,0:T(8,128)(2,1)}, bf16[512,512]{1,0:T(8,128)(2,1)}, bf16[512,512]{1,0:T(8,128)(2,1)}) custom-call(s32[6]{0:T(128)} %stack.27.place, f32[2]{0:T(128)} %occupations.1, s32[2]{0:T(128)} %offsets.1, bf16[2,512,512]{2,1,0:T(8,128)(2,1)} %coupling.1, bf16[2,2,2,512,512]{4,3,2,1,0:T(8,128)(2,1)} %lesser.1), custom_call_target="tpu_custom_call" | custom-call | tf_op jit(solution)/shard_map/prepare/pallas_call | solution.py:68
  4.7 3.3 %collective-permute-start = (bf16[528,512]{1,0:T(8,128)(2,1)}, bf16[528,512]{1,0:T(8,128)(2,1)S(1)}, u32[]{:S(2)}, u32[]{:S(2)}) collective-permute-start(bf16[528,512]{1,0:T(8,128)(2,1)} %get-tuple-element.18), channel_id=1, source_target_pairs={{0,64},{16,80},{32,96},{48,112},{64,0},{80,16},{96,32},{112,48},{1... | collective-permute-start | bytes 1622024 | tf_op jit(solution)/shard_map/ppermute | solution.py:225
  8.0 0.7 collective-permute-start.1
  8.7 1.0 copy-done
  9.8 1.0 copy-done.1
  10.8 0.8 mix.1
  11.6 8.9 %collective-permute-done.half = bf16[528,512]{1,0:T(8,128)(2,1)S(1)} collective-permute-done((bf16[528,512]{1,0:T(8,128)(2,1)}, bf16[528,512]{1,0:T(8,128)(2,1)S(1)}, u32[]{:S(2)}, u32[]{:S(2)}) %collective-permute-start) | collective-permute-done | bytes 540704 | tf_op jit(solution)/shard_map/ppermute | solution.py:225
  20.5 6.9 %collective-permute-start.6 = (bf16[2,528,512]{2,1,0:T(8,128)(2,1)S(1)}, bf16[2,528,512]{2,1,0:T(8,128)(2,1)S(1)}, u32[]{:S(2)}, u32[]{:S(2)}) collective-permute-start(bf16[2,528,512]{2,1,0:T(8,128)(2,1)S(1)} %copy-done.5), channel_id=1, source_target_pairs={{0,32},{16,48},{32,0},{48,16},{64,96},{80,112},{96,64},{112,80},{1... | collective-permute-start | bytes 3244040 | tf_op jit(solution)/shard_map/ppermute | solution.py:225
  27.5 0.4 collective-permute-start.7
  27.9 5.5 %collective-permute-start.3 = (bf16[512,512]{1,0:T(8,128)(2,1)S(1)}, bf16[512,512]{1,0:T(8,128)(2,1)S(1)}, u32[]{:S(2)}, u32[]{:S(2)}) collective-permute-start(bf16[512,512]{1,0:T(8,128)(2,1)S(1)} %mix.1), channel_id=1, source_target_pairs={{1,16},{2,17},{3,18},{4,19},{5,20},{6,21},{7,22},{8,23},{9,24},{10... | collective-permute-start | bytes 1572872 | tf_op jit(solution)/shard_map/ppermute | solution.py:245
  33.4 0.1 collective-permute-start.2
  33.5 5.2 %collective-permute-start.5 = (bf16[512,512]{1,0:T(8,128)(2,1)S(1)}, bf16[512,512]{1,0:T(8,128)(2,1)S(1)}, u32[]{:S(2)}, u32[]{:S(2)}) collective-permute-start(bf16[512,512]{1,0:T(8,128)(2,1)S(1)} %mix.1), channel_id=1, source_target_pairs={{0,1},{1,2},{2,3},{3,4},{4,5},{5,6},{6,7},{7,8},{8,9},{9,10},{10,1... | collective-permute-start | bytes 1572872 | tf_op jit(solution)/shard_map/ppermute | solution.py:246
  38.7 18.0 %collective-permute-done.3.near = bf16[512,512]{1,0:T(8,128)(2,1)S(1)} collective-permute-done((bf16[512,512]{1,0:T(8,128)(2,1)S(1)}, bf16[512,512]{1,0:T(8,128)(2,1)S(1)}, u32[]{:S(2)}, u32[]{:S(2)}) %collective-permute-start.3) | collective-permute-done | bytes 524320 | tf_op jit(solution)/shard_map/ppermute | solution.py:245
  56.7 0.0 collective-permute-start.4
  56.7 0.0 collective-permute-done.2.own
  56.7 0.8 collective-permute-start.8
  57.5 0.4 collective-permute-done.5.far
  57.9 0.7 collective-permute-done.4.shared
  58.6 0.1 collective-permute-start.9
  58.7 0.0 collective-permute-done.6.c1
  58.7 0.4 collective-permute-start.10
  59.1 0.1 collective-permute-start.11
  59.3 0.4 collective-permute-start.12
  59.6 11.8 %collective-permute-done.8.other = bf16[528,512]{1,0:T(8,128)(2,1)S(1)} collective-permute-done((bf16[528,512]{1,0:T(8,128)(2,1)S(1)}, bf16[528,512]{1,0:T(8,128)(2,1)S(1)}, u32[]{:S(2)}, u32[]{:S(2)}) %collective-permute-start.8) | collective-permute-done | bytes 540704 | tf_op jit(solution)/shard_map/ppermute | solution.py:247
  71.4 0.0 collective-permute-start.13
  71.4 4.5 %sandwich_first.1 = (f32[512,512]{1,0:T(8,128)S(1)}, bf16[4,512,512]{2,1,0:T(8,128)(2,1)S(1)}) custom-call(s32[6]{0:T(128)S(1)} %copy-done.2, bf16[512,512]{1,0:T(8,128)(2,1)S(1)} %collective-permute-done.2.own, bf16[512,512]{1,0:T(8,128)(2,1)S(1)} %collective-permute-done.3.near, bf16[512,512]{1,0:T(8,128)(2,1)S(1)} %collective-permute-done.4.shared, ...), custom_call_target="tpu_custom_call" | custom-call | flops 3221225472 | bytes 8388608 | tf_op jit(solution)/shard_map/sandwich_first/pallas_call | solution.py:168
  75.9 0.0 collective-permute-done.13.other
  75.9 0.0 collective-permute-done.9.s0
  75.9 8.6 %sandwich_last.1 = bf16[8,2,64,512]{3,2,1,0:T(8,128)(2,1)S(1)} custom-call(s32[6]{0:T(128)S(1)} %copy-done.2, bf16[4,512,512]{2,1,0:T(8,128)(2,1)S(1)} %get-tuple-element.28.green, f32[512,512]{1,0:T(8,128)S(1)} %get-tuple-element.29.start, bf16[2,528,512]{2,1,0:T(8,128)(2,1)S(1)} %copy-done.5, bf16[2,528,512]{2,1,0:T(8,128)(2,1)S(1)} %collective-permute-done.9.s0, ...), custom_call_target="tpu_custom_call" | custom-call | flops 6979321856 | bytes 12058624 | tf_op jit(solution)/shard_map/sandwich_last/pallas_call | solution.py:181
  84.6 20.1 %all_to_all.5.pieces = bf16[8,2,64,512]{3,2,1,0:T(8,128)(2,1)S(1)} all-to-all(bf16[8,2,64,512]{3,2,1,0:T(8,128)(2,1)S(1)} %sandwich_last.1), channel_id=1, replica_groups=mesh['slab'=2,'freq'=8,'energy'=16] {'freq'}, dimensions={0} | all-to-all | bytes 2097152 | tf_op jit(solution)/shard_map/all_to_all | solution.py:254
  104.7 1.6 %collect.1 = f32[2,2,2,64,512]{4,3,2,1,0:T(8,128)} custom-call(s32[6]{0:T(128)S(1)} %copy-done.2, bf16[8,2,64,512]{3,2,1,0:T(8,128)(2,1)S(1)} %all_to_all.5.pieces), custom_call_target="tpu_custom_call" | custom-call | tf_op jit(solution)/shard_map/collect/pallas_call | solution.py:207
  (15 shorter events, 0.0 us)
Async XLA Ops:
  0.7 8.0 %copy-start.2 = (s32[6]{0:T(128)S(1)}, s32[6]{0:T(128)}, u32[]{:S(2)}) copy-start(s32[6]{0:T(128)} %stack.27.place) | copy-start | bytes 76
  0.7 8.1 %copy-start.3 = (f32[2]{0:T(128)S(1)}, f32[2]{0:T(128)}, u32[]{:S(2)}) copy-start(f32[2]{0:T(128)} %weight.1) | copy-start | bytes 28
  4.7 15.8 %collective-permute-start = (bf16[528,512]{1,0:T(8,128)(2,1)}, bf16[528,512]{1,0:T(8,128)(2,1)S(1)}, u32[]{:S(2)}, u32[]{:S(2)}) collective-permute-start(bf16[528,512]{1,0:T(8,128)(2,1)} %get-tuple-element.18), channel_id=1, source_target_pairs={{0,64},{16,80},{32,96},{48,112},{64,0},{80,16},{96,32},{112,48},{1... | collective-permute-start | bytes 1622024 | tf_op jit(solution)/shard_map/ppermute | solution.py:225
  8.0 0.7 collective-permute-start.1
  8.7 1.0 copy-start
  9.8 1.0 copy-start.1
  10.8 9.7 %copy-start.5 = (bf16[2,528,512]{2,1,0:T(8,128)(2,1)S(1)}, bf16[2,528,512]{2,1,0:T(8,128)(2,1)}, u32[]{:S(2)}) copy-start(bf16[2,528,512]{2,1,0:T(8,128)(2,1)} %get-tuple-element.30.home) | copy-start | bytes 3244036
  20.5 55.4 %copy-start.4 = (bf16[2,2,2,512,512]{4,3,2,1,0:T(8,128)(2,1)S(1)}, bf16[2,2,2,512,512]{4,3,2,1,0:T(8,128)(2,1)}, u32[]{:S(2)}) copy-start(bf16[2,2,2,512,512]{4,3,2,1,0:T(8,128)(2,1)} %retarded.1) | copy-start | bytes 12582916
  20.5 38.2 %collective-permute-start.6 = (bf16[2,528,512]{2,1,0:T(8,128)(2,1)S(1)}, bf16[2,528,512]{2,1,0:T(8,128)(2,1)S(1)}, u32[]{:S(2)}, u32[]{:S(2)}) collective-permute-start(bf16[2,528,512]{2,1,0:T(8,128)(2,1)S(1)} %copy-done.5), channel_id=1, source_target_pairs={{0,32},{16,48},{32,0},{48,16},{64,96},{80,112},{96,64},{112,80},{1... | collective-permute-start | bytes 3244040 | tf_op jit(solution)/shard_map/ppermute | solution.py:225
  27.5 31.6 %collective-permute-start.7 = (bf16[2,528,512]{2,1,0:T(8,128)(2,1)S(1)}, bf16[2,528,512]{2,1,0:T(8,128)(2,1)S(1)}, u32[]{:S(2)}, u32[]{:S(2)}) collective-permute-start(bf16[2,528,512]{2,1,0:T(8,128)(2,1)S(1)} %copy-done.5), channel_id=1, source_target_pairs={{0,96},{16,112},{32,64},{48,80},{64,32},{80,48},{96,0},{112,16},{1... | collective-permute-start | bytes 3244040 | tf_op jit(solution)/shard_map/ppermute | solution.py:225
  27.9 28.8 %collective-permute-start.3 = (bf16[512,512]{1,0:T(8,128)(2,1)S(1)}, bf16[512,512]{1,0:T(8,128)(2,1)S(1)}, u32[]{:S(2)}, u32[]{:S(2)}) collective-permute-start(bf16[512,512]{1,0:T(8,128)(2,1)S(1)} %mix.1), channel_id=1, source_target_pairs={{1,16},{2,17},{3,18},{4,19},{5,20},{6,21},{7,22},{8,23},{9,24},{10... | collective-permute-start | bytes 1572872 | tf_op jit(solution)/shard_map/ppermute | solution.py:245
  33.4 23.3 %collective-permute-start.2 = (bf16[512,512]{1,0:T(8,128)(2,1)S(1)}, bf16[512,512]{1,0:T(8,128)(2,1)S(1)}, u32[]{:S(2)}, u32[]{:S(2)}) collective-permute-start(bf16[512,512]{1,0:T(8,128)(2,1)S(1)} %mix.1), channel_id=1, source_target_pairs={{0,16},{16,0},{32,48},{48,32},{64,80},{80,64},{96,112},{112,96},{1... | collective-permute-start | bytes 1572872 | tf_op jit(solution)/shard_map/ppermute | solution.py:225
  33.5 24.4 %collective-permute-start.5 = (bf16[512,512]{1,0:T(8,128)(2,1)S(1)}, bf16[512,512]{1,0:T(8,128)(2,1)S(1)}, u32[]{:S(2)}, u32[]{:S(2)}) collective-permute-start(bf16[512,512]{1,0:T(8,128)(2,1)S(1)} %mix.1), channel_id=1, source_target_pairs={{0,1},{1,2},{2,3},{3,4},{4,5},{5,6},{6,7},{7,8},{8,9},{9,10},{10,1... | collective-permute-start | bytes 1572872 | tf_op jit(solution)/shard_map/ppermute | solution.py:246
  56.7 1.9 %collective-permute-start.4 = (bf16[512,512]{1,0:T(8,128)(2,1)S(1)}, bf16[512,512]{1,0:T(8,128)(2,1)S(1)}, u32[]{:S(2)}, u32[]{:S(2)}) collective-permute-start(bf16[512,512]{1,0:T(8,128)(2,1)S(1)} %collective-permute-done.3.near), channel_id=1, source_target_pairs={{0,16},{16,0},{32,48},{48,32},{64,80},{80,64},{96,112},{112,96},{1... | collective-permute-start | bytes 1572872 | tf_op jit(solution)/shard_map/ppermute | solution.py:225
  56.7 14.7 %collective-permute-start.8 = (bf16[528,512]{1,0:T(8,128)(2,1)S(1)}, bf16[528,512]{1,0:T(8,128)(2,1)S(1)}, u32[]{:S(2)}, u32[]{:S(2)}) collective-permute-start(bf16[528,512]{1,0:T(8,128)(2,1)S(1)} %collective-permute-done.half), channel_id=1, source_target_pairs={{0,4},{1,5},{2,6},{3,7},{4,0},{5,1},{6,2},{7,3},{8,12},{9,13},{10,... | collective-permute-start | bytes 1622024 | tf_op jit(solution)/shard_map/ppermute | solution.py:247
  58.6 17.3 %collective-permute-start.9 = (bf16[2,528,512]{2,1,0:T(8,128)(2,1)S(1)}, bf16[2,528,512]{2,1,0:T(8,128)(2,1)S(1)}, u32[]{:S(2)}, u32[]{:S(2)}) collective-permute-start(bf16[2,528,512]{2,1,0:T(8,128)(2,1)S(1)} %copy-done.5), channel_id=1, source_target_pairs={{0,16},{16,0},{32,48},{48,32},{64,80},{80,64},{96,112},{112,96},{1... | collective-permute-start | bytes 3244040 | tf_op jit(solution)/shard_map/ppermute | solution.py:225
  58.7 17.2 %collective-permute-start.10 = (bf16[2,528,512]{2,1,0:T(8,128)(2,1)S(1)}, bf16[2,528,512]{2,1,0:T(8,128)(2,1)S(1)}, u32[]{:S(2)}, u32[]{:S(2)}) collective-permute-start(bf16[2,528,512]{2,1,0:T(8,128)(2,1)S(1)} %collective-permute-done.6.c1), channel_id=1, source_target_pairs={{0,16},{16,0},{32,48},{48,32},{64,80},{80,64},{96,112},{112,96},{1... | collective-permute-start | bytes 3244040 | tf_op jit(solution)/shard_map/ppermute | solution.py:225
  59.1 16.8 %collective-permute-start.11 = (bf16[2,528,512]{2,1,0:T(8,128)(2,1)S(1)}, bf16[2,528,512]{2,1,0:T(8,128)(2,1)S(1)}, u32[]{:S(2)}, u32[]{:S(2)}) collective-permute-start(bf16[2,528,512]{2,1,0:T(8,128)(2,1)S(1)} %collective-permute-done.7.c3), channel_id=1, source_target_pairs={{0,16},{16,0},{32,48},{48,32},{64,80},{80,64},{96,112},{112,96},{1... | collective-permute-start | bytes 3244040 | tf_op jit(solution)/shard_map/ppermute | solution.py:225
  59.3 16.6 %collective-permute-start.12 = (bf16[528,512]{1,0:T(8,128)(2,1)S(1)}, bf16[528,512]{1,0:T(8,128)(2,1)S(1)}, u32[]{:S(2)}, u32[]{:S(2)}) collective-permute-start(bf16[528,512]{1,0:T(8,128)(2,1)S(1)} %collective-permute-done.half), channel_id=1, source_target_pairs={{0,16},{16,0},{32,48},{48,32},{64,80},{80,64},{96,112},{112,96},{1... | collective-permute-start | bytes 1622024 | tf_op jit(solution)/shard_map/ppermute | solution.py:225
  71.4 4.5 %collective-permute-start.13 = (bf16[528,512]{1,0:T(8,128)(2,1)S(1)}, bf16[528,512]{1,0:T(8,128)(2,1)S(1)}, u32[]{:S(2)}, u32[]{:S(2)}) collective-permute-start(bf16[528,512]{1,0:T(8,128)(2,1)S(1)} %collective-permute-done.8.other), channel_id=1, source_target_pairs={{0,16},{16,0},{32,48},{48,32},{64,80},{80,64},{96,112},{112,96},{1... | collective-permute-start | bytes 1622024 | tf_op jit(solution)/shard_map/ppermute | solution.py:225

commit v7 on v6

--- a/solution.py
+++ b/solution.py
@@ -30,18 +30,12 @@
     return lax.dot_general(a, b, (((1,), (1,)), ((), ())), preferred_element_type=F32)
 
 
-def prepare_kernel(
-    place, occupations, offsets, coupling, lesser, packed, half, mine, pair, sem
-):
-    k, sl, c, x = place[1], place[2], place[4], place[5]
-    copies = [
-        pltpu.make_async_copy(lesser.at[k, sl, c], mine, sem.at[0]),
-        pltpu.make_async_copy(lesser.at[k, 1 - sl, c], pair, sem.at[1]),
-        pltpu.make_async_copy(coupling.at[x], half.at[pl.ds(0, NO)], sem.at[2]),
-    ]
+def prepare_kernel(place, occupations, offsets, coupling, packed, half, sem):
+    x = place[5]
+    copies = [pltpu.make_async_copy(coupling.at[x], half.at[pl.ds(0, NO)], sem.at[2])]
     for t in range(2):
         copies.append(
-            pltpu.make_async_copy(coupling.at[t], packed.at[t, pl.ds(0, NO)], sem.at[3 + t])
+            pltpu.make_async_copy(coupling.at[t], packed.at[t, pl.ds(0, NO)], sem.at[t])
         )
     for copy in copies:
         copy.start()
@@ -63,17 +57,17 @@
         copy.wait()
 
 
-def prepare(place, occupations, offsets, coupling, lesser):
+def prepare(place, occupations, offsets, coupling):
     block = (NO + TAIL, NO)
     return pl.pallas_call(
         prepare_kernel,
-        out_shape=[shape((2, *block), BF16), shape(block, BF16)] + [shape((NO, NO), BF16)] * 2,
-        in_specs=[SMEM] * 3 + [HBM] * 2,
-        out_specs=[VMEM] * 4,
-        scratch_shapes=[pltpu.SemaphoreType.DMA((5,))],
+        out_shape=[shape((2, *block), BF16), shape(block, BF16)],
+        in_specs=[SMEM] * 3 + [HBM],
+        out_specs=[VMEM] * 2,
+        scratch_shapes=[pltpu.SemaphoreType.DMA((3,))],
         compiler_params=pltpu.CompilerParams(vmem_limit_bytes=60 * MIB),
         name="prepare",
-    )(place, occupations, offsets, coupling, lesser)
+    )(place, occupations, offsets, coupling)
 
 
 def mix_kernel(place, weight, mine, pair, cross, out):
@@ -235,18 +229,22 @@
                 if 0 <= e + step < count:
                     pairs.append((d * count + e, target * count + e + step))
 
-    packed, part, mine, pair = prepare(place, occupations, offsets, coupling, lesser)
-    half = flip(part, 4)
+    sl, c = (y & 1) ^ b, y >> 1
+    mine, pair = lesser[k, sl, c], lesser[k, 1 - sl, c]
     edge = [(s * 8 + d, (1 - s) * 8 + d) for s in range(2) for d in range(8) if (d // 2) % 2]
     cross = lax.ppermute(mine, ("slab", "freq"), edge)
+    packed, part = prepare(place, occupations, offsets, coupling)
+    half = flip(part, 4)
     mixed = mix(place, intersection, mine, pair, cross)
-    half, mixed, packed = lax.optimization_barrier((half, mixed, packed))
+    half, packed = lax.optimization_barrier((half, packed))
     c1, c3 = flip(packed, 2), flip(packed, 6)
     near = lax.ppermute(mixed, ("freq", "energy"), near_pairs)
     far = lax.ppermute(mixed, ("freq", "energy"), far_pairs)
     other = lax.ppermute(half, "energy", [(e, e ^ 4) for e in range(count)])
     own, shared = flip(mixed, 1), flip(near, 1)
-    own, shared, far, packed = lax.optimization_barrier((own, shared, far, packed))
+    own, shared, far, packed, half, other = lax.optimization_barrier(
+        (own, shared, far, packed, half, other)
+    )
     swapped = [flip(x, 1) for x in (packed, c1, c3, half, other)]
 
     first, green = sandwich_first(place, [own, near, shared, far], [c1, c3, half, other])

time: 107 us -> 99.7 us (0.932)
  the two profiles are of different devices: /device:TPU:38 before, /device:TPU:6 now
where the time goes in v7:
time: 99.7 us; the launch traced here: 99.4 us
  waiting for transfers between devices  36.4 us (37%)
  starting transfers between devices  23.4 us (23%)
  Pallas kernels  18.8 us (19%)
  blocking collectives  18.8 us (19%)
  local copies, waits for them, and re-layouts  1.95 us (2%)
    all_to_all x1, blocking collectives, shards(): return collect(place, lax.all_to_all(pieces, 'freq', 0, 0))  18.8 us
    ppermute x10, starting transfers between devices, flip(): return lax.ppermute(x, 'freq', [(d, d ^ bits) for d in range(8)])  13.4 us
    ppermute x1, waiting for transfers between devices, shards(): far = lax.ppermute(mixed, ('freq', 'energy'), far_pairs)  12.6 us
    ppermute x10, waiting for transfers between devices, flip(): return lax.ppermute(x, 'freq', [(d, d ^ bits) for d in range(8)])  12.3 us
    ppermute x1, waiting for transfers between devices, shards(): near = lax.ppermute(mixed, ('freq', 'energy'), near_pairs)  11.5 us
    pallas_call x1, Pallas kernels, sandwich_last(): pl.pallas_call(last_kernel, out_shape=shape((8, 2, ROWS, NO), BF16), in_s...  8.61 us
    ppermute x1, starting transfers between devices, shards(): near = lax.ppermute(mixed, ('freq', 'energy'), near_pairs)  6.67 us
    pallas_call x1, Pallas kernels, sandwich_first(): pl.pallas_call(first_kernel, out_shape=[shape((NO, NO), F32), shape((4, N...  4.48 us
  transfers between devices with their start and end apart: 14, of which 5 were waited for; matrix products, arithmetic and copies ran while one was open for 1% of the time, Pallas kernels for 5%

profile of v7, /device:TPU:6, one launch (start us, length us, event | category | flops | bytes accessed | tf_op | source)
XLA Modules:
  0.0 99.4 jit_solution(5717278023147002521)
XLA Ops:
  0.0 0.7 stack.27.place
  0.7 3.3 %prepare.1 = (bf16[2,528,512]{2,1,0:T(8,128)(2,1)}, bf16[528,512]{1,0:T(8,128)(2,1)}) custom-call(s32[6]{0:T(128)} %stack.27.place, f32[2]{0:T(128)} %occupations.1, s32[2]{0:T(128)} %offsets.1, bf16[2,512,512]{2,1,0:T(8,128)(2,1)} %coupling.1), custom_call_target="tpu_custom_call" | custom-call | tf_op jit(solution)/shard_map/prepare/pallas_call | solution.py:62
  4.0 0.0 copy-start.1
  4.0 3.3 %collective-permute-start.5 = (bf16[528,512]{1,0:T(8,128)(2,1)}, bf16[528,512]{1,0:T(8,128)(2,1)S(1)}, u32[]{:S(2)}, u32[]{:S(2)}) collective-permute-start(bf16[528,512]{1,0:T(8,128)(2,1)} %get-tuple-element.17), channel_id=1, source_target_pairs={{0,64},{16,80},{32,96},{48,112},{64,0},{80,16},{96,32},{112,48},{1... | collective-permute-start | bytes 1622024 | tf_op jit(solution)/shard_map/ppermute | solution.py:219
  7.3 1.3 %dynamic-slice_bitcast_fusion = (bf16[512,512]{1,0:T(8,128)(2,1)S(1)}, bf16[512,512]{1,0:T(8,128)(2,1)S(1)}) fusion(bf16[2,2,2,512,512]{4,3,2,1,0:T(8,128)(2,1)} %param.6, s32[]{:T(128)S(6)} %select_n.14, s32[]{:T(128)S(6)} %select_n.17, s32[]{:T(128)S(6)} %select_n.16, s32[]{:T(128)S(6)} %select_n.15), kind=kLoop, calls=%fused_computation | loop fusion | bytes 2097168 | tf_op jit(solution)/shard_map/squeeze | solution.py:233
  8.5 0.7 collective-permute-start
  9.3 10.6 %collective-permute-done.5.half = bf16[528,512]{1,0:T(8,128)(2,1)S(1)} collective-permute-done((bf16[528,512]{1,0:T(8,128)(2,1)}, bf16[528,512]{1,0:T(8,128)(2,1)S(1)}, u32[]{:S(2)}, u32[]{:S(2)}) %collective-permute-start.5) | collective-permute-done | bytes 540704 | tf_op jit(solution)/shard_map/ppermute | solution.py:219
  19.8 1.6 %collective-permute-start.7 = (bf16[2,528,512]{2,1,0:T(8,128)(2,1)S(1)}, bf16[2,528,512]{2,1,0:T(8,128)(2,1)S(1)}, u32[]{:S(2)}, u32[]{:S(2)}) collective-permute-start(bf16[2,528,512]{2,1,0:T(8,128)(2,1)S(1)} %copy-done.3), channel_id=1, source_target_pairs={{0,32},{16,48},{32,0},{48,16},{64,96},{80,112},{96,64},{112,80},{1... | collective-permute-start | bytes 3244040 | tf_op jit(solution)/shard_map/ppermute | solution.py:219
  21.4 2.2 %collective-permute-start.8 = (bf16[2,528,512]{2,1,0:T(8,128)(2,1)S(1)}, bf16[2,528,512]{2,1,0:T(8,128)(2,1)S(1)}, u32[]{:S(2)}, u32[]{:S(2)}) collective-permute-start(bf16[2,528,512]{2,1,0:T(8,128)(2,1)S(1)} %copy-done.3), channel_id=1, source_target_pairs={{0,96},{16,112},{32,64},{48,80},{64,32},{80,48},{96,0},{112,16},{1... | collective-permute-start | bytes 3244040 | tf_op jit(solution)/shard_map/ppermute | solution.py:219
  23.6 0.0 collective-permute-done.cross
  23.6 0.8 mix.1
  24.4 0.0 copy-start.2
  24.4 6.7 %collective-permute-start.2 = (bf16[512,512]{1,0:T(8,128)(2,1)S(1)}, bf16[512,512]{1,0:T(8,128)(2,1)S(1)}, u32[]{:S(2)}, u32[]{:S(2)}) collective-permute-start(bf16[512,512]{1,0:T(8,128)(2,1)S(1)} %mix.1), channel_id=1, source_target_pairs={{1,16},{2,17},{3,18},{4,19},{5,20},{6,21},{7,22},{8,23},{9,24},{10... | collective-permute-start | bytes 1572872 | tf_op jit(solution)/shard_map/ppermute | solution.py:241
  31.1 0.1 collective-permute-start.1
  31.2 0.7 collective-permute-start.6
  31.9 11.5 %collective-permute-done.2.near = bf16[512,512]{1,0:T(8,128)(2,1)S(1)} collective-permute-done((bf16[512,512]{1,0:T(8,128)(2,1)S(1)}, bf16[512,512]{1,0:T(8,128)(2,1)S(1)}, u32[]{:S(2)}, u32[]{:S(2)}) %collective-permute-start.2) | collective-permute-done | bytes 524320 | tf_op jit(solution)/shard_map/ppermute | solution.py:241
  43.4 1.9 %collective-permute-start.4 = (bf16[512,512]{1,0:T(8,128)(2,1)S(1)}, bf16[512,512]{1,0:T(8,128)(2,1)S(1)}, u32[]{:S(2)}, u32[]{:S(2)}) collective-permute-start(bf16[512,512]{1,0:T(8,128)(2,1)S(1)} %mix.1), channel_id=1, source_target_pairs={{0,1},{1,2},{2,3},{3,4},{4,5},{5,6},{6,7},{7,8},{8,9},{9,10},{10,1... | collective-permute-start | bytes 1572872 | tf_op jit(solution)/shard_map/ppermute | solution.py:242
  45.3 5.2 %collective-permute-start.3 = (bf16[512,512]{1,0:T(8,128)(2,1)S(1)}, bf16[512,512]{1,0:T(8,128)(2,1)S(1)}, u32[]{:S(2)}, u32[]{:S(2)}) collective-permute-start(bf16[512,512]{1,0:T(8,128)(2,1)S(1)} %collective-permute-done.2.near), channel_id=1, source_target_pairs={{0,16},{16,0},{32,48},{48,32},{64,80},{80,64},{96,112},{112,96},{1... | collective-permute-start | bytes 1572872 | tf_op jit(solution)/shard_map/ppermute | solution.py:219
  50.5 12.6 %collective-permute-done.4.far = bf16[512,512]{1,0:T(8,128)(2,1)S(1)} collective-permute-done((bf16[512,512]{1,0:T(8,128)(2,1)S(1)}, bf16[512,512]{1,0:T(8,128)(2,1)S(1)}, u32[]{:S(2)}, u32[]{:S(2)}) %collective-permute-start.4) | collective-permute-done | bytes 524320 | tf_op jit(solution)/shard_map/ppermute | solution.py:242
  63.1 0.0 collective-permute-start.9
  63.1 0.0 collective-permute-done.7.c1
  63.1 0.5 collective-permute-start.10
  63.6 0.1 collective-permute-start.11
  63.7 0.4 collective-permute-start.12
  64.1 0.1 collective-permute-start.13
  64.2 4.5 %sandwich_first.1 = (f32[512,512]{1,0:T(8,128)S(1)}, bf16[4,512,512]{2,1,0:T(8,128)(2,1)S(1)}) custom-call(s32[6]{0:T(128)S(1)} %copy-done, bf16[512,512]{1,0:T(8,128)(2,1)S(1)} %collective-permute-done.1.own, bf16[512,512]{1,0:T(8,128)(2,1)S(1)} %collective-permute-done.2.near, bf16[512,512]{1,0:T(8,128)(2,1)S(1)} %collective-permute-done.3.shared, ...), custom_call_target="tpu_custom_call" | custom-call | flops 3221225472 | bytes 8388608 | tf_op jit(solution)/shard_map/sandwich_first/pallas_call | solution.py:162
  68.7 1.0 collective-permute-done.12.half
  69.7 0.8 collective-permute-done.13.other
  70.4 0.0 collective-permute-done.9.s0
  70.5 8.6 %sandwich_last.1 = bf16[8,2,64,512]{3,2,1,0:T(8,128)(2,1)S(1)} custom-call(s32[6]{0:T(128)S(1)} %copy-done, bf16[4,512,512]{2,1,0:T(8,128)(2,1)S(1)} %get-tuple-element.26.green, f32[512,512]{1,0:T(8,128)S(1)} %get-tuple-element.27.start, bf16[2,528,512]{2,1,0:T(8,128)(2,1)S(1)} %copy-done.3, bf16[2,528,512]{2,1,0:T(8,128)(2,1)S(1)} %collective-permute-done.9.s0, ...), custom_call_target="tpu_custom_call" | custom-call | flops 6979321856 | bytes 12058624 | tf_op jit(solution)/shard_map/sandwich_last/pallas_call | solution.py:175
  79.1 18.8 %all_to_all.5.pieces = bf16[8,2,64,512]{3,2,1,0:T(8,128)(2,1)S(1)} all-to-all(bf16[8,2,64,512]{3,2,1,0:T(8,128)(2,1)S(1)} %sandwich_last.1), channel_id=1, replica_groups=mesh['slab'=2,'freq'=8,'energy'=16] {'freq'}, dimensions={0} | all-to-all | bytes 2097152 | tf_op jit(solution)/shard_map/all_to_all | solution.py:252
  97.8 1.6 %collect.1 = f32[2,2,2,64,512]{4,3,2,1,0:T(8,128)} custom-call(s32[6]{0:T(128)S(1)} %copy-done, bf16[8,2,64,512]{3,2,1,0:T(8,128)(2,1)S(1)} %all_to_all.5.pieces), custom_call_target="tpu_custom_call" | custom-call | tf_op jit(solution)/shard_map/collect/pallas_call | solution.py:201
  (12 shorter events, 0.0 us)
Async XLA Ops:
  4.0 15.9 %copy-start.3 = (bf16[2,528,512]{2,1,0:T(8,128)(2,1)S(1)}, bf16[2,528,512]{2,1,0:T(8,128)(2,1)}, u32[]{:S(2)}) copy-start(bf16[2,528,512]{2,1,0:T(8,128)(2,1)} %get-tuple-element.28.home) | copy-start | bytes 3244036
  4.0 19.6 %copy-start = (s32[6]{0:T(128)S(1)}, s32[6]{0:T(128)}, u32[]{:S(2)}) copy-start(s32[6]{0:T(128)} %stack.27.place) | copy-start | bytes 76
  4.0 19.6 %copy-start.1 = (f32[2]{0:T(128)S(1)}, f32[2]{0:T(128)}, u32[]{:S(2)}) copy-start(f32[2]{0:T(128)} %weight.1) | copy-start | bytes 28
  4.0 15.8 %collective-permute-start.5 = (bf16[528,512]{1,0:T(8,128)(2,1)}, bf16[528,512]{1,0:T(8,128)(2,1)S(1)}, u32[]{:S(2)}, u32[]{:S(2)}) collective-permute-start(bf16[528,512]{1,0:T(8,128)(2,1)} %get-tuple-element.17), channel_id=1, source_target_pairs={{0,64},{16,80},{32,96},{48,112},{64,0},{80,16},{96,32},{112,48},{1... | collective-permute-start | bytes 1622024 | tf_op jit(solution)/shard_map/ppermute | solution.py:219
  8.5 15.0 %collective-permute-start = (bf16[512,512]{1,0:T(8,128)(2,1)S(1)}, bf16[512,512]{1,0:T(8,128)(2,1)S(1)}, u32[]{:S(2)}, u32[]{:S(2)}) collective-permute-start(bf16[512,512]{1,0:T(8,128)(2,1)S(1)} %get-tuple-element.30.mine), channel_id=1, source_target_pairs={{32,160},{48,176},{96,224},{112,240},{160,32},{176,48},{224,96},{2... | collective-permute-start | bytes 1572872 | tf_op jit(solution)/shard_map/ppermute | solution.py:235
  19.8 43.3 %collective-permute-start.7 = (bf16[2,528,512]{2,1,0:T(8,128)(2,1)S(1)}, bf16[2,528,512]{2,1,0:T(8,128)(2,1)S(1)}, u32[]{:S(2)}, u32[]{:S(2)}) collective-permute-start(bf16[2,528,512]{2,1,0:T(8,128)(2,1)S(1)} %copy-done.3), channel_id=1, source_target_pairs={{0,32},{16,48},{32,0},{48,16},{64,96},{80,112},{96,64},{112,80},{1... | collective-permute-start | bytes 3244040 | tf_op jit(solution)/shard_map/ppermute | solution.py:219
  21.4 42.2 %collective-permute-start.8 = (bf16[2,528,512]{2,1,0:T(8,128)(2,1)S(1)}, bf16[2,528,512]{2,1,0:T(8,128)(2,1)S(1)}, u32[]{:S(2)}, u32[]{:S(2)}) collective-permute-start(bf16[2,528,512]{2,1,0:T(8,128)(2,1)S(1)} %copy-done.3), channel_id=1, source_target_pairs={{0,96},{16,112},{32,64},{48,80},{64,32},{80,48},{96,0},{112,16},{1... | collective-permute-start | bytes 3244040 | tf_op jit(solution)/shard_map/ppermute | solution.py:219
  24.4 46.1 %copy-start.2 = (bf16[2,2,2,512,512]{4,3,2,1,0:T(8,128)(2,1)S(1)}, bf16[2,2,2,512,512]{4,3,2,1,0:T(8,128)(2,1)}, u32[]{:S(2)}) copy-start(bf16[2,2,2,512,512]{4,3,2,1,0:T(8,128)(2,1)} %retarded.1) | copy-start | bytes 12582916
  24.4 19.0 %collective-permute-start.2 = (bf16[512,512]{1,0:T(8,128)(2,1)S(1)}, bf16[512,512]{1,0:T(8,128)(2,1)S(1)}, u32[]{:S(2)}, u32[]{:S(2)}) collective-permute-start(bf16[512,512]{1,0:T(8,128)(2,1)S(1)} %mix.1), channel_id=1, source_target_pairs={{1,16},{2,17},{3,18},{4,19},{5,20},{6,21},{7,22},{8,23},{9,24},{10... | collective-permute-start | bytes 1572872 | tf_op jit(solution)/shard_map/ppermute | solution.py:241
  31.1 14.2 %collective-permute-start.1 = (bf16[512,512]{1,0:T(8,128)(2,1)S(1)}, bf16[512,512]{1,0:T(8,128)(2,1)S(1)}, u32[]{:S(2)}, u32[]{:S(2)}) collective-permute-start(bf16[512,512]{1,0:T(8,128)(2,1)S(1)} %mix.1), channel_id=1, source_target_pairs={{0,16},{16,0},{32,48},{48,32},{64,80},{80,64},{96,112},{112,96},{1... | collective-permute-start | bytes 1572872 | tf_op jit(solution)/shard_map/ppermute | solution.py:219
  31.2 31.9 %collective-permute-start.6 = (bf16[528,512]{1,0:T(8,128)(2,1)S(1)}, bf16[528,512]{1,0:T(8,128)(2,1)S(1)}, u32[]{:S(2)}, u32[]{:S(2)}) collective-permute-start(bf16[528,512]{1,0:T(8,128)(2,1)S(1)} %collective-permute-done.5.half), channel_id=1, source_target_pairs={{0,4},{1,5},{2,6},{3,7},{4,0},{5,1},{6,2},{7,3},{8,12},{9,13},{10,... | collective-permute-start | bytes 1622024 | tf_op jit(solution)/shard_map/ppermute | solution.py:243
  43.4 19.7 %collective-permute-start.4 = (bf16[512,512]{1,0:T(8,128)(2,1)S(1)}, bf16[512,512]{1,0:T(8,128)(2,1)S(1)}, u32[]{:S(2)}, u32[]{:S(2)}) collective-permute-start(bf16[512,512]{1,0:T(8,128)(2,1)S(1)} %mix.1), channel_id=1, source_target_pairs={{0,1},{1,2},{2,3},{3,4},{4,5},{5,6},{6,7},{7,8},{8,9},{9,10},{10,1... | collective-permute-start | bytes 1572872 | tf_op jit(solution)/shard_map/ppermute | solution.py:242
  45.3 17.8 %collective-permute-start.3 = (bf16[512,512]{1,0:T(8,128)(2,1)S(1)}, bf16[512,512]{1,0:T(8,128)(2,1)S(1)}, u32[]{:S(2)}, u32[]{:S(2)}) collective-permute-start(bf16[512,512]{1,0:T(8,128)(2,1)S(1)} %collective-permute-done.2.near), channel_id=1, source_target_pairs={{0,16},{16,0},{32,48},{48,32},{64,80},{80,64},{96,112},{112,96},{1... | collective-permute-start | bytes 1572872 | tf_op jit(solution)/shard_map/ppermute | solution.py:219
  63.1 7.4 %collective-permute-start.9 = (bf16[2,528,512]{2,1,0:T(8,128)(2,1)S(1)}, bf16[2,528,512]{2,1,0:T(8,128)(2,1)S(1)}, u32[]{:S(2)}, u32[]{:S(2)}) collective-permute-start(bf16[2,528,512]{2,1,0:T(8,128)(2,1)S(1)} %copy-done.3), channel_id=1, source_target_pairs={{0,16},{16,0},{32,48},{48,32},{64,80},{80,64},{96,112},{112,96},{1... | collective-permute-start | bytes 3244040 | tf_op jit(solution)/shard_map/ppermute | solution.py:219
  63.1 7.3 %collective-permute-start.10 = (bf16[2,528,512]{2,1,0:T(8,128)(2,1)S(1)}, bf16[2,528,512]{2,1,0:T(8,128)(2,1)S(1)}, u32[]{:S(2)}, u32[]{:S(2)}) collective-permute-start(bf16[2,528,512]{2,1,0:T(8,128)(2,1)S(1)} %collective-permute-done.7.c1), channel_id=1, source_target_pairs={{0,16},{16,0},{32,48},{48,32},{64,80},{80,64},{96,112},{112,96},{1... | collective-permute-start | bytes 3244040 | tf_op jit(solution)/shard_map/ppermute | solution.py:219
  63.6 6.8 %collective-permute-start.11 = (bf16[2,528,512]{2,1,0:T(8,128)(2,1)S(1)}, bf16[2,528,512]{2,1,0:T(8,128)(2,1)S(1)}, u32[]{:S(2)}, u32[]{:S(2)}) collective-permute-start(bf16[2,528,512]{2,1,0:T(8,128)(2,1)S(1)} %collective-permute-done.8.c3), channel_id=1, source_target_pairs={{0,16},{16,0},{32,48},{48,32},{64,80},{80,64},{96,112},{112,96},{1... | collective-permute-start | bytes 3244040 | tf_op jit(solution)/shard_map/ppermute | solution.py:219
  63.7 6.0 %collective-permute-start.12 = (bf16[528,512]{1,0:T(8,128)(2,1)S(1)}, bf16[528,512]{1,0:T(8,128)(2,1)S(1)}, u32[]{:S(2)}, u32[]{:S(2)}) collective-permute-start(bf16[528,512]{1,0:T(8,128)(2,1)S(1)} %collective-permute-done.5.half), channel_id=1, source_target_pairs={{0,16},{16,0},{32,48},{48,32},{64,80},{80,64},{96,112},{112,96},{1... | collective-permute-start | bytes 1622024 | tf_op jit(solution)/shard_map/ppermute | solution.py:219
  64.1 6.3 %collective-permute-start.13 = (bf16[528,512]{1,0:T(8,128)(2,1)S(1)}, bf16[528,512]{1,0:T(8,128)(2,1)S(1)}, u32[]{:S(2)}, u32[]{:S(2)}) collective-permute-start(bf16[528,512]{1,0:T(8,128)(2,1)S(1)} %collective-permute-done.6.other), channel_id=1, source_target_pairs={{0,16},{16,0},{32,48},{48,32},{64,80},{80,64},{96,112},{112,96},{1... | collective-permute-start | bytes 1622024 | tf_op jit(solution)/shard_map/ppermute | solution.py:219

commit v8 on v7

--- a/solution.py
+++ b/solution.py
@@ -236,12 +236,12 @@
     packed, part = prepare(place, occupations, offsets, coupling)
     half = flip(part, 4)
     mixed = mix(place, intersection, mine, pair, cross)
-    half, packed = lax.optimization_barrier((half, packed))
+    near = lax.ppermute(mixed, ("freq", "energy"), near_pairs)
+    own, shared = flip(mixed, 1), flip(near, 1)
+    own, mixed, half, packed = lax.optimization_barrier((own, mixed, half, packed))
     c1, c3 = flip(packed, 2), flip(packed, 6)
-    near = lax.ppermute(mixed, ("freq", "energy"), near_pairs)
     far = lax.ppermute(mixed, ("freq", "energy"), far_pairs)
     other = lax.ppermute(half, "energy", [(e, e ^ 4) for e in range(count)])
-    own, shared = flip(mixed, 1), flip(near, 1)
     own, shared, far, packed, half, other = lax.optimization_barrier(
         (own, shared, far, packed, half, other)
     )

time: 99.7 us -> 95.4 us (0.957)
  the two profiles are of different devices: /device:TPU:6 before, /device:TPU:2 now
where the time goes in v8:
time: 95.4 us; the launch traced here: 95.1 us
  waiting for transfers between devices  34.4 us (36%)
  starting transfers between devices  20.3 us (21%)
  blocking collectives  18.9 us (20%)
  Pallas kernels  18.8 us (20%)
  local copies, waits for them, and re-layouts  2.62 us (3%)
    all_to_all x1, blocking collectives, shards(): return collect(place, lax.all_to_all(pieces, 'freq', 0, 0))  18.9 us
    ppermute x1, waiting for transfers between devices, shards(): near = lax.ppermute(mixed, ('freq', 'energy'), near_pairs)  18.6 us
    ppermute x10, waiting for transfers between devices, flip(): return lax.ppermute(x, 'freq', [(d, d ^ bits) for d in range(8)])  14.3 us
    ppermute x10, starting transfers between devices, flip(): return lax.ppermute(x, 'freq', [(d, d ^ bits) for d in range(8)])  12 us
    pallas_call x1, Pallas kernels, sandwich_last(): pl.pallas_call(last_kernel, out_shape=shape((8, 2, ROWS, NO), BF16), in_s...  8.64 us
    ppermute x1, starting transfers between devices, shards(): near = lax.ppermute(mixed, ('freq', 'energy'), near_pairs)  5.17 us
    pallas_call x1, Pallas kernels, sandwich_first(): pl.pallas_call(first_kernel, out_shape=[shape((NO, NO), F32), shape((4, N...  4.49 us
    pallas_call x1, Pallas kernels, prepare(): pl.pallas_call(prepare_kernel, out_shape=[shape((2, *block), BF16), shape...  3.29 us
  transfers between devices with their start and end apart: 14, of which 6 were waited for; matrix products, arithmetic and copies ran while one was open for 1% of the time, Pallas kernels for 9%

profile of v8, /device:TPU:2, one launch (start us, length us, event | category | flops | bytes accessed | tf_op | source)
XLA Modules:
  0.0 95.1 jit_solution(7448825002138397510)
XLA Ops:
  0.0 1.3 %dynamic-slice_bitcast_fusion = (bf16[512,512]{1,0:T(8,128)(2,1)S(1)}, bf16[512,512]{1,0:T(8,128)(2,1)S(1)}) fusion(bf16[2,2,2,512,512]{4,3,2,1,0:T(8,128)(2,1)} %param.6, s32[]{:T(128)S(6)} %select_n.14, s32[]{:T(128)S(6)} %select_n.17, s32[]{:T(128)S(6)} %select_n.16, s32[]{:T(128)S(6)} %select_n.15), kind=kLoop, calls=%fused_computation | loop fusion | bytes 2097168 | tf_op jit(solution)/shard_map/squeeze | solution.py:233
  1.3 0.7 collective-permute-start
  2.0 0.7 stack.27.place
  2.7 3.3 %prepare.1 = (bf16[2,528,512]{2,1,0:T(8,128)(2,1)}, bf16[528,512]{1,0:T(8,128)(2,1)}) custom-call(s32[6]{0:T(128)} %stack.27.place, f32[2]{0:T(128)} %occupations.1, s32[2]{0:T(128)} %offsets.1, bf16[2,512,512]{2,1,0:T(8,128)(2,1)} %coupling.1), custom_call_target="tpu_custom_call" | custom-call | tf_op jit(solution)/shard_map/prepare/pallas_call | solution.py:62
  6.0 3.3 %collective-permute-start.2 = (bf16[528,512]{1,0:T(8,128)(2,1)}, bf16[528,512]{1,0:T(8,128)(2,1)S(1)}, u32[]{:S(2)}, u32[]{:S(2)}) collective-permute-start(bf16[528,512]{1,0:T(8,128)(2,1)} %get-tuple-element.19), channel_id=1, source_target_pairs={{0,64},{16,80},{32,96},{48,112},{64,0},{80,16},{96,32},{112,48},{1... | collective-permute-start | bytes 1622024 | tf_op jit(solution)/shard_map/ppermute | solution.py:219
  9.2 0.7 copy-done
  9.9 0.8 mix.1
  10.7 0.1 collective-permute-start.1
  10.8 11.0 %collective-permute-done.2.half = bf16[528,512]{1,0:T(8,128)(2,1)S(1)} collective-permute-done((bf16[528,512]{1,0:T(8,128)(2,1)}, bf16[528,512]{1,0:T(8,128)(2,1)S(1)}, u32[]{:S(2)}, u32[]{:S(2)}) %collective-permute-start.2) | collective-permute-done | bytes 540704 | tf_op jit(solution)/shard_map/ppermute | solution.py:219
  21.8 0.0 collective-permute-done.1.own
  21.8 4.5 %collective-permute-start.7 = (bf16[2,528,512]{2,1,0:T(8,128)(2,1)S(1)}, bf16[2,528,512]{2,1,0:T(8,128)(2,1)S(1)}, u32[]{:S(2)}, u32[]{:S(2)}) collective-permute-start(bf16[2,528,512]{2,1,0:T(8,128)(2,1)S(1)} %copy-done.3), channel_id=1, source_target_pairs={{0,32},{16,48},{32,0},{48,16},{64,96},{80,112},{96,64},{112,80},{1... | collective-permute-start | bytes 3244040 | tf_op jit(solution)/shard_map/ppermute | solution.py:219
  26.3 1.5 %collective-permute-start.8 = (bf16[2,528,512]{2,1,0:T(8,128)(2,1)S(1)}, bf16[2,528,512]{2,1,0:T(8,128)(2,1)S(1)}, u32[]{:S(2)}, u32[]{:S(2)}) collective-permute-start(bf16[2,528,512]{2,1,0:T(8,128)(2,1)S(1)} %copy-done.3), channel_id=1, source_target_pairs={{0,96},{16,112},{32,64},{48,80},{64,32},{80,48},{96,0},{112,16},{1... | collective-permute-start | bytes 3244040 | tf_op jit(solution)/shard_map/ppermute | solution.py:219
  27.8 5.2 %collective-permute-start.3 = (bf16[512,512]{1,0:T(8,128)(2,1)S(1)}, bf16[512,512]{1,0:T(8,128)(2,1)S(1)}, u32[]{:S(2)}, u32[]{:S(2)}) collective-permute-start(bf16[512,512]{1,0:T(8,128)(2,1)S(1)} %mix.1), channel_id=1, source_target_pairs={{1,16},{2,17},{3,18},{4,19},{5,20},{6,21},{7,22},{8,23},{9,24},{10... | collective-permute-start | bytes 1572872 | tf_op jit(solution)/shard_map/ppermute | solution.py:239
  33.0 0.1 collective-permute-start.6
  33.1 2.4 %collective-permute-start.5 = (bf16[512,512]{1,0:T(8,128)(2,1)S(1)}, bf16[512,512]{1,0:T(8,128)(2,1)S(1)}, u32[]{:S(2)}, u32[]{:S(2)}) collective-permute-start(bf16[512,512]{1,0:T(8,128)(2,1)S(1)} %mix.1), channel_id=1, source_target_pairs={{0,1},{1,2},{2,3},{3,4},{4,5},{5,6},{6,7},{7,8},{8,9},{9,10},{10,1... | collective-permute-start | bytes 1572872 | tf_op jit(solution)/shard_map/ppermute | solution.py:243
  35.5 18.6 %collective-permute-done.3.near = bf16[512,512]{1,0:T(8,128)(2,1)S(1)} collective-permute-done((bf16[512,512]{1,0:T(8,128)(2,1)S(1)}, bf16[512,512]{1,0:T(8,128)(2,1)S(1)}, u32[]{:S(2)}, u32[]{:S(2)}) %collective-permute-start.3) | collective-permute-done | bytes 524320 | tf_op jit(solution)/shard_map/ppermute | solution.py:239
  54.1 1.4 %collective-permute-start.4 = (bf16[512,512]{1,0:T(8,128)(2,1)S(1)}, bf16[512,512]{1,0:T(8,128)(2,1)S(1)}, u32[]{:S(2)}, u32[]{:S(2)}) collective-permute-start(bf16[512,512]{1,0:T(8,128)(2,1)S(1)} %collective-permute-done.3.near), channel_id=1, source_target_pairs={{0,16},{16,0},{32,48},{48,32},{64,80},{80,64},{96,112},{112,96},{1... | collective-permute-start | bytes 1572872 | tf_op jit(solution)/shard_map/ppermute | solution.py:219
  55.6 0.0 collective-permute-done.5.far
  55.6 1.5 %collective-permute-done.4.shared = bf16[512,512]{1,0:T(8,128)(2,1)S(1)} collective-permute-done((bf16[512,512]{1,0:T(8,128)(2,1)S(1)}, bf16[512,512]{1,0:T(8,128)(2,1)S(1)}, u32[]{:S(2)}, u32[]{:S(2)}) %collective-permute-start.4) | collective-permute-done | bytes 524320 | tf_op jit(solution)/shard_map/ppermute | solution.py:219
  57.1 1.5 %collective-permute-done.6.other = bf16[528,512]{1,0:T(8,128)(2,1)S(1)} collective-permute-done((bf16[528,512]{1,0:T(8,128)(2,1)S(1)}, bf16[528,512]{1,0:T(8,128)(2,1)S(1)}, u32[]{:S(2)}, u32[]{:S(2)}) %collective-permute-start.6) | collective-permute-done | bytes 540704 | tf_op jit(solution)/shard_map/ppermute | solution.py:244
  58.6 0.5 collective-permute-start.10
  59.1 0.1 collective-permute-start.11
  59.2 0.4 collective-permute-start.12
  59.7 0.1 collective-permute-start.13
  59.7 4.5 %sandwich_first.1 = (f32[512,512]{1,0:T(8,128)S(1)}, bf16[4,512,512]{2,1,0:T(8,128)(2,1)S(1)}) custom-call(s32[6]{0:T(128)S(1)} %copy-done, bf16[512,512]{1,0:T(8,128)(2,1)S(1)} %collective-permute-done.1.own, bf16[512,512]{1,0:T(8,128)(2,1)S(1)} %collective-permute-done.3.near, bf16[512,512]{1,0:T(8,128)(2,1)S(1)} %collective-permute-done.4.shared, ...), custom_call_target="tpu_custom_call" | custom-call | flops 3221225472 | bytes 8388608 | tf_op jit(solution)/shard_map/sandwich_first/pallas_call | solution.py:162
  64.2 1.0 %collective-permute-done.12.half = bf16[528,512]{1,0:T(8,128)(2,1)S(1)} collective-permute-done((bf16[528,512]{1,0:T(8,128)(2,1)S(1)}, bf16[528,512]{1,0:T(8,128)(2,1)S(1)}, u32[]{:S(2)}, u32[]{:S(2)}) %collective-permute-start.12) | collective-permute-done | bytes 540704 | tf_op jit(solution)/shard_map/ppermute | solution.py:219
  65.2 0.8 collective-permute-done.13.other
  66.0 0.0 collective-permute-done.9.s0
  66.0 0.0 collective-permute-done.10.s1
  66.0 8.6 %sandwich_last.1 = bf16[8,2,64,512]{3,2,1,0:T(8,128)(2,1)S(1)} custom-call(s32[6]{0:T(128)S(1)} %copy-done, bf16[4,512,512]{2,1,0:T(8,128)(2,1)S(1)} %get-tuple-element.30.green, f32[512,512]{1,0:T(8,128)S(1)} %get-tuple-element.31.start, bf16[2,528,512]{2,1,0:T(8,128)(2,1)S(1)} %copy-done.3, bf16[2,528,512]{2,1,0:T(8,128)(2,1)S(1)} %collective-permute-done.9.s0, ...), custom_call_target="tpu_custom_call" | custom-call | flops 6979321856 | bytes 12058624 | tf_op jit(solution)/shard_map/sandwich_last/pallas_call | solution.py:175
  74.6 18.9 %all_to_all.5.pieces = bf16[8,2,64,512]{3,2,1,0:T(8,128)(2,1)S(1)} all-to-all(bf16[8,2,64,512]{3,2,1,0:T(8,128)(2,1)S(1)} %sandwich_last.1), channel_id=1, replica_groups=mesh['slab'=2,'freq'=8,'energy'=16] {'freq'}, dimensions={0} | all-to-all | bytes 2097152 | tf_op jit(solution)/shard_map/all_to_all | solution.py:252
  93.5 1.6 %collect.1 = f32[2,2,2,64,512]{4,3,2,1,0:T(8,128)} custom-call(s32[6]{0:T(128)S(1)} %copy-done, bf16[8,2,64,512]{3,2,1,0:T(8,128)(2,1)S(1)} %all_to_all.5.pieces), custom_call_target="tpu_custom_call" | custom-call | tf_op jit(solution)/shard_map/collect/pallas_call | solution.py:201
  (12 shorter events, 0.0 us)
Async XLA Ops:
  0.0 9.2 %copy-start.1 = (f32[2]{0:T(128)S(1)}, f32[2]{0:T(128)}, u32[]{:S(2)}) copy-start(f32[2]{0:T(128)} %weight.1) | copy-start | bytes 28
  1.3 8.0 %collective-permute-start = (bf16[512,512]{1,0:T(8,128)(2,1)S(1)}, bf16[512,512]{1,0:T(8,128)(2,1)S(1)}, u32[]{:S(2)}, u32[]{:S(2)}) collective-permute-start(bf16[512,512]{1,0:T(8,128)(2,1)S(1)} %get-tuple-element.34.mine), channel_id=1, source_target_pairs={{32,160},{48,176},{96,224},{112,240},{160,32},{176,48},{224,96},{2... | collective-permute-start | bytes 1572872 | tf_op jit(solution)/shard_map/ppermute | solution.py:235
  6.0 15.8 %collective-permute-start.2 = (bf16[528,512]{1,0:T(8,128)(2,1)}, bf16[528,512]{1,0:T(8,128)(2,1)S(1)}, u32[]{:S(2)}, u32[]{:S(2)}) collective-permute-start(bf16[528,512]{1,0:T(8,128)(2,1)} %get-tuple-element.19), channel_id=1, source_target_pairs={{0,64},{16,80},{32,96},{48,112},{64,0},{80,16},{96,32},{112,48},{1... | collective-permute-start | bytes 1622024 | tf_op jit(solution)/shard_map/ppermute | solution.py:219
  9.2 0.7 copy-start
  9.9 11.9 %copy-start.3 = (bf16[2,528,512]{2,1,0:T(8,128)(2,1)S(1)}, bf16[2,528,512]{2,1,0:T(8,128)(2,1)}, u32[]{:S(2)}) copy-start(bf16[2,528,512]{2,1,0:T(8,128)(2,1)} %get-tuple-element.32.home) | copy-start | bytes 3244036
  10.7 11.1 %collective-permute-start.1 = (bf16[512,512]{1,0:T(8,128)(2,1)S(1)}, bf16[512,512]{1,0:T(8,128)(2,1)S(1)}, u32[]{:S(2)}, u32[]{:S(2)}) collective-permute-start(bf16[512,512]{1,0:T(8,128)(2,1)S(1)} %mix.1), channel_id=1, source_target_pairs={{0,16},{16,0},{32,48},{48,32},{64,80},{80,64},{96,112},{112,96},{1... | collective-permute-start | bytes 1572872 | tf_op jit(solution)/shard_map/ppermute | solution.py:219
  21.8 44.2 %copy-start.2 = (bf16[2,2,2,512,512]{4,3,2,1,0:T(8,128)(2,1)S(1)}, bf16[2,2,2,512,512]{4,3,2,1,0:T(8,128)(2,1)}, u32[]{:S(2)}) copy-start(bf16[2,2,2,512,512]{4,3,2,1,0:T(8,128)(2,1)} %retarded.1) | copy-start | bytes 12582916
  21.8 36.8 %collective-permute-start.7 = (bf16[2,528,512]{2,1,0:T(8,128)(2,1)S(1)}, bf16[2,528,512]{2,1,0:T(8,128)(2,1)S(1)}, u32[]{:S(2)}, u32[]{:S(2)}) collective-permute-start(bf16[2,528,512]{2,1,0:T(8,128)(2,1)S(1)} %copy-done.3), channel_id=1, source_target_pairs={{0,32},{16,48},{32,0},{48,16},{64,96},{80,112},{96,64},{112,80},{1... | collective-permute-start | bytes 3244040 | tf_op jit(solution)/shard_map/ppermute | solution.py:219
  26.3 32.8 %collective-permute-start.8 = (bf16[2,528,512]{2,1,0:T(8,128)(2,1)S(1)}, bf16[2,528,512]{2,1,0:T(8,128)(2,1)S(1)}, u32[]{:S(2)}, u32[]{:S(2)}) collective-permute-start(bf16[2,528,512]{2,1,0:T(8,128)(2,1)S(1)} %copy-done.3), channel_id=1, source_target_pairs={{0,96},{16,112},{32,64},{48,80},{64,32},{80,48},{96,0},{112,16},{1... | collective-permute-start | bytes 3244040 | tf_op jit(solution)/shard_map/ppermute | solution.py:219
  27.8 26.3 %collective-permute-start.3 = (bf16[512,512]{1,0:T(8,128)(2,1)S(1)}, bf16[512,512]{1,0:T(8,128)(2,1)S(1)}, u32[]{:S(2)}, u32[]{:S(2)}) collective-permute-start(bf16[512,512]{1,0:T(8,128)(2,1)S(1)} %mix.1), channel_id=1, source_target_pairs={{1,16},{2,17},{3,18},{4,19},{5,20},{6,21},{7,22},{8,23},{9,24},{10... | collective-permute-start | bytes 1572872 | tf_op jit(solution)/shard_map/ppermute | solution.py:239
  33.0 25.6 %collective-permute-start.6 = (bf16[528,512]{1,0:T(8,128)(2,1)S(1)}, bf16[528,512]{1,0:T(8,128)(2,1)S(1)}, u32[]{:S(2)}, u32[]{:S(2)}) collective-permute-start(bf16[528,512]{1,0:T(8,128)(2,1)S(1)} %collective-permute-done.2.half), channel_id=1, source_target_pairs={{0,4},{1,5},{2,6},{3,7},{4,0},{5,1},{6,2},{7,3},{8,12},{9,13},{10,... | collective-permute-start | bytes 1622024 | tf_op jit(solution)/shard_map/ppermute | solution.py:244
  33.1 22.5 %collective-permute-start.5 = (bf16[512,512]{1,0:T(8,128)(2,1)S(1)}, bf16[512,512]{1,0:T(8,128)(2,1)S(1)}, u32[]{:S(2)}, u32[]{:S(2)}) collective-permute-start(bf16[512,512]{1,0:T(8,128)(2,1)S(1)} %mix.1), channel_id=1, source_target_pairs={{0,1},{1,2},{2,3},{3,4},{4,5},{5,6},{6,7},{7,8},{8,9},{9,10},{10,1... | collective-permute-start | bytes 1572872 | tf_op jit(solution)/shard_map/ppermute | solution.py:243
  54.1 3.0 %collective-permute-start.4 = (bf16[512,512]{1,0:T(8,128)(2,1)S(1)}, bf16[512,512]{1,0:T(8,128)(2,1)S(1)}, u32[]{:S(2)}, u32[]{:S(2)}) collective-permute-start(bf16[512,512]{1,0:T(8,128)(2,1)S(1)} %collective-permute-done.3.near), channel_id=1, source_target_pairs={{0,16},{16,0},{32,48},{48,32},{64,80},{80,64},{96,112},{112,96},{1... | collective-permute-start | bytes 1572872 | tf_op jit(solution)/shard_map/ppermute | solution.py:219
  58.6 7.3 %collective-permute-start.9 = (bf16[2,528,512]{2,1,0:T(8,128)(2,1)S(1)}, bf16[2,528,512]{2,1,0:T(8,128)(2,1)S(1)}, u32[]{:S(2)}, u32[]{:S(2)}) collective-permute-start(bf16[2,528,512]{2,1,0:T(8,128)(2,1)S(1)} %copy-done.3), channel_id=1, source_target_pairs={{0,16},{16,0},{32,48},{48,32},{64,80},{80,64},{96,112},{112,96},{1... | collective-permute-start | bytes 3244040 | tf_op jit(solution)/shard_map/ppermute | solution.py:219
  58.6 7.3 %collective-permute-start.10 = (bf16[2,528,512]{2,1,0:T(8,128)(2,1)S(1)}, bf16[2,528,512]{2,1,0:T(8,128)(2,1)S(1)}, u32[]{:S(2)}, u32[]{:S(2)}) collective-permute-start(bf16[2,528,512]{2,1,0:T(8,128)(2,1)S(1)} %collective-permute-done.7.c1), channel_id=1, source_target_pairs={{0,16},{16,0},{32,48},{48,32},{64,80},{80,64},{96,112},{112,96},{1... | collective-permute-start | bytes 3244040 | tf_op jit(solution)/shard_map/ppermute | solution.py:219
  59.1 6.8 %collective-permute-start.11 = (bf16[2,528,512]{2,1,0:T(8,128)(2,1)S(1)}, bf16[2,528,512]{2,1,0:T(8,128)(2,1)S(1)}, u32[]{:S(2)}, u32[]{:S(2)}) collective-permute-start(bf16[2,528,512]{2,1,0:T(8,128)(2,1)S(1)} %collective-permute-done.8.c3), channel_id=1, source_target_pairs={{0,16},{16,0},{32,48},{48,32},{64,80},{80,64},{96,112},{112,96},{1... | collective-permute-start | bytes 3244040 | tf_op jit(solution)/shard_map/ppermute | solution.py:219
  59.2 6.0 %collective-permute-start.12 = (bf16[528,512]{1,0:T(8,128)(2,1)S(1)}, bf16[528,512]{1,0:T(8,128)(2,1)S(1)}, u32[]{:S(2)}, u32[]{:S(2)}) collective-permute-start(bf16[528,512]{1,0:T(8,128)(2,1)S(1)} %collective-permute-done.2.half), channel_id=1, source_target_pairs={{0,16},{16,0},{32,48},{48,32},{64,80},{80,64},{96,112},{112,96},{1... | collective-permute-start | bytes 1622024 | tf_op jit(solution)/shard_map/ppermute | solution.py:219
  59.7 6.3 %collective-permute-start.13 = (bf16[528,512]{1,0:T(8,128)(2,1)S(1)}, bf16[528,512]{1,0:T(8,128)(2,1)S(1)}, u32[]{:S(2)}, u32[]{:S(2)}) collective-permute-start(bf16[528,512]{1,0:T(8,128)(2,1)S(1)} %collective-permute-done.6.other), channel_id=1, source_target_pairs={{0,16},{16,0},{32,48},{48,32},{64,80},{80,64},{96,112},{112,96},{1... | collective-permute-start | bytes 1622024 | tf_op jit(solution)/shard_map/ppermute | solution.py:219

commit v9 on v8

--- a/solution.py
+++ b/solution.py
@@ -236,11 +236,12 @@
     packed, part = prepare(place, occupations, offsets, coupling)
     half = flip(part, 4)
     mixed = mix(place, intersection, mine, pair, cross)
+    mixed, packed = lax.optimization_barrier((mixed, packed))
     near = lax.ppermute(mixed, ("freq", "energy"), near_pairs)
+    far = lax.ppermute(mixed, ("freq", "energy"), far_pairs)
+    c1, c3 = flip(packed, 2), flip(packed, 6)
+    near, mixed = lax.optimization_barrier((near, mixed))
     own, shared = flip(mixed, 1), flip(near, 1)
-    own, mixed, half, packed = lax.optimization_barrier((own, mixed, half, packed))
-    c1, c3 = flip(packed, 2), flip(packed, 6)
-    far = lax.ppermute(mixed, ("freq", "energy"), far_pairs)
     other = lax.ppermute(half, "energy", [(e, e ^ 4) for e in range(count)])
     own, shared, far, packed, half, other = lax.optimization_barrier(
         (own, shared, far, packed, half, other)

time: 95.4 us -> 92.5 us (0.970)
  the two profiles are of different devices: /device:TPU:2 before, /device:TPU:38 now
where the time goes in v9:
time: 92.5 us; the launch traced here: 92.2 us
  waiting for transfers between devices  27.2 us (29%)
  starting transfers between devices  24.1 us (26%)
  blocking collectives  19 us (21%)
  Pallas kernels  18.8 us (20%)
  local copies, waits for them, and re-layouts  3.07 us (3%)
    ppermute x1, waiting for transfers between devices, shards(): near = lax.ppermute(mixed, ('freq', 'energy'), near_pairs)  20.5 us
    all_to_all x1, blocking collectives, shards(): return collect(place, lax.all_to_all(pieces, 'freq', 0, 0))  19 us
    ppermute x10, starting transfers between devices, flip(): return lax.ppermute(x, 'freq', [(d, d ^ bits) for d in range(8)])  15 us
    pallas_call x1, Pallas kernels, sandwich_last(): pl.pallas_call(last_kernel, out_shape=shape((8, 2, ROWS, NO), BF16), in_s...  8.63 us
    ppermute x1, starting transfers between devices, shards(): near = lax.ppermute(mixed, ('freq', 'energy'), near_pairs)  5.85 us
    pallas_call x1, Pallas kernels, sandwich_first(): pl.pallas_call(first_kernel, out_shape=[shape((NO, NO), F32), shape((4, N...  4.49 us
    ppermute x1, waiting for transfers between devices, shards(): other = lax.ppermute(half, 'energy', [(e, e ^ 4) for e in range(count)])  3.67 us
    pallas_call x1, Pallas kernels, prepare(): pl.pallas_call(prepare_kernel, out_shape=[shape((2, *block), BF16), shape...  3.29 us
  transfers between devices with their start and end apart: 14, of which 5 were waited for; matrix products, arithmetic and copies ran while one was open for 1% of the time, Pallas kernels for 9%

profile of v9, /device:TPU:38, one launch (start us, length us, event | category | flops | bytes accessed | tf_op | source)
XLA Modules:
  0.0 92.2 jit_solution(17098253048196504978)
XLA Ops:
  0.0 1.3 %dynamic-slice_bitcast_fusion = (bf16[512,512]{1,0:T(8,128)(2,1)S(1)}, bf16[512,512]{1,0:T(8,128)(2,1)S(1)}) fusion(bf16[2,2,2,512,512]{4,3,2,1,0:T(8,128)(2,1)} %param.6, s32[]{:T(128)S(6)} %select_n.14, s32[]{:T(128)S(6)} %select_n.17, s32[]{:T(128)S(6)} %select_n.16, s32[]{:T(128)S(6)} %select_n.15), kind=kLoop, calls=%fused_computation | loop fusion | bytes 2097168 | tf_op jit(solution)/shard_map/squeeze | solution.py:233
  1.3 0.7 collective-permute-start
  2.0 0.7 stack.27.place
  2.7 3.3 %prepare.1 = (bf16[2,528,512]{2,1,0:T(8,128)(2,1)}, bf16[528,512]{1,0:T(8,128)(2,1)}) custom-call(s32[6]{0:T(128)} %stack.27.place, f32[2]{0:T(128)} %occupations.1, s32[2]{0:T(128)} %offsets.1, bf16[2,512,512]{2,1,0:T(8,128)(2,1)} %coupling.1), custom_call_target="tpu_custom_call" | custom-call | tf_op jit(solution)/shard_map/prepare/pallas_call | solution.py:62
  6.0 3.3 %collective-permute-start.5 = (bf16[528,512]{1,0:T(8,128)(2,1)}, bf16[528,512]{1,0:T(8,128)(2,1)S(1)}, u32[]{:S(2)}, u32[]{:S(2)}) collective-permute-start(bf16[528,512]{1,0:T(8,128)(2,1)} %get-tuple-element.24), channel_id=1, source_target_pairs={{0,64},{16,80},{32,96},{48,112},{64,0},{80,16},{96,32},{112,48},{1... | collective-permute-start | bytes 1622024 | tf_op jit(solution)/shard_map/ppermute | solution.py:219
  9.2 0.0 collective-permute-done.cross
  9.2 0.7 copy-done
  9.9 0.8 mix.1
  10.7 0.5 copy-done.3
  11.2 9.2 %collective-permute-start.7 = (bf16[2,528,512]{2,1,0:T(8,128)(2,1)S(1)}, bf16[2,528,512]{2,1,0:T(8,128)(2,1)S(1)}, u32[]{:S(2)}, u32[]{:S(2)}) collective-permute-start(bf16[2,528,512]{2,1,0:T(8,128)(2,1)S(1)} %copy-done.3), channel_id=1, source_target_pairs={{0,32},{16,48},{32,0},{48,16},{64,96},{80,112},{96,64},{112,80},{1... | collective-permute-start | bytes 3244040 | tf_op jit(solution)/shard_map/ppermute | solution.py:219
  20.3 1.4 %collective-permute-start.8 = (bf16[2,528,512]{2,1,0:T(8,128)(2,1)S(1)}, bf16[2,528,512]{2,1,0:T(8,128)(2,1)S(1)}, u32[]{:S(2)}, u32[]{:S(2)}) collective-permute-start(bf16[2,528,512]{2,1,0:T(8,128)(2,1)S(1)} %copy-done.3), channel_id=1, source_target_pairs={{0,96},{16,112},{32,64},{48,80},{64,32},{80,48},{96,0},{112,16},{1... | collective-permute-start | bytes 3244040 | tf_op jit(solution)/shard_map/ppermute | solution.py:219
  21.8 5.9 %collective-permute-start.1 = (bf16[512,512]{1,0:T(8,128)(2,1)S(1)}, bf16[512,512]{1,0:T(8,128)(2,1)S(1)}, u32[]{:S(2)}, u32[]{:S(2)}) collective-permute-start(bf16[512,512]{1,0:T(8,128)(2,1)S(1)} %mix.1), channel_id=1, source_target_pairs={{1,16},{2,17},{3,18},{4,19},{5,20},{6,21},{7,22},{8,23},{9,24},{10... | collective-permute-start | bytes 1572872 | tf_op jit(solution)/shard_map/ppermute | solution.py:240
  27.6 1.9 %collective-permute-start.4 = (bf16[512,512]{1,0:T(8,128)(2,1)S(1)}, bf16[512,512]{1,0:T(8,128)(2,1)S(1)}, u32[]{:S(2)}, u32[]{:S(2)}) collective-permute-start(bf16[512,512]{1,0:T(8,128)(2,1)S(1)} %mix.1), channel_id=1, source_target_pairs={{0,1},{1,2},{2,3},{3,4},{4,5},{5,6},{6,7},{7,8},{8,9},{9,10},{10,1... | collective-permute-start | bytes 1572872 | tf_op jit(solution)/shard_map/ppermute | solution.py:241
  29.6 0.6 collective-permute-start.6
  30.2 20.5 %collective-permute-done.1.near = bf16[512,512]{1,0:T(8,128)(2,1)S(1)} collective-permute-done((bf16[512,512]{1,0:T(8,128)(2,1)S(1)}, bf16[512,512]{1,0:T(8,128)(2,1)S(1)}, u32[]{:S(2)}, u32[]{:S(2)}) %collective-permute-start.1) | collective-permute-done | bytes 524320 | tf_op jit(solution)/shard_map/ppermute | solution.py:240
  50.7 0.0 collective-permute-start.2
  50.7 1.2 %collective-permute-done.4.far = bf16[512,512]{1,0:T(8,128)(2,1)S(1)} collective-permute-done((bf16[512,512]{1,0:T(8,128)(2,1)S(1)}, bf16[512,512]{1,0:T(8,128)(2,1)S(1)}, u32[]{:S(2)}, u32[]{:S(2)}) %collective-permute-start.4) | collective-permute-done | bytes 524320 | tf_op jit(solution)/shard_map/ppermute | solution.py:241
  52.0 0.0 collective-permute-start.3
  52.0 3.7 %collective-permute-done.6.other = bf16[528,512]{1,0:T(8,128)(2,1)S(1)} collective-permute-done((bf16[528,512]{1,0:T(8,128)(2,1)S(1)}, bf16[528,512]{1,0:T(8,128)(2,1)S(1)}, u32[]{:S(2)}, u32[]{:S(2)}) %collective-permute-start.6) | collective-permute-done | bytes 540704 | tf_op jit(solution)/shard_map/ppermute | solution.py:245
  55.6 0.0 collective-permute-done.2.own
  55.6 0.0 collective-permute-done.3.shared
  55.6 0.1 collective-permute-start.9
  55.7 0.4 collective-permute-start.10
  56.2 0.1 collective-permute-start.11
  56.3 0.4 collective-permute-start.12
  56.7 0.1 collective-permute-start.13
  56.8 4.5 %sandwich_first.1 = (f32[512,512]{1,0:T(8,128)S(1)}, bf16[4,512,512]{2,1,0:T(8,128)(2,1)S(1)}) custom-call(s32[6]{0:T(128)S(1)} %copy-done, bf16[512,512]{1,0:T(8,128)(2,1)S(1)} %collective-permute-done.2.own, bf16[512,512]{1,0:T(8,128)(2,1)S(1)} %collective-permute-done.1.near, bf16[512,512]{1,0:T(8,128)(2,1)S(1)} %collective-permute-done.3.shared, ...), custom_call_target="tpu_custom_call" | custom-call | flops 3221225472 | bytes 8388608 | tf_op jit(solution)/shard_map/sandwich_first/pallas_call | solution.py:162
  61.3 0.9 %collective-permute-done.12.half = bf16[528,512]{1,0:T(8,128)(2,1)S(1)} collective-permute-done((bf16[528,512]{1,0:T(8,128)(2,1)S(1)}, bf16[528,512]{1,0:T(8,128)(2,1)S(1)}, u32[]{:S(2)}, u32[]{:S(2)}) %collective-permute-start.12) | collective-permute-done | bytes 540704 | tf_op jit(solution)/shard_map/ppermute | solution.py:219
  62.2 0.8 collective-permute-done.13.other
  63.0 8.6 %sandwich_last.1 = bf16[8,2,64,512]{3,2,1,0:T(8,128)(2,1)S(1)} custom-call(s32[6]{0:T(128)S(1)} %copy-done, bf16[4,512,512]{2,1,0:T(8,128)(2,1)S(1)} %get-tuple-element.30.green, f32[512,512]{1,0:T(8,128)S(1)} %get-tuple-element.31.start, bf16[2,528,512]{2,1,0:T(8,128)(2,1)S(1)} %copy-done.3, bf16[2,528,512]{2,1,0:T(8,128)(2,1)S(1)} %collective-permute-done.9.s0, ...), custom_call_target="tpu_custom_call" | custom-call | flops 6979321856 | bytes 12058624 | tf_op jit(solution)/shard_map/sandwich_last/pallas_call | solution.py:175
  71.6 19.0 %all_to_all.5.pieces = bf16[8,2,64,512]{3,2,1,0:T(8,128)(2,1)S(1)} all-to-all(bf16[8,2,64,512]{3,2,1,0:T(8,128)(2,1)S(1)} %sandwich_last.1), channel_id=1, replica_groups=mesh['slab'=2,'freq'=8,'energy'=16] {'freq'}, dimensions={0} | all-to-all | bytes 2097152 | tf_op jit(solution)/shard_map/all_to_all | solution.py:253
  90.6 1.6 %collect.1 = f32[2,2,2,64,512]{4,3,2,1,0:T(8,128)} custom-call(s32[6]{0:T(128)S(1)} %copy-done, bf16[8,2,64,512]{3,2,1,0:T(8,128)(2,1)S(1)} %all_to_all.5.pieces), custom_call_target="tpu_custom_call" | custom-call | tf_op jit(solution)/shard_map/collect/pallas_call | solution.py:201
  (12 shorter events, 0.0 us)
Async XLA Ops:
  0.0 9.2 %copy-start.1 = (f32[2]{0:T(128)S(1)}, f32[2]{0:T(128)}, u32[]{:S(2)}) copy-start(f32[2]{0:T(128)} %weight.1) | copy-start | bytes 28
  1.3 8.0 %collective-permute-start = (bf16[512,512]{1,0:T(8,128)(2,1)S(1)}, bf16[512,512]{1,0:T(8,128)(2,1)S(1)}, u32[]{:S(2)}, u32[]{:S(2)}) collective-permute-start(bf16[512,512]{1,0:T(8,128)(2,1)S(1)} %get-tuple-element.34.mine), channel_id=1, source_target_pairs={{32,160},{48,176},{96,224},{112,240},{160,32},{176,48},{224,96},{2... | collective-permute-start | bytes 1572872 | tf_op jit(solution)/shard_map/ppermute | solution.py:235
  6.0 23.6 %collective-permute-start.5 = (bf16[528,512]{1,0:T(8,128)(2,1)}, bf16[528,512]{1,0:T(8,128)(2,1)S(1)}, u32[]{:S(2)}, u32[]{:S(2)}) collective-permute-start(bf16[528,512]{1,0:T(8,128)(2,1)} %get-tuple-element.24), channel_id=1, source_target_pairs={{0,64},{16,80},{32,96},{48,112},{64,0},{80,16},{96,32},{112,48},{1... | collective-permute-start | bytes 1622024 | tf_op jit(solution)/shard_map/ppermute | solution.py:219
  9.2 0.7 copy-start
  9.9 1.2 %copy-start.3 = (bf16[2,528,512]{2,1,0:T(8,128)(2,1)S(1)}, bf16[2,528,512]{2,1,0:T(8,128)(2,1)}, u32[]{:S(2)}) copy-start(bf16[2,528,512]{2,1,0:T(8,128)(2,1)} %get-tuple-element.32.home) | copy-start | bytes 3244036
  11.1 51.8 %copy-start.2 = (bf16[2,2,2,512,512]{4,3,2,1,0:T(8,128)(2,1)S(1)}, bf16[2,2,2,512,512]{4,3,2,1,0:T(8,128)(2,1)}, u32[]{:S(2)}) copy-start(bf16[2,2,2,512,512]{4,3,2,1,0:T(8,128)(2,1)} %retarded.1) | copy-start | bytes 12582916
  11.2 44.6 %collective-permute-start.7 = (bf16[2,528,512]{2,1,0:T(8,128)(2,1)S(1)}, bf16[2,528,512]{2,1,0:T(8,128)(2,1)S(1)}, u32[]{:S(2)}, u32[]{:S(2)}) collective-permute-start(bf16[2,528,512]{2,1,0:T(8,128)(2,1)S(1)} %copy-done.3), channel_id=1, source_target_pairs={{0,32},{16,48},{32,0},{48,16},{64,96},{80,112},{96,64},{112,80},{1... | collective-permute-start | bytes 3244040 | tf_op jit(solution)/shard_map/ppermute | solution.py:219
  20.3 35.8 %collective-permute-start.8 = (bf16[2,528,512]{2,1,0:T(8,128)(2,1)S(1)}, bf16[2,528,512]{2,1,0:T(8,128)(2,1)S(1)}, u32[]{:S(2)}, u32[]{:S(2)}) collective-permute-start(bf16[2,528,512]{2,1,0:T(8,128)(2,1)S(1)} %copy-done.3), channel_id=1, source_target_pairs={{0,96},{16,112},{32,64},{48,80},{64,32},{80,48},{96,0},{112,16},{1... | collective-permute-start | bytes 3244040 | tf_op jit(solution)/shard_map/ppermute | solution.py:219
  21.8 28.9 %collective-permute-start.1 = (bf16[512,512]{1,0:T(8,128)(2,1)S(1)}, bf16[512,512]{1,0:T(8,128)(2,1)S(1)}, u32[]{:S(2)}, u32[]{:S(2)}) collective-permute-start(bf16[512,512]{1,0:T(8,128)(2,1)S(1)} %mix.1), channel_id=1, source_target_pairs={{1,16},{2,17},{3,18},{4,19},{5,20},{6,21},{7,22},{8,23},{9,24},{10... | collective-permute-start | bytes 1572872 | tf_op jit(solution)/shard_map/ppermute | solution.py:240
  27.6 24.3 %collective-permute-start.4 = (bf16[512,512]{1,0:T(8,128)(2,1)S(1)}, bf16[512,512]{1,0:T(8,128)(2,1)S(1)}, u32[]{:S(2)}, u32[]{:S(2)}) collective-permute-start(bf16[512,512]{1,0:T(8,128)(2,1)S(1)} %mix.1), channel_id=1, source_target_pairs={{0,1},{1,2},{2,3},{3,4},{4,5},{5,6},{6,7},{7,8},{8,9},{9,10},{10,1... | collective-permute-start | bytes 1572872 | tf_op jit(solution)/shard_map/ppermute | solution.py:241
  29.6 26.1 %collective-permute-start.6 = (bf16[528,512]{1,0:T(8,128)(2,1)S(1)}, bf16[528,512]{1,0:T(8,128)(2,1)S(1)}, u32[]{:S(2)}, u32[]{:S(2)}) collective-permute-start(bf16[528,512]{1,0:T(8,128)(2,1)S(1)} %collective-permute-done.5.half), channel_id=1, source_target_pairs={{0,4},{1,5},{2,6},{3,7},{4,0},{5,1},{6,2},{7,3},{8,12},{9,13},{10,... | collective-permute-start | bytes 1622024 | tf_op jit(solution)/shard_map/ppermute | solution.py:245
  50.7 4.9 %collective-permute-start.2 = (bf16[512,512]{1,0:T(8,128)(2,1)S(1)}, bf16[512,512]{1,0:T(8,128)(2,1)S(1)}, u32[]{:S(2)}, u32[]{:S(2)}) collective-permute-start(bf16[512,512]{1,0:T(8,128)(2,1)S(1)} %mix.1), channel_id=1, source_target_pairs={{0,16},{16,0},{32,48},{48,32},{64,80},{80,64},{96,112},{112,96},{1... | collective-permute-start | bytes 1572872 | tf_op jit(solution)/shard_map/ppermute | solution.py:219
  52.0 3.7 %collective-permute-start.3 = (bf16[512,512]{1,0:T(8,128)(2,1)S(1)}, bf16[512,512]{1,0:T(8,128)(2,1)S(1)}, u32[]{:S(2)}, u32[]{:S(2)}) collective-permute-start(bf16[512,512]{1,0:T(8,128)(2,1)S(1)} %collective-permute-done.1.near), channel_id=1, source_target_pairs={{0,16},{16,0},{32,48},{48,32},{64,80},{80,64},{96,112},{112,96},{1... | collective-permute-start | bytes 1572872 | tf_op jit(solution)/shard_map/ppermute | solution.py:219
  55.6 7.4 %collective-permute-start.9 = (bf16[2,528,512]{2,1,0:T(8,128)(2,1)S(1)}, bf16[2,528,512]{2,1,0:T(8,128)(2,1)S(1)}, u32[]{:S(2)}, u32[]{:S(2)}) collective-permute-start(bf16[2,528,512]{2,1,0:T(8,128)(2,1)S(1)} %copy-done.3), channel_id=1, source_target_pairs={{0,16},{16,0},{32,48},{48,32},{64,80},{80,64},{96,112},{112,96},{1... | collective-permute-start | bytes 3244040 | tf_op jit(solution)/shard_map/ppermute | solution.py:219
  55.7 7.2 %collective-permute-start.10 = (bf16[2,528,512]{2,1,0:T(8,128)(2,1)S(1)}, bf16[2,528,512]{2,1,0:T(8,128)(2,1)S(1)}, u32[]{:S(2)}, u32[]{:S(2)}) collective-permute-start(bf16[2,528,512]{2,1,0:T(8,128)(2,1)S(1)} %collective-permute-done.7.c1), channel_id=1, source_target_pairs={{0,16},{16,0},{32,48},{48,32},{64,80},{80,64},{96,112},{112,96},{1... | collective-permute-start | bytes 3244040 | tf_op jit(solution)/shard_map/ppermute | solution.py:219
  56.2 6.8 %collective-permute-start.11 = (bf16[2,528,512]{2,1,0:T(8,128)(2,1)S(1)}, bf16[2,528,512]{2,1,0:T(8,128)(2,1)S(1)}, u32[]{:S(2)}, u32[]{:S(2)}) collective-permute-start(bf16[2,528,512]{2,1,0:T(8,128)(2,1)S(1)} %collective-permute-done.8.c3), channel_id=1, source_target_pairs={{0,16},{16,0},{32,48},{48,32},{64,80},{80,64},{96,112},{112,96},{1... | collective-permute-start | bytes 3244040 | tf_op jit(solution)/shard_map/ppermute | solution.py:219
  56.3 5.9 %collective-permute-start.12 = (bf16[528,512]{1,0:T(8,128)(2,1)S(1)}, bf16[528,512]{1,0:T(8,128)(2,1)S(1)}, u32[]{:S(2)}, u32[]{:S(2)}) collective-permute-start(bf16[528,512]{1,0:T(8,128)(2,1)S(1)} %collective-permute-done.5.half), channel_id=1, source_target_pairs={{0,16},{16,0},{32,48},{48,32},{64,80},{80,64},{96,112},{112,96},{1... | collective-permute-start | bytes 1622024 | tf_op jit(solution)/shard_map/ppermute | solution.py:219
  56.7 6.3 %collective-permute-start.13 = (bf16[528,512]{1,0:T(8,128)(2,1)S(1)}, bf16[528,512]{1,0:T(8,128)(2,1)S(1)}, u32[]{:S(2)}, u32[]{:S(2)}) collective-permute-start(bf16[528,512]{1,0:T(8,128)(2,1)S(1)} %collective-permute-done.6.other), channel_id=1, source_target_pairs={{0,16},{16,0},{32,48},{48,32},{64,80},{80,64},{96,112},{112,96},{1... | collective-permute-start | bytes 1622024 | tf_op jit(solution)/shard_map/ppermute | solution.py:219

commit v10 on v9

--- a/solution.py
+++ b/solution.py
@@ -70,20 +70,22 @@
     )(place, occupations, offsets, coupling)
 
 
-def mix_kernel(place, weight, mine, pair, cross, out):
-    beside = pair[...].astype(F32) + cross[...].astype(F32)
-    out[...] = (mine[...].astype(F32) + weight[place[2]] * beside).astype(BF16)
-
-
-def mix(place, weight, mine, pair, cross):
+def mix_kernel(place, weight, mine, pair, top, bottom, out):
+    for cross, first in ((top, 0), (bottom, NO // 2)):
+        rows = pl.ds(first, NO // 2)
+        beside = pair[rows].astype(F32) + cross[...].astype(F32)
+        out[rows] = (mine[rows].astype(F32) + weight[place[2]] * beside).astype(BF16)
+
+
+def mix(place, weight, mine, pair, top, bottom):
     return pl.pallas_call(
         mix_kernel,
         out_shape=shape((NO, NO), BF16),
-        in_specs=[SMEM] * 2 + [VMEM] * 3,
+        in_specs=[SMEM] * 2 + [VMEM] * 4,
         out_specs=VMEM,
         compiler_params=PARAMS,
         name="mix",
-    )(place, weight, mine, pair, cross)
+    )(place, weight, mine, pair, top, bottom)
 
 
 def add_terms(k, green, todo):
@@ -114,7 +116,7 @@
     return todo
 
 
-def first_kernel(place, own, near, shared, far, c1, c3, half, other, out, green, gsem):
+def first_kernel(place, own, near, shared, far, home, c1, c3, half, other, out, green, gsem):
     copies = [
         pltpu.make_async_copy(src, green.at[n], gsem.at[n])
         for n, src in enumerate((own, near, shared, far))
@@ -123,18 +125,18 @@
         copy.start()
     for copy in copies:
         copy.wait()
-    todo = blocks_of((c1, c3, half, other))
+    todo = blocks_of((home, c1, c3, half, other))
     for n, term in enumerate(add_terms(place[1], green, todo)):
         out[...] = term if n == 0 else out[...] + term
 
 
 def last_kernel(
-    place, green, start, home, s0, s1, s3, half, other, retarded, out, whole, acc, rsem
+    place, green, start, s0, s1, s3, half, other, retarded, out, whole, acc, rsem
 ):
     k, sl, c = place[1], place[2], place[4]
     copy = pltpu.make_async_copy(retarded.at[k, sl], whole, rsem.at[0])
     copy.start()
-    todo = blocks_of((home, s0, s1, s3, half, other))
+    todo = blocks_of((s0, s1, s3, half, other))
     for n, term in enumerate(add_terms(k, green, todo)):
         acc[...] = (start if n == 0 else acc)[...] + term
     combined = acc[...].astype(BF16)
@@ -162,11 +164,11 @@
     return pl.pallas_call(
         first_kernel,
         out_shape=[shape((NO, NO), F32), shape((4, NO, NO), BF16)],
-        in_specs=[SMEM] + [VMEM] * 8,
+        in_specs=[SMEM] + [VMEM] * 9,
         out_specs=[VMEM] * 2,
         scratch_shapes=[pltpu.SemaphoreType.DMA((4,))],
         compiler_params=PARAMS,
-        cost_estimate=cost(6),
+        cost_estimate=cost(8),
         name="sandwich_first",
     )(place, *greens, *arrays)
 
@@ -175,7 +177,7 @@
     return pl.pallas_call(
         last_kernel,
         out_shape=shape((8, 2, ROWS, NO), BF16),
-        in_specs=[SMEM] + [VMEM] * 8 + [HBM],
+        in_specs=[SMEM] + [VMEM] * 7 + [HBM],
         out_specs=VMEM,
         scratch_shapes=[
             pltpu.VMEM((2, NO, NO), BF16),
@@ -183,7 +185,7 @@
             pltpu.SemaphoreType.DMA((1,)),
         ],
         compiler_params=PARAMS,
-        cost_estimate=cost(13),
+        cost_estimate=cost(11),
         name="sandwich_last",
     )(place, green, start, *arrays, retarded)
 
@@ -231,11 +233,15 @@
 
     sl, c = (y & 1) ^ b, y >> 1
     mine, pair = lesser[k, sl, c], lesser[k, 1 - sl, c]
-    edge = [(s * 8 + d, (1 - s) * 8 + d) for s in range(2) for d in range(8) if (d // 2) % 2]
-    cross = lax.ppermute(mine, ("slab", "freq"), edge)
+    odd = [d for d in range(8) if d & 2]
+    upper = [(s * 8 + d, (1 - s) * 8 + d) for s in range(2) for d in odd]
+    lower = [(s * 8 + (d ^ 2), (1 - s) * 8 + d) for s in range(2) for d in odd]
+    rim = lesser[k, 1 - b, c]
+    top = lax.ppermute(rim[: NO // 2], ("slab", "freq"), upper)
+    bottom = lax.ppermute(rim[NO // 2 :], ("slab", "freq"), lower)
     packed, part = prepare(place, occupations, offsets, coupling)
     half = flip(part, 4)
-    mixed = mix(place, intersection, mine, pair, cross)
+    mixed = mix(place, intersection, mine, pair, top, bottom)
     mixed, packed = lax.optimization_barrier((mixed, packed))
     near = lax.ppermute(mixed, ("freq", "energy"), near_pairs)
     far = lax.ppermute(mixed, ("freq", "energy"), far_pairs)
@@ -248,8 +254,8 @@
     )
     swapped = [flip(x, 1) for x in (packed, c1, c3, half, other)]
 
-    first, green = sandwich_first(place, [own, near, shared, far], [c1, c3, half, other])
-    pieces = sandwich_last(place, green, first, [packed, *swapped], retarded)
+    first, green = sandwich_first(place, [own, near, shared, far], [packed, c1, c3, half, other])
+    pieces = sandwich_last(place, green, first, swapped, retarded)
     return collect(place, lax.all_to_all(pieces, "freq", 0, 0))
 
 

time: 92.5 us -> 89.1 us (0.963)
  starting transfers between devices: 24.1 us -> 20.5 us
  blocking collectives: 19 us -> 20.3 us
  waiting for transfers between devices: 27.2 us -> 25.9 us
    ppermute x10, starting transfers between devices: 15 us -> 5.3 us  [flip(): return lax.ppermute(x, 'freq', [(d, d ^ bits) for d in range(8)])]
    ppermute x1 -> x2, starting transfers between devices: 0.69 us -> 6.87 us  [the longest x1 6.19 us: shards(): bottom = lax.ppermute(rim[NO // 2:], ('slab', 'freq'), lower)]
    ppermute x1, waiting for transfers between devices: 20.5 us -> 17.8 us  [shards(): near = lax.ppermute(mixed, ('freq', 'energy'), near_pairs)]
    ppermute x10, waiting for transfers between devices: 1.73 us -> 3.45 us  [flip(): return lax.ppermute(x, 'freq', [(d, d ^ bits) for d in range(8)])]
    all_to_all x1, blocking collectives: 19 us -> 20.3 us  [shards(): return collect(place, lax.all_to_all(pieces, 'freq', 0, 0))]
    pallas_call x1, Pallas kernels: 8.63 us -> 7.37 us  [sandwich_last(): pl.pallas_call(last_kernel, out_shape=shape((8, 2, ROWS, NO), BF16), in_s...]
    slice x0 -> x1, local copies, waits for them, and re-layouts: none -> 1.06 us  [shards(): bottom = lax.ppermute(rim[NO // 2:], ('slab', 'freq'), lower)]
    pallas_call x1, Pallas kernels: 4.49 us -> 5.53 us  [sandwich_first(): pl.pallas_call(first_kernel, out_shape=[shape((NO, NO), F32), shape((4, N...]
  transfers between devices with their start and end apart: 14 -> 15, of which waited for: 5 -> 5; matrix products, arithmetic and copies ran while one was open for 1% -> 2% of each run, Pallas kernels for 9% -> 11%
where the time goes in v10:
time: 89.1 us; the launch traced here: 88.8 us
  waiting for transfers between devices  25.9 us (29%)
  starting transfers between devices  20.5 us (23%)
  blocking collectives  20.3 us (23%)
  Pallas kernels  18.6 us (21%)
  local copies, waits for them, and re-layouts  3.36 us (4%)
    all_to_all x1, blocking collectives, shards(): return collect(place, lax.all_to_all(pieces, 'freq', 0, 0))  20.3 us
    ppermute x1, waiting for transfers between devices, shards(): near = lax.ppermute(mixed, ('freq', 'energy'), near_pairs)  17.8 us
    pallas_call x1, Pallas kernels, sandwich_last(): pl.pallas_call(last_kernel, out_shape=shape((8, 2, ROWS, NO), BF16), in_s...  7.37 us
    ppermute x1, starting transfers between devices, shards(): bottom = lax.ppermute(rim[NO // 2:], ('slab', 'freq'), lower)  6.19 us
    ppermute x1, starting transfers between devices, shards(): near = lax.ppermute(mixed, ('freq', 'energy'), near_pairs)  5.66 us
    pallas_call x1, Pallas kernels, sandwich_first(): pl.pallas_call(first_kernel, out_shape=[shape((NO, NO), F32), shape((4, N...  5.53 us
    ppermute x10, starting transfers between devices, flip(): return lax.ppermute(x, 'freq', [(d, d ^ bits) for d in range(8)])  5.3 us
    ppermute x10, waiting for transfers between devices, flip(): return lax.ppermute(x, 'freq', [(d, d ^ bits) for d in range(8)])  3.45 us
  transfers between devices with their start and end apart: 15, of which 5 were waited for; matrix products, arithmetic and copies ran while one was open for 2% of the time, Pallas kernels for 11%

profile of v10, /device:TPU:38, one launch (start us, length us, event | category | flops | bytes accessed | tf_op | source)
XLA Modules:
  0.0 88.8 jit_solution(9413938883655726036)
XLA Ops:
  0.0 1.1 %dynamic-slice_bitcast_fusion.2 = (bf16[256,512]{1,0:T(8,128)(2,1)S(1)}, bf16[256,512]{1,0:T(8,128)(2,1)S(1)}) fusion(bf16[2,2,2,512,512]{4,3,2,1,0:T(8,128)(2,1)} %param.6, s32[]{:T(128)S(6)} %select_n.19, s32[]{:T(128)S(6)} %select_n.23, s32[]{:T(128)S(6)} %select_n.21, s32[]{:T(128)S(6)} %add.26), kind=kLoop, calls=%fused_computation.2 | loop fusion | bytes 1048592 | tf_op jit(solution)/shard_map/slice | solution.py:241
  1.1 0.7 collective-permute-start
  1.8 6.2 %collective-permute-start.1 = (bf16[256,512]{1,0:T(8,128)(2,1)S(1)}, bf16[256,512]{1,0:T(8,128)(2,1)S(1)}, u32[]{:S(2)}, u32[]{:S(2)}) collective-permute-start(bf16[256,512]{1,0:T(8,128)(2,1)S(1)} %get-tuple-element.33), channel_id=1, source_target_pairs={{0,160},{16,176},{64,224},{80,240},{128,32},{144,48},{192,96},{208... | collective-permute-start | bytes 786440 | tf_op jit(solution)/shard_map/ppermute | solution.py:241
  8.0 0.6 stack.27.place
  8.6 3.3 %prepare.1 = (bf16[2,528,512]{2,1,0:T(8,128)(2,1)}, bf16[528,512]{1,0:T(8,128)(2,1)}) custom-call(s32[6]{0:T(128)} %stack.27.place, f32[2]{0:T(128)} %occupations.1, s32[2]{0:T(128)} %offsets.1, bf16[2,512,512]{2,1,0:T(8,128)(2,1)} %coupling.1), custom_call_target="tpu_custom_call" | custom-call | tf_op jit(solution)/shard_map/prepare/pallas_call | solution.py:62
  11.9 0.0 copy-start.1
  11.9 3.0 %collective-permute-start.6 = (bf16[528,512]{1,0:T(8,128)(2,1)}, bf16[528,512]{1,0:T(8,128)(2,1)S(1)}, u32[]{:S(2)}, u32[]{:S(2)}) collective-permute-start(bf16[528,512]{1,0:T(8,128)(2,1)} %get-tuple-element.24), channel_id=1, source_target_pairs={{0,64},{16,80},{32,96},{48,112},{64,0},{80,16},{96,32},{112,48},{1... | collective-permute-start | bytes 1622024 | tf_op jit(solution)/shard_map/ppermute | solution.py:221
  14.9 1.3 %dynamic-slice_bitcast_fusion = (bf16[512,512]{1,0:T(8,128)(2,1)S(1)}, bf16[512,512]{1,0:T(8,128)(2,1)S(1)}) fusion(bf16[2,2,2,512,512]{4,3,2,1,0:T(8,128)(2,1)} %param.6, s32[]{:T(128)S(6)} %select_n.19, s32[]{:T(128)S(6)} %select_n.22, s32[]{:T(128)S(6)} %select_n.21, s32[]{:T(128)S(6)} %select_n.20), kind=kLoop, calls=%fused_computation | loop fusion | bytes 2097168 | tf_op jit(solution)/shard_map/squeeze | solution.py:235
  16.2 0.0 collective-permute-done.top
  16.2 0.8 mix.1
  17.0 0.4 copy-done.3
  17.4 0.0 collective-permute-start.8
  17.4 1.2 %collective-permute-start.9 = (bf16[2,528,512]{2,1,0:T(8,128)(2,1)S(1)}, bf16[2,528,512]{2,1,0:T(8,128)(2,1)S(1)}, u32[]{:S(2)}, u32[]{:S(2)}) collective-permute-start(bf16[2,528,512]{2,1,0:T(8,128)(2,1)S(1)} %copy-done.3), channel_id=1, source_target_pairs={{0,96},{16,112},{32,64},{48,80},{64,32},{80,48},{96,0},{112,16},{1... | collective-permute-start | bytes 3244040 | tf_op jit(solution)/shard_map/ppermute | solution.py:221
  18.6 5.7 %collective-permute-start.2 = (bf16[512,512]{1,0:T(8,128)(2,1)S(1)}, bf16[512,512]{1,0:T(8,128)(2,1)S(1)}, u32[]{:S(2)}, u32[]{:S(2)}) collective-permute-start(bf16[512,512]{1,0:T(8,128)(2,1)S(1)} %mix.1), channel_id=1, source_target_pairs={{1,16},{2,17},{3,18},{4,19},{5,20},{6,21},{7,22},{8,23},{9,24},{10... | collective-permute-start | bytes 1572872 | tf_op jit(solution)/shard_map/ppermute | solution.py:246
  24.3 1.9 %collective-permute-start.5 = (bf16[512,512]{1,0:T(8,128)(2,1)S(1)}, bf16[512,512]{1,0:T(8,128)(2,1)S(1)}, u32[]{:S(2)}, u32[]{:S(2)}) collective-permute-start(bf16[512,512]{1,0:T(8,128)(2,1)S(1)} %mix.1), channel_id=1, source_target_pairs={{0,1},{1,2},{2,3},{3,4},{4,5},{5,6},{6,7},{7,8},{8,9},{9,10},{10,1... | collective-permute-start | bytes 1572872 | tf_op jit(solution)/shard_map/ppermute | solution.py:247
  26.2 2.8 %collective-permute-done.6.half = bf16[528,512]{1,0:T(8,128)(2,1)S(1)} collective-permute-done((bf16[528,512]{1,0:T(8,128)(2,1)}, bf16[528,512]{1,0:T(8,128)(2,1)S(1)}, u32[]{:S(2)}, u32[]{:S(2)}) %collective-permute-start.6) | collective-permute-done | bytes 540704 | tf_op jit(solution)/shard_map/ppermute | solution.py:221
  29.0 0.8 collective-permute-start.7
  29.7 17.8 %collective-permute-done.2.near = bf16[512,512]{1,0:T(8,128)(2,1)S(1)} collective-permute-done((bf16[512,512]{1,0:T(8,128)(2,1)S(1)}, bf16[512,512]{1,0:T(8,128)(2,1)S(1)}, u32[]{:S(2)}, u32[]{:S(2)}) %collective-permute-start.2) | collective-permute-done | bytes 524320 | tf_op jit(solution)/shard_map/ppermute | solution.py:246
  47.5 0.0 collective-permute-start.3
  47.5 1.7 %collective-permute-done.5.far = bf16[512,512]{1,0:T(8,128)(2,1)S(1)} collective-permute-done((bf16[512,512]{1,0:T(8,128)(2,1)S(1)}, bf16[512,512]{1,0:T(8,128)(2,1)S(1)}, u32[]{:S(2)}, u32[]{:S(2)}) %collective-permute-start.5) | collective-permute-done | bytes 524320 | tf_op jit(solution)/shard_map/ppermute | solution.py:247
  49.2 0.0 collective-permute-start.4
  49.2 2.9 %collective-permute-done.7.other = bf16[528,512]{1,0:T(8,128)(2,1)S(1)} collective-permute-done((bf16[528,512]{1,0:T(8,128)(2,1)S(1)}, bf16[528,512]{1,0:T(8,128)(2,1)S(1)}, u32[]{:S(2)}, u32[]{:S(2)}) %collective-permute-start.7) | collective-permute-done | bytes 540704 | tf_op jit(solution)/shard_map/ppermute | solution.py:251
  52.1 0.0 collective-permute-done.3.own
  52.1 0.5 collective-permute-start.11
  52.6 0.1 collective-permute-start.12
  52.8 0.4 collective-permute-start.13
  53.2 0.1 collective-permute-start.14
  53.3 5.5 %sandwich_first.1 = (f32[512,512]{1,0:T(8,128)S(1)}, bf16[4,512,512]{2,1,0:T(8,128)(2,1)S(1)}) custom-call(s32[6]{0:T(128)S(1)} %copy-done, bf16[512,512]{1,0:T(8,128)(2,1)S(1)} %collective-permute-done.3.own, bf16[512,512]{1,0:T(8,128)(2,1)S(1)} %collective-permute-done.2.near, bf16[512,512]{1,0:T(8,128)(2,1)S(1)} %collective-permute-done.4.shared, ...), custom_call_target="tpu_custom_call" | custom-call | flops 4294967296 | bytes 9437184 | tf_op jit(solution)/shard_map/sandwich_first/pallas_call | solution.py:164
  58.8 0.7 collective-permute-done.14.other
  59.5 7.4 %sandwich_last.1 = bf16[8,2,64,512]{3,2,1,0:T(8,128)(2,1)S(1)} custom-call(s32[6]{0:T(128)S(1)} %copy-done, bf16[4,512,512]{2,1,0:T(8,128)(2,1)S(1)} %get-tuple-element.31.green, f32[512,512]{1,0:T(8,128)S(1)} %get-tuple-element.32.start, bf16[2,528,512]{2,1,0:T(8,128)(2,1)S(1)} %collective-permute-done.10.s0, ...), custom_call_target="tpu_custom_call" | custom-call | flops 5905580032 | bytes 11010048 | tf_op jit(solution)/shard_map/sandwich_last/pallas_call | solution.py:177
  66.9 20.3 %all_to_all.5.pieces = bf16[8,2,64,512]{3,2,1,0:T(8,128)(2,1)S(1)} all-to-all(bf16[8,2,64,512]{3,2,1,0:T(8,128)(2,1)S(1)} %sandwich_last.1), channel_id=1, replica_groups=mesh['slab'=2,'freq'=8,'energy'=16] {'freq'}, dimensions={0} | all-to-all | bytes 2097152 | tf_op jit(solution)/shard_map/all_to_all | solution.py:259
  87.2 1.6 %collect.1 = f32[2,2,2,64,512]{4,3,2,1,0:T(8,128)} custom-call(s32[6]{0:T(128)S(1)} %copy-done, bf16[8,2,64,512]{3,2,1,0:T(8,128)(2,1)S(1)} %all_to_all.5.pieces), custom_call_target="tpu_custom_call" | custom-call | tf_op jit(solution)/shard_map/collect/pallas_call | solution.py:203
  (15 shorter events, 0.0 us)
Async XLA Ops:
  1.1 15.1 %collective-permute-start = (bf16[256,512]{1,0:T(8,128)(2,1)S(1)}, bf16[256,512]{1,0:T(8,128)(2,1)S(1)}, u32[]{:S(2)}, u32[]{:S(2)}) collective-permute-start(bf16[256,512]{1,0:T(8,128)(2,1)S(1)} %get-tuple-element.34), channel_id=1, source_target_pairs={{32,160},{48,176},{96,224},{112,240},{160,32},{176,48},{224,96},{2... | collective-permute-start | bytes 786440 | tf_op jit(solution)/shard_map/ppermute | solution.py:240
  1.8 14.4 %collective-permute-start.1 = (bf16[256,512]{1,0:T(8,128)(2,1)S(1)}, bf16[256,512]{1,0:T(8,128)(2,1)S(1)}, u32[]{:S(2)}, u32[]{:S(2)}) collective-permute-start(bf16[256,512]{1,0:T(8,128)(2,1)S(1)} %get-tuple-element.33), channel_id=1, source_target_pairs={{0,160},{16,176},{64,224},{80,240},{128,32},{144,48},{192,96},{208... | collective-permute-start | bytes 786440 | tf_op jit(solution)/shard_map/ppermute | solution.py:241
  11.9 4.3 %copy-start = (s32[6]{0:T(128)S(1)}, s32[6]{0:T(128)}, u32[]{:S(2)}) copy-start(s32[6]{0:T(128)} %stack.27.place) | copy-start | bytes 76
  11.9 4.3 %copy-start.1 = (f32[2]{0:T(128)S(1)}, f32[2]{0:T(128)}, u32[]{:S(2)}) copy-start(f32[2]{0:T(128)} %weight.1) | copy-start | bytes 28
  11.9 17.1 %collective-permute-start.6 = (bf16[528,512]{1,0:T(8,128)(2,1)}, bf16[528,512]{1,0:T(8,128)(2,1)S(1)}, u32[]{:S(2)}, u32[]{:S(2)}) collective-permute-start(bf16[528,512]{1,0:T(8,128)(2,1)} %get-tuple-element.24), channel_id=1, source_target_pairs={{0,64},{16,80},{32,96},{48,112},{64,0},{80,16},{96,32},{112,48},{1... | collective-permute-start | bytes 1622024 | tf_op jit(solution)/shard_map/ppermute | solution.py:221
  16.2 1.2 %copy-start.3 = (bf16[2,528,512]{2,1,0:T(8,128)(2,1)S(1)}, bf16[2,528,512]{2,1,0:T(8,128)(2,1)}, u32[]{:S(2)}) copy-start(bf16[2,528,512]{2,1,0:T(8,128)(2,1)} %get-tuple-element.28.home) | copy-start | bytes 3244036
  17.4 42.1 %copy-start.2 = (bf16[2,2,2,512,512]{4,3,2,1,0:T(8,128)(2,1)S(1)}, bf16[2,2,2,512,512]{4,3,2,1,0:T(8,128)(2,1)}, u32[]{:S(2)}) copy-start(bf16[2,2,2,512,512]{4,3,2,1,0:T(8,128)(2,1)} %retarded.1) | copy-start | bytes 12582916
  17.4 34.7 %collective-permute-start.8 = (bf16[2,528,512]{2,1,0:T(8,128)(2,1)S(1)}, bf16[2,528,512]{2,1,0:T(8,128)(2,1)S(1)}, u32[]{:S(2)}, u32[]{:S(2)}) collective-permute-start(bf16[2,528,512]{2,1,0:T(8,128)(2,1)S(1)} %copy-done.3), channel_id=1, source_target_pairs={{0,32},{16,48},{32,0},{48,16},{64,96},{80,112},{96,64},{112,80},{1... | collective-permute-start | bytes 3244040 | tf_op jit(solution)/shard_map/ppermute | solution.py:221
  17.4 35.2 %collective-permute-start.9 = (bf16[2,528,512]{2,1,0:T(8,128)(2,1)S(1)}, bf16[2,528,512]{2,1,0:T(8,128)(2,1)S(1)}, u32[]{:S(2)}, u32[]{:S(2)}) collective-permute-start(bf16[2,528,512]{2,1,0:T(8,128)(2,1)S(1)} %copy-done.3), channel_id=1, source_target_pairs={{0,96},{16,112},{32,64},{48,80},{64,32},{80,48},{96,0},{112,16},{1... | collective-permute-start | bytes 3244040 | tf_op jit(solution)/shard_map/ppermute | solution.py:221
  18.6 28.9 %collective-permute-start.2 = (bf16[512,512]{1,0:T(8,128)(2,1)S(1)}, bf16[512,512]{1,0:T(8,128)(2,1)S(1)}, u32[]{:S(2)}, u32[]{:S(2)}) collective-permute-start(bf16[512,512]{1,0:T(8,128)(2,1)S(1)} %mix.1), channel_id=1, source_target_pairs={{1,16},{2,17},{3,18},{4,19},{5,20},{6,21},{7,22},{8,23},{9,24},{10... | collective-permute-start | bytes 1572872 | tf_op jit(solution)/shard_map/ppermute | solution.py:246
  24.3 24.9 %collective-permute-start.5 = (bf16[512,512]{1,0:T(8,128)(2,1)S(1)}, bf16[512,512]{1,0:T(8,128)(2,1)S(1)}, u32[]{:S(2)}, u32[]{:S(2)}) collective-permute-start(bf16[512,512]{1,0:T(8,128)(2,1)S(1)} %mix.1), channel_id=1, source_target_pairs={{0,1},{1,2},{2,3},{3,4},{4,5},{5,6},{6,7},{7,8},{8,9},{9,10},{10,1... | collective-permute-start | bytes 1572872 | tf_op jit(solution)/shard_map/ppermute | solution.py:247
  29.0 23.2 %collective-permute-start.7 = (bf16[528,512]{1,0:T(8,128)(2,1)S(1)}, bf16[528,512]{1,0:T(8,128)(2,1)S(1)}, u32[]{:S(2)}, u32[]{:S(2)}) collective-permute-start(bf16[528,512]{1,0:T(8,128)(2,1)S(1)} %collective-permute-done.6.half), channel_id=1, source_target_pairs={{0,4},{1,5},{2,6},{3,7},{4,0},{5,1},{6,2},{7,3},{8,12},{9,13},{10,... | collective-permute-start | bytes 1622024 | tf_op jit(solution)/shard_map/ppermute | solution.py:251
  47.5 4.6 %collective-permute-start.3 = (bf16[512,512]{1,0:T(8,128)(2,1)S(1)}, bf16[512,512]{1,0:T(8,128)(2,1)S(1)}, u32[]{:S(2)}, u32[]{:S(2)}) collective-permute-start(bf16[512,512]{1,0:T(8,128)(2,1)S(1)} %mix.1), channel_id=1, source_target_pairs={{0,16},{16,0},{32,48},{48,32},{64,80},{80,64},{96,112},{112,96},{1... | collective-permute-start | bytes 1572872 | tf_op jit(solution)/shard_map/ppermute | solution.py:221
  49.2 2.9 %collective-permute-start.4 = (bf16[512,512]{1,0:T(8,128)(2,1)S(1)}, bf16[512,512]{1,0:T(8,128)(2,1)S(1)}, u32[]{:S(2)}, u32[]{:S(2)}) collective-permute-start(bf16[512,512]{1,0:T(8,128)(2,1)S(1)} %collective-permute-done.2.near), channel_id=1, source_target_pairs={{0,16},{16,0},{32,48},{48,32},{64,80},{80,64},{96,112},{112,96},{1... | collective-permute-start | bytes 1572872 | tf_op jit(solution)/shard_map/ppermute | solution.py:221
  52.1 7.4 %collective-permute-start.10 = (bf16[2,528,512]{2,1,0:T(8,128)(2,1)S(1)}, bf16[2,528,512]{2,1,0:T(8,128)(2,1)S(1)}, u32[]{:S(2)}, u32[]{:S(2)}) collective-permute-start(bf16[2,528,512]{2,1,0:T(8,128)(2,1)S(1)} %copy-done.3), channel_id=1, source_target_pairs={{0,16},{16,0},{32,48},{48,32},{64,80},{80,64},{96,112},{112,96},{1... | collective-permute-start | bytes 3244040 | tf_op jit(solution)/shard_map/ppermute | solution.py:221
  52.1 7.3 %collective-permute-start.11 = (bf16[2,528,512]{2,1,0:T(8,128)(2,1)S(1)}, bf16[2,528,512]{2,1,0:T(8,128)(2,1)S(1)}, u32[]{:S(2)}, u32[]{:S(2)}) collective-permute-start(bf16[2,528,512]{2,1,0:T(8,128)(2,1)S(1)} %collective-permute-done.8.c1), channel_id=1, source_target_pairs={{0,16},{16,0},{32,48},{48,32},{64,80},{80,64},{96,112},{112,96},{1... | collective-permute-start | bytes 3244040 | tf_op jit(solution)/shard_map/ppermute | solution.py:221
  52.6 6.8 %collective-permute-start.12 = (bf16[2,528,512]{2,1,0:T(8,128)(2,1)S(1)}, bf16[2,528,512]{2,1,0:T(8,128)(2,1)S(1)}, u32[]{:S(2)}, u32[]{:S(2)}) collective-permute-start(bf16[2,528,512]{2,1,0:T(8,128)(2,1)S(1)} %collective-permute-done.9.c3), channel_id=1, source_target_pairs={{0,16},{16,0},{32,48},{48,32},{64,80},{80,64},{96,112},{112,96},{1... | collective-permute-start | bytes 3244040 | tf_op jit(solution)/shard_map/ppermute | solution.py:221
  52.8 6.1 %collective-permute-start.13 = (bf16[528,512]{1,0:T(8,128)(2,1)S(1)}, bf16[528,512]{1,0:T(8,128)(2,1)S(1)}, u32[]{:S(2)}, u32[]{:S(2)}) collective-permute-start(bf16[528,512]{1,0:T(8,128)(2,1)S(1)} %collective-permute-done.6.half), channel_id=1, source_target_pairs={{0,16},{16,0},{32,48},{48,32},{64,80},{80,64},{96,112},{112,96},{1... | collective-permute-start | bytes 1622024 | tf_op jit(solution)/shard_map/ppermute | solution.py:221
  53.2 6.3 %collective-permute-start.14 = (bf16[528,512]{1,0:T(8,128)(2,1)S(1)}, bf16[528,512]{1,0:T(8,128)(2,1)S(1)}, u32[]{:S(2)}, u32[]{:S(2)}) collective-permute-start(bf16[528,512]{1,0:T(8,128)(2,1)S(1)} %collective-permute-done.7.other), channel_id=1, source_target_pairs={{0,16},{16,0},{32,48},{48,32},{64,80},{80,64},{96,112},{112,96},{1... | collective-permute-start | bytes 1622024 | tf_op jit(solution)/shard_map/ppermute | solution.py:221

commit v11 on v10

--- a/solution.py
+++ b/solution.py
@@ -30,62 +30,72 @@
     return lax.dot_general(a, b, (((1,), (1,)), ((), ())), preferred_element_type=F32)
 
 
-def prepare_kernel(place, occupations, offsets, coupling, packed, half, sem):
-    x = place[5]
-    copies = [pltpu.make_async_copy(coupling.at[x], half.at[pl.ds(0, NO)], sem.at[2])]
-    for t in range(2):
-        copies.append(
-            pltpu.make_async_copy(coupling.at[t], packed.at[t, pl.ds(0, NO)], sem.at[t])
-        )
+def place():
+    device, b = lax.axis_index("freq"), lax.axis_index("slab")
+    y, k = device >> 1, device & 1
+    return y, k, (y & 1) ^ b, b, y >> 1, (lax.axis_index("energy") >> 2) & 1
+
+
+def prepare_kernel(occupations, offsets, coupling, packed, half, blocks, sem):
+    x = place()[5]
+    copies = [
+        pltpu.make_async_copy(coupling.at[t], blocks.at[t, pl.ds(0, NO)], sem.at[t])
+        for t in range(2)
+    ]
     for copy in copies:
         copy.start()
     row = lax.broadcasted_iota(jnp.int32, (TAIL, NO), 0)
-
-    def tail_of(t):
+    for t in range(2):
         whole = jnp.full((TAIL, NO), occupations[t], F32)
         high = whole.astype(BF16).astype(F32)
         middle = (whole - high).astype(BF16).astype(F32)
         low = whole - high - middle
         steps = jnp.full((TAIL, NO), offsets[t], jnp.int32).astype(F32)
         rows = jnp.where(row == 2, low, steps)
-        return jnp.where(row == 0, high, jnp.where(row == 1, middle, rows)).astype(BF16)
-
-    packed[0, NO:] = tail_of(0)
-    packed[1, NO:] = tail_of(1)
-    half[NO:] = tail_of(x)
-    for copy in copies:
-        copy.wait()
-
-
-def prepare(place, occupations, offsets, coupling):
+        rows = jnp.where(row == 0, high, jnp.where(row == 1, middle, rows))
+        blocks[t, NO:] = rows.astype(BF16)
+    for copy in copies:
+        copy.wait()
+    copies = [
+        pltpu.make_async_copy(blocks.at[x], half, sem.at[2]),
+        pltpu.make_async_copy(blocks, packed, sem.at[3]),
+    ]
+    for copy in copies:
+        copy.start()
+    for copy in copies:
+        copy.wait()
+
+
+def prepare(occupations, offsets, coupling):
     block = (NO + TAIL, NO)
     return pl.pallas_call(
         prepare_kernel,
         out_shape=[shape((2, *block), BF16), shape(block, BF16)],
-        in_specs=[SMEM] * 3 + [HBM],
-        out_specs=[VMEM] * 2,
-        scratch_shapes=[pltpu.SemaphoreType.DMA((3,))],
+        in_specs=[SMEM] * 2 + [HBM],
+        out_specs=[HBM] * 2,
+        scratch_shapes=[pltpu.VMEM((2, *block), BF16), pltpu.SemaphoreType.DMA((4,))],
         compiler_params=pltpu.CompilerParams(vmem_limit_bytes=60 * MIB),
         name="prepare",
-    )(place, occupations, offsets, coupling)
-
-
-def mix_kernel(place, weight, mine, pair, top, bottom, out):
+    )(occupations, offsets, coupling)
+
+
+def mix_kernel(weight, mine, pair, top, bottom, out):
+    scale = weight[place()[2]]
     for cross, first in ((top, 0), (bottom, NO // 2)):
         rows = pl.ds(first, NO // 2)
         beside = pair[rows].astype(F32) + cross[...].astype(F32)
-        out[rows] = (mine[rows].astype(F32) + weight[place[2]] * beside).astype(BF16)
-
-
-def mix(place, weight, mine, pair, top, bottom):
+        out[rows] = (mine[rows].astype(F32) + scale * beside).astype(BF16)
+
+
+def mix(weight, mine, pair, top, bottom):
     return pl.pallas_call(
         mix_kernel,
         out_shape=shape((NO, NO), BF16),
-        in_specs=[SMEM] * 2 + [VMEM] * 4,
+        in_specs=[SMEM] + [VMEM] * 4,
         out_specs=VMEM,
         compiler_params=PARAMS,
         name="mix",
-    )(place, weight, mine, pair, top, bottom)
+    )(weight, mine, pair, top, bottom)
 
 
 def add_terms(k, green, todo):
@@ -116,7 +126,7 @@
     return todo
 
 
-def first_kernel(place, own, near, shared, far, home, c1, c3, half, other, out, green, gsem):
+def first_kernel(own, near, shared, far, home, c1, c3, half, other, out, green, gsem):
     copies = [
         pltpu.make_async_copy(src, green.at[n], gsem.at[n])
         for n, src in enumerate((own, near, shared, far))
@@ -126,14 +136,14 @@
     for copy in copies:
         copy.wait()
     todo = blocks_of((home, c1, c3, half, other))
-    for n, term in enumerate(add_terms(place[1], green, todo)):
+    for n, term in enumerate(add_terms(place()[1], green, todo)):
         out[...] = term if n == 0 else out[...] + term
 
 
 def last_kernel(
-    place, green, start, s0, s1, s3, half, other, retarded, out, whole, acc, rsem
+    green, start, s0, s1, s3, half, other, retarded, out, whole, acc, rsem
 ):
-    k, sl, c = place[1], place[2], place[4]
+    _, k, sl, _, c, _ = place()
     copy = pltpu.make_async_copy(retarded.at[k, sl], whole, rsem.at[0])
     copy.start()
     todo = blocks_of((s0, s1, s3, half, other))
@@ -160,24 +170,24 @@
     )
 
 
-def sandwich_first(place, greens, arrays):
+def sandwich_first(greens, arrays):
     return pl.pallas_call(
         first_kernel,
         out_shape=[shape((NO, NO), F32), shape((4, NO, NO), BF16)],
-        in_specs=[SMEM] + [VMEM] * 9,
+        in_specs=[VMEM] * 9,
         out_specs=[VMEM] * 2,
         scratch_shapes=[pltpu.SemaphoreType.DMA((4,))],
         compiler_params=PARAMS,
         cost_estimate=cost(8),
         name="sandwich_first",
-    )(place, *greens, *arrays)
-
-
-def sandwich_last(place, green, start, arrays, retarded):
+    )(*greens, *arrays)
+
+
+def sandwich_last(green, start, arrays, retarded):
     return pl.pallas_call(
         last_kernel,
         out_shape=shape((8, 2, ROWS, NO), BF16),
-        in_specs=[SMEM] + [VMEM] * 7 + [HBM],
+        in_specs=[VMEM] * 7 + [HBM],
         out_specs=VMEM,
         scratch_shapes=[
             pltpu.VMEM((2, NO, NO), BF16),
@@ -187,35 +197,35 @@
         compiler_params=PARAMS,
         cost_estimate=cost(11),
         name="sandwich_last",
-    )(place, green, start, *arrays, retarded)
-
-
-def collect_kernel(place, pieces, out):
-    b = place[3]
-    for k in range(2):
-        for parity in range(2):
-            source = 2 * parity + k
-            total = pieces[source].astype(F32) + pieces[source + 4].astype(F32)
-            out[k, parity ^ b] = total
-
-
-def collect(place, pieces):
+    )(green, start, *arrays, retarded)
+
+
+def collect_kernel(pieces, out, total, sem):
+    b = place()[3]
+    copies = []
+    for n in range(4):
+        k, parity = n % 2, n // 2
+        total[n] = pieces[n].astype(F32) + pieces[n + 4].astype(F32)
+        copies.append(pltpu.make_async_copy(total.at[n], out.at[k, parity ^ b], sem.at[n]))
+        copies[-1].start()
+    for copy in copies:
+        copy.wait()
+
+
+def collect(pieces):
     return pl.pallas_call(
         collect_kernel,
         out_shape=shape((2, 2, 2, ROWS, NO), F32),
-        in_specs=[SMEM, VMEM],
-        out_specs=VMEM,
+        in_specs=[VMEM],
+        out_specs=HBM,
+        scratch_shapes=[pltpu.VMEM((4, 2, ROWS, NO), F32), pltpu.SemaphoreType.DMA((4,))],
         compiler_params=PARAMS,
         name="collect",
-    )(place, pieces)
+    )(pieces)
 
 
 def shards(lesser, retarded, coupling, occupations, offsets, intersection):
-    fr = lax.axis_index("freq")
-    b = lax.axis_index("slab")
-    y, k = fr >> 1, fr & 1
-    x = (lax.axis_index("energy") >> 2) & 1
-    place = jnp.stack([y, k, (y & 1) ^ b, b, y >> 1, x]).astype(jnp.int32)
+    _, k, sl, b, c, _ = place()
 
     def flip(x, bits):
         return lax.ppermute(x, "freq", [(d, d ^ bits) for d in range(8)])
@@ -231,7 +241,6 @@
                 if 0 <= e + step < count:
                     pairs.append((d * count + e, target * count + e + step))
 
-    sl, c = (y & 1) ^ b, y >> 1
     mine, pair = lesser[k, sl, c], lesser[k, 1 - sl, c]
     odd = [d for d in range(8) if d & 2]
     upper = [(s * 8 + d, (1 - s) * 8 + d) for s in range(2) for d in odd]
@@ -239,9 +248,9 @@
     rim = lesser[k, 1 - b, c]
     top = lax.ppermute(rim[: NO // 2], ("slab", "freq"), upper)
     bottom = lax.ppermute(rim[NO // 2 :], ("slab", "freq"), lower)
-    packed, part = prepare(place, occupations, offsets, coupling)
+    packed, part = prepare(occupations, offsets, coupling)
     half = flip(part, 4)
-    mixed = mix(place, intersection, mine, pair, top, bottom)
+    mixed = mix(intersection, mine, pair, top, bottom)
     mixed, packed = lax.optimization_barrier((mixed, packed))
     near = lax.ppermute(mixed, ("freq", "energy"), near_pairs)
     far = lax.ppermute(mixed, ("freq", "energy"), far_pairs)
@@ -254,9 +263,9 @@
     )
     swapped = [flip(x, 1) for x in (packed, c1, c3, half, other)]
 
-    first, green = sandwich_first(place, [own, near, shared, far], [packed, c1, c3, half, other])
-    pieces = sandwich_last(place, green, first, swapped, retarded)
-    return collect(place, lax.all_to_all(pieces, "freq", 0, 0))
+    first, green = sandwich_first([own, near, shared, far], [packed, c1, c3, half, other])
+    pieces = sandwich_last(green, first, swapped, retarded)
+    return collect(lax.all_to_all(pieces, "freq", 0, 0))
 
 
 def solution(mesh):

time: 89.1 us -> 87.4 us (0.981)
  Pallas kernels: 18.6 us -> 16.7 us
  transfers between devices with their start and end apart: 15 -> 15, of which waited for: 5 -> 6; matrix products, arithmetic and copies ran while one was open for 2% -> 1% of each run, Pallas kernels for 11% -> 10%
where the time goes in v11:
time: 87.4 us; the launch traced here: 87.1 us
  waiting for transfers between devices  25.9 us (30%)
  starting transfers between devices  21.2 us (24%)
  blocking collectives  20.2 us (23%)
  Pallas kernels  16.7 us (19%)
  local copies, waits for them, and re-layouts  2.77 us (3%)
    all_to_all x1, blocking collectives, shards(): return collect(lax.all_to_all(pieces, 'freq', 0, 0))  20.2 us
    ppermute x1, waiting for transfers between devices, shards(): near = lax.ppermute(mixed, ('freq', 'energy'), near_pairs)  17.1 us
    pallas_call x1, Pallas kernels, sandwich_last(): pl.pallas_call(last_kernel, out_shape=shape((8, 2, ROWS, NO), BF16), in_s...  6.84 us
    ppermute x1, starting transfers between devices, shards(): bottom = lax.ppermute(rim[NO // 2:], ('slab', 'freq'), lower)  6.19 us
    ppermute x1, starting transfers between devices, shards(): near = lax.ppermute(mixed, ('freq', 'energy'), near_pairs)  6.15 us
    ppermute x10, starting transfers between devices, flip(): return lax.ppermute(x, 'freq', [(d, d ^ bits) for d in range(8)])  5.47 us
    pallas_call x1, Pallas kernels, sandwich_first(): pl.pallas_call(first_kernel, out_shape=[shape((NO, NO), F32), shape((4, N...  4.99 us
    ppermute x10, waiting for transfers between devices, flip(): return lax.ppermute(x, 'freq', [(d, d ^ bits) for d in range(8)])  3.28 us
  transfers between devices with their start and end apart: 15, of which 6 were waited for; matrix products, arithmetic and copies ran while one was open for 1% of the time, Pallas kernels for 10%

profile of v11, /device:TPU:38, one launch (start us, length us, event | category | flops | bytes accessed | tf_op | source)
XLA Modules:
  0.0 87.1 jit_solution(12086298392177539619)
XLA Ops:
  0.0 1.1 %dynamic-slice_bitcast_fusion.2 = (bf16[256,512]{1,0:T(8,128)(2,1)S(1)}, bf16[256,512]{1,0:T(8,128)(2,1)S(1)}) fusion(bf16[2,2,2,512,512]{4,3,2,1,0:T(8,128)(2,1)} %param.6, s32[]{:T(128)S(6)} %select_n.19, s32[]{:T(128)S(6)} %select_n.23, s32[]{:T(128)S(6)} %select_n.21, s32[]{:T(128)S(6)} %add.26), kind=kLoop, calls=%fused_computation.2 | loop fusion | bytes 1048592 | tf_op jit(solution)/shard_map/slice | solution.py:250
  1.1 0.7 collective-permute-start
  1.8 6.2 %collective-permute-start.1 = (bf16[256,512]{1,0:T(8,128)(2,1)S(1)}, bf16[256,512]{1,0:T(8,128)(2,1)S(1)}, u32[]{:S(2)}, u32[]{:S(2)}) collective-permute-start(bf16[256,512]{1,0:T(8,128)(2,1)S(1)} %get-tuple-element.33), channel_id=1, source_target_pairs={{0,160},{16,176},{64,224},{80,240},{128,32},{144,48},{192,96},{208... | collective-permute-start | bytes 786440 | tf_op jit(solution)/shard_map/ppermute | solution.py:250
  7.9 3.1 %prepare.1 = (bf16[2,528,512]{2,1,0:T(8,128)(2,1)}, bf16[528,512]{1,0:T(8,128)(2,1)}) custom-call(f32[2]{0:T(128)} %occupations.1, s32[2]{0:T(128)} %offsets.1, bf16[2,512,512]{2,1,0:T(8,128)(2,1)} %coupling.1), custom_call_target="tpu_custom_call" | custom-call | tf_op jit(solution)/shard_map/prepare/pallas_call | solution.py:71
  11.0 0.0 copy-start
  11.1 3.0 %collective-permute-start.6 = (bf16[528,512]{1,0:T(8,128)(2,1)}, bf16[528,512]{1,0:T(8,128)(2,1)S(1)}, u32[]{:S(2)}, u32[]{:S(2)}) collective-permute-start(bf16[528,512]{1,0:T(8,128)(2,1)} %get-tuple-element.24), channel_id=1, source_target_pairs={{0,64},{16,80},{32,96},{48,112},{64,0},{80,16},{96,32},{112,48},{1... | collective-permute-start | bytes 1622024 | tf_op jit(solution)/shard_map/ppermute | solution.py:231
  14.0 1.3 %dynamic-slice_bitcast_fusion = (bf16[512,512]{1,0:T(8,128)(2,1)S(1)}, bf16[512,512]{1,0:T(8,128)(2,1)S(1)}) fusion(bf16[2,2,2,512,512]{4,3,2,1,0:T(8,128)(2,1)} %param.6, s32[]{:T(128)S(6)} %select_n.19, s32[]{:T(128)S(6)} %select_n.22, s32[]{:T(128)S(6)} %select_n.21, s32[]{:T(128)S(6)} %select_n.20), kind=kLoop, calls=%fused_computation | loop fusion | bytes 2097168 | tf_op jit(solution)/shard_map/squeeze | solution.py:244
  15.3 0.0 collective-permute-done.1.bottom
  15.4 0.8 mix.1
  16.1 0.4 copy-done.2
  16.6 1.4 %collective-permute-start.9 = (bf16[2,528,512]{2,1,0:T(8,128)(2,1)S(1)}, bf16[2,528,512]{2,1,0:T(8,128)(2,1)S(1)}, u32[]{:S(2)}, u32[]{:S(2)}) collective-permute-start(bf16[2,528,512]{2,1,0:T(8,128)(2,1)S(1)} %copy-done.2), channel_id=1, source_target_pairs={{0,96},{16,112},{32,64},{48,80},{64,32},{80,48},{96,0},{112,16},{1... | collective-permute-start | bytes 3244040 | tf_op jit(solution)/shard_map/ppermute | solution.py:231
  17.9 6.1 %collective-permute-start.2 = (bf16[512,512]{1,0:T(8,128)(2,1)S(1)}, bf16[512,512]{1,0:T(8,128)(2,1)S(1)}, u32[]{:S(2)}, u32[]{:S(2)}) collective-permute-start(bf16[512,512]{1,0:T(8,128)(2,1)S(1)} %mix.1), channel_id=1, source_target_pairs={{1,16},{2,17},{3,18},{4,19},{5,20},{6,21},{7,22},{8,23},{9,24},{10... | collective-permute-start | bytes 1572872 | tf_op jit(solution)/shard_map/ppermute | solution.py:255
  24.1 1.9 %collective-permute-start.5 = (bf16[512,512]{1,0:T(8,128)(2,1)S(1)}, bf16[512,512]{1,0:T(8,128)(2,1)S(1)}, u32[]{:S(2)}, u32[]{:S(2)}) collective-permute-start(bf16[512,512]{1,0:T(8,128)(2,1)S(1)} %mix.1), channel_id=1, source_target_pairs={{0,1},{1,2},{2,3},{3,4},{4,5},{5,6},{6,7},{7,8},{8,9},{9,10},{10,1... | collective-permute-start | bytes 1572872 | tf_op jit(solution)/shard_map/ppermute | solution.py:256
  26.0 2.0 %collective-permute-done.6.half = bf16[528,512]{1,0:T(8,128)(2,1)S(1)} collective-permute-done((bf16[528,512]{1,0:T(8,128)(2,1)}, bf16[528,512]{1,0:T(8,128)(2,1)S(1)}, u32[]{:S(2)}, u32[]{:S(2)}) %collective-permute-start.6) | collective-permute-done | bytes 540704 | tf_op jit(solution)/shard_map/ppermute | solution.py:231
  28.1 0.8 collective-permute-start.7
  28.9 17.1 %collective-permute-done.2.near = bf16[512,512]{1,0:T(8,128)(2,1)S(1)} collective-permute-done((bf16[512,512]{1,0:T(8,128)(2,1)S(1)}, bf16[512,512]{1,0:T(8,128)(2,1)S(1)}, u32[]{:S(2)}, u32[]{:S(2)}) %collective-permute-start.2) | collective-permute-done | bytes 524320 | tf_op jit(solution)/shard_map/ppermute | solution.py:255
  46.0 0.0 collective-permute-start.3
  46.0 2.5 %collective-permute-done.5.far = bf16[512,512]{1,0:T(8,128)(2,1)S(1)} collective-permute-done((bf16[512,512]{1,0:T(8,128)(2,1)S(1)}, bf16[512,512]{1,0:T(8,128)(2,1)S(1)}, u32[]{:S(2)}, u32[]{:S(2)}) %collective-permute-start.5) | collective-permute-done | bytes 524320 | tf_op jit(solution)/shard_map/ppermute | solution.py:256
  48.4 3.1 %collective-permute-done.7.other = bf16[528,512]{1,0:T(8,128)(2,1)S(1)} collective-permute-done((bf16[528,512]{1,0:T(8,128)(2,1)S(1)}, bf16[528,512]{1,0:T(8,128)(2,1)S(1)}, u32[]{:S(2)}, u32[]{:S(2)}) %collective-permute-start.7) | collective-permute-done | bytes 540704 | tf_op jit(solution)/shard_map/ppermute | solution.py:260
  51.5 0.0 collective-permute-start.10
  51.5 0.0 collective-permute-done.8.c1
  51.6 0.5 collective-permute-start.11
  52.1 0.1 collective-permute-start.12
  52.2 0.4 collective-permute-start.13
  52.6 0.1 collective-permute-start.14
  52.7 5.0 %sandwich_first.1 = (f32[512,512]{1,0:T(8,128)S(1)}, bf16[4,512,512]{2,1,0:T(8,128)(2,1)S(1)}) custom-call(bf16[512,512]{1,0:T(8,128)(2,1)S(1)} %collective-permute-done.3.own, bf16[512,512]{1,0:T(8,128)(2,1)S(1)} %collective-permute-done.2.near, bf16[512,512]{1,0:T(8,128)(2,1)S(1)} %collective-permute-done.4.shared, ...), custom_call_target="tpu_custom_call" | custom-call | flops 4294967296 | bytes 9437184 | tf_op jit(solution)/shard_map/sandwich_first/pallas_call | solution.py:174
  57.7 0.4 collective-permute-done.13.half
  58.1 0.8 collective-permute-done.14.other
  58.9 0.0 collective-permute-done.10.s0
  58.9 6.8 %sandwich_last.1 = bf16[8,2,64,512]{3,2,1,0:T(8,128)(2,1)S(1)} custom-call(bf16[4,512,512]{2,1,0:T(8,128)(2,1)S(1)} %get-tuple-element.31.green, f32[512,512]{1,0:T(8,128)S(1)} %get-tuple-element.32.start, bf16[2,528,512]{2,1,0:T(8,128)(2,1)S(1)} %collective-permute-done.10.s0, bf16[2,528,512]{2,1,0:T(8,128)(2,1)S(1)} %collective-permute-done.11.s1, ...), custom_call_target="tpu_custom_call" | custom-call | flops 5905580032 | bytes 11010048 | tf_op jit(solution)/shard_map/sandwich_last/pallas_call | solution.py:187
  65.8 20.2 %all_to_all.5.pieces = bf16[8,2,64,512]{3,2,1,0:T(8,128)(2,1)S(1)} all-to-all(bf16[8,2,64,512]{3,2,1,0:T(8,128)(2,1)S(1)} %sandwich_last.1), channel_id=1, replica_groups=mesh['slab'=2,'freq'=8,'energy'=16] {'freq'}, dimensions={0} | all-to-all | bytes 2097152 | tf_op jit(solution)/shard_map/all_to_all | solution.py:268
  85.9 1.0 %collect.1 = f32[2,2,2,64,512]{4,3,2,1,0:T(8,128)} custom-call(bf16[8,2,64,512]{3,2,1,0:T(8,128)(2,1)S(1)} %all_to_all.5.pieces), custom_call_target="tpu_custom_call" | custom-call | tf_op jit(solution)/shard_map/collect/pallas_call | solution.py:216
  (12 shorter events, 0.0 us)
Async XLA Ops:
  1.1 14.3 %collective-permute-start = (bf16[256,512]{1,0:T(8,128)(2,1)S(1)}, bf16[256,512]{1,0:T(8,128)(2,1)S(1)}, u32[]{:S(2)}, u32[]{:S(2)}) collective-permute-start(bf16[256,512]{1,0:T(8,128)(2,1)S(1)} %get-tuple-element.34), channel_id=1, source_target_pairs={{32,160},{48,176},{96,224},{112,240},{160,32},{176,48},{224,96},{2... | collective-permute-start | bytes 786440 | tf_op jit(solution)/shard_map/ppermute | solution.py:249
  1.8 13.6 %collective-permute-start.1 = (bf16[256,512]{1,0:T(8,128)(2,1)S(1)}, bf16[256,512]{1,0:T(8,128)(2,1)S(1)}, u32[]{:S(2)}, u32[]{:S(2)}) collective-permute-start(bf16[256,512]{1,0:T(8,128)(2,1)S(1)} %get-tuple-element.33), channel_id=1, source_target_pairs={{0,160},{16,176},{64,224},{80,240},{128,32},{144,48},{192,96},{208... | collective-permute-start | bytes 786440 | tf_op jit(solution)/shard_map/ppermute | solution.py:250
  11.0 4.3 %copy-start = (f32[2]{0:T(128)S(1)}, f32[2]{0:T(128)}, u32[]{:S(2)}) copy-start(f32[2]{0:T(128)} %weight.1) | copy-start | bytes 28
  11.1 17.0 %collective-permute-start.6 = (bf16[528,512]{1,0:T(8,128)(2,1)}, bf16[528,512]{1,0:T(8,128)(2,1)S(1)}, u32[]{:S(2)}, u32[]{:S(2)}) collective-permute-start(bf16[528,512]{1,0:T(8,128)(2,1)} %get-tuple-element.24), channel_id=1, source_target_pairs={{0,64},{16,80},{32,96},{48,112},{64,0},{80,16},{96,32},{112,48},{1... | collective-permute-start | bytes 1622024 | tf_op jit(solution)/shard_map/ppermute | solution.py:231
  15.3 1.2 %copy-start.2 = (bf16[2,528,512]{2,1,0:T(8,128)(2,1)S(1)}, bf16[2,528,512]{2,1,0:T(8,128)(2,1)}, u32[]{:S(2)}) copy-start(bf16[2,528,512]{2,1,0:T(8,128)(2,1)} %get-tuple-element.28.home) | copy-start | bytes 3244036
  16.6 42.3 %copy-start.1 = (bf16[2,2,2,512,512]{4,3,2,1,0:T(8,128)(2,1)S(1)}, bf16[2,2,2,512,512]{4,3,2,1,0:T(8,128)(2,1)}, u32[]{:S(2)}) copy-start(bf16[2,2,2,512,512]{4,3,2,1,0:T(8,128)(2,1)} %retarded.1) | copy-start | bytes 12582916
  16.6 35.0 %collective-permute-start.8 = (bf16[2,528,512]{2,1,0:T(8,128)(2,1)S(1)}, bf16[2,528,512]{2,1,0:T(8,128)(2,1)S(1)}, u32[]{:S(2)}, u32[]{:S(2)}) collective-permute-start(bf16[2,528,512]{2,1,0:T(8,128)(2,1)S(1)} %copy-done.2), channel_id=1, source_target_pairs={{0,32},{16,48},{32,0},{48,16},{64,96},{80,112},{96,64},{112,80},{1... | collective-permute-start | bytes 3244040 | tf_op jit(solution)/shard_map/ppermute | solution.py:231
  16.6 35.5 %collective-permute-start.9 = (bf16[2,528,512]{2,1,0:T(8,128)(2,1)S(1)}, bf16[2,528,512]{2,1,0:T(8,128)(2,1)S(1)}, u32[]{:S(2)}, u32[]{:S(2)}) collective-permute-start(bf16[2,528,512]{2,1,0:T(8,128)(2,1)S(1)} %copy-done.2), channel_id=1, source_target_pairs={{0,96},{16,112},{32,64},{48,80},{64,32},{80,48},{96,0},{112,16},{1... | collective-permute-start | bytes 3244040 | tf_op jit(solution)/shard_map/ppermute | solution.py:231
  17.9 28.0 %collective-permute-start.2 = (bf16[512,512]{1,0:T(8,128)(2,1)S(1)}, bf16[512,512]{1,0:T(8,128)(2,1)S(1)}, u32[]{:S(2)}, u32[]{:S(2)}) collective-permute-start(bf16[512,512]{1,0:T(8,128)(2,1)S(1)} %mix.1), channel_id=1, source_target_pairs={{1,16},{2,17},{3,18},{4,19},{5,20},{6,21},{7,22},{8,23},{9,24},{10... | collective-permute-start | bytes 1572872 | tf_op jit(solution)/shard_map/ppermute | solution.py:255
  24.1 24.3 %collective-permute-start.5 = (bf16[512,512]{1,0:T(8,128)(2,1)S(1)}, bf16[512,512]{1,0:T(8,128)(2,1)S(1)}, u32[]{:S(2)}, u32[]{:S(2)}) collective-permute-start(bf16[512,512]{1,0:T(8,128)(2,1)S(1)} %mix.1), channel_id=1, source_target_pairs={{0,1},{1,2},{2,3},{3,4},{4,5},{5,6},{6,7},{7,8},{8,9},{9,10},{10,1... | collective-permute-start | bytes 1572872 | tf_op jit(solution)/shard_map/ppermute | solution.py:256
  28.1 23.5 %collective-permute-start.7 = (bf16[528,512]{1,0:T(8,128)(2,1)S(1)}, bf16[528,512]{1,0:T(8,128)(2,1)S(1)}, u32[]{:S(2)}, u32[]{:S(2)}) collective-permute-start(bf16[528,512]{1,0:T(8,128)(2,1)S(1)} %collective-permute-done.6.half), channel_id=1, source_target_pairs={{0,4},{1,5},{2,6},{3,7},{4,0},{5,1},{6,2},{7,3},{8,12},{9,13},{10,... | collective-permute-start | bytes 1622024 | tf_op jit(solution)/shard_map/ppermute | solution.py:260
  46.0 5.6 %collective-permute-start.3 = (bf16[512,512]{1,0:T(8,128)(2,1)S(1)}, bf16[512,512]{1,0:T(8,128)(2,1)S(1)}, u32[]{:S(2)}, u32[]{:S(2)}) collective-permute-start(bf16[512,512]{1,0:T(8,128)(2,1)S(1)} %mix.1), channel_id=1, source_target_pairs={{0,16},{16,0},{32,48},{48,32},{64,80},{80,64},{96,112},{112,96},{1... | collective-permute-start | bytes 1572872 | tf_op jit(solution)/shard_map/ppermute | solution.py:231
  48.4 3.1 %collective-permute-start.4 = (bf16[512,512]{1,0:T(8,128)(2,1)S(1)}, bf16[512,512]{1,0:T(8,128)(2,1)S(1)}, u32[]{:S(2)}, u32[]{:S(2)}) collective-permute-start(bf16[512,512]{1,0:T(8,128)(2,1)S(1)} %collective-permute-done.2.near), channel_id=1, source_target_pairs={{0,16},{16,0},{32,48},{48,32},{64,80},{80,64},{96,112},{112,96},{1... | collective-permute-start | bytes 1572872 | tf_op jit(solution)/shard_map/ppermute | solution.py:231
  51.5 7.4 %collective-permute-start.10 = (bf16[2,528,512]{2,1,0:T(8,128)(2,1)S(1)}, bf16[2,528,512]{2,1,0:T(8,128)(2,1)S(1)}, u32[]{:S(2)}, u32[]{:S(2)}) collective-permute-start(bf16[2,528,512]{2,1,0:T(8,128)(2,1)S(1)} %copy-done.2), channel_id=1, source_target_pairs={{0,16},{16,0},{32,48},{48,32},{64,80},{80,64},{96,112},{112,96},{1... | collective-permute-start | bytes 3244040 | tf_op jit(solution)/shard_map/ppermute | solution.py:231
  51.6 7.3 %collective-permute-start.11 = (bf16[2,528,512]{2,1,0:T(8,128)(2,1)S(1)}, bf16[2,528,512]{2,1,0:T(8,128)(2,1)S(1)}, u32[]{:S(2)}, u32[]{:S(2)}) collective-permute-start(bf16[2,528,512]{2,1,0:T(8,128)(2,1)S(1)} %collective-permute-done.8.c1), channel_id=1, source_target_pairs={{0,16},{16,0},{32,48},{48,32},{64,80},{80,64},{96,112},{112,96},{1... | collective-permute-start | bytes 3244040 | tf_op jit(solution)/shard_map/ppermute | solution.py:231
  52.1 6.8 %collective-permute-start.12 = (bf16[2,528,512]{2,1,0:T(8,128)(2,1)S(1)}, bf16[2,528,512]{2,1,0:T(8,128)(2,1)S(1)}, u32[]{:S(2)}, u32[]{:S(2)}) collective-permute-start(bf16[2,528,512]{2,1,0:T(8,128)(2,1)S(1)} %collective-permute-done.9.c3), channel_id=1, source_target_pairs={{0,16},{16,0},{32,48},{48,32},{64,80},{80,64},{96,112},{112,96},{1... | collective-permute-start | bytes 3244040 | tf_op jit(solution)/shard_map/ppermute | solution.py:231
  52.2 6.0 %collective-permute-start.13 = (bf16[528,512]{1,0:T(8,128)(2,1)S(1)}, bf16[528,512]{1,0:T(8,128)(2,1)S(1)}, u32[]{:S(2)}, u32[]{:S(2)}) collective-permute-start(bf16[528,512]{1,0:T(8,128)(2,1)S(1)} %collective-permute-done.6.half), channel_id=1, source_target_pairs={{0,16},{16,0},{32,48},{48,32},{64,80},{80,64},{96,112},{112,96},{1... | collective-permute-start | bytes 1622024 | tf_op jit(solution)/shard_map/ppermute | solution.py:231
  52.6 6.3 %collective-permute-start.14 = (bf16[528,512]{1,0:T(8,128)(2,1)S(1)}, bf16[528,512]{1,0:T(8,128)(2,1)S(1)}, u32[]{:S(2)}, u32[]{:S(2)}) collective-permute-start(bf16[528,512]{1,0:T(8,128)(2,1)S(1)} %collective-permute-done.7.other), channel_id=1, source_target_pairs={{0,16},{16,0},{32,48},{48,32},{64,80},{80,64},{96,112},{112,96},{1... | collective-permute-start | bytes 1622024 | tf_op jit(solution)/shard_map/ppermute | solution.py:231

commit v12 on v11

--- a/solution.py
+++ b/solution.py
@@ -253,11 +253,13 @@
     mixed = mix(intersection, mine, pair, top, bottom)
     mixed, packed = lax.optimization_barrier((mixed, packed))
     near = lax.ppermute(mixed, ("freq", "energy"), near_pairs)
+    c1, c3 = flip(packed, 2), flip(packed, 6)
+    half, mixed = lax.optimization_barrier((half, mixed))
     far = lax.ppermute(mixed, ("freq", "energy"), far_pairs)
-    c1, c3 = flip(packed, 2), flip(packed, 6)
-    near, mixed = lax.optimization_barrier((near, mixed))
-    own, shared = flip(mixed, 1), flip(near, 1)
     other = lax.ppermute(half, "energy", [(e, e ^ 4) for e in range(count)])
+    shared = flip(near, 1)
+    other, shared, mixed = lax.optimization_barrier((other, shared, mixed))
+    own = flip(mixed, 1)
     own, shared, far, packed, half, other = lax.optimization_barrier(
         (own, shared, far, packed, half, other)
     )

time: 87.4 us -> 88.3 us (1.010)
  starting transfers between devices: 21.2 us -> 23 us
  blocking collectives: 20.2 us -> 19.3 us
    ppermute x1, waiting for transfers between devices: 3.08 us -> 13.9 us  [shards(): other = lax.ppermute(half, 'energy', [(e, e ^ 4) for e in range(count)])]
    ppermute x1, waiting for transfers between devices: 17.1 us -> 6.73 us  [shards(): near = lax.ppermute(mixed, ('freq', 'energy'), near_pairs)]
    ppermute x1, waiting for transfers between devices: 2.47 us -> 0.01 us  [shards(): far = lax.ppermute(mixed, ('freq', 'energy'), far_pairs)]
    ppermute x10, waiting for transfers between devices: 3.28 us -> 5.25 us  [flip(): return lax.ppermute(x, 'freq', [(d, d ^ bits) for d in range(8)])]
  transfers between devices with their start and end apart: 15 -> 15, of which waited for: 6 -> 5; matrix products, arithmetic and copies ran while one was open for 1% -> 1% of each run, Pallas kernels for 10% -> 10%
where the time goes in v12:
time: 88.3 us; the launch traced here: 87.5 us
  waiting for transfers between devices  25.9 us (29%)
  starting transfers between devices  23 us (26%)
  blocking collectives  19.3 us (22%)
  Pallas kernels  16.7 us (19%)
  local copies, waits for them, and re-layouts  2.35 us (3%)
    all_to_all x1, blocking collectives, shards(): return collect(lax.all_to_all(pieces, 'freq', 0, 0))  19.3 us
    ppermute x1, waiting for transfers between devices, shards(): other = lax.ppermute(half, 'energy', [(e, e ^ 4) for e in range(count)])  13.9 us
    pallas_call x1, Pallas kernels, sandwich_last(): pl.pallas_call(last_kernel, out_shape=shape((8, 2, ROWS, NO), BF16), in_s...  6.84 us
    ppermute x1, waiting for transfers between devices, shards(): near = lax.ppermute(mixed, ('freq', 'energy'), near_pairs)  6.73 us
    ppermute x1, starting transfers between devices, shards(): near = lax.ppermute(mixed, ('freq', 'energy'), near_pairs)  6.44 us
    ppermute x10, starting transfers between devices, flip(): return lax.ppermute(x, 'freq', [(d, d ^ bits) for d in range(8)])  6.28 us
    ppermute x1, starting transfers between devices, shards(): bottom = lax.ppermute(rim[NO // 2:], ('slab', 'freq'), lower)  6.19 us
    ppermute x10, waiting for transfers between devices, flip(): return lax.ppermute(x, 'freq', [(d, d ^ bits) for d in range(8)])  5.25 us
  transfers between devices with their start and end apart: 15, of which 5 were waited for; matrix products, arithmetic and copies ran while one was open for 1% of the time, Pallas kernels for 10%

profile of v12, /device:TPU:38, one launch (start us, length us, event | category | flops | bytes accessed | tf_op | source)
XLA Modules:
  0.0 87.5 jit_solution(247767166806823408)
XLA Ops:
  0.0 1.1 %dynamic-slice_bitcast_fusion.2 = (bf16[256,512]{1,0:T(8,128)(2,1)S(1)}, bf16[256,512]{1,0:T(8,128)(2,1)S(1)}) fusion(bf16[2,2,2,512,512]{4,3,2,1,0:T(8,128)(2,1)} %param.6, s32[]{:T(128)S(6)} %select_n.19, s32[]{:T(128)S(6)} %select_n.23, s32[]{:T(128)S(6)} %select_n.21, s32[]{:T(128)S(6)} %add.26), kind=kLoop, calls=%fused_computation.2 | loop fusion | bytes 1048592 | tf_op jit(solution)/shard_map/slice | solution.py:250
  1.1 0.7 collective-permute-start.1
  1.8 6.2 %collective-permute-start.2 = (bf16[256,512]{1,0:T(8,128)(2,1)S(1)}, bf16[256,512]{1,0:T(8,128)(2,1)S(1)}, u32[]{:S(2)}, u32[]{:S(2)}) collective-permute-start(bf16[256,512]{1,0:T(8,128)(2,1)S(1)} %get-tuple-element.39), channel_id=1, source_target_pairs={{0,160},{16,176},{64,224},{80,240},{128,32},{144,48},{192,96},{208... | collective-permute-start | bytes 786440 | tf_op jit(solution)/shard_map/ppermute | solution.py:250
  7.9 3.1 %prepare.1 = (bf16[2,528,512]{2,1,0:T(8,128)(2,1)}, bf16[528,512]{1,0:T(8,128)(2,1)}) custom-call(f32[2]{0:T(128)} %occupations.1, s32[2]{0:T(128)} %offsets.1, bf16[2,512,512]{2,1,0:T(8,128)(2,1)} %coupling.1), custom_call_target="tpu_custom_call" | custom-call | tf_op jit(solution)/shard_map/prepare/pallas_call | solution.py:71
  11.0 0.0 copy-start
  11.1 3.0 %collective-permute-start = (bf16[528,512]{1,0:T(8,128)(2,1)}, bf16[528,512]{1,0:T(8,128)(2,1)S(1)}, u32[]{:S(2)}, u32[]{:S(2)}) collective-permute-start(bf16[528,512]{1,0:T(8,128)(2,1)} %get-tuple-element.22), channel_id=1, source_target_pairs={{0,64},{16,80},{32,96},{48,112},{64,0},{80,16},{96,32},{112,48},{1... | collective-permute-start | bytes 1622024 | tf_op jit(solution)/shard_map/ppermute | solution.py:231
  14.0 1.3 %dynamic-slice_bitcast_fusion = (bf16[512,512]{1,0:T(8,128)(2,1)S(1)}, bf16[512,512]{1,0:T(8,128)(2,1)S(1)}) fusion(bf16[2,2,2,512,512]{4,3,2,1,0:T(8,128)(2,1)} %param.6, s32[]{:T(128)S(6)} %select_n.19, s32[]{:T(128)S(6)} %select_n.22, s32[]{:T(128)S(6)} %select_n.21, s32[]{:T(128)S(6)} %select_n.20), kind=kLoop, calls=%fused_computation | loop fusion | bytes 2097168 | tf_op jit(solution)/shard_map/squeeze | solution.py:244
  15.3 0.0 collective-permute-done.1.top
  15.3 0.0 collective-permute-done.2.bottom
  15.4 0.8 mix.1
  16.1 0.0 copy-start.1
  16.1 6.4 %collective-permute-start.4 = (bf16[512,512]{1,0:T(8,128)(2,1)S(1)}, bf16[512,512]{1,0:T(8,128)(2,1)S(1)}, u32[]{:S(2)}, u32[]{:S(2)}) collective-permute-start(bf16[512,512]{1,0:T(8,128)(2,1)S(1)} %mix.1), channel_id=1, source_target_pairs={{1,16},{2,17},{3,18},{4,19},{5,20},{6,21},{7,22},{8,23},{9,24},{10... | collective-permute-start | bytes 1572872 | tf_op jit(solution)/shard_map/ppermute | solution.py:255
  22.6 0.5 collective-permute-start.8
  23.1 1.5 %collective-permute-start.9 = (bf16[2,528,512]{2,1,0:T(8,128)(2,1)S(1)}, bf16[2,528,512]{2,1,0:T(8,128)(2,1)S(1)}, u32[]{:S(2)}, u32[]{:S(2)}) collective-permute-start(bf16[2,528,512]{2,1,0:T(8,128)(2,1)S(1)} %copy-done.2), channel_id=1, source_target_pairs={{0,96},{16,112},{32,64},{48,80},{64,32},{80,48},{96,0},{112,16},{1... | collective-permute-start | bytes 3244040 | tf_op jit(solution)/shard_map/ppermute | solution.py:231
  24.6 3.4 %collective-permute-done.half = bf16[528,512]{1,0:T(8,128)(2,1)S(1)} collective-permute-done((bf16[528,512]{1,0:T(8,128)(2,1)}, bf16[528,512]{1,0:T(8,128)(2,1)S(1)}, u32[]{:S(2)}, u32[]{:S(2)}) %collective-permute-start) | collective-permute-done | bytes 540704 | tf_op jit(solution)/shard_map/ppermute | solution.py:231
  28.1 0.8 collective-permute-start.3
  28.9 6.7 %collective-permute-done.4.near = bf16[512,512]{1,0:T(8,128)(2,1)S(1)} collective-permute-done((bf16[512,512]{1,0:T(8,128)(2,1)S(1)}, bf16[512,512]{1,0:T(8,128)(2,1)S(1)}, u32[]{:S(2)}, u32[]{:S(2)}) %collective-permute-start.4) | collective-permute-done | bytes 524320 | tf_op jit(solution)/shard_map/ppermute | solution.py:255
  35.6 0.0 collective-permute-start.5
  35.6 2.6 %collective-permute-start.7 = (bf16[512,512]{1,0:T(8,128)(2,1)S(1)}, bf16[512,512]{1,0:T(8,128)(2,1)S(1)}, u32[]{:S(2)}, u32[]{:S(2)}) collective-permute-start(bf16[512,512]{1,0:T(8,128)(2,1)S(1)} %mix.1), channel_id=1, source_target_pairs={{0,1},{1,2},{2,3},{3,4},{4,5},{5,6},{6,7},{7,8},{8,9},{9,10},{10,1... | collective-permute-start | bytes 1572872 | tf_op jit(solution)/shard_map/ppermute | solution.py:258
  38.3 13.9 %collective-permute-done.3.other = bf16[528,512]{1,0:T(8,128)(2,1)S(1)} collective-permute-done((bf16[528,512]{1,0:T(8,128)(2,1)S(1)}, bf16[528,512]{1,0:T(8,128)(2,1)S(1)}, u32[]{:S(2)}, u32[]{:S(2)}) %collective-permute-start.3) | collective-permute-done | bytes 540704 | tf_op jit(solution)/shard_map/ppermute | solution.py:259
  52.1 0.0 collective-permute-done.5.shared
  52.1 0.5 collective-permute-start.11
  52.6 0.1 collective-permute-start.12
  52.7 1.3 %collective-permute-done.6.own = bf16[512,512]{1,0:T(8,128)(2,1)S(1)} collective-permute-done((bf16[512,512]{1,0:T(8,128)(2,1)S(1)}, bf16[512,512]{1,0:T(8,128)(2,1)S(1)}, u32[]{:S(2)}, u32[]{:S(2)}) %collective-permute-start.6) | collective-permute-done | bytes 524320 | tf_op jit(solution)/shard_map/ppermute | solution.py:231
  54.0 0.1 collective-permute-start.10
  54.2 0.4 collective-permute-start.13
  54.5 0.1 collective-permute-start.14
  54.7 5.0 %sandwich_first.1 = (f32[512,512]{1,0:T(8,128)S(1)}, bf16[4,512,512]{2,1,0:T(8,128)(2,1)S(1)}) custom-call(bf16[512,512]{1,0:T(8,128)(2,1)S(1)} %collective-permute-done.6.own, bf16[512,512]{1,0:T(8,128)(2,1)S(1)} %collective-permute-done.4.near, bf16[512,512]{1,0:T(8,128)(2,1)S(1)} %collective-permute-done.5.shared, ...), custom_call_target="tpu_custom_call" | custom-call | flops 4294967296 | bytes 9437184 | tf_op jit(solution)/shard_map/sandwich_first/pallas_call | solution.py:174
  59.7 0.5 collective-permute-done.14.other
  60.2 6.8 %sandwich_last.1 = bf16[8,2,64,512]{3,2,1,0:T(8,128)(2,1)S(1)} custom-call(bf16[4,512,512]{2,1,0:T(8,128)(2,1)S(1)} %get-tuple-element.37.green, f32[512,512]{1,0:T(8,128)S(1)} %get-tuple-element.38.start, bf16[2,528,512]{2,1,0:T(8,128)(2,1)S(1)} %collective-permute-done.10.s0, bf16[2,528,512]{2,1,0:T(8,128)(2,1)S(1)} %collective-permute-done.11.s1, ...), custom_call_target="tpu_custom_call" | custom-call | flops 5905580032 | bytes 11010048 | tf_op jit(solution)/shard_map/sandwich_last/pallas_call | solution.py:187
  67.1 19.3 %all_to_all.5.pieces = bf16[8,2,64,512]{3,2,1,0:T(8,128)(2,1)S(1)} all-to-all(bf16[8,2,64,512]{3,2,1,0:T(8,128)(2,1)S(1)} %sandwich_last.1), channel_id=1, replica_groups=mesh['slab'=2,'freq'=8,'energy'=16] {'freq'}, dimensions={0} | all-to-all | bytes 2097152 | tf_op jit(solution)/shard_map/all_to_all | solution.py:270
  86.4 1.0 %collect.1 = f32[2,2,2,64,512]{4,3,2,1,0:T(8,128)} custom-call(bf16[8,2,64,512]{3,2,1,0:T(8,128)(2,1)S(1)} %all_to_all.5.pieces), custom_call_target="tpu_custom_call" | custom-call | tf_op jit(solution)/shard_map/collect/pallas_call | solution.py:216
  (12 shorter events, 0.0 us)
Async XLA Ops:
  1.1 14.3 %collective-permute-start.1 = (bf16[256,512]{1,0:T(8,128)(2,1)S(1)}, bf16[256,512]{1,0:T(8,128)(2,1)S(1)}, u32[]{:S(2)}, u32[]{:S(2)}) collective-permute-start(bf16[256,512]{1,0:T(8,128)(2,1)S(1)} %get-tuple-element.40), channel_id=1, source_target_pairs={{32,160},{48,176},{96,224},{112,240},{160,32},{176,48},{224,96},{2... | collective-permute-start | bytes 786440 | tf_op jit(solution)/shard_map/ppermute | solution.py:249
  1.8 13.6 %collective-permute-start.2 = (bf16[256,512]{1,0:T(8,128)(2,1)S(1)}, bf16[256,512]{1,0:T(8,128)(2,1)S(1)}, u32[]{:S(2)}, u32[]{:S(2)}) collective-permute-start(bf16[256,512]{1,0:T(8,128)(2,1)S(1)} %get-tuple-element.39), channel_id=1, source_target_pairs={{0,160},{16,176},{64,224},{80,240},{128,32},{144,48},{192,96},{208... | collective-permute-start | bytes 786440 | tf_op jit(solution)/shard_map/ppermute | solution.py:250
  11.0 4.3 %copy-start = (f32[2]{0:T(128)S(1)}, f32[2]{0:T(128)}, u32[]{:S(2)}) copy-start(f32[2]{0:T(128)} %weight.1) | copy-start | bytes 28
  11.1 17.0 %collective-permute-start = (bf16[528,512]{1,0:T(8,128)(2,1)}, bf16[528,512]{1,0:T(8,128)(2,1)S(1)}, u32[]{:S(2)}, u32[]{:S(2)}) collective-permute-start(bf16[528,512]{1,0:T(8,128)(2,1)} %get-tuple-element.22), channel_id=1, source_target_pairs={{0,64},{16,80},{32,96},{48,112},{64,0},{80,16},{96,32},{112,48},{1... | collective-permute-start | bytes 1622024 | tf_op jit(solution)/shard_map/ppermute | solution.py:231
  15.3 7.3 %copy-start.2 = (bf16[2,528,512]{2,1,0:T(8,128)(2,1)S(1)}, bf16[2,528,512]{2,1,0:T(8,128)(2,1)}, u32[]{:S(2)}) copy-start(bf16[2,528,512]{2,1,0:T(8,128)(2,1)} %get-tuple-element.34.home) | copy-start | bytes 3244036
  16.1 44.1 %copy-start.1 = (bf16[2,2,2,512,512]{4,3,2,1,0:T(8,128)(2,1)S(1)}, bf16[2,2,2,512,512]{4,3,2,1,0:T(8,128)(2,1)}, u32[]{:S(2)}) copy-start(bf16[2,2,2,512,512]{4,3,2,1,0:T(8,128)(2,1)} %retarded.1) | copy-start | bytes 12582916
  16.1 19.5 %collective-permute-start.4 = (bf16[512,512]{1,0:T(8,128)(2,1)S(1)}, bf16[512,512]{1,0:T(8,128)(2,1)S(1)}, u32[]{:S(2)}, u32[]{:S(2)}) collective-permute-start(bf16[512,512]{1,0:T(8,128)(2,1)S(1)} %mix.1), channel_id=1, source_target_pairs={{1,16},{2,17},{3,18},{4,19},{5,20},{6,21},{7,22},{8,23},{9,24},{10... | collective-permute-start | bytes 1572872 | tf_op jit(solution)/shard_map/ppermute | solution.py:255
  22.6 29.5 %collective-permute-start.8 = (bf16[2,528,512]{2,1,0:T(8,128)(2,1)S(1)}, bf16[2,528,512]{2,1,0:T(8,128)(2,1)S(1)}, u32[]{:S(2)}, u32[]{:S(2)}) collective-permute-start(bf16[2,528,512]{2,1,0:T(8,128)(2,1)S(1)} %copy-done.2), channel_id=1, source_target_pairs={{0,32},{16,48},{32,0},{48,16},{64,96},{80,112},{96,64},{112,80},{1... | collective-permute-start | bytes 3244040 | tf_op jit(solution)/shard_map/ppermute | solution.py:231
  23.1 29.5 %collective-permute-start.9 = (bf16[2,528,512]{2,1,0:T(8,128)(2,1)S(1)}, bf16[2,528,512]{2,1,0:T(8,128)(2,1)S(1)}, u32[]{:S(2)}, u32[]{:S(2)}) collective-permute-start(bf16[2,528,512]{2,1,0:T(8,128)(2,1)S(1)} %copy-done.2), channel_id=1, source_target_pairs={{0,96},{16,112},{32,64},{48,80},{64,32},{80,48},{96,0},{112,16},{1... | collective-permute-start | bytes 3244040 | tf_op jit(solution)/shard_map/ppermute | solution.py:231
  28.1 24.1 %collective-permute-start.3 = (bf16[528,512]{1,0:T(8,128)(2,1)S(1)}, bf16[528,512]{1,0:T(8,128)(2,1)S(1)}, u32[]{:S(2)}, u32[]{:S(2)}) collective-permute-start(bf16[528,512]{1,0:T(8,128)(2,1)S(1)} %collective-permute-done.half), channel_id=1, source_target_pairs={{0,4},{1,5},{2,6},{3,7},{4,0},{5,1},{6,2},{7,3},{8,12},{9,13},{10,... | collective-permute-start | bytes 1622024 | tf_op jit(solution)/shard_map/ppermute | solution.py:259
  35.6 16.5 %collective-permute-start.5 = (bf16[512,512]{1,0:T(8,128)(2,1)S(1)}, bf16[512,512]{1,0:T(8,128)(2,1)S(1)}, u32[]{:S(2)}, u32[]{:S(2)}) collective-permute-start(bf16[512,512]{1,0:T(8,128)(2,1)S(1)} %collective-permute-done.4.near), channel_id=1, source_target_pairs={{0,16},{16,0},{32,48},{48,32},{64,80},{80,64},{96,112},{112,96},{1... | collective-permute-start | bytes 1572872 | tf_op jit(solution)/shard_map/ppermute | solution.py:231
  35.6 17.1 %collective-permute-start.7 = (bf16[512,512]{1,0:T(8,128)(2,1)S(1)}, bf16[512,512]{1,0:T(8,128)(2,1)S(1)}, u32[]{:S(2)}, u32[]{:S(2)}) collective-permute-start(bf16[512,512]{1,0:T(8,128)(2,1)S(1)} %mix.1), channel_id=1, source_target_pairs={{0,1},{1,2},{2,3},{3,4},{4,5},{5,6},{6,7},{7,8},{8,9},{9,10},{10,1... | collective-permute-start | bytes 1572872 | tf_op jit(solution)/shard_map/ppermute | solution.py:258
  52.1 1.9 %collective-permute-start.6 = (bf16[512,512]{1,0:T(8,128)(2,1)S(1)}, bf16[512,512]{1,0:T(8,128)(2,1)S(1)}, u32[]{:S(2)}, u32[]{:S(2)}) collective-permute-start(bf16[512,512]{1,0:T(8,128)(2,1)S(1)} %mix.1), channel_id=1, source_target_pairs={{0,16},{16,0},{32,48},{48,32},{64,80},{80,64},{96,112},{112,96},{1... | collective-permute-start | bytes 1572872 | tf_op jit(solution)/shard_map/ppermute | solution.py:231
  52.1 8.1 %collective-permute-start.11 = (bf16[2,528,512]{2,1,0:T(8,128)(2,1)S(1)}, bf16[2,528,512]{2,1,0:T(8,128)(2,1)S(1)}, u32[]{:S(2)}, u32[]{:S(2)}) collective-permute-start(bf16[2,528,512]{2,1,0:T(8,128)(2,1)S(1)} %collective-permute-done.8.c1), channel_id=1, source_target_pairs={{0,16},{16,0},{32,48},{48,32},{64,80},{80,64},{96,112},{112,96},{1... | collective-permute-start | bytes 3244040 | tf_op jit(solution)/shard_map/ppermute | solution.py:231
  52.6 7.6 %collective-permute-start.12 = (bf16[2,528,512]{2,1,0:T(8,128)(2,1)S(1)}, bf16[2,528,512]{2,1,0:T(8,128)(2,1)S(1)}, u32[]{:S(2)}, u32[]{:S(2)}) collective-permute-start(bf16[2,528,512]{2,1,0:T(8,128)(2,1)S(1)} %collective-permute-done.9.c3), channel_id=1, source_target_pairs={{0,16},{16,0},{32,48},{48,32},{64,80},{80,64},{96,112},{112,96},{1... | collective-permute-start | bytes 3244040 | tf_op jit(solution)/shard_map/ppermute | solution.py:231
  54.0 6.2 %collective-permute-start.10 = (bf16[2,528,512]{2,1,0:T(8,128)(2,1)S(1)}, bf16[2,528,512]{2,1,0:T(8,128)(2,1)S(1)}, u32[]{:S(2)}, u32[]{:S(2)}) collective-permute-start(bf16[2,528,512]{2,1,0:T(8,128)(2,1)S(1)} %copy-done.2), channel_id=1, source_target_pairs={{0,16},{16,0},{32,48},{48,32},{64,80},{80,64},{96,112},{112,96},{1... | collective-permute-start | bytes 3244040 | tf_op jit(solution)/shard_map/ppermute | solution.py:231
  54.2 5.5 %collective-permute-start.13 = (bf16[528,512]{1,0:T(8,128)(2,1)S(1)}, bf16[528,512]{1,0:T(8,128)(2,1)S(1)}, u32[]{:S(2)}, u32[]{:S(2)}) collective-permute-start(bf16[528,512]{1,0:T(8,128)(2,1)S(1)} %collective-permute-done.half), channel_id=1, source_target_pairs={{0,16},{16,0},{32,48},{48,32},{64,80},{80,64},{96,112},{112,96},{1... | collective-permute-start | bytes 1622024 | tf_op jit(solution)/shard_map/ppermute | solution.py:231
  54.5 5.7 %collective-permute-start.14 = (bf16[528,512]{1,0:T(8,128)(2,1)S(1)}, bf16[528,512]{1,0:T(8,128)(2,1)S(1)}, u32[]{:S(2)}, u32[]{:S(2)}) collective-permute-start(bf16[528,512]{1,0:T(8,128)(2,1)S(1)} %collective-permute-done.3.other), channel_id=1, source_target_pairs={{0,16},{16,0},{32,48},{48,32},{64,80},{80,64},{96,112},{112,96},{1... | collective-permute-start | bytes 1622024 | tf_op jit(solution)/shard_map/ppermute | solution.py:231

commit v13 on v11

--- a/solution.py
+++ b/solution.py
@@ -247,17 +247,18 @@
     lower = [(s * 8 + (d ^ 2), (1 - s) * 8 + d) for s in range(2) for d in odd]
     rim = lesser[k, 1 - b, c]
     top = lax.ppermute(rim[: NO // 2], ("slab", "freq"), upper)
-    bottom = lax.ppermute(rim[NO // 2 :], ("slab", "freq"), lower)
     packed, part = prepare(occupations, offsets, coupling)
+    last, part = lax.optimization_barrier((rim[NO // 2 :], part))
+    bottom = lax.ppermute(last, ("slab", "freq"), lower)
     half = flip(part, 4)
     mixed = mix(intersection, mine, pair, top, bottom)
     mixed, packed = lax.optimization_barrier((mixed, packed))
     near = lax.ppermute(mixed, ("freq", "energy"), near_pairs)
     far = lax.ppermute(mixed, ("freq", "energy"), far_pairs)
     c1, c3 = flip(packed, 2), flip(packed, 6)
-    near, mixed = lax.optimization_barrier((near, mixed))
+    other = lax.ppermute(half, "energy", [(e, e ^ 4) for e in range(count)])
+    near, mixed, other = lax.optimization_barrier((near, mixed, other))
     own, shared = flip(mixed, 1), flip(near, 1)
-    other = lax.ppermute(half, "energy", [(e, e ^ 4) for e in range(count)])
     own, shared, far, packed, half, other = lax.optimization_barrier(
         (own, shared, far, packed, half, other)
     )

time: 87.4 us -> 94.8 us (1.085)
  waiting for transfers between devices: 25.9 us -> 33.9 us
    ppermute x10, waiting for transfers between devices: 3.28 us -> 8.52 us  [flip(): return lax.ppermute(x, 'freq', [(d, d ^ bits) for d in range(8)])]
    ppermute x1, waiting for transfers between devices: 17.1 us -> 22.1 us  [shards(): near = lax.ppermute(mixed, ('freq', 'energy'), near_pairs)]
    ppermute x10, starting transfers between devices: 5.47 us -> 9.7 us  [flip(): return lax.ppermute(x, 'freq', [(d, d ^ bits) for d in range(8)])]
    ppermute x1, starting transfers between devices: 6.19 us -> 2.13 us  [shards(): bottom = lax.ppermute(last, ('slab', 'freq'), lower)]
    ppermute x1, waiting for transfers between devices: 0.01 us -> 3.3 us  [shards(): bottom = lax.ppermute(last, ('slab', 'freq'), lower)]
    ppermute x1, waiting for transfers between devices: 3.08 us -> 0.01 us  [shards(): other = lax.ppermute(half, 'energy', [(e, e ^ 4) for e in range(count)])]
    ppermute x1, waiting for transfers between devices: 2.47 us -> 0.01 us  [shards(): far = lax.ppermute(mixed, ('freq', 'energy'), far_pairs)]
    ppermute x1, starting transfers between devices: 6.15 us -> 5.07 us  [shards(): near = lax.ppermute(mixed, ('freq', 'energy'), near_pairs)]
  transfers between devices with their start and end apart: 15 -> 15, of which waited for: 6 -> 6; matrix products, arithmetic and copies ran while one was open for 1% -> 1% of each run, Pallas kernels for 10% -> 6%
where the time goes in v13:
time: 94.8 us; the launch traced here: 94.1 us
  waiting for transfers between devices  33.9 us (36%)
  starting transfers between devices  20.4 us (22%)
  blocking collectives  20.4 us (22%)
  Pallas kernels  16.7 us (18%)
  local copies, waits for them, and re-layouts  2.37 us (2%)
    ppermute x1, waiting for transfers between devices, shards(): near = lax.ppermute(mixed, ('freq', 'energy'), near_pairs)  22.1 us
    all_to_all x1, blocking collectives, shards(): return collect(lax.all_to_all(pieces, 'freq', 0, 0))  20.4 us
    ppermute x10, starting transfers between devices, flip(): return lax.ppermute(x, 'freq', [(d, d ^ bits) for d in range(8)])  9.7 us
    ppermute x10, waiting for transfers between devices, flip(): return lax.ppermute(x, 'freq', [(d, d ^ bits) for d in range(8)])  8.52 us
    pallas_call x1, Pallas kernels, sandwich_last(): pl.pallas_call(last_kernel, out_shape=shape((8, 2, ROWS, NO), BF16), in_s...  6.84 us
    ppermute x1, starting transfers between devices, shards(): near = lax.ppermute(mixed, ('freq', 'energy'), near_pairs)  5.07 us
    pallas_call x1, Pallas kernels, sandwich_first(): pl.pallas_call(first_kernel, out_shape=[shape((NO, NO), F32), shape((4, N...  4.99 us
    ppermute x1, waiting for transfers between devices, shards(): bottom = lax.ppermute(last, ('slab', 'freq'), lower)  3.3 us
  transfers between devices with their start and end apart: 15, of which 6 were waited for; matrix products, arithmetic and copies ran while one was open for 1% of the time, Pallas kernels for 6%

profile of v13, /device:TPU:38, one launch (start us, length us, event | category | flops | bytes accessed | tf_op | source)
XLA Modules:
  0.0 94.1 jit_solution(4363899444287204784)
XLA Ops:
  0.0 3.1 %prepare.1 = (bf16[2,528,512]{2,1,0:T(8,128)(2,1)}, bf16[528,512]{1,0:T(8,128)(2,1)}) custom-call(f32[2]{0:T(128)} %occupations.1, s32[2]{0:T(128)} %offsets.1, bf16[2,512,512]{2,1,0:T(8,128)(2,1)} %coupling.1), custom_call_target="tpu_custom_call" | custom-call | tf_op jit(solution)/shard_map/prepare/pallas_call | solution.py:71
  3.1 1.1 %dynamic-slice_bitcast_fusion.2 = (bf16[256,512]{1,0:T(8,128)(2,1)S(1)}, bf16[256,512]{1,0:T(8,128)(2,1)S(1)}) fusion(bf16[2,2,2,512,512]{4,3,2,1,0:T(8,128)(2,1)} %param.6, s32[]{:T(128)S(6)} %select_n.19, s32[]{:T(128)S(6)} %select_n.23, s32[]{:T(128)S(6)} %select_n.21, s32[]{:T(128)S(6)} %add.26), kind=kLoop, calls=%fused_computation.2 | loop fusion | bytes 1048592 | tf_op jit(solution)/shard_map/slice | solution.py:251
  4.2 0.0 copy-start
  4.2 3.3 %collective-permute-start.3 = (bf16[528,512]{1,0:T(8,128)(2,1)}, bf16[528,512]{1,0:T(8,128)(2,1)S(1)}, u32[]{:S(2)}, u32[]{:S(2)}) collective-permute-start(bf16[528,512]{1,0:T(8,128)(2,1)} %get-tuple-element.26), channel_id=1, source_target_pairs={{0,64},{16,80},{32,96},{48,112},{64,0},{80,16},{96,32},{112,48},{1... | collective-permute-start | bytes 1622024 | tf_op jit(solution)/shard_map/ppermute | solution.py:231
  7.5 2.1 %collective-permute-start.1 = (bf16[256,512]{1,0:T(8,128)(2,1)S(1)}, bf16[256,512]{1,0:T(8,128)(2,1)S(1)}, u32[]{:S(2)}, u32[]{:S(2)}) collective-permute-start(bf16[256,512]{1,0:T(8,128)(2,1)S(1)} %get-tuple-element.23), channel_id=1, source_target_pairs={{0,160},{16,176},{64,224},{80,240},{128,32},{144,48},{192,96},{208... | collective-permute-start | bytes 786440 | tf_op jit(solution)/shard_map/ppermute | solution.py:252
  9.6 0.7 collective-permute-start
  10.3 1.3 %dynamic-slice_bitcast_fusion = (bf16[512,512]{1,0:T(8,128)(2,1)S(1)}, bf16[512,512]{1,0:T(8,128)(2,1)S(1)}) fusion(bf16[2,2,2,512,512]{4,3,2,1,0:T(8,128)(2,1)} %param.6, s32[]{:T(128)S(6)} %select_n.19, s32[]{:T(128)S(6)} %select_n.22, s32[]{:T(128)S(6)} %select_n.21, s32[]{:T(128)S(6)} %select_n.20), kind=kLoop, calls=%fused_computation | loop fusion | bytes 2097168 | tf_op jit(solution)/shard_map/squeeze | solution.py:244
  11.6 3.3 %collective-permute-done.1.bottom = bf16[256,512]{1,0:T(8,128)(2,1)S(1)} collective-permute-done((bf16[256,512]{1,0:T(8,128)(2,1)S(1)}, bf16[256,512]{1,0:T(8,128)(2,1)S(1)}, u32[]{:S(2)}, u32[]{:S(2)}) %collective-permute-start.1) | collective-permute-done | bytes 262176 | tf_op jit(solution)/shard_map/ppermute | solution.py:252
  14.9 0.8 mix.1
  15.7 0.0 copy-start.1
  15.7 4.3 %collective-permute-start.8 = (bf16[2,528,512]{2,1,0:T(8,128)(2,1)S(1)}, bf16[2,528,512]{2,1,0:T(8,128)(2,1)S(1)}, u32[]{:S(2)}, u32[]{:S(2)}) collective-permute-start(bf16[2,528,512]{2,1,0:T(8,128)(2,1)S(1)} %copy-done.2), channel_id=1, source_target_pairs={{0,32},{16,48},{32,0},{48,16},{64,96},{80,112},{96,64},{112,80},{1... | collective-permute-start | bytes 3244040 | tf_op jit(solution)/shard_map/ppermute | solution.py:231
  20.0 0.5 collective-permute-start.9
  20.5 6.3 %collective-permute-done.3.half = bf16[528,512]{1,0:T(8,128)(2,1)S(1)} collective-permute-done((bf16[528,512]{1,0:T(8,128)(2,1)}, bf16[528,512]{1,0:T(8,128)(2,1)S(1)}, u32[]{:S(2)}, u32[]{:S(2)}) %collective-permute-start.3) | collective-permute-done | bytes 540704 | tf_op jit(solution)/shard_map/ppermute | solution.py:231
  26.8 0.8 collective-permute-start.4
  27.6 5.1 %collective-permute-start.2 = (bf16[512,512]{1,0:T(8,128)(2,1)S(1)}, bf16[512,512]{1,0:T(8,128)(2,1)S(1)}, u32[]{:S(2)}, u32[]{:S(2)}) collective-permute-start(bf16[512,512]{1,0:T(8,128)(2,1)S(1)} %mix.1), channel_id=1, source_target_pairs={{1,16},{2,17},{3,18},{4,19},{5,20},{6,21},{7,22},{8,23},{9,24},{10... | collective-permute-start | bytes 1572872 | tf_op jit(solution)/shard_map/ppermute | solution.py:256
  32.7 2.0 %collective-permute-start.7 = (bf16[512,512]{1,0:T(8,128)(2,1)S(1)}, bf16[512,512]{1,0:T(8,128)(2,1)S(1)}, u32[]{:S(2)}, u32[]{:S(2)}) collective-permute-start(bf16[512,512]{1,0:T(8,128)(2,1)S(1)} %mix.1), channel_id=1, source_target_pairs={{0,1},{1,2},{2,3},{3,4},{4,5},{5,6},{6,7},{7,8},{8,9},{9,10},{10,1... | collective-permute-start | bytes 1572872 | tf_op jit(solution)/shard_map/ppermute | solution.py:257
  34.7 22.1 %collective-permute-done.2.near = bf16[512,512]{1,0:T(8,128)(2,1)S(1)} collective-permute-done((bf16[512,512]{1,0:T(8,128)(2,1)S(1)}, bf16[512,512]{1,0:T(8,128)(2,1)S(1)}, u32[]{:S(2)}, u32[]{:S(2)}) %collective-permute-start.2) | collective-permute-done | bytes 524320 | tf_op jit(solution)/shard_map/ppermute | solution.py:256
  56.9 0.5 collective-permute-start.6
  57.4 0.0 collective-permute-done.8.c1
  57.4 0.0 collective-permute-start.11
  57.4 0.0 collective-permute-done.9.c3
  57.4 0.5 collective-permute-start.12
  57.9 0.9 collective-permute-done.5.own
  58.8 0.7 collective-permute-done.6.shared
  59.5 0.1 collective-permute-start.10
  59.7 0.4 collective-permute-start.13
  60.0 0.1 collective-permute-start.14
  60.2 5.0 %sandwich_first.1 = (f32[512,512]{1,0:T(8,128)S(1)}, bf16[4,512,512]{2,1,0:T(8,128)(2,1)S(1)}) custom-call(bf16[512,512]{1,0:T(8,128)(2,1)S(1)} %collective-permute-done.5.own, bf16[512,512]{1,0:T(8,128)(2,1)S(1)} %collective-permute-done.2.near, bf16[512,512]{1,0:T(8,128)(2,1)S(1)} %collective-permute-done.6.shared, ...), custom_call_target="tpu_custom_call" | custom-call | flops 4294967296 | bytes 9437184 | tf_op jit(solution)/shard_map/sandwich_first/pallas_call | solution.py:174
  65.2 0.5 collective-permute-done.14.other
  65.7 6.8 %sandwich_last.1 = bf16[8,2,64,512]{3,2,1,0:T(8,128)(2,1)S(1)} custom-call(bf16[4,512,512]{2,1,0:T(8,128)(2,1)S(1)} %get-tuple-element.37.green, f32[512,512]{1,0:T(8,128)S(1)} %get-tuple-element.38.start, bf16[2,528,512]{2,1,0:T(8,128)(2,1)S(1)} %collective-permute-done.10.s0, bf16[2,528,512]{2,1,0:T(8,128)(2,1)S(1)} %collective-permute-done.11.s1, ...), custom_call_target="tpu_custom_call" | custom-call | flops 5905580032 | bytes 11010048 | tf_op jit(solution)/shard_map/sandwich_last/pallas_call | solution.py:187
  72.6 20.4 %all_to_all.5.pieces = bf16[8,2,64,512]{3,2,1,0:T(8,128)(2,1)S(1)} all-to-all(bf16[8,2,64,512]{3,2,1,0:T(8,128)(2,1)S(1)} %sandwich_last.1), channel_id=1, replica_groups=mesh['slab'=2,'freq'=8,'energy'=16] {'freq'}, dimensions={0} | all-to-all | bytes 2097152 | tf_op jit(solution)/shard_map/all_to_all | solution.py:269
  93.0 1.0 %collect.1 = f32[2,2,2,64,512]{4,3,2,1,0:T(8,128)} custom-call(bf16[8,2,64,512]{3,2,1,0:T(8,128)(2,1)S(1)} %all_to_all.5.pieces), custom_call_target="tpu_custom_call" | custom-call | tf_op jit(solution)/shard_map/collect/pallas_call | solution.py:216
  (12 shorter events, 0.0 us)
Async XLA Ops:
  4.2 10.7 %copy-start = (f32[2]{0:T(128)S(1)}, f32[2]{0:T(128)}, u32[]{:S(2)}) copy-start(f32[2]{0:T(128)} %weight.1) | copy-start | bytes 28
  4.2 22.6 %collective-permute-start.3 = (bf16[528,512]{1,0:T(8,128)(2,1)}, bf16[528,512]{1,0:T(8,128)(2,1)S(1)}, u32[]{:S(2)}, u32[]{:S(2)}) collective-permute-start(bf16[528,512]{1,0:T(8,128)(2,1)} %get-tuple-element.26), channel_id=1, source_target_pairs={{0,64},{16,80},{32,96},{48,112},{64,0},{80,16},{96,32},{112,48},{1... | collective-permute-start | bytes 1622024 | tf_op jit(solution)/shard_map/ppermute | solution.py:231
  7.5 7.4 %collective-permute-start.1 = (bf16[256,512]{1,0:T(8,128)(2,1)S(1)}, bf16[256,512]{1,0:T(8,128)(2,1)S(1)}, u32[]{:S(2)}, u32[]{:S(2)}) collective-permute-start(bf16[256,512]{1,0:T(8,128)(2,1)S(1)} %get-tuple-element.23), channel_id=1, source_target_pairs={{0,160},{16,176},{64,224},{80,240},{128,32},{144,48},{192,96},{208... | collective-permute-start | bytes 786440 | tf_op jit(solution)/shard_map/ppermute | solution.py:252
  9.6 5.3 %collective-permute-start = (bf16[256,512]{1,0:T(8,128)(2,1)S(1)}, bf16[256,512]{1,0:T(8,128)(2,1)S(1)}, u32[]{:S(2)}, u32[]{:S(2)}) collective-permute-start(bf16[256,512]{1,0:T(8,128)(2,1)S(1)} %get-tuple-element.40), channel_id=1, source_target_pairs={{32,160},{48,176},{96,224},{112,240},{160,32},{176,48},{224,96},{2... | collective-permute-start | bytes 786440 | tf_op jit(solution)/shard_map/ppermute | solution.py:249
  11.6 4.1 %copy-start.2 = (bf16[2,528,512]{2,1,0:T(8,128)(2,1)S(1)}, bf16[2,528,512]{2,1,0:T(8,128)(2,1)}, u32[]{:S(2)}) copy-start(bf16[2,528,512]{2,1,0:T(8,128)(2,1)} %get-tuple-element.34.home) | copy-start | bytes 3244036
  15.7 50.0 %copy-start.1 = (bf16[2,2,2,512,512]{4,3,2,1,0:T(8,128)(2,1)S(1)}, bf16[2,2,2,512,512]{4,3,2,1,0:T(8,128)(2,1)}, u32[]{:S(2)}) copy-start(bf16[2,2,2,512,512]{4,3,2,1,0:T(8,128)(2,1)} %retarded.1) | copy-start | bytes 12582916
  15.7 41.7 %collective-permute-start.8 = (bf16[2,528,512]{2,1,0:T(8,128)(2,1)S(1)}, bf16[2,528,512]{2,1,0:T(8,128)(2,1)S(1)}, u32[]{:S(2)}, u32[]{:S(2)}) collective-permute-start(bf16[2,528,512]{2,1,0:T(8,128)(2,1)S(1)} %copy-done.2), channel_id=1, source_target_pairs={{0,32},{16,48},{32,0},{48,16},{64,96},{80,112},{96,64},{112,80},{1... | collective-permute-start | bytes 3244040 | tf_op jit(solution)/shard_map/ppermute | solution.py:231
  20.0 37.4 %collective-permute-start.9 = (bf16[2,528,512]{2,1,0:T(8,128)(2,1)S(1)}, bf16[2,528,512]{2,1,0:T(8,128)(2,1)S(1)}, u32[]{:S(2)}, u32[]{:S(2)}) collective-permute-start(bf16[2,528,512]{2,1,0:T(8,128)(2,1)S(1)} %copy-done.2), channel_id=1, source_target_pairs={{0,96},{16,112},{32,64},{48,80},{64,32},{80,48},{96,0},{112,16},{1... | collective-permute-start | bytes 3244040 | tf_op jit(solution)/shard_map/ppermute | solution.py:231
  26.8 30.1 %collective-permute-start.4 = (bf16[528,512]{1,0:T(8,128)(2,1)S(1)}, bf16[528,512]{1,0:T(8,128)(2,1)S(1)}, u32[]{:S(2)}, u32[]{:S(2)}) collective-permute-start(bf16[528,512]{1,0:T(8,128)(2,1)S(1)} %collective-permute-done.3.half), channel_id=1, source_target_pairs={{0,4},{1,5},{2,6},{3,7},{4,0},{5,1},{6,2},{7,3},{8,12},{9,13},{10,... | collective-permute-start | bytes 1622024 | tf_op jit(solution)/shard_map/ppermute | solution.py:259
  27.6 29.2 %collective-permute-start.2 = (bf16[512,512]{1,0:T(8,128)(2,1)S(1)}, bf16[512,512]{1,0:T(8,128)(2,1)S(1)}, u32[]{:S(2)}, u32[]{:S(2)}) collective-permute-start(bf16[512,512]{1,0:T(8,128)(2,1)S(1)} %mix.1), channel_id=1, source_target_pairs={{1,16},{2,17},{3,18},{4,19},{5,20},{6,21},{7,22},{8,23},{9,24},{10... | collective-permute-start | bytes 1572872 | tf_op jit(solution)/shard_map/ppermute | solution.py:256
  32.7 25.2 %collective-permute-start.7 = (bf16[512,512]{1,0:T(8,128)(2,1)S(1)}, bf16[512,512]{1,0:T(8,128)(2,1)S(1)}, u32[]{:S(2)}, u32[]{:S(2)}) collective-permute-start(bf16[512,512]{1,0:T(8,128)(2,1)S(1)} %mix.1), channel_id=1, source_target_pairs={{0,1},{1,2},{2,3},{3,4},{4,5},{5,6},{6,7},{7,8},{8,9},{9,10},{10,1... | collective-permute-start | bytes 1572872 | tf_op jit(solution)/shard_map/ppermute | solution.py:257
  56.9 1.9 %collective-permute-start.5 = (bf16[512,512]{1,0:T(8,128)(2,1)S(1)}, bf16[512,512]{1,0:T(8,128)(2,1)S(1)}, u32[]{:S(2)}, u32[]{:S(2)}) collective-permute-start(bf16[512,512]{1,0:T(8,128)(2,1)S(1)} %mix.1), channel_id=1, source_target_pairs={{0,16},{16,0},{32,48},{48,32},{64,80},{80,64},{96,112},{112,96},{1... | collective-permute-start | bytes 1572872 | tf_op jit(solution)/shard_map/ppermute | solution.py:231
  56.9 2.7 %collective-permute-start.6 = (bf16[512,512]{1,0:T(8,128)(2,1)S(1)}, bf16[512,512]{1,0:T(8,128)(2,1)S(1)}, u32[]{:S(2)}, u32[]{:S(2)}) collective-permute-start(bf16[512,512]{1,0:T(8,128)(2,1)S(1)} %collective-permute-done.2.near), channel_id=1, source_target_pairs={{0,16},{16,0},{32,48},{48,32},{64,80},{80,64},{96,112},{112,96},{1... | collective-permute-start | bytes 1572872 | tf_op jit(solution)/shard_map/ppermute | solution.py:231
  57.4 8.3 %collective-permute-start.11 = (bf16[2,528,512]{2,1,0:T(8,128)(2,1)S(1)}, bf16[2,528,512]{2,1,0:T(8,128)(2,1)S(1)}, u32[]{:S(2)}, u32[]{:S(2)}) collective-permute-start(bf16[2,528,512]{2,1,0:T(8,128)(2,1)S(1)} %collective-permute-done.8.c1), channel_id=1, source_target_pairs={{0,16},{16,0},{32,48},{48,32},{64,80},{80,64},{96,112},{112,96},{1... | collective-permute-start | bytes 3244040 | tf_op jit(solution)/shard_map/ppermute | solution.py:231
  57.4 8.3 %collective-permute-start.12 = (bf16[2,528,512]{2,1,0:T(8,128)(2,1)S(1)}, bf16[2,528,512]{2,1,0:T(8,128)(2,1)S(1)}, u32[]{:S(2)}, u32[]{:S(2)}) collective-permute-start(bf16[2,528,512]{2,1,0:T(8,128)(2,1)S(1)} %collective-permute-done.9.c3), channel_id=1, source_target_pairs={{0,16},{16,0},{32,48},{48,32},{64,80},{80,64},{96,112},{112,96},{1... | collective-permute-start | bytes 3244040 | tf_op jit(solution)/shard_map/ppermute | solution.py:231
  59.5 6.2 %collective-permute-start.10 = (bf16[2,528,512]{2,1,0:T(8,128)(2,1)S(1)}, bf16[2,528,512]{2,1,0:T(8,128)(2,1)S(1)}, u32[]{:S(2)}, u32[]{:S(2)}) collective-permute-start(bf16[2,528,512]{2,1,0:T(8,128)(2,1)S(1)} %copy-done.2), channel_id=1, source_target_pairs={{0,16},{16,0},{32,48},{48,32},{64,80},{80,64},{96,112},{112,96},{1... | collective-permute-start | bytes 3244040 | tf_op jit(solution)/shard_map/ppermute | solution.py:231
  59.7 5.5 %collective-permute-start.13 = (bf16[528,512]{1,0:T(8,128)(2,1)S(1)}, bf16[528,512]{1,0:T(8,128)(2,1)S(1)}, u32[]{:S(2)}, u32[]{:S(2)}) collective-permute-start(bf16[528,512]{1,0:T(8,128)(2,1)S(1)} %collective-permute-done.3.half), channel_id=1, source_target_pairs={{0,16},{16,0},{32,48},{48,32},{64,80},{80,64},{96,112},{112,96},{1... | collective-permute-start | bytes 1622024 | tf_op jit(solution)/shard_map/ppermute | solution.py:231
  60.0 5.7 %collective-permute-start.14 = (bf16[528,512]{1,0:T(8,128)(2,1)S(1)}, bf16[528,512]{1,0:T(8,128)(2,1)S(1)}, u32[]{:S(2)}, u32[]{:S(2)}) collective-permute-start(bf16[528,512]{1,0:T(8,128)(2,1)S(1)} %collective-permute-done.4.other), channel_id=1, source_target_pairs={{0,16},{16,0},{32,48},{48,32},{64,80},{80,64},{96,112},{112,96},{1... | collective-permute-start | bytes 1622024 | tf_op jit(solution)/shard_map/ppermute | solution.py:231

commit v14 on v11

--- a/solution.py
+++ b/solution.py
@@ -9,6 +9,7 @@
 NO = 512
 ROWS = 64
 TAIL = 16
+UPPER = 384
 F32 = jnp.float32
 BF16 = jnp.bfloat16
 MIB = 1 << 20
@@ -81,8 +82,7 @@
 
 def mix_kernel(weight, mine, pair, top, bottom, out):
     scale = weight[place()[2]]
-    for cross, first in ((top, 0), (bottom, NO // 2)):
-        rows = pl.ds(first, NO // 2)
+    for cross, rows in ((top, pl.ds(0, UPPER)), (bottom, pl.ds(UPPER, NO - UPPER))):
         beside = pair[rows].astype(F32) + cross[...].astype(F32)
         out[rows] = (mine[rows].astype(F32) + scale * beside).astype(BF16)
 
@@ -246,8 +246,8 @@
     upper = [(s * 8 + d, (1 - s) * 8 + d) for s in range(2) for d in odd]
     lower = [(s * 8 + (d ^ 2), (1 - s) * 8 + d) for s in range(2) for d in odd]
     rim = lesser[k, 1 - b, c]
-    top = lax.ppermute(rim[: NO // 2], ("slab", "freq"), upper)
-    bottom = lax.ppermute(rim[NO // 2 :], ("slab", "freq"), lower)
+    top = lax.ppermute(rim[:UPPER], ("slab", "freq"), upper)
+    bottom = lax.ppermute(rim[UPPER:], ("slab", "freq"), lower)
     packed, part = prepare(occupations, offsets, coupling)
     half = flip(part, 4)
     mixed = mix(intersection, mine, pair, top, bottom)

time: 87.4 us -> 88.1 us (level)
    ppermute x1, waiting for transfers between devices: 2.47 us -> 1.25 us  [shards(): far = lax.ppermute(mixed, ('freq', 'energy'), far_pairs)]
    slice x1 -> x2, local copies, waits for them, and re-layouts: 1.06 us -> 1.96 us  [the longest x1 1.03 us: shards(): top = lax.ppermute(rim[:UPPER], ('slab', 'freq'), upper)]
    ppermute x10, waiting for transfers between devices: 3.28 us -> 4.16 us  [flip(): return lax.ppermute(x, 'freq', [(d, d ^ bits) for d in range(8)])]
  transfers between devices with their start and end apart: 15 -> 15, of which waited for: 6 -> 6; matrix products, arithmetic and copies ran while one was open for 1% -> 3% of each run, Pallas kernels for 10% -> 10%
where the time goes in v14:
time: 88.1 us; the launch traced here: 87.8 us
  waiting for transfers between devices  26.6 us (30%)
  starting transfers between devices  20.7 us (23%)
  blocking collectives  20.1 us (23%)
  Pallas kernels  16.7 us (19%)
  local copies, waits for them, and re-layouts  3.33 us (4%)
    all_to_all x1, blocking collectives, shards(): return collect(lax.all_to_all(pieces, 'freq', 0, 0))  20.1 us
    ppermute x1, waiting for transfers between devices, shards(): near = lax.ppermute(mixed, ('freq', 'energy'), near_pairs)  17.3 us
    pallas_call x1, Pallas kernels, sandwich_last(): pl.pallas_call(last_kernel, out_shape=shape((8, 2, ROWS, NO), BF16), in_s...  6.84 us
    ppermute x1, starting transfers between devices, shards(): bottom = lax.ppermute(rim[UPPER:], ('slab', 'freq'), lower)  6.17 us
    ppermute x1, starting transfers between devices, shards(): near = lax.ppermute(mixed, ('freq', 'energy'), near_pairs)  5.73 us
    ppermute x10, starting transfers between devices, flip(): return lax.ppermute(x, 'freq', [(d, d ^ bits) for d in range(8)])  5.38 us
    pallas_call x1, Pallas kernels, sandwich_first(): pl.pallas_call(first_kernel, out_shape=[shape((NO, NO), F32), shape((4, N...  4.99 us
    ppermute x10, waiting for transfers between devices, flip(): return lax.ppermute(x, 'freq', [(d, d ^ bits) for d in range(8)])  4.16 us
  transfers between devices with their start and end apart: 15, of which 6 were waited for; matrix products, arithmetic and copies ran while one was open for 3% of the time, Pallas kernels for 10%

profile of v14, /device:TPU:38, one launch (start us, length us, event | category | flops | bytes accessed | tf_op | source)
XLA Modules:
  0.0 87.8 jit_solution(8930782665618737699)
XLA Ops:
  0.0 1.0 %dynamic-slice_bitcast_fusion.2 = bf16[384,512]{1,0:T(8,128)(2,1)S(1)} fusion(bf16[2,2,2,512,512]{4,3,2,1,0:T(8,128)(2,1)} %param.6, s32[]{:T(128)S(6)} %select_n.19, s32[]{:T(128)S(6)} %select_n.23, s32[]{:T(128)S(6)} %select_n.21), kind=kLoop, calls=%fused_computation.2 | loop fusion | bytes 786444 | tf_op jit(solution)/shard_map/slice | solution.py:249
  1.0 0.7 collective-permute-start
  1.7 0.9 %dynamic-slice_bitcast_fusion.3 = bf16[128,512]{1,0:T(8,128)(2,1)S(1)} fusion(bf16[2,2,2,512,512]{4,3,2,1,0:T(8,128)(2,1)} %param.6, s32[]{:T(128)S(6)} %select_n.19, s32[]{:T(128)S(6)} %select_n.23, s32[]{:T(128)S(6)} %select_n.21, s32[]{:T(128)S(6)} %add.26), kind=kLoop, calls=%fused_computation.3 | loop fusion | bytes 262160 | tf_op jit(solution)/shard_map/slice | solution.py:250
  2.7 6.2 %collective-permute-start.1 = (bf16[128,512]{1,0:T(8,128)(2,1)S(1)}, bf16[128,512]{1,0:T(8,128)(2,1)S(1)}, u32[]{:S(2)}, u32[]{:S(2)}) collective-permute-start(bf16[128,512]{1,0:T(8,128)(2,1)S(1)} %dynamic-slice_bitcast_fusion.3), channel_id=1, source_target_pairs={{0,160},{16,176},{64,224},{80,240},{128,32},{144,48},{192,96},{208... | collective-permute-start | bytes 393224 | tf_op jit(solution)/shard_map/ppermute | solution.py:250
  8.8 3.1 %prepare.1 = (bf16[2,528,512]{2,1,0:T(8,128)(2,1)}, bf16[528,512]{1,0:T(8,128)(2,1)}) custom-call(f32[2]{0:T(128)} %occupations.1, s32[2]{0:T(128)} %offsets.1, bf16[2,512,512]{2,1,0:T(8,128)(2,1)} %coupling.1), custom_call_target="tpu_custom_call" | custom-call | tf_op jit(solution)/shard_map/prepare/pallas_call | solution.py:72
  11.9 3.0 %collective-permute-start.6 = (bf16[528,512]{1,0:T(8,128)(2,1)}, bf16[528,512]{1,0:T(8,128)(2,1)S(1)}, u32[]{:S(2)}, u32[]{:S(2)}) collective-permute-start(bf16[528,512]{1,0:T(8,128)(2,1)} %get-tuple-element.24), channel_id=1, source_target_pairs={{0,64},{16,80},{32,96},{48,112},{64,0},{80,16},{96,32},{112,48},{1... | collective-permute-start | bytes 1622024 | tf_op jit(solution)/shard_map/ppermute | solution.py:231
  14.9 1.4 %dynamic-slice_bitcast_fusion = (bf16[512,512]{1,0:T(8,128)(2,1)S(1)}, bf16[512,512]{1,0:T(8,128)(2,1)S(1)}) fusion(bf16[2,2,2,512,512]{4,3,2,1,0:T(8,128)(2,1)} %param.6, s32[]{:T(128)S(6)} %select_n.19, s32[]{:T(128)S(6)} %select_n.22, s32[]{:T(128)S(6)} %select_n.21, s32[]{:T(128)S(6)} %select_n.20), kind=kLoop, calls=%fused_computation | loop fusion | bytes 2097168 | tf_op jit(solution)/shard_map/squeeze | solution.py:244
  16.3 0.0 collective-permute-done.1.bottom
  16.3 0.0 collective-permute-done.top
  16.3 0.8 mix.1
  17.1 0.0 copy-start.1
  17.1 0.1 collective-permute-start.8
  17.2 1.2 %collective-permute-start.9 = (bf16[2,528,512]{2,1,0:T(8,128)(2,1)S(1)}, bf16[2,528,512]{2,1,0:T(8,128)(2,1)S(1)}, u32[]{:S(2)}, u32[]{:S(2)}) collective-permute-start(bf16[2,528,512]{2,1,0:T(8,128)(2,1)S(1)} %copy-done.2), channel_id=1, source_target_pairs={{0,96},{16,112},{32,64},{48,80},{64,32},{80,48},{96,0},{112,16},{1... | collective-permute-start | bytes 3244040 | tf_op jit(solution)/shard_map/ppermute | solution.py:231
  18.4 5.7 %collective-permute-start.2 = (bf16[512,512]{1,0:T(8,128)(2,1)S(1)}, bf16[512,512]{1,0:T(8,128)(2,1)S(1)}, u32[]{:S(2)}, u32[]{:S(2)}) collective-permute-start(bf16[512,512]{1,0:T(8,128)(2,1)S(1)} %mix.1), channel_id=1, source_target_pairs={{1,16},{2,17},{3,18},{4,19},{5,20},{6,21},{7,22},{8,23},{9,24},{10... | collective-permute-start | bytes 1572872 | tf_op jit(solution)/shard_map/ppermute | solution.py:255
  24.2 1.9 %collective-permute-start.5 = (bf16[512,512]{1,0:T(8,128)(2,1)S(1)}, bf16[512,512]{1,0:T(8,128)(2,1)S(1)}, u32[]{:S(2)}, u32[]{:S(2)}) collective-permute-start(bf16[512,512]{1,0:T(8,128)(2,1)S(1)} %mix.1), channel_id=1, source_target_pairs={{0,1},{1,2},{2,3},{3,4},{4,5},{5,6},{6,7},{7,8},{8,9},{9,10},{10,1... | collective-permute-start | bytes 1572872 | tf_op jit(solution)/shard_map/ppermute | solution.py:256
  26.1 2.9 %collective-permute-done.6.half = bf16[528,512]{1,0:T(8,128)(2,1)S(1)} collective-permute-done((bf16[528,512]{1,0:T(8,128)(2,1)}, bf16[528,512]{1,0:T(8,128)(2,1)S(1)}, u32[]{:S(2)}, u32[]{:S(2)}) %collective-permute-start.6) | collective-permute-done | bytes 540704 | tf_op jit(solution)/shard_map/ppermute | solution.py:231
  29.0 0.8 collective-permute-start.7
  29.8 17.3 %collective-permute-done.2.near = bf16[512,512]{1,0:T(8,128)(2,1)S(1)} collective-permute-done((bf16[512,512]{1,0:T(8,128)(2,1)S(1)}, bf16[512,512]{1,0:T(8,128)(2,1)S(1)}, u32[]{:S(2)}, u32[]{:S(2)}) %collective-permute-start.2) | collective-permute-done | bytes 524320 | tf_op jit(solution)/shard_map/ppermute | solution.py:255
  47.2 1.3 %collective-permute-done.5.far = bf16[512,512]{1,0:T(8,128)(2,1)S(1)} collective-permute-done((bf16[512,512]{1,0:T(8,128)(2,1)S(1)}, bf16[512,512]{1,0:T(8,128)(2,1)S(1)}, u32[]{:S(2)}, u32[]{:S(2)}) %collective-permute-start.5) | collective-permute-done | bytes 524320 | tf_op jit(solution)/shard_map/ppermute | solution.py:256
  48.4 3.8 %collective-permute-done.7.other = bf16[528,512]{1,0:T(8,128)(2,1)S(1)} collective-permute-done((bf16[528,512]{1,0:T(8,128)(2,1)S(1)}, bf16[528,512]{1,0:T(8,128)(2,1)S(1)}, u32[]{:S(2)}, u32[]{:S(2)}) %collective-permute-start.7) | collective-permute-done | bytes 540704 | tf_op jit(solution)/shard_map/ppermute | solution.py:260
  52.3 0.0 collective-permute-done.3.own
  52.3 0.0 collective-permute-done.4.shared
  52.3 0.5 collective-permute-start.11
  52.8 0.1 collective-permute-start.12
  52.9 0.4 collective-permute-start.13
  53.3 0.1 collective-permute-start.14
  53.4 5.0 %sandwich_first.1 = (f32[512,512]{1,0:T(8,128)S(1)}, bf16[4,512,512]{2,1,0:T(8,128)(2,1)S(1)}) custom-call(bf16[512,512]{1,0:T(8,128)(2,1)S(1)} %collective-permute-done.3.own, bf16[512,512]{1,0:T(8,128)(2,1)S(1)} %collective-permute-done.2.near, bf16[512,512]{1,0:T(8,128)(2,1)S(1)} %collective-permute-done.4.shared, ...), custom_call_target="tpu_custom_call" | custom-call | flops 4294967296 | bytes 9437184 | tf_op jit(solution)/shard_map/sandwich_first/pallas_call | solution.py:174
  58.4 0.4 collective-permute-done.13.half
  58.9 0.8 collective-permute-done.14.other
  59.6 6.8 %sandwich_last.1 = bf16[8,2,64,512]{3,2,1,0:T(8,128)(2,1)S(1)} custom-call(bf16[4,512,512]{2,1,0:T(8,128)(2,1)S(1)} %get-tuple-element.31.green, f32[512,512]{1,0:T(8,128)S(1)} %get-tuple-element.32.start, bf16[2,528,512]{2,1,0:T(8,128)(2,1)S(1)} %collective-permute-done.10.s0, bf16[2,528,512]{2,1,0:T(8,128)(2,1)S(1)} %collective-permute-done.11.s1, ...), custom_call_target="tpu_custom_call" | custom-call | flops 5905580032 | bytes 11010048 | tf_op jit(solution)/shard_map/sandwich_last/pallas_call | solution.py:187
  66.5 20.1 %all_to_all.5.pieces = bf16[8,2,64,512]{3,2,1,0:T(8,128)(2,1)S(1)} all-to-all(bf16[8,2,64,512]{3,2,1,0:T(8,128)(2,1)S(1)} %sandwich_last.1), channel_id=1, replica_groups=mesh['slab'=2,'freq'=8,'energy'=16] {'freq'}, dimensions={0} | all-to-all | bytes 2097152 | tf_op jit(solution)/shard_map/all_to_all | solution.py:268
  86.6 1.0 %collect.1 = f32[2,2,2,64,512]{4,3,2,1,0:T(8,128)} custom-call(bf16[8,2,64,512]{3,2,1,0:T(8,128)(2,1)S(1)} %all_to_all.5.pieces), custom_call_target="tpu_custom_call" | custom-call | tf_op jit(solution)/shard_map/collect/pallas_call | solution.py:216
  (13 shorter events, 0.0 us)
Async XLA Ops:
  0.0 16.3 %copy-start = (f32[2]{0:T(128)S(1)}, f32[2]{0:T(128)}, u32[]{:S(2)}) copy-start(f32[2]{0:T(128)} %weight.1) | copy-start | bytes 28
  1.0 15.3 %collective-permute-start = (bf16[384,512]{1,0:T(8,128)(2,1)S(1)}, bf16[384,512]{1,0:T(8,128)(2,1)S(1)}, u32[]{:S(2)}, u32[]{:S(2)}) collective-permute-start(bf16[384,512]{1,0:T(8,128)(2,1)S(1)} %dynamic-slice_bitcast_fusion.2), channel_id=1, source_target_pairs={{32,160},{48,176},{96,224},{112,240},{160,32},{176,48},{224,96},{2... | collective-permute-start | bytes 1179656 | tf_op jit(solution)/shard_map/ppermute | solution.py:249
  2.7 13.6 %collective-permute-start.1 = (bf16[128,512]{1,0:T(8,128)(2,1)S(1)}, bf16[128,512]{1,0:T(8,128)(2,1)S(1)}, u32[]{:S(2)}, u32[]{:S(2)}) collective-permute-start(bf16[128,512]{1,0:T(8,128)(2,1)S(1)} %dynamic-slice_bitcast_fusion.3), channel_id=1, source_target_pairs={{0,160},{16,176},{64,224},{80,240},{128,32},{144,48},{192,96},{208... | collective-permute-start | bytes 393224 | tf_op jit(solution)/shard_map/ppermute | solution.py:250
  11.9 17.1 %collective-permute-start.6 = (bf16[528,512]{1,0:T(8,128)(2,1)}, bf16[528,512]{1,0:T(8,128)(2,1)S(1)}, u32[]{:S(2)}, u32[]{:S(2)}) collective-permute-start(bf16[528,512]{1,0:T(8,128)(2,1)} %get-tuple-element.24), channel_id=1, source_target_pairs={{0,64},{16,80},{32,96},{48,112},{64,0},{80,16},{96,32},{112,48},{1... | collective-permute-start | bytes 1622024 | tf_op jit(solution)/shard_map/ppermute | solution.py:231
  14.9 2.2 %copy-start.2 = (bf16[2,528,512]{2,1,0:T(8,128)(2,1)S(1)}, bf16[2,528,512]{2,1,0:T(8,128)(2,1)}, u32[]{:S(2)}) copy-start(bf16[2,528,512]{2,1,0:T(8,128)(2,1)} %get-tuple-element.28.home) | copy-start | bytes 3244036
  17.1 42.5 %copy-start.1 = (bf16[2,2,2,512,512]{4,3,2,1,0:T(8,128)(2,1)S(1)}, bf16[2,2,2,512,512]{4,3,2,1,0:T(8,128)(2,1)}, u32[]{:S(2)}) copy-start(bf16[2,2,2,512,512]{4,3,2,1,0:T(8,128)(2,1)} %retarded.1) | copy-start | bytes 12582916
  17.1 35.2 %collective-permute-start.8 = (bf16[2,528,512]{2,1,0:T(8,128)(2,1)S(1)}, bf16[2,528,512]{2,1,0:T(8,128)(2,1)S(1)}, u32[]{:S(2)}, u32[]{:S(2)}) collective-permute-start(bf16[2,528,512]{2,1,0:T(8,128)(2,1)S(1)} %copy-done.2), channel_id=1, source_target_pairs={{0,32},{16,48},{32,0},{48,16},{64,96},{80,112},{96,64},{112,80},{1... | collective-permute-start | bytes 3244040 | tf_op jit(solution)/shard_map/ppermute | solution.py:231
  17.2 35.6 %collective-permute-start.9 = (bf16[2,528,512]{2,1,0:T(8,128)(2,1)S(1)}, bf16[2,528,512]{2,1,0:T(8,128)(2,1)S(1)}, u32[]{:S(2)}, u32[]{:S(2)}) collective-permute-start(bf16[2,528,512]{2,1,0:T(8,128)(2,1)S(1)} %copy-done.2), channel_id=1, source_target_pairs={{0,96},{16,112},{32,64},{48,80},{64,32},{80,48},{96,0},{112,16},{1... | collective-permute-start | bytes 3244040 | tf_op jit(solution)/shard_map/ppermute | solution.py:231
  18.4 28.7 %collective-permute-start.2 = (bf16[512,512]{1,0:T(8,128)(2,1)S(1)}, bf16[512,512]{1,0:T(8,128)(2,1)S(1)}, u32[]{:S(2)}, u32[]{:S(2)}) collective-permute-start(bf16[512,512]{1,0:T(8,128)(2,1)S(1)} %mix.1), channel_id=1, source_target_pairs={{1,16},{2,17},{3,18},{4,19},{5,20},{6,21},{7,22},{8,23},{9,24},{10... | collective-permute-start | bytes 1572872 | tf_op jit(solution)/shard_map/ppermute | solution.py:255
  24.2 24.3 %collective-permute-start.5 = (bf16[512,512]{1,0:T(8,128)(2,1)S(1)}, bf16[512,512]{1,0:T(8,128)(2,1)S(1)}, u32[]{:S(2)}, u32[]{:S(2)}) collective-permute-start(bf16[512,512]{1,0:T(8,128)(2,1)S(1)} %mix.1), channel_id=1, source_target_pairs={{0,1},{1,2},{2,3},{3,4},{4,5},{5,6},{6,7},{7,8},{8,9},{9,10},{10,1... | collective-permute-start | bytes 1572872 | tf_op jit(solution)/shard_map/ppermute | solution.py:256
  29.0 23.3 %collective-permute-start.7 = (bf16[528,512]{1,0:T(8,128)(2,1)S(1)}, bf16[528,512]{1,0:T(8,128)(2,1)S(1)}, u32[]{:S(2)}, u32[]{:S(2)}) collective-permute-start(bf16[528,512]{1,0:T(8,128)(2,1)S(1)} %collective-permute-done.6.half), channel_id=1, source_target_pairs={{0,4},{1,5},{2,6},{3,7},{4,0},{5,1},{6,2},{7,3},{8,12},{9,13},{10,... | collective-permute-start | bytes 1622024 | tf_op jit(solution)/shard_map/ppermute | solution.py:260
  47.2 5.1 %collective-permute-start.3 = (bf16[512,512]{1,0:T(8,128)(2,1)S(1)}, bf16[512,512]{1,0:T(8,128)(2,1)S(1)}, u32[]{:S(2)}, u32[]{:S(2)}) collective-permute-start(bf16[512,512]{1,0:T(8,128)(2,1)S(1)} %mix.1), channel_id=1, source_target_pairs={{0,16},{16,0},{32,48},{48,32},{64,80},{80,64},{96,112},{112,96},{1... | collective-permute-start | bytes 1572872 | tf_op jit(solution)/shard_map/ppermute | solution.py:231
  48.4 3.9 %collective-permute-start.4 = (bf16[512,512]{1,0:T(8,128)(2,1)S(1)}, bf16[512,512]{1,0:T(8,128)(2,1)S(1)}, u32[]{:S(2)}, u32[]{:S(2)}) collective-permute-start(bf16[512,512]{1,0:T(8,128)(2,1)S(1)} %collective-permute-done.2.near), channel_id=1, source_target_pairs={{0,16},{16,0},{32,48},{48,32},{64,80},{80,64},{96,112},{112,96},{1... | collective-permute-start | bytes 1572872 | tf_op jit(solution)/shard_map/ppermute | solution.py:231
  52.3 7.4 %collective-permute-start.10 = (bf16[2,528,512]{2,1,0:T(8,128)(2,1)S(1)}, bf16[2,528,512]{2,1,0:T(8,128)(2,1)S(1)}, u32[]{:S(2)}, u32[]{:S(2)}) collective-permute-start(bf16[2,528,512]{2,1,0:T(8,128)(2,1)S(1)} %copy-done.2), channel_id=1, source_target_pairs={{0,16},{16,0},{32,48},{48,32},{64,80},{80,64},{96,112},{112,96},{1... | collective-permute-start | bytes 3244040 | tf_op jit(solution)/shard_map/ppermute | solution.py:231
  52.3 7.3 %collective-permute-start.11 = (bf16[2,528,512]{2,1,0:T(8,128)(2,1)S(1)}, bf16[2,528,512]{2,1,0:T(8,128)(2,1)S(1)}, u32[]{:S(2)}, u32[]{:S(2)}) collective-permute-start(bf16[2,528,512]{2,1,0:T(8,128)(2,1)S(1)} %collective-permute-done.8.c1), channel_id=1, source_target_pairs={{0,16},{16,0},{32,48},{48,32},{64,80},{80,64},{96,112},{112,96},{1... | collective-permute-start | bytes 3244040 | tf_op jit(solution)/shard_map/ppermute | solution.py:231
  52.8 6.8 %collective-permute-start.12 = (bf16[2,528,512]{2,1,0:T(8,128)(2,1)S(1)}, bf16[2,528,512]{2,1,0:T(8,128)(2,1)S(1)}, u32[]{:S(2)}, u32[]{:S(2)}) collective-permute-start(bf16[2,528,512]{2,1,0:T(8,128)(2,1)S(1)} %collective-permute-done.9.c3), channel_id=1, source_target_pairs={{0,16},{16,0},{32,48},{48,32},{64,80},{80,64},{96,112},{112,96},{1... | collective-permute-start | bytes 3244040 | tf_op jit(solution)/shard_map/ppermute | solution.py:231
  52.9 6.0 %collective-permute-start.13 = (bf16[528,512]{1,0:T(8,128)(2,1)S(1)}, bf16[528,512]{1,0:T(8,128)(2,1)S(1)}, u32[]{:S(2)}, u32[]{:S(2)}) collective-permute-start(bf16[528,512]{1,0:T(8,128)(2,1)S(1)} %collective-permute-done.6.half), channel_id=1, source_target_pairs={{0,16},{16,0},{32,48},{48,32},{64,80},{80,64},{96,112},{112,96},{1... | collective-permute-start | bytes 1622024 | tf_op jit(solution)/shard_map/ppermute | solution.py:231
  53.3 6.3 %collective-permute-start.14 = (bf16[528,512]{1,0:T(8,128)(2,1)S(1)}, bf16[528,512]{1,0:T(8,128)(2,1)S(1)}, u32[]{:S(2)}, u32[]{:S(2)}) collective-permute-start(bf16[528,512]{1,0:T(8,128)(2,1)S(1)} %collective-permute-done.7.other), channel_id=1, source_target_pairs={{0,16},{16,0},{32,48},{48,32},{64,80},{80,64},{96,112},{112,96},{1... | collective-permute-start | bytes 1622024 | tf_op jit(solution)/shard_map/ppermute | solution.py:231
